TPU v7x, 32 devices: a whole 2x2x4 slice. The times are simulated.
32 devices in a mesh: seq: 8 (over y, x, core), tp: 4 (over z).
Axes of the slice: x: 2, y: 2, z: 4, core: 2. Of those that a mesh axis runs over, the one named last changes fastest.
Arguments:
- tokens: bfloat16 [1, 4096, 2048], P(None, 'seq'), may hold values from -6 to 6
- gain_attn: float32 [2048], replicated, may hold values from 0.5 to 1.5
- w_query: bfloat16 [2048, 2048], P(None, 'tp'), may hold values from -0.21875 to 0.21875
- w_key: bfloat16 [2048, 2048], P(None, 'tp'), may hold values from -0.21875 to 0.21875
- w_value: bfloat16 [2048, 2048], P(None, 'tp'), may hold values from -0.125 to 0.125
- w_out: bfloat16 [2048, 2048], P('tp'), may hold values from -0.25 to 0.25
- gain_ffn: float32 [2048], replicated, may hold values from 0.5 to 1.5
- w_gate: bfloat16 [2048, 8192], P(None, 'tp'), may hold values from -0.125 to 0.125
- w_up: bfloat16 [2048, 8192], P(None, 'tp'), may hold values from -0.125 to 0.125
- w_down: bfloat16 [8192, 2048], P('tp'), may hold values from -0.0625 to 0.0625
- cotangent: bfloat16 [1, 4096, 2048], P(None, 'seq'), may hold values from -6 to 6
- doc_ids: int32 [1, 4096], replicated, may hold values from 0 to 15, never falling along the last dimension, each value on 1 to 2048 neighbouring positions
- valid: int32 [1, 4096], replicated, may hold values 0 or 1
- group_order: int32 [1, 16], replicated, may hold values from 0 to 15, each once within a row
Outputs:
- layer_out: bfloat16 [1, 4096, 2048], P(None, 'seq')
- grad_tokens: float32 [1, 4096, 2048], P(None, 'seq')
- grad_gain_attn: float32 [2048], P('seq')
- grad_query: float32 [2048, 2048], P('seq', 'tp')
- grad_key: float32 [2048, 2048], P('seq', 'tp')
- grad_value: float32 [2048, 2048], P('seq', 'tp')
- grad_out: float32 [2048, 2048], P('tp', 'seq')
- grad_gain_ffn: float32 [2048], P('seq')
- grad_gate: float32 [2048, 8192], P('seq', 'tp')
- grad_up: float32 [2048, 8192], P('seq', 'tp')
- grad_down: float32 [8192, 2048], P('tp', 'seq')
Inputs may be any that keep to these rules, and one draw needn't show every extreme that they name: `doc_ids`: document numbers never fall along a sequence; a document holds 1 to 2048 positions. `group_order`: each row is a permutation; device i of seq stores storage blocks 2 i and 2 i + 1 of every sequence.
All inputs are finite; a program needn't handle non-finite values.
Results may differ from a plain program's by a relative error of at most 0.014.
The roundings to bfloat16 on the way count: a program that leaves them out, or rounds other values in their place, can miss the bound.
Values may be sent and summed in bfloat16 or wider, within the bound.
No kernel may reach another device: no remote copies, remote signals or barrier semaphores. Data moves between devices by JAX's collectives and lax.ppermute only.
A program may use at most 320 MiB of HBM per device.

v0:
```python
import math

import jax
import jax.numpy as jnp
from jax import lax
from jax.sharding import PartitionSpec as P

HEAD_WIDTH = 128


norm_eps = 1e-05
rope_base = 10000.0


def rope_tables(places, head_size):
    half_size = head_size // 2
    freqs = rope_base ** (-jnp.arange(half_size, dtype=jnp.float32) * 2.0 / head_size)
    angles = places.astype(jnp.float32)[..., None] * freqs
    return (jnp.cos(angles), jnp.sin(angles))


def rotate(values, cosine, sine, forward):
    half_size = values.shape[-1] // 2
    first = values[..., :half_size]
    second = values[..., half_size:]
    cos_b = cosine[..., None, :]
    sin_b = sine[..., None, :]
    if forward:
        return jnp.concatenate(
            [first * cos_b - second * sin_b, second * cos_b + first * sin_b], axis=-1
        )
    return jnp.concatenate(
        [first * cos_b + second * sin_b, second * cos_b - first * sin_b], axis=-1
    )


def visible(place_q, doc_q, place_k, doc_k, live_k):
    allowed = (
        (place_k[None, :] <= place_q[:, None])
        & (doc_k[None, :] == doc_q[:, None])
        & (live_k[None, :] == 1)
    )
    return allowed.astype(jnp.float32)


def score_block(query_heads, key_heads, head_size, length):
    scores = jnp.einsum("qhe,khe->hqk", query_heads, key_heads, preferred_element_type=jnp.float32)
    return scores * (1.0 / math.sqrt(head_size)) - math.log(length)


def score_grads(query_heads, key_heads, value_heads, grad_heads, mask, head_size, length):
    sigma = jax.nn.sigmoid(score_block(query_heads, key_heads, head_size, length))
    weights = (sigma * mask).astype(jnp.bfloat16)
    grad_weights = jnp.einsum(
        "qhe,khe->hqk", grad_heads, value_heads, preferred_element_type=jnp.float32
    )
    grad_scores = (grad_weights * (sigma * (1.0 - sigma)) * mask).astype(jnp.bfloat16)
    return (weights, grad_scores)


def local(
    tokens,
    gain_attn,
    w_query,
    w_key,
    w_value,
    w_out,
    gain_ffn,
    w_gate,
    w_up,
    w_down,
    cotangent,
    doc_ids,
    valid,
    group_order,
):
    seq_count, row_count, model_width = tokens.shape
    length = doc_ids.shape[1]
    span = length // group_order.shape[1]
    head_size = HEAD_WIDTH
    local_width = w_query.shape[1]
    local_heads = local_width // head_size
    flat_rows = seq_count * row_count
    factor = 1.0 / math.sqrt(head_size)
    own_rows = lax.axis_index("seq") * row_count + jnp.arange(row_count, dtype=jnp.int32)
    all_rows = jnp.arange(length, dtype=jnp.int32)
    place_all = jnp.take(group_order, all_rows // span, axis=1) * span + (all_rows % span)[None, :]
    place_own = jnp.take(group_order, own_rows // span, axis=1) * span + (own_rows % span)[None, :]
    doc_all = jnp.take_along_axis(doc_ids, place_all, axis=1)
    live_all = jnp.take_along_axis(valid, place_all, axis=1)
    doc_own = jnp.take_along_axis(doc_ids, place_own, axis=1)
    cosine, sine = rope_tables(place_own, head_size)
    input_rows = tokens.astype(jnp.float32).reshape(flat_rows, model_width)
    scale_attn = lax.rsqrt(jnp.mean(input_rows * input_rows, axis=-1, keepdims=True) + norm_eps)
    unit_attn = input_rows * scale_attn
    normed_attn = (unit_attn * gain_attn).astype(jnp.bfloat16)

    def project(weight_matrix):
        return jnp.dot(normed_attn, weight_matrix, preferred_element_type=jnp.float32).reshape(
            seq_count, row_count, local_heads, head_size
        )

    query_rot = (
        rotate(project(w_query), cosine, sine, True)
        .astype(jnp.bfloat16)
        .reshape(seq_count, row_count, local_width)
    )
    key_rot = (
        rotate(project(w_key), cosine, sine, True)
        .astype(jnp.bfloat16)
        .reshape(seq_count, row_count, local_width)
    )
    value_low = (
        jnp.dot(normed_attn, w_value, preferred_element_type=jnp.float32)
        .astype(jnp.bfloat16)
        .reshape(seq_count, row_count, local_width)
    )
    key_all, value_all = (
        lax.all_gather(key_rot, "seq", axis=1, tiled=True),
        lax.all_gather(value_low, "seq", axis=1, tiled=True),
    )

    def attend(items):
        query_seq, key_seq, value_seq, place_q, doc_q, place_k, doc_k, live_k = items
        query_heads = query_seq.reshape(row_count, local_heads, head_size)
        key_heads = key_seq.reshape(length, local_heads, head_size)
        value_heads = value_seq.reshape(length, local_heads, head_size)
        mask = visible(place_q, doc_q, place_k, doc_k, live_k)
        weights = (
            jax.nn.sigmoid(score_block(query_heads, key_heads, head_size, length)) * mask
        ).astype(jnp.bfloat16)
        mixed = jnp.einsum("hqk,khe->qhe", weights, value_heads, preferred_element_type=jnp.float32)
        return mixed.astype(jnp.bfloat16).reshape(row_count, local_width)

    attention_output = lax.map(
        attend, (query_rot, key_all, value_all, place_own, doc_own, place_all, doc_all, live_all)
    )
    attended_flat = attention_output.reshape(flat_rows, local_width)
    branch_attn = lax.psum(jnp.dot(attended_flat, w_out, preferred_element_type=jnp.float32), "tp")
    hidden_rows = input_rows + branch_attn
    scale_ffn = lax.rsqrt(jnp.mean(hidden_rows * hidden_rows, axis=-1, keepdims=True) + norm_eps)
    unit_ffn = hidden_rows * scale_ffn
    normalized_feedforward = (unit_ffn * gain_ffn).astype(jnp.bfloat16)
    gate_rows = jnp.dot(normalized_feedforward, w_gate, preferred_element_type=jnp.float32)
    up_projected = jnp.dot(normalized_feedforward, w_up, preferred_element_type=jnp.float32)
    gate_sig = jax.nn.sigmoid(gate_rows)
    activation_rows = (gate_rows * gate_sig * up_projected).astype(jnp.bfloat16)
    branch_ffn = lax.psum(
        jnp.dot(activation_rows, w_down, preferred_element_type=jnp.float32).astype(jnp.bfloat16),
        "tp",
    ).astype(jnp.float32)
    layer_out = (
        (hidden_rows + branch_ffn).astype(jnp.bfloat16).reshape(seq_count, row_count, model_width)
    )
    upstream = cotangent.astype(jnp.float32).reshape(flat_rows, model_width)
    upstream_low = upstream.astype(jnp.bfloat16)
    grad_down = jnp.einsum(
        "tf,td->fd", activation_rows, upstream_low, preferred_element_type=jnp.float32
    )
    grad_act = jnp.einsum("td,fd->tf", upstream_low, w_down, preferred_element_type=jnp.float32)
    gate_pre = (grad_act * up_projected * (gate_sig * (1.0 + gate_rows * (1.0 - gate_sig)))).astype(
        jnp.bfloat16
    )
    up_pre = (grad_act * (gate_rows * gate_sig)).astype(jnp.bfloat16)
    grad_gate = jnp.einsum(
        "td,tf->df", normalized_feedforward, gate_pre, preferred_element_type=jnp.float32
    )
    grad_up = jnp.einsum(
        "td,tf->df", normalized_feedforward, up_pre, preferred_element_type=jnp.float32
    )
    normed_ffn_part = jnp.einsum(
        "tf,df->td", gate_pre, w_gate, preferred_element_type=jnp.float32
    ) + jnp.einsum("tf,df->td", up_pre, w_up, preferred_element_type=jnp.float32)
    grad_normed_ffn = lax.psum(normed_ffn_part, "tp")
    gain_ffn_part = jnp.sum(grad_normed_ffn * unit_ffn, axis=0)
    back_ffn = grad_normed_ffn * gain_ffn
    grad_middle = upstream + scale_ffn * (
        back_ffn - unit_ffn * jnp.mean(back_ffn * unit_ffn, axis=-1, keepdims=True)
    )
    middle_low = grad_middle.astype(jnp.bfloat16)
    grad_out = jnp.einsum(
        "te,td->ed", attended_flat, middle_low, preferred_element_type=jnp.float32
    )
    grad_attended = (
        jnp.einsum("td,ed->te", middle_low, w_out, preferred_element_type=jnp.float32)
        .astype(jnp.bfloat16)
        .reshape(seq_count, row_count, local_width)
    )
    key_back, value_back = (key_all, value_all)

    def attend_back(items):
        query_seq, key_seq, value_seq, grad_seq, place_q, doc_q, place_k, doc_k, live_k = items
        query_heads = query_seq.reshape(row_count, local_heads, head_size)
        key_heads = key_seq.reshape(length, local_heads, head_size)
        value_heads = value_seq.reshape(length, local_heads, head_size)
        grad_heads = grad_seq.reshape(row_count, local_heads, head_size)
        mask = visible(place_q, doc_q, place_k, doc_k, live_k)
        weights, grad_scores = score_grads(
            query_heads, key_heads, value_heads, grad_heads, mask, head_size, length
        )
        grad_value_seq = jnp.einsum(
            "hqk,qhe->khe", weights, grad_heads, preferred_element_type=jnp.float32
        )
        grad_query_seq = (
            jnp.einsum("hqk,khe->qhe", grad_scores, key_heads, preferred_element_type=jnp.float32)
            * factor
        )
        grad_key_seq = (
            jnp.einsum("hqk,qhe->khe", grad_scores, query_heads, preferred_element_type=jnp.float32)
            * factor
        )
        return (
            grad_query_seq,
            grad_key_seq.reshape(length, local_width),
            grad_value_seq.reshape(length, local_width),
        )

    grad_query_rot, grad_key_all, grad_value_all = lax.map(
        attend_back,
        (
            query_rot,
            key_back,
            value_back,
            grad_attended,
            place_own,
            doc_own,
            place_all,
            doc_all,
            live_all,
        ),
    )
    grad_key_rot, grad_value_own = (
        lax.psum_scatter(grad_key_all, "seq", scatter_dimension=1, tiled=True),
        lax.psum_scatter(grad_value_all, "seq", scatter_dimension=1, tiled=True),
    )
    query_low = (
        rotate(grad_query_rot, cosine, sine, False)
        .astype(jnp.bfloat16)
        .reshape(flat_rows, local_width)
    )
    key_low = (
        rotate(
            grad_key_rot.reshape(seq_count, row_count, local_heads, head_size), cosine, sine, False
        )
        .astype(jnp.bfloat16)
        .reshape(flat_rows, local_width)
    )
    value_grad_low = grad_value_own.astype(jnp.bfloat16).reshape(flat_rows, local_width)
    grad_query = jnp.einsum("td,te->de", normed_attn, query_low, preferred_element_type=jnp.float32)
    grad_key = jnp.einsum("td,te->de", normed_attn, key_low, preferred_element_type=jnp.float32)
    grad_value = jnp.einsum(
        "td,te->de", normed_attn, value_grad_low, preferred_element_type=jnp.float32
    )
    normed_attn_part = (
        jnp.einsum("te,de->td", query_low, w_query, preferred_element_type=jnp.float32)
        + jnp.einsum("te,de->td", key_low, w_key, preferred_element_type=jnp.float32)
        + jnp.einsum("te,de->td", value_grad_low, w_value, preferred_element_type=jnp.float32)
    )
    grad_normed_attn = lax.psum(normed_attn_part, "tp")
    gain_attn_part = jnp.sum(grad_normed_attn * unit_attn, axis=0)
    back_attn = grad_normed_attn * gain_attn
    grad_inputs = grad_middle + scale_attn * (
        back_attn - unit_attn * jnp.mean(back_attn * unit_attn, axis=-1, keepdims=True)
    )
    grad_tokens = grad_inputs.reshape(seq_count, row_count, model_width)
    (
        query_shard,
        key_shard,
        value_shard,
        out_shard,
        gain_attn_shard,
        gate_shard,
        up_shard,
        down_shard,
        gain_ffn_shard,
    ) = (
        lax.psum_scatter(grad_query, "seq", scatter_dimension=0, tiled=True),
        lax.psum_scatter(grad_key, "seq", scatter_dimension=0, tiled=True),
        lax.psum_scatter(grad_value, "seq", scatter_dimension=0, tiled=True),
        lax.psum_scatter(grad_out, "seq", scatter_dimension=1, tiled=True),
        lax.psum_scatter(gain_attn_part, "seq", scatter_dimension=0, tiled=True),
        lax.psum_scatter(grad_gate, "seq", scatter_dimension=0, tiled=True),
        lax.psum_scatter(grad_up, "seq", scatter_dimension=0, tiled=True),
        lax.psum_scatter(grad_down, "seq", scatter_dimension=1, tiled=True),
        lax.psum_scatter(gain_ffn_part, "seq", scatter_dimension=0, tiled=True),
    )
    return (
        layer_out,
        grad_tokens,
        gain_attn_shard,
        query_shard,
        key_shard,
        value_shard,
        out_shard,
        gain_ffn_shard,
        gate_shard,
        up_shard,
        down_shard,
    )


def solution(mesh):
    placed = (
        P(None, "seq", None),
        P(),
        P(None, "tp"),
        P(None, "tp"),
        P(None, "tp"),
        P("tp", None),
        P(),
        P(None, "tp"),
        P(None, "tp"),
        P("tp", None),
        P(None, "seq", None),
        P(),
        P(),
        P(),
    )
    return jax.shard_map(
        local,
        mesh=mesh,
        in_specs=placed,
        out_specs=(
            P(None, "seq", None),
            P(None, "seq", None),
            P("seq"),
            P("seq", "tp"),
            P("seq", "tp"),
            P("seq", "tp"),
            P("tp", "seq"),
            P("seq"),
            P("seq", "tp"),
            P("seq", "tp"),
            P("tp", "seq"),
        ),
        check_vma=False,
    )
```

profile of v0, /device:TPU:0, one launch (start us, length us, event | category | flops | bytes accessed | tf_op | source)
XLA Modules:
  0.0 1533.5 jit_solution(12664565859678444474)
XLA Ops:
  9.4 4.4 compare_select_fusion.12
  13.8 5.7 select_select_fusion.1
  25.1 3.9 copy.49
  29.0 3.9 copy.50
  32.9 3.7 fusion.46
  40.6 4.3 fusion.53
  44.9 4.4 compare_select_fusion.3
  50.1 5.7 fusion.75
  55.9 23.0 %gather_fusion.1 = s32[4096]{0:T(1024)S(1)} fusion(s32[4096]{0:T(1024)S(1)} %bitcast.181, s32[4096]{0:T(1024)S(1)} %broadcast_clamp_fusion), kind=kCustom, calls=%fused_computation.clone | custom fusion | bytes 49152 | tf_op jit(solution)/shard_map/jit(take_along_axis)/gather | solution.py:89
  79.0 23.0 %gather_fusion.2 = s32[4096]{0:T(1024)S(1)} fusion(s32[4096]{0:T(1024)S(1)} %bitcast.182, s32[4096]{0:T(1024)S(1)} %broadcast_clamp_fusion), kind=kCustom, calls=%fused_computation.1.clone | custom fusion | bytes 49152 | tf_op jit(solution)/shard_map/jit(take_along_axis)/gather | solution.py:90
  102.2 4.3 and_convert_fusion
  106.5 17.4 %add_divide_fusion = f32[4,512,4096]{2,1,0:T(8,128)} fusion(bf16[4096,4,128]{0,2,1:T(8,128)(2,1)} %bitcast.193, bf16[512,4,64]{0,2,1:T(8,128)(2,1)S(1)} %get-tuple-element.103, bf16[512,4,64]{0,2,1:T(8,128)(2,1)S(1)} %get-tuple-element.102), kind=kOutput, calls=%fused_computation.8 | convolution fusion | flops 2190475264 | bytes 38273024 | tf_op jit(solution)/shard_map/while/body/eval_jaxpr/qhe,khe->hqk/dot_general | solution.py:47
  124.0 16.5 %fusion.56 = bf16[4,128,512]{2,1,0:T(8,128)(2,1)S(1)} fusion(f32[4,512,4096]{2,1,0:T(8,128)} %add_divide_fusion, f32[512,4096]{1,0:T(8,128)} %and_convert_fusion, bf16[4096,512]{1,0:T(8,128)(2,1)} %all-gather.6.cloned.1.call-done), kind=kOutput, calls=%fused_computation.74 | convolution fusion | flops 2164523008 | bytes 46661632 | tf_op jit(solution)/shard_map/while/body/eval_jaxpr/hqk,khe->qhe/dot_general | solution.py:132
  145.2 157.1 %all-reduce.8.cloned.1.call-done = f32[512,2048]{1,0:T(8,128)} async-done(((f32[512,2048]{1,0:T(8,128)}), f32[512,2048]{1,0:T(8,128)}) %all-reduce.8.cloned.1.call-update) | async-done | bytes 4194320 | tf_op jit(solution)/shard_map/psum | solution.py:139
  302.3 3.5 multiply_reduce_fusion.2
  306.2 11.8 fusion.96
  318.1 6.2 fusion.97
  324.3 11.6 multiply_convert_fusion.1
  335.9 8.5 fusion.98
  344.4 9.5 convolution_add_fusion
  354.2 9.8 convolution_convert_fusion
  364.1 144.0 %all-reduce.12.cloned.1.call-done = f32[512,2048]{1,0:T(8,128)} async-done(((f32[512,2048]{1,0:T(8,128)}), f32[512,2048]{1,0:T(8,128)}) %all-reduce.12.cloned.1.call-update) | async-done | bytes 4194320 | tf_op jit(solution)/shard_map/psum | solution.py:174
  508.1 4.4 multiply_reduce_fusion
  512.6 83.9 %all-reduce.10.cloned.1.call-done = bf16[512,2048]{1,0:T(8,128)(2,1)} async-done(((bf16[512,2048]{1,0:T(8,128)(2,1)}), bf16[512,2048]{1,0:T(8,128)(2,1)}) %all-reduce.10.cloned.1.call-update) | async-done | bytes 2097168 | tf_op jit(solution)/shard_map/psum | solution.py:148
  596.4 6.6 multiply_add_fusion
  606.3 21.1 %fusion.2 = bf16[4,512,4096]{2,1,0:T(8,128)(2,1)} fusion(f32[4,512,4096]{2,1,0:T(8,128)} %add_divide_fusion, f32[512,4096]{1,0:T(8,128)} %and_convert_fusion, bf16[512,4,128]{0,2,1:T(8,128)(2,1)S(1)} %bitcast.195, bf16[4096,512]{1,0:T(8,128)(2,1)} %all-gather.6.cloned.1.call-done), kind=kOutput, calls=%fused_computation.6 | convolution fusion | flops 2189426688 | bytes 63438848 | tf_op jit(solution)/shard_map/while/body/eval_jaxpr/qhe,khe->hqk/dot_general | solution.py:54
  627.4 11.4 convolution_multiply_fusion
  639.0 21.6 %fusion.26 = f32[4,128,4096]{2,1,0:T(8,128)} fusion(bf16[512,4,128]{0,2,1:T(8,128)(2,1)S(1)} %bitcast.196, f32[4,512,4096]{2,1,0:T(8,128)} %add_divide_fusion, f32[512,4096]{1,0:T(8,128)} %and_convert_fusion), kind=kOutput, calls=%fused_computation.49 | convolution fusion | flops 2164260864 | bytes 50855936 | tf_op jit(solution)/shard_map/while/body/eval_jaxpr/hqk,qhe->khe/dot_general | solution.py:201
  660.8 13.5 fusion.52
  674.3 35.0 %reduce-scatter.10.cloned.1.call-done = f32[1,512,512]{1,2,0:T(8,128)} async-done(((f32[1,4096,512]{1,2,0:T(8,128)}), f32[1,512,512]{1,2,0:T(8,128)}) %reduce-scatter.10.cloned.1.call-update) | async-done | bytes 1048592 | tf_op jit(solution)/shard_map/reduce_scatter | solution.py:233
  717.4 66.6 %reduce-scatter.12.cloned.1.call-done = f32[1,512,512]{1,2,0:T(8,128)} async-done(((f32[1,4096,512]{1,2,0:T(8,128)}), f32[1,512,512]{1,2,0:T(8,128)}) %reduce-scatter.12.cloned.1.call-update) | async-done | bytes 1048592 | tf_op jit(solution)/shard_map/reduce_scatter | solution.py:234
  784.0 7.0 add_add_fusion
  792.1 5.6 fusion.59
  799.3 4.6 fusion.40
  804.4 3.5 fusion.42
  811.4 12.6 fusion.101
  824.1 12.6 fusion.102
  836.9 12.5 fusion.30
  851.3 94.9 %all-reduce.14.cloned.1.call-done = f32[512,2048]{1,0:T(8,128)} async-done(((f32[512,2048]{1,0:T(8,128)}), f32[512,2048]{1,0:T(8,128)}) %all-reduce.14.cloned.1.call-update) | async-done | bytes 4194320 | tf_op jit(solution)/shard_map/psum | solution.py:259
  949.4 24.0 %all-reduce.2 = (f32[2048]{0:T(1024)S(1)}, f32[2048]{0:T(1024)S(1)}) all-reduce(f32[2048]{0:T(1024)S(1)} %get-tuple-element.70, f32[2048]{0:T(1024)S(1)} %get-tuple-element.68), channel_id=5, replica_groups=mesh['seq'=8,'tp'=4] {'seq'}, use_global_device_ids=true, to_apply=%region_11.13.clone | all-reduce | flops 4096 | bytes 32768
  974.7 7.4 fusion.15
  982.1 18.4 %reduce-scatter.20.cloned.1.call-done = f32[512,256]{1,0:T(8,128)} async-done(((f32[512,2048]{1,0:T(8,128)}), f32[512,256]{1,0:T(8,128)}) %reduce-scatter.20.cloned.1.call-update) | async-done | bytes 524304 | tf_op jit(solution)/shard_map/reduce_scatter | solution.py:280
  1000.5 55.5 %reduce-scatter.18.cloned.1.call-done = f32[256,512]{1,0:T(8,128)} async-done(((f32[2048,512]{1,0:T(8,128)}), f32[256,512]{1,0:T(8,128)}) %reduce-scatter.18.cloned.1.call-update) | async-done | bytes 524304 | tf_op jit(solution)/shard_map/reduce_scatter | solution.py:279
  1056.0 55.3 %reduce-scatter.16.cloned.1.call-done = f32[256,512]{1,0:T(8,128)} async-done(((f32[2048,512]{1,0:T(8,128)}), f32[256,512]{1,0:T(8,128)}) %reduce-scatter.16.cloned.1.call-update) | async-done | bytes 524304 | tf_op jit(solution)/shard_map/reduce_scatter | solution.py:278
  1111.2 55.5 %reduce-scatter.14.cloned.1.call-done = f32[256,512]{1,0:T(8,128)} async-done(((f32[2048,512]{1,0:T(8,128)}), f32[256,512]{1,0:T(8,128)}) %reduce-scatter.14.cloned.1.call-update) | async-done | bytes 524304 | tf_op jit(solution)/shard_map/reduce_scatter | solution.py:277
  1166.8 120.1 %reduce-scatter.22.cloned.1.call-done = f32[256,2048]{1,0:T(8,128)} async-done(((f32[2048,2048]{1,0:T(8,128)}), f32[256,2048]{1,0:T(8,128)}) %reduce-scatter.22.cloned.1.call-update) | async-done | bytes 2097168 | tf_op jit(solution)/shard_map/reduce_scatter | solution.py:282
  1286.9 120.0 %reduce-scatter.24.cloned.1.call-done = f32[256,2048]{1,0:T(8,128)} async-done(((f32[2048,2048]{1,0:T(8,128)}), f32[256,2048]{1,0:T(8,128)}) %reduce-scatter.24.cloned.1.call-update) | async-done | bytes 2097168 | tf_op jit(solution)/shard_map/reduce_scatter | solution.py:283
  1406.9 120.0 %reduce-scatter.26.cloned.1.call-done = f32[2048,256]{1,0:T(8,128)} async-done(((f32[2048,2048]{1,0:T(8,128)}), f32[2048,256]{1,0:T(8,128)}) %reduce-scatter.26.cloned.1.call-update) | async-done | bytes 2097168 | tf_op jit(solution)/shard_map/reduce_scatter | solution.py:284
  (140 shorter events, 42.5 us)
Async XLA Ops:
  7.2 134.1 %copy-start = (bf16[512,2048]{1,0:T(8,128)(2,1)S(1)}, bf16[512,2048]{1,0:T(8,128)(2,1)}, u32[]{:S(2)}) copy-start(bf16[512,2048]{1,0:T(8,128)(2,1)} %param.21) | copy-start | bytes 6291460
  7.2 99.3 %all-gather.4.cloned.1.call-start = ((), (), s32[]{:S(2)}) async-start(), calls=%async_computation.9 | async-start | bytes 4718592 | tf_op jit(solution)/shard_map/all_gather | solution.py:119
  25.0 15.5 %copy-start.22 = (f32[512]{0:T(512)}, f32[512]{0:T(512)S(1)}, u32[]{:S(2)}) copy-start(f32[512]{0:T(512)S(1)} %add_rsqrt_fusion.1) | copy-start | bytes 6148
  25.1 7.8 copy-start.20
  32.9 3.7 copy-start.4
  32.9 3.8 copy-start.15
  38.6 0.7 copy-start.16
  38.6 1.0 copy-start.18
  40.5 15.4 %copy-start.2 = (s32[1,4096]{1,0:T(1,128)S(1)}, s32[1,4096]{1,0:T(1,128)}, u32[]{:S(2)}) copy-start(s32[1,4096]{1,0:T(1,128)} %param.27) | copy-start | bytes 49156
  40.5 83.5 %all-gather.6.cloned.1.call-start = ((), (), s32[]{:S(2)}) async-start(), calls=%async_computation.23 | async-start | bytes 4718592 | tf_op jit(solution)/shard_map/all_gather | solution.py:120
  44.9 257.4 %all-reduce.8.cloned.1.call-start = ((), (), s32[]{:S(2)}) async-start(), calls=%async_computation.10 | async-start | bytes 8388608 | tf_op jit(solution)/shard_map/psum | solution.py:139
  55.9 23.1 %copy-start.3 = (s32[1,4096]{1,0:T(1,128)S(1)}, s32[1,4096]{1,0:T(1,128)}, u32[]{:S(2)}) copy-start(s32[1,4096]{1,0:T(1,128)} %param.28) | copy-start | bytes 49156
  140.5 0.8 copy-start.10
  144.6 161.2 %copy-start.24 = (f32[2048]{0:T(1024)S(1)}, f32[2048]{0:T(1024)}, u32[]{:S(2)}) copy-start(f32[2048]{0:T(1024)} %param.22) | copy-start | bytes 24580
  144.6 363.5 %all-reduce.12.cloned.1.call-start = ((), (), s32[]{:S(2)}) async-start(), calls=%async_computation.12 | async-start | bytes 8388608 | tf_op jit(solution)/shard_map/psum | solution.py:174
  305.7 12.3 copy-start.6
  305.8 12.3 slice-start
  306.2 11.9 copy-start.14
  306.2 11.9 slice-start.1
  318.1 6.2 copy-start.13
  335.9 8.5 copy-start.27
  335.9 8.5 copy-start.26
  354.0 242.5 %all-reduce.10.cloned.1.call-start = ((), (), s32[]{:S(2)}) async-start(), calls=%async_computation.11 | async-start | bytes 4194304 | tf_op jit(solution)/shard_map/psum | solution.py:148
  364.0 345.2 %reduce-scatter.10.cloned.1.call-start = ((), (), s32[]{:S(2)}) async-start(), calls=%async_computation.13 | async-start | bytes 9437184 | tf_op jit(solution)/shard_map/reduce_scatter | solution.py:233
  603.0 2.0 copy-start.7
  638.9 145.1 %reduce-scatter.12.cloned.1.call-start = ((), (), s32[]{:S(2)}) async-start(), calls=%async_computation.14 | async-start | bytes 9437184 | tf_op jit(solution)/shard_map/reduce_scatter | solution.py:234
  660.5 48.7 %copy-start.17 = (f32[512,64]{0,1:T(8,128)S(1)}, f32[512,64]{0,1:T(8,128)}, u32[]{:S(2)}) copy-start(f32[512,64]{0,1:T(8,128)} %copy-done.16) | copy-start | bytes 393220
  660.5 48.7 %copy-start.19 = (f32[512,64]{0,1:T(8,128)S(1)}, f32[512,64]{0,1:T(8,128)}, u32[]{:S(2)}) copy-start(f32[512,64]{0,1:T(8,128)} %copy-done.18) | copy-start | bytes 393220
  660.6 285.6 %all-reduce.14.cloned.1.call-start = ((), (), s32[]{:S(2)}) async-start(), calls=%async_computation.15 | async-start | bytes 8388608 | tf_op jit(solution)/shard_map/psum | solution.py:259
  674.3 36.6 %copy-start.8 = (bf16[2048,512]{1,0:T(8,128)(2,1)S(1)}, bf16[2048,512]{1,0:T(8,128)(2,1)}, u32[]{:S(2)}) copy-start(bf16[2048,512]{1,0:T(8,128)(2,1)} %param.19) | copy-start | bytes 6291460
  710.9 3.3 copy-start.9
  714.2 69.9 %copy-start.12 = (bf16[2048,512]{1,0:T(8,128)(2,1)S(1)}, bf16[2048,512]{1,0:T(8,128)(2,1)}, u32[]{:S(2)}) copy-start(bf16[2048,512]{1,0:T(8,128)(2,1)} %param.20) | copy-start | bytes 6291460
  791.0 1.0 copy-start.11
  791.0 209.4 %reduce-scatter.20.cloned.1.call-start = ((), (), s32[]{:S(2)}) async-start(), calls=%async_computation.19 | async-start | bytes 4718592 | tf_op jit(solution)/shard_map/reduce_scatter | solution.py:280
  797.7 1.6 copy-start.5
  797.7 1.6 copy-start.21
  797.7 1.6 copy-start.23
  797.7 258.3 %reduce-scatter.18.cloned.1.call-start = ((), (), s32[]{:S(2)}) async-start(), calls=%async_computation.18 | async-start | bytes 4718592 | tf_op jit(solution)/shard_map/reduce_scatter | solution.py:279
  803.9 307.3 %reduce-scatter.16.cloned.1.call-start = ((), (), s32[]{:S(2)}) async-start(), calls=%async_computation.17 | async-start | bytes 4718592 | tf_op jit(solution)/shard_map/reduce_scatter | solution.py:278
  807.9 358.9 %reduce-scatter.14.cloned.1.call-start = ((), (), s32[]{:S(2)}) async-start(), calls=%async_computation.16 | async-start | bytes 4718592 | tf_op jit(solution)/shard_map/reduce_scatter | solution.py:277
  811.3 475.5 %reduce-scatter.22.cloned.1.call-start = ((), (), s32[]{:S(2)}) async-start(), calls=%async_computation.20 | async-start | bytes 18874368 | tf_op jit(solution)/shard_map/reduce_scatter | solution.py:282
  824.0 582.8 %reduce-scatter.24.cloned.1.call-start = ((), (), s32[]{:S(2)}) async-start(), calls=%async_computation.21 | async-start | bytes 18874368 | tf_op jit(solution)/shard_map/reduce_scatter | solution.py:283
  836.6 690.2 %reduce-scatter.26.cloned.1.call-start = ((), (), s32[]{:S(2)}) async-start(), calls=%async_computation.22 | async-start | bytes 18874368 | tf_op jit(solution)/shard_map/reduce_scatter | solution.py:284
  849.4 0.7 copy-start.25
  974.7 552.1 %copy-start.1 = (bf16[512,2048]{1,0:T(8,128)(2,1)S(1)}, bf16[512,2048]{1,0:T(8,128)(2,1)}, u32[]{:S(2)}) copy-start(bf16[512,2048]{1,0:T(8,128)(2,1)} %param.21) | copy-start | bytes 6291460
Sparse Core Ops, SparseCore 0:
  40.6 40.1 all-gather.3
  83.2 36.7 all-gather.5
  144.7 157.5 all-reduce.7
  354.1 153.9 all-reduce.11
  510.9 85.5 all-reduce.9
  639.0 70.1 reduce-scatter.9
  712.7 71.2 reduce-scatter.11
  791.2 154.9 all-reduce.13
  950.1 50.3 reduce-scatter.19
  1004.6 51.2 reduce-scatter.17
  1059.9 51.2 reduce-scatter.15
  1115.4 51.3 reduce-scatter.13
  1170.9 115.9 reduce-scatter.21
  1290.9 115.9 reduce-scatter.23
  1410.8 115.9 reduce-scatter.25
where the time goes:
time: 1540 us; the launch traced here: 1530 us
  waiting for transfers between devices  1130 us (73%)
  matrix products  241 us (16%)
  local copies, waits for them, and re-layouts  67.8 us (4%)
  other arithmetic  56.7 us (4%)
  blocking collectives  24 us (2%)
    psum x1, waiting for transfers between devices, local(): lax.psum(jnp.dot(attended_flat, w_out, preferred_element_type=jnp.float32...  157 us
    psum x1, waiting for transfers between devices, local(): grad_normed_ffn = lax.psum(normed_ffn_part, 'tp')  144 us
    reduce_scatter x1, waiting for transfers between devices, local(): lax.psum_scatter(grad_gate, 'seq', scatter_dimension=0, tiled=True)  120 us
    reduce_scatter x1, waiting for transfers between devices, local(): lax.psum_scatter(grad_up, 'seq', scatter_dimension=0, tiled=True)  120 us
    reduce_scatter x1, waiting for transfers between devices, local(): lax.psum_scatter(grad_down, 'seq', scatter_dimension=1, tiled=True)  120 us
    psum x1, waiting for transfers between devices, local(): grad_normed_attn = lax.psum(normed_attn_part, 'tp')  94.9 us
    psum x1, waiting for transfers between devices, local(): lax.psum(jnp.dot(activation_rows, w_down, preferred_element_type=jnp.floa...  83.9 us
    reduce_scatter x1, waiting for transfers between devices, local(): lax.psum_scatter(grad_value_all, 'seq', scatter_dimension=1, tiled=True)  66.6 us
  transfers between devices with their start and end apart: 15, of which 13 were waited for; matrix products, arithmetic and copies ran while one was open for 14% of the time, Pallas kernels for 0%

commit v1 on v0

--- a/solution.py
+++ b/solution.py
@@ -58,7 +58,7 @@
     return (weights, grad_scores)
 
 
-def local(
+def local_general(
     tokens,
     gain_attn,
     w_query,
@@ -299,6 +299,295 @@
     )
 
 
+def line_gather(shard, axis, count):
+    upward, downward, below, above = shard, shard, {}, {}
+    for step in range(1, count):
+        upward = lax.ppermute(upward, axis, [(i, i + 1) for i in range(step - 1, count - 1)])
+        downward = lax.ppermute(downward, axis, [(i, i - 1) for i in range(1, count - step + 1)])
+        below[step], above[step] = upward, downward
+    return [shard] + [above[d] + below[count - d] for d in range(1, count)]
+
+
+def line_scatter_sum(parts, axis, count):
+    upward, downward = None, None
+    for step in range(1, count):
+        up_part, down_part = parts[count - step], parts[step]
+        if upward is not None:
+            up_part = up_part.astype(jnp.float32) + upward.astype(jnp.float32)
+            down_part = down_part.astype(jnp.float32) + downward.astype(jnp.float32)
+        upward = lax.ppermute(
+            up_part.astype(jnp.bfloat16), axis, [(i, i + 1) for i in range(0, step)]
+        )
+        downward = lax.ppermute(
+            down_part.astype(jnp.bfloat16), axis, [(i, i - 1) for i in range(count - step, count)]
+        )
+    return parts[0].astype(jnp.float32) + (
+        upward.astype(jnp.float32) + downward.astype(jnp.float32)
+    )
+
+
+def dense(left, right):
+    return jnp.dot(left, right, preferred_element_type=jnp.float32)
+
+
+def dense_t(left, right):
+    return lax.dot_general(
+        left, right, (((1,), (1,)), ((), ())), preferred_element_type=jnp.float32
+    )
+
+
+def local_heads_apart(
+    tokens,
+    gain_attn,
+    w_query,
+    w_key,
+    w_value,
+    w_out,
+    gain_ffn,
+    w_gate,
+    w_up,
+    w_down,
+    cotangent,
+    doc_ids,
+    valid,
+    group_order,
+    *,
+    seq_size,
+    tp_size,
+):
+    _, row_count, width = tokens.shape
+    length = doc_ids.shape[1]
+    groups = group_order.shape[1]
+    span = length // groups
+    head = HEAD_WIDTH
+    heads = w_query.shape[1] // head
+    chips = seq_size // 2
+    part = row_count // tp_size
+    factor = 1.0 / math.sqrt(head)
+    bf16, f32 = jnp.bfloat16, jnp.float32
+    same_core = [[2 * p + c for p in range(chips)] for c in range(2)]
+    other_core = [(i, i ^ 1) for i in range(seq_size)]
+    own_seq, own_tp = lax.axis_index("seq"), lax.axis_index("tp")
+    core = own_seq % 2
+    block = width // seq_size
+
+    def swap(values):
+        return lax.ppermute(values, "seq", other_core)
+
+    def to_heads(values):
+        return lax.all_to_all(values, "seq", 0, 0, axis_index_groups=same_core, tiled=True)
+
+    w_out_all = lax.all_gather(w_out, "tp", axis=0, tiled=True)
+
+    order = group_order[0]
+    per_device = row_count // span
+
+    def blocks_of(which):
+        devices = 2 * jnp.arange(chips, dtype=jnp.int32) + which
+        storage = (devices[:, None] * per_device + jnp.arange(per_device)[None, :]).reshape(-1)
+        return jnp.take(order, storage)
+
+    def places_of(block_ids):
+        return (block_ids[:, None] * span + jnp.arange(span, dtype=jnp.int32)[None, :]).reshape(-1)
+
+    own_blocks, other_blocks = blocks_of(core), blocks_of(1 - core)
+    key_blocks = jnp.concatenate([own_blocks, other_blocks])
+    place_q, place_k = places_of(own_blocks), places_of(key_blocks)
+    doc_k = jnp.take(doc_ids.reshape(groups, span), key_blocks, axis=0).reshape(-1)
+    live_k = jnp.take(valid.reshape(groups, span), key_blocks, axis=0).reshape(-1)
+    doc_q = doc_k[: length // 2]
+
+    own_rows = own_seq * per_device + jnp.arange(per_device, dtype=jnp.int32)
+    cosine, sine = rope_tables(places_of(jnp.take(order, own_rows)), head)
+    cosine_q, sine_q = rope_tables(place_q, head)
+
+    rows = tokens.astype(f32).reshape(row_count, width)
+    scale_attn = lax.rsqrt(jnp.mean(rows * rows, axis=-1, keepdims=True) + norm_eps)
+    unit_attn = rows * scale_attn
+    normed_attn = (unit_attn * gain_attn).astype(bf16)
+
+    def project(weight):
+        return dense(normed_attn, weight).reshape(row_count, heads, head)
+
+    packed = jnp.concatenate(
+        [
+            rotate(project(w_query), cosine, sine, True).astype(bf16),
+            rotate(project(w_key), cosine, sine, True).astype(bf16),
+            project(w_value).astype(bf16),
+        ],
+        axis=-1,
+    ).transpose(1, 0, 2)
+    mine = to_heads(packed).reshape(chips * row_count, 3 * head)
+    query, key_value = mine[:, :head], mine[:, head:]
+    key_value = jnp.concatenate([key_value, swap(key_value)], axis=0)
+    key, value = key_value[:, :head], key_value[:, head:]
+
+    upstream_low = cotangent.reshape(row_count, width)
+
+    def relative(values):
+        twice = jnp.concatenate([values, values], axis=0)
+        return lax.dynamic_slice_in_dim(twice, own_tp * part, row_count, 0)
+
+    upstream_rel = relative(upstream_low)
+    grad_act = dense_t(upstream_rel, w_down)
+
+    mask = visible(place_q, doc_q, place_k, doc_k, live_k)
+    sigma = jax.nn.sigmoid(dense_t(query, key) * factor - math.log(length))
+    probs = (sigma * mask).astype(bf16)
+    attended = dense(probs, value).astype(bf16)
+    attended = to_heads(attended.reshape(chips, row_count, head))
+    attended = attended.transpose(1, 0, 2).reshape(row_count, heads * head)
+    attended_part = lax.all_to_all(attended, "tp", 0, 0, tiled=True)
+    attended_part = (
+        attended_part.reshape(tp_size, part, heads * head).transpose(1, 0, 2).reshape(part, -1)
+    )
+
+    def own_part(values):
+        return lax.dynamic_slice_in_dim(values, own_tp * part, part, 0)
+
+    middle = own_part(rows) + dense(attended_part, w_out_all)
+    scale_ffn = lax.rsqrt(jnp.mean(middle * middle, axis=-1, keepdims=True) + norm_eps)
+    unit_ffn = middle * scale_ffn
+    normed_part = (unit_ffn * gain_ffn).astype(bf16)
+    normed_ffn = jnp.concatenate(line_gather(normed_part, "tp", tp_size), axis=0)
+
+    gate = dense(normed_ffn, w_gate)
+    up = dense(normed_ffn, w_up)
+    gate_sig = jax.nn.sigmoid(gate)
+    activated = (gate * gate_sig * up).astype(bf16)
+    gate_pre = (grad_act * up * (gate_sig * (1.0 + gate * (1.0 - gate_sig)))).astype(bf16)
+    up_pre = (grad_act * (gate * gate_sig)).astype(bf16)
+    normed_grad = (dense_t(gate_pre, w_gate) + dense_t(up_pre, w_up)).astype(bf16)
+
+    def relative_parts(values):
+        return [values[d * part : (d + 1) * part] for d in range(tp_size)]
+
+    grad_normed = line_scatter_sum(relative_parts(normed_grad), "tp", tp_size)
+    gain_ffn_part = jnp.sum(grad_normed * unit_ffn, axis=0)
+    back = grad_normed * gain_ffn
+    grad_middle = own_part(upstream_low).astype(f32) + scale_ffn * (
+        back - unit_ffn * jnp.mean(back * unit_ffn, axis=-1, keepdims=True)
+    )
+    middle_low = grad_middle.astype(bf16)
+    grad_attended = dense_t(middle_low, w_out_all).astype(bf16)
+    grad_attended = grad_attended.reshape(part, tp_size, heads * head).transpose(1, 0, 2)
+    grad_attended = lax.all_to_all(grad_attended, "tp", 0, 0, tiled=True)
+    grad_attended = grad_attended.reshape(row_count, heads, head).transpose(1, 0, 2)
+    grad_heads = to_heads(grad_attended).reshape(chips * row_count, head)
+
+    branch = dense(activated, w_down).astype(bf16)
+    branch_part = line_scatter_sum(relative_parts(branch), "tp", tp_size)
+    layer_part = (middle + branch_part).astype(bf16)
+    layer_out = lax.all_gather(layer_part, "tp", axis=0, tiled=True)
+    middle_all = lax.all_gather(middle_low, "tp", axis=0, tiled=True)
+
+    grad_value = lax.dot_general(
+        probs, grad_heads, (((0,), (0,)), ((), ())), preferred_element_type=f32
+    )
+    grad_scores = (dense_t(grad_heads, value) * (sigma * (1.0 - sigma)) * mask).astype(bf16)
+    grad_query = dense(grad_scores, key) * factor
+    grad_key = (
+        lax.dot_general(grad_scores, query, (((0,), (0,)), ((), ())), preferred_element_type=f32)
+        * factor
+    )
+    both = jnp.concatenate([grad_key, grad_value], axis=-1)
+    half = length // 2
+    both = both[:half] + swap(both[half:].astype(bf16)).astype(f32)
+
+    def turn_back(values):
+        return rotate(values[:, None, :], cosine_q, sine_q, False)[:, 0, :].astype(bf16)
+
+    packed_back = jnp.concatenate(
+        [turn_back(grad_query), turn_back(both[:, :head]), both[:, head:].astype(bf16)], axis=-1
+    ).reshape(chips, row_count, 3 * head)
+    back_heads = to_heads(packed_back).transpose(1, 0, 2)
+    query_low = back_heads[:, :, :head].reshape(row_count, heads * head)
+    key_low = back_heads[:, :, head : 2 * head].reshape(row_count, heads * head)
+    value_low = back_heads[:, :, 2 * head :].reshape(row_count, heads * head)
+
+    normed_grad1 = dense_t(query_low, w_query) + dense_t(key_low, w_key) + dense_t(
+        value_low, w_value
+    )
+    gain_attn_part = jnp.sum(normed_grad1 * unit_attn, axis=0)
+    grad_normed1 = line_scatter_sum(
+        relative_parts(relative(normed_grad1.astype(bf16))), "tp", tp_size
+    )
+    back1 = grad_normed1 * gain_attn
+    unit_part = own_part(unit_attn)
+    grad_inputs = grad_middle + own_part(scale_attn) * (
+        back1 - unit_part * jnp.mean(back1 * unit_part, axis=-1, keepdims=True)
+    )
+    tokens_rel = jnp.concatenate(
+        line_gather(grad_inputs.astype(bf16), "tp", tp_size), axis=0
+    )
+    twice = jnp.concatenate([tokens_rel, tokens_rel], axis=0)
+    grad_tokens = lax.dynamic_slice_in_dim(
+        twice, row_count - own_tp * part, row_count, 0
+    ).astype(f32)
+
+    def parity(values, which):
+        return lax.dynamic_index_in_dim(
+            values.reshape(row_count, chips, 2, block), which, 2, keepdims=False
+        ).reshape(row_count, chips * block)
+
+    def both_tokens_parity(values):
+        return jnp.concatenate([parity(values, core), swap(parity(values, 1 - core))], axis=0)
+
+    def both_tokens(values):
+        return jnp.concatenate([values, swap(values)], axis=0)
+
+    def outer(left, right):
+        return lax.dot_general(
+            left, right, (((0,), (0,)), ((), ())), preferred_element_type=f32
+        ).astype(bf16)
+
+    def spread(values):
+        return lax.psum_scatter(
+            values, "seq", scatter_dimension=0, axis_index_groups=same_core, tiled=True
+        )
+
+    upstream_cols = both_tokens_parity(upstream_rel)
+    normed2_cols = both_tokens_parity(normed_ffn)
+    normed1_cols = both_tokens_parity(normed_attn)
+    middle_cols = both_tokens_parity(middle_all)
+    ffn_grads = jnp.concatenate(
+        [
+            outer(normed2_cols, both_tokens(gate_pre)),
+            outer(normed2_cols, both_tokens(up_pre)),
+            outer(upstream_cols, both_tokens(activated)),
+        ],
+        axis=1,
+    )
+    ffn_shard = spread(ffn_grads).astype(f32)
+    hidden = w_gate.shape[1]
+    attn_grads = jnp.concatenate(
+        [
+            outer(middle_cols, both_tokens(attended)),
+            outer(normed1_cols, both_tokens(query_low)),
+            outer(normed1_cols, both_tokens(key_low)),
+            outer(normed1_cols, both_tokens(value_low)),
+        ],
+        axis=1,
+    )
+    attn_shard = spread(attn_grads).astype(f32)
+    own_width = heads * head
+    gains = lax.psum(jnp.stack([gain_attn_part, gain_ffn_part]), ("seq", "tp"))
+    gains = lax.dynamic_slice_in_dim(gains, own_seq * block, block, 1)
+    return (
+        layer_out.reshape(1, row_count, width),
+        grad_tokens.reshape(1, row_count, width),
+        gains[0],
+        attn_shard[:, own_width : 2 * own_width],
+        attn_shard[:, 2 * own_width : 3 * own_width],
+        attn_shard[:, 3 * own_width :],
+        attn_shard[:, :own_width].T,
+        gains[1],
+        ffn_shard[:, :hidden],
+        ffn_shard[:, hidden : 2 * hidden],
+        ffn_shard[:, 2 * hidden :].T,
+    )
+
+
 def solution(mesh):
     placed = (
         P(None, "seq", None),
@@ -316,6 +605,14 @@
         P(),
         P(),
     )
+    seq_size, tp_size = mesh.shape["seq"], mesh.shape["tp"]
+
+    def local(*args):
+        heads = args[2].shape[1] // HEAD_WIDTH
+        if seq_size == 2 * heads and args[0].shape[0] == 1:
+            return local_heads_apart(*args, seq_size=seq_size, tp_size=tp_size)
+        return local_general(*args)
+
     return jax.shard_map(
         local,
         mesh=mesh,

time: 1540 us -> 744 us (0.48)
  waiting for transfers between devices: 1130 us -> 179 us
  starting transfers between devices: 2.11 us -> 90.7 us
  blocking collectives: 24 us -> 78.7 us
  local copies, waits for them, and re-layouts: 67.8 us -> 118 us
  matrix products: 241 us -> 195 us
    reduce_scatter x9 -> x2, waiting for transfers between devices: 646 us -> 0.01 us  [spread(): lax.psum_scatter(values, 'seq', scatter_dimension=0, axis_index_groups=sa...]
    psum x4 -> x0, waiting for transfers between devices: 480 us -> none  [the longest x1 157 us: local(): lax.psum(jnp.dot(attended_flat, w_out, preferred_element_type=jnp.float32...]
    ppermute x0 -> x43, waiting for transfers between devices: none -> 98.8 us  [the longest x9 50.8 us: line_scatter_sum(): lax.ppermute(up_part.astype(jnp.bfloat16), axis, [(i, i + 1) for i in ran...]
    ppermute x0 -> x43, starting transfers between devices: none -> 71.7 us  [the longest x9 38.9 us: line_scatter_sum(): lax.ppermute(up_part.astype(jnp.bfloat16), axis, [(i, i + 1) for i in ran...]
    all_to_all x0 -> x4, waiting for transfers between devices: none -> 50.3 us  [the longest x1 28 us: local_heads_apart(): attended_part = lax.all_to_all(attended, 'tp', 0, 0, tiled=True)]
    psum x0 -> x1, blocking collectives: none -> 49.6 us  [local_heads_apart(): gains = lax.psum(jnp.stack([gain_attn_part, gain_ffn_part]), ('seq', 'tp'))]
    gather x4 -> x5, local copies, waits for them, and re-layouts: 51.4 us -> 3.08 us  [the longest x2 1.29 us: blocks_of(): return jnp.take(order, storage)]
    dot_general x27, matrix products: 241 us -> 195 us  [the longest x9 82 us: dense_t(): lax.dot_general(left, right, (((1,), (1,)), ((), ())), preferred_element_...]
  transfers between devices with their start and end apart: 15 -> 52, of which waited for: 13 -> 21; matrix products, arithmetic and copies ran while one was open for 14% -> 41% of each run, Pallas kernels for 0% -> 0%
where the time goes in v1:
time: 744 us; the launch traced here: 736 us
  matrix products  195 us (26%)
  waiting for transfers between devices  179 us (24%)
  local copies, waits for them, and re-layouts  118 us (16%)
  starting transfers between devices  90.7 us (12%)
  blocking collectives  78.7 us (11%)
  other arithmetic  60.2 us (8%)
  between operations  15.4 us (2%)
    dot_general x9, matrix products, dense_t(): lax.dot_general(left, right, (((1,), (1,)), ((), ())), preferred_element_...  82 us
    dot_general x9, matrix products, dense(): return jnp.dot(left, right, preferred_element_type=jnp.float32)  63.9 us
    ppermute x9, waiting for transfers between devices, line_scatter_sum(): lax.ppermute(up_part.astype(jnp.bfloat16), axis, [(i, i + 1) for i in ran...  50.8 us
    psum x1, blocking collectives, local_heads_apart(): gains = lax.psum(jnp.stack([gain_attn_part, gain_ffn_part]), ('seq', 'tp'))  49.6 us
    unnamed x114, local copies, waits for them, and re-layouts  40 us
    ppermute x9, starting transfers between devices, line_scatter_sum(): lax.ppermute(up_part.astype(jnp.bfloat16), axis, [(i, i + 1) for i in ran...  38.9 us
    dot_general x7, matrix products, outer(): lax.dot_general(left, right, (((0,), (0,)), ((), ())), preferred_element_...  31.6 us
    ppermute x6, waiting for transfers between devices, line_gather(): lax.ppermute(downward, axis, [(i, i - 1) for i in range(1, count - step +...  29.3 us
  transfers between devices with their start and end apart: 52, of which 21 were waited for; matrix products, arithmetic and copies ran while one was open for 41% of the time, Pallas kernels for 0%

profile of v1, /device:TPU:0, one launch (start us, length us, event | category | flops | bytes accessed | tf_op | source)
XLA Modules:
  0.0 735.9 jit_solution(12318888664986360500)
XLA Ops:
  34.8 5.9 all-to-all-start
  44.4 16.3 %all-to-all-done = bf16[4,512,384]{1,2,0:T(8,128)(2,1)} async-done(((bf16[4,512,384]{1,2,0:T(8,128)(2,1)}), bf16[4,512,384]{1,2,0:T(8,128)(2,1)}, u32[]{:S(2)}, u32[]{:S(2)}) %all-to-all-start) | async-done | bytes 1572896 | tf_op jit(solution)/shard_map/all_to_all | solution.py:378
  67.5 20.8 %select_convert_fusion = (bf16[2048,4096]{1,0:T(8,128)(2,1)S(1)}, f32[2048,4096]{1,0:T(8,128)}) fusion(s32[4096]{0:T(1024)S(1)} %bitcast.178, s32[4096]{0:T(1024)S(1)} %bitcast.180, s32[2048]{0:T(1024)S(1)} %bitcast.183, s32[2048]{0:T(1024)S(1)} %bitcast.175, pred[4096]{0:T(1024)(128)(4,1)S(1)} %eq.40, bf16[2048,256]{1,0:T(8,128)(2,1)S(1)} %slice.183, ...), kind=kOutput, calls=%fused_computation.9 | convolution fusion | flops 2233466880 | bytes 53006336 | tf_op jit(solution)/shard_map/dot_general | solution.py:334
  88.2 6.9 convolution_convert_fusion.2
  96.4 11.5 %all_to_all.34 = bf16[4,512,128]{1,2,0:T(8,128)(2,1)S(1)} all-to-all(bf16[4,512,128]{1,2,0:T(8,128)(2,1)S(1)} %copy.76), channel_id=1, replica_groups={{0,8,16,24},{4,12,20,28},{1,9,17,25},{5,13,21,29},{2,10,18,26},{6,14,22..., dimensions={0} | all-to-all | bytes 1048576 | tf_op jit(solution)/shard_map/all_to_all | solution.py:378
  116.7 28.0 %all-to-all-done.2 = bf16[4,128,512]{2,1,0:T(8,128)(2,1)S(1)} async-done(((bf16[4,128,512]{2,1,0:T(8,128)(2,1)}), bf16[4,128,512]{2,1,0:T(8,128)(2,1)S(1)}, u32[]{:S(2)}, u32[]{:S(2)}) %all-to-all-start.2) | async-done | bytes 524320 | tf_op jit(solution)/shard_map/all_to_all | solution.py:440
  145.7 27.4 %all-gather.4.cloned.1.call-done = bf16[2048,2048]{1,0:T(8,128)(2,1)} async-done(((bf16[512,2048]{1,0:T(8,128)(2,1)}), bf16[2048,2048]{1,0:T(8,128)(2,1)}) %all-gather.4.cloned.1.call-update) | async-done | bytes 8388624 | tf_op jit(solution)/shard_map/all_gather | solution.py:380
  173.2 5.1 multiply_reduce_fusion.4
  179.8 5.4 collective-permute-start.2
  185.2 9.2 %collective-permute-done.1 = bf16[128,2048]{1,0:T(8,128)(2,1)} collective-permute-done((bf16[128,2048]{1,0:T(8,128)(2,1)S(1)}, bf16[128,2048]{1,0:T(8,128)(2,1)}, u32[]{:S(2)}, u32[]{:S(2)}) %collective-permute-start.1) | collective-permute-done | bytes 524320 | tf_op jit(solution)/shard_map/ppermute | solution.py:306
  203.5 6.1 collective-permute-done.5
  211.8 9.6 %fusion.113 = f32[512,2048]{1,0:T(8,128)} fusion(bf16[512,2048]{0,1:T(8,128)(2,1)S(1)} %fusion.31, bf16[2048,2048]{1,0:T(8,128)(2,1)} %param.27), kind=kOutput, calls=%fused_computation.235 | convolution fusion | flops 4294967296 | bytes 14680064 | tf_op jit(solution)/shard_map/dot_general | solution.py:334
  226.4 11.2 %fusion.103 = f32[512,2048]{1,0:T(8,128)} fusion(bf16[2048,2048]{1,0:T(8,128)(2,1)} %param.26, bf16[128,2048]{1,0:T(8,128)(2,1)S(1)} %add.390, bf16[128,2048]{1,0:T(8,128)(2,1)S(1)} %add.389, bf16[128,2048]{1,0:T(8,128)(2,1)S(1)} %add.388, bf16[128,2048]{1,0:T(8,128)(2,1)S(1)} %copy-done.22), kind=kOutput, calls=%fused_computation.225 | convolution fusion | flops 4303355904 | bytes 14680064 | tf_op jit(solution)/shard_map/dot_general | solution.py:330
  237.7 10.3 %multiply_convert_fusion.1 = (bf16[512,2048]{1,0:T(8,128)(2,1)S(1)}, bf16[512,2048]{1,0:T(8,128)(2,1)S(1)}, bf16[512,2048]{1,0:T(8,128)(2,1)S(1)}) fusion(f32[512,2048]{1,0:T(8,128)} %fusion.113, f32[512,2048]{1,0:T(8,128)} %fusion.103, bf16[2048,2048]{1,0:T(8,128)(2,1)S(1)} %bitcast.188, bf16[128,2048]{1,0:T(8,128)(2,1)S(1)} %add.390, ...), kind=kOutput, calls=%fused_computation.40 | convolution fusion | flops 4319084544 | bytes 25165824 | tf_op jit(solution)/shard_map/dot_general | solution.py:330
  248.0 6.1 fusion.114
  254.1 9.2 %add_convert_fusion = bf16[512,2048]{1,0:T(8,128)(2,1)S(1)} fusion(f32[512,2048]{1,0:T(8,128)} %fusion.114, bf16[512,2048]{1,0:T(8,128)(2,1)S(1)} %get-tuple-element.73, bf16[2048,2048]{1,0:T(8,128)(2,1)} %param.26), kind=kOutput, calls=%fused_computation.39 | convolution fusion | flops 4297064448 | bytes 16777216 | tf_op jit(solution)/shard_map/dot_general | solution.py:334
  268.3 8.1 %convolution_convert_fusion = bf16[512,2048]{1,0:T(8,128)(2,1)S(1)} fusion(bf16[512,2048]{1,0:T(8,128)(2,1)S(1)} %get-tuple-element.75, bf16[2048,2048]{1,0:T(8,128)(2,1)} %param.27), kind=kOutput, calls=%fused_computation.49 | convolution fusion | flops 4296015872 | bytes 12582912 | tf_op jit(solution)/shard_map/dot_general | solution.py:330
  283.2 7.0 collective-permute-done.7
  295.6 5.8 collective-permute-done.14
  303.1 5.0 collective-permute-start.15
  314.3 5.0 collective-permute-start.9
  325.5 7.6 %collective-permute-done.9 = bf16[128,2048]{1,0:T(8,128)(2,1)S(1)} collective-permute-done((bf16[128,2048]{1,0:T(8,128)(2,1)S(1)}, bf16[128,2048]{1,0:T(8,128)(2,1)S(1)}, u32[]{:S(2)}, u32[]{:S(2)}) %collective-permute-start.9) | collective-permute-done | bytes 524320 | tf_op jit(solution)/shard_map/ppermute | solution.py:318
  335.9 6.4 convolution_convert_fusion.1
  342.4 17.6 %all_to_all.35 = bf16[4,128,512]{2,1,0:T(8,128)(2,1)S(1)} all-to-all(bf16[4,128,512]{2,1,0:T(8,128)(2,1)S(1)} %bitcast.159), channel_id=1, replica_groups=mesh['seq'=8,'tp'=4] {'tp'}, dimensions={0} | all-to-all | bytes 1048576 | tf_op jit(solution)/shard_map/all_to_all | solution.py:474
  365.4 6.0 all-to-all-done.4
  372.2 8.9 %fusion.115 = f32[4096,128]{0,1:T(8,128)S(1)} fusion(bf16[2048,4096]{1,0:T(8,128)(2,1)} %copy-done.44, bf16[2048,128]{1,0:T(8,128)(2,1)} %bitcast.170), kind=kOutput, calls=%fused_computation.237 | convolution fusion | flops 2147483648 | bytes 19398656 | tf_op jit(solution)/shard_map/dot_general | solution.py:484
  381.1 22.4 %fusion.2 = bf16[2048,4096]{1,0:T(8,128)(2,1)} fusion(f32[2048,4096]{1,0:T(8,128)} %get-tuple-element.125, s32[4096]{0:T(1024)S(1)} %bitcast.179, s32[4096]{0:T(1024)S(1)} %bitcast.181, s32[2048]{0:T(1024)S(1)} %bitcast.184, s32[2048]{0:T(1024)S(1)} %bitcast.177, pred[4096]{0:T(1024)(128)(4,1)S(1)} %eq.40, bf16[2048,128]{1,0:T(8,128)(2,1)S(1)} %bitcast.171, ...), kind=kOutput, calls=%fused_computation.8 | convolution fusion | flops 2225078272 | bytes 53006336 | tf_op jit(solution)/shard_map/dot_general | solution.py:334
  403.5 8.3 %convolution_multiply_fusion = f32[4096,128]{0,1:T(8,128)S(1)} fusion(bf16[2048,4096]{1,0:T(8,128)(2,1)} %fusion.2, bf16[2048,384]{1,0:T(8,128)(2,1)} %bitcast.141), kind=kOutput, calls=%fused_computation.13 | convolution fusion | flops 2148007936 | bytes 19398656 | tf_op jit(solution)/shard_map/dot_general | solution.py:490
  413.4 12.4 %fusion.26 = f32[2048,1,128]{0,2,1:T(8,128)} fusion(bf16[2048,4096]{1,0:T(8,128)(2,1)} %fusion.2, bf16[2048,256]{1,0:T(8,128)(2,1)S(1)} %copy-done.11, bf16[2048,256]{1,0:T(8,128)(2,1)} %collective-permute-done), kind=kOutput, calls=%fused_computation.51 | convolution fusion | flops 2149842944 | bytes 19922944 | tf_op jit(solution)/shard_map/dot_general | solution.py:330
  437.4 5.3 reshape.533
  442.7 7.4 copy.85
  461.7 6.3 constant_dynamic-slice_fusion.7
  468.0 5.8 copy.98
  474.8 5.8 copy.97
  503.0 8.5 %constant_dynamic-slice_fusion.3 = (bf16[512,4,1,256]{3,2,1,0:T(2,128)(2,1)}, bf16[512,4,1,256]{3,2,1,0:T(2,128)(2,1)}) fusion(bf16[512,4,2,256]{3,2,1,0:T(2,128)(2,1)} %reshape.536, s32[]{:T(128)S(6)} %select_n.85, s32[]{:T(128)S(6)} %select_n.86), kind=kLoop, calls=%fused_computation.179 | loop fusion | bytes 4194312 | tf_op jit(solution)/shard_map/jit(dynamic_index_in_dim)/dynamic_slice | solution.py:529
  511.5 5.8 copy.100
  521.3 5.8 copy.99
  527.2 7.5 %fusion.20 = bf16[1024,2048]{1,0:T(8,128)(2,1)S(1)} fusion(bf16[512,2048]{1,0:T(8,128)(2,1)} %collective-permute-done.40, bf16[512,2048]{1,0:T(8,128)(2,1)} %copy-done.43, bf16[512,1024]{0,1:T(8,128)(2,1)} %collective-permute-done.38, bf16[512,1024]{0,1:T(8,128)(2,1)} %bitcast.168), kind=kOutput, calls=%fused_computation.47 | convolution fusion | flops 4309647360 | bytes 10485760 | tf_op jit(solution)/shard_map/dot_general | solution.py:540
  534.7 6.6 fusion.23
  541.3 6.4 fusion.17
  547.8 11.6 %pad_maximum_fusion = bf16[1024,6144]{1,0:T(8,128)(2,1)} fusion(bf16[1024,2048]{1,0:T(8,128)(2,1)S(1)} %fusion.17, bf16[1024,2048]{1,0:T(8,128)(2,1)S(1)} %fusion.20, bf16[1024,2048]{1,0:T(8,128)(2,1)S(1)} %fusion.23), kind=kLoop, calls=%fused_computation.12 | loop fusion | flops 37748736 | bytes 25165824 | tf_op jit(solution)/shard_map/concatenate | solution.py:553
  572.4 10.5 %collective-permute-done.20 = bf16[128,2048]{1,0:T(8,128)(2,1)S(1)} collective-permute-done((bf16[128,2048]{1,0:T(8,128)(2,1)S(1)}, bf16[128,2048]{1,0:T(8,128)(2,1)S(1)}, u32[]{:S(2)}, u32[]{:S(2)}) %collective-permute-start.20) | collective-permute-done | bytes 524320 | tf_op jit(solution)/shard_map/ppermute | solution.py:318
  588.3 9.9 %collective-permute-done.21 = bf16[128,2048]{1,0:T(8,128)(2,1)S(1)} collective-permute-done((bf16[128,2048]{1,0:T(8,128)(2,1)S(1)}, bf16[128,2048]{1,0:T(8,128)(2,1)S(1)}, u32[]{:S(2)}, u32[]{:S(2)}) %collective-permute-start.21) | collective-permute-done | bytes 524320 | tf_op jit(solution)/shard_map/ppermute | solution.py:318
  599.9 8.9 %collective-permute-start.22 = (bf16[128,2048]{1,0:T(8,128)(2,1)S(1)}, bf16[128,2048]{1,0:T(8,128)(2,1)S(1)}, u32[]{:S(2)}, u32[]{:S(2)}) collective-permute-start(bf16[128,2048]{1,0:T(8,128)(2,1)S(1)} %get-tuple-element.89), channel_id=1, source_target_pairs={{0,1},{1,2},{2,3},{4,5},{5,6},{6,7},{8,9},{9,10},{10,11},{12,13},{... | collective-permute-start | bytes 1572872 | tf_op jit(solution)/shard_map/ppermute | solution.py:318
  608.9 8.6 %collective-permute-done.25 = bf16[128,2048]{1,0:T(8,128)(2,1)S(1)} collective-permute-done((bf16[128,2048]{1,0:T(8,128)(2,1)S(1)}, bf16[128,2048]{1,0:T(8,128)(2,1)S(1)}, u32[]{:S(2)}, u32[]{:S(2)}) %collective-permute-start.25) | collective-permute-done | bytes 524320 | tf_op jit(solution)/shard_map/ppermute | solution.py:321
  626.1 7.7 %collective-permute-done.27 = bf16[128,2048]{1,0:T(8,128)(2,1)S(1)} collective-permute-done((bf16[128,2048]{1,0:T(8,128)(2,1)S(1)}, bf16[128,2048]{1,0:T(8,128)(2,1)S(1)}, u32[]{:S(2)}, u32[]{:S(2)}) %collective-permute-start.27) | collective-permute-done | bytes 524320 | tf_op jit(solution)/shard_map/ppermute | solution.py:305
  640.1 49.6 %psum.7 = f32[2,2048]{1,0:T(2,128)S(1)} all-reduce(f32[2,2048]{1,0:T(2,128)S(1)} %pad_maximum_fusion.15), channel_id=1, replica_groups=mesh['seq'=8,'tp'=4] {'seq','tp'}, use_global_device_ids=true, to_apply=%region_6.9 | all-reduce | flops 4096 | bytes 32768 | tf_op jit(solution)/shard_map/psum | solution.py:574
  695.5 9.6 %collective-permute-done.31 = bf16[128,2048]{1,0:T(8,128)(2,1)S(1)} collective-permute-done((bf16[128,2048]{1,0:T(8,128)(2,1)S(1)}, bf16[128,2048]{1,0:T(8,128)(2,1)S(1)}, u32[]{:S(2)}, u32[]{:S(2)}) %collective-permute-start.31) | collective-permute-done | bytes 524320 | tf_op jit(solution)/shard_map/ppermute | solution.py:306
  (321 shorter events, 223.1 us)
Async XLA Ops:
  7.2 166.0 %all-gather.4.cloned.1.call-start = ((), (), s32[]{:S(2)}) async-start(), calls=%async_computation.8 | async-start | bytes 10485760 | tf_op jit(solution)/shard_map/all_gather | solution.py:380
  34.8 25.9 %all-to-all-start = ((bf16[4,512,384]{1,2,0:T(8,128)(2,1)}), bf16[4,512,384]{1,2,0:T(8,128)(2,1)}, u32[]{:S(2)}, u32[]{:S(2)}) async-start(bf16[4,512,384]{1,2,0:T(8,128)(2,1)} %bitcast.149), calls=%async_computation | async-start | bytes 3145728 | tf_op jit(solution)/shard_map/all_to_all | solution.py:378
  109.1 35.6 %all-to-all-start.2 = ((bf16[4,128,512]{2,1,0:T(8,128)(2,1)}), bf16[4,128,512]{2,1,0:T(8,128)(2,1)S(1)}, u32[]{:S(2)}, u32[]{:S(2)}) async-start(bf16[4,128,512]{2,1,0:T(8,128)(2,1)} %copy.96), calls=%async_computation.2 | async-start | bytes 1048576 | tf_op jit(solution)/shard_map/all_to_all | solution.py:440
  178.5 15.9 %collective-permute-start.1 = (bf16[128,2048]{1,0:T(8,128)(2,1)S(1)}, bf16[128,2048]{1,0:T(8,128)(2,1)}, u32[]{:S(2)}, u32[]{:S(2)}) collective-permute-start(bf16[128,2048]{1,0:T(8,128)(2,1)S(1)} %multiply_convert_fusion.5), channel_id=1, source_target_pairs={{1,0},{2,1},{3,2},{5,4},{6,5},{7,6},{9,8},{10,9},{11,10},{13,12},{... | collective-permute-start | bytes 1572872 | tf_op jit(solution)/shard_map/ppermute | solution.py:306
  179.8 15.9 %collective-permute-start.2 = (bf16[128,2048]{1,0:T(8,128)(2,1)S(1)}, bf16[128,2048]{1,0:T(8,128)(2,1)}, u32[]{:S(2)}, u32[]{:S(2)}) collective-permute-start(bf16[128,2048]{1,0:T(8,128)(2,1)S(1)} %multiply_convert_fusion.5), channel_id=1, source_target_pairs={{0,1},{1,2},{2,3},{4,5},{5,6},{6,7},{8,9},{9,10},{10,11},{12,13},{... | collective-permute-start | bytes 1572872 | tf_op jit(solution)/shard_map/ppermute | solution.py:305
  194.4 15.2 %collective-permute-start.5 = (bf16[128,2048]{1,0:T(8,128)(2,1)}, bf16[128,2048]{1,0:T(8,128)(2,1)}, u32[]{:S(2)}, u32[]{:S(2)}) collective-permute-start(bf16[128,2048]{1,0:T(8,128)(2,1)} %collective-permute-done.1), channel_id=1, source_target_pairs={{1,0},{2,1},{5,4},{6,5},{9,8},{10,9},{13,12},{14,13},{17,16},{18,1... | collective-permute-start | bytes 1572872 | tf_op jit(solution)/shard_map/ppermute | solution.py:306
  195.7 15.2 %collective-permute-start.3 = (bf16[128,2048]{1,0:T(8,128)(2,1)}, bf16[128,2048]{1,0:T(8,128)(2,1)}, u32[]{:S(2)}, u32[]{:S(2)}) collective-permute-start(bf16[128,2048]{1,0:T(8,128)(2,1)} %collective-permute-done.2), channel_id=1, source_target_pairs={{1,2},{2,3},{5,6},{6,7},{9,10},{10,11},{13,14},{14,15},{17,18},{18... | collective-permute-start | bytes 1572872 | tf_op jit(solution)/shard_map/ppermute | solution.py:305
  209.6 14.2 %collective-permute-start.6 = (bf16[128,2048]{1,0:T(8,128)(2,1)}, bf16[128,2048]{1,0:T(8,128)(2,1)S(1)}, u32[]{:S(2)}, u32[]{:S(2)}) collective-permute-start(bf16[128,2048]{1,0:T(8,128)(2,1)} %collective-permute-done.5), channel_id=1, source_target_pairs={{1,0},{5,4},{9,8},{13,12},{17,16},{21,20},{25,24},{29,28}} | collective-permute-start | bytes 1572872 | tf_op jit(solution)/shard_map/ppermute | solution.py:306
  210.9 14.1 %collective-permute-start.4 = (bf16[128,2048]{1,0:T(8,128)(2,1)}, bf16[128,2048]{1,0:T(8,128)(2,1)S(1)}, u32[]{:S(2)}, u32[]{:S(2)}) collective-permute-start(bf16[128,2048]{1,0:T(8,128)(2,1)} %collective-permute-done.3), channel_id=1, source_target_pairs={{2,3},{6,7},{10,11},{14,15},{18,19},{22,23},{26,27},{30,31}} | collective-permute-start | bytes 1572872 | tf_op jit(solution)/shard_map/ppermute | solution.py:305
  263.4 15.1 %collective-permute-start.13 = (bf16[128,2048]{1,0:T(8,128)(2,1)S(1)}, bf16[128,2048]{1,0:T(8,128)(2,1)S(1)}, u32[]{:S(2)}, u32[]{:S(2)}) collective-permute-start(bf16[128,2048]{1,0:T(8,128)(2,1)S(1)} %get-tuple-element.99), channel_id=1, source_target_pairs={{0,1},{4,5},{8,9},{12,13},{16,17},{20,21},{24,25},{28,29}} | collective-permute-start | bytes 1572872 | tf_op jit(solution)/shard_map/ppermute | solution.py:318
  267.6 11.0 %collective-permute-start.16 = (bf16[128,2048]{1,0:T(8,128)(2,1)S(1)}, bf16[128,2048]{1,0:T(8,128)(2,1)S(1)}, u32[]{:S(2)}, u32[]{:S(2)}) collective-permute-start(bf16[128,2048]{1,0:T(8,128)(2,1)S(1)} %get-tuple-element.100), channel_id=1, source_target_pairs={{3,2},{7,6},{11,10},{15,14},{19,18},{23,22},{27,26},{31,30}} | collective-permute-start | bytes 1572872 | tf_op jit(solution)/shard_map/ppermute | solution.py:321
  276.5 13.7 %collective-permute-start.7 = (bf16[128,2048]{1,0:T(8,128)(2,1)S(1)}, bf16[128,2048]{1,0:T(8,128)(2,1)S(1)}, u32[]{:S(2)}, u32[]{:S(2)}) collective-permute-start(bf16[128,2048]{1,0:T(8,128)(2,1)S(1)} %get-tuple-element.105), channel_id=1, source_target_pairs={{0,1},{4,5},{8,9},{12,13},{16,17},{20,21},{24,25},{28,29}} | collective-permute-start | bytes 1572872 | tf_op jit(solution)/shard_map/ppermute | solution.py:318
  277.8 12.3 %collective-permute-start.10 = (bf16[128,2048]{1,0:T(8,128)(2,1)S(1)}, bf16[128,2048]{1,0:T(8,128)(2,1)S(1)}, u32[]{:S(2)}, u32[]{:S(2)}) collective-permute-start(bf16[128,2048]{1,0:T(8,128)(2,1)S(1)} %get-tuple-element.106), channel_id=1, source_target_pairs={{3,2},{7,6},{11,10},{15,14},{19,18},{23,22},{27,26},{31,30}} | collective-permute-start | bytes 1572872 | tf_op jit(solution)/shard_map/ppermute | solution.py:321
  278.9 22.5 %collective-permute-start.14 = (bf16[128,2048]{1,0:T(8,128)(2,1)S(1)}, bf16[128,2048]{1,0:T(8,128)(2,1)S(1)}, u32[]{:S(2)}, u32[]{:S(2)}) collective-permute-start(bf16[128,2048]{1,0:T(8,128)(2,1)S(1)} %get-tuple-element.97), channel_id=1, source_target_pairs={{0,1},{1,2},{4,5},{5,6},{8,9},{9,10},{12,13},{13,14},{16,17},{17,1... | collective-permute-start | bytes 1572872 | tf_op jit(solution)/shard_map/ppermute | solution.py:318
  282.5 18.9 %collective-permute-start.17 = (bf16[128,2048]{1,0:T(8,128)(2,1)S(1)}, bf16[128,2048]{1,0:T(8,128)(2,1)S(1)}, u32[]{:S(2)}, u32[]{:S(2)}) collective-permute-start(bf16[128,2048]{1,0:T(8,128)(2,1)S(1)} %get-tuple-element.98), channel_id=1, source_target_pairs={{2,1},{3,2},{6,5},{7,6},{10,9},{11,10},{14,13},{15,14},{18,17},{19... | collective-permute-start | bytes 1572872 | tf_op jit(solution)/shard_map/ppermute | solution.py:321
  290.5 22.1 %collective-permute-start.8 = (bf16[128,2048]{1,0:T(8,128)(2,1)S(1)}, bf16[128,2048]{1,0:T(8,128)(2,1)S(1)}, u32[]{:S(2)}, u32[]{:S(2)}) collective-permute-start(bf16[128,2048]{1,0:T(8,128)(2,1)S(1)} %get-tuple-element.103), channel_id=1, source_target_pairs={{0,1},{1,2},{4,5},{5,6},{8,9},{9,10},{12,13},{13,14},{16,17},{17,1... | collective-permute-start | bytes 1572872 | tf_op jit(solution)/shard_map/ppermute | solution.py:318
  294.9 17.7 %collective-permute-start.11 = (bf16[128,2048]{1,0:T(8,128)(2,1)S(1)}, bf16[128,2048]{1,0:T(8,128)(2,1)S(1)}, u32[]{:S(2)}, u32[]{:S(2)}) collective-permute-start(bf16[128,2048]{1,0:T(8,128)(2,1)S(1)} %get-tuple-element.104), channel_id=1, source_target_pairs={{2,1},{3,2},{6,5},{7,6},{10,9},{11,10},{14,13},{15,14},{18,17},{19... | collective-permute-start | bytes 1572872 | tf_op jit(solution)/shard_map/ppermute | solution.py:321
  301.8 17.6 %collective-permute-start.18 = (bf16[128,2048]{1,0:T(8,128)(2,1)S(1)}, bf16[128,2048]{1,0:T(8,128)(2,1)S(1)}, u32[]{:S(2)}, u32[]{:S(2)}) collective-permute-start(bf16[128,2048]{1,0:T(8,128)(2,1)S(1)} %get-tuple-element.96), channel_id=1, source_target_pairs={{1,0},{2,1},{3,2},{5,4},{6,5},{7,6},{9,8},{10,9},{11,10},{13,12},{... | collective-permute-start | bytes 1572872 | tf_op jit(solution)/shard_map/ppermute | solution.py:321
  303.1 20.8 %collective-permute-start.15 = (bf16[128,2048]{1,0:T(8,128)(2,1)S(1)}, bf16[128,2048]{1,0:T(8,128)(2,1)S(1)}, u32[]{:S(2)}, u32[]{:S(2)}) collective-permute-start(bf16[128,2048]{1,0:T(8,128)(2,1)S(1)} %get-tuple-element.95), channel_id=1, source_target_pairs={{0,1},{1,2},{2,3},{4,5},{5,6},{6,7},{8,9},{9,10},{10,11},{12,13},{... | collective-permute-start | bytes 1572872 | tf_op jit(solution)/shard_map/ppermute | solution.py:318
  313.0 12.4 %collective-permute-start.12 = (bf16[128,2048]{1,0:T(8,128)(2,1)S(1)}, bf16[128,2048]{1,0:T(8,128)(2,1)S(1)}, u32[]{:S(2)}, u32[]{:S(2)}) collective-permute-start(bf16[128,2048]{1,0:T(8,128)(2,1)S(1)} %get-tuple-element.102), channel_id=1, source_target_pairs={{1,0},{2,1},{3,2},{5,4},{6,5},{7,6},{9,8},{10,9},{11,10},{13,12},{... | collective-permute-start | bytes 1572872 | tf_op jit(solution)/shard_map/ppermute | solution.py:321
  314.3 18.7 %collective-permute-start.9 = (bf16[128,2048]{1,0:T(8,128)(2,1)S(1)}, bf16[128,2048]{1,0:T(8,128)(2,1)S(1)}, u32[]{:S(2)}, u32[]{:S(2)}) collective-permute-start(bf16[128,2048]{1,0:T(8,128)(2,1)S(1)} %get-tuple-element.101), channel_id=1, source_target_pairs={{0,1},{1,2},{2,3},{4,5},{5,6},{6,7},{8,9},{9,10},{10,11},{12,13},{... | collective-permute-start | bytes 1572872 | tf_op jit(solution)/shard_map/ppermute | solution.py:318
  361.0 10.3 %all-to-all-start.4 = ((bf16[4,512,128]{2,1,0:T(8,128)(2,1)}), bf16[4,512,128]{2,1,0:T(8,128)(2,1)S(1)}, u32[]{:S(2)}, u32[]{:S(2)}) async-start(bf16[4,512,128]{2,1,0:T(8,128)(2,1)} %copy.81), calls=%async_computation.4 | async-start | bytes 1048576 | tf_op jit(solution)/shard_map/all_to_all | solution.py:378
  364.6 90.1 %all-gather.8.cloned.1.call-start = ((), (), s32[]{:S(2)}) async-start(), calls=%async_computation.10 | async-start | bytes 2621440 | tf_op jit(solution)/shard_map/all_gather | solution.py:482
  413.4 12.5 %collective-permute-start.19 = (bf16[2048,256]{0,1:T(8,128)(2,1)}, bf16[2048,256]{0,1:T(8,128)(2,1)}, u32[]{:S(2)}, u32[]{:S(2)}) collective-permute-start(bf16[2048,256]{0,1:T(8,128)(2,1)} %fusion.32), channel_id=1, source_target_pairs={{0,4},{4,0},{8,12},{12,8},{16,20},{20,16},{24,28},{28,24},{1,5},{5... | collective-permute-start | bytes 3145736 | tf_op jit(solution)/shard_map/ppermute | solution.py:375
  432.2 27.0 %all-to-all-start.5 = ((bf16[4,512,384]{1,2,0:T(8,128)(2,1)}), bf16[4,512,384]{1,2,0:T(8,128)(2,1)}, u32[]{:S(2)}, u32[]{:S(2)}) async-start(bf16[4,512,384]{1,2,0:T(8,128)(2,1)} %bitcast.137), calls=%async_computation.5 | async-start | bytes 3145728 | tf_op jit(solution)/shard_map/all_to_all | solution.py:378
  436.6 203.4 %all-gather.6.cloned.1.call-start = ((), (), s32[]{:S(2)}) async-start(), calls=%async_computation.9 | async-start | bytes 2621440 | tf_op jit(solution)/shard_map/all_gather | solution.py:481
  437.3 276.3 %reduce-scatter.3.cloned.1.call-start = ((), (), s32[]{:S(2)}) async-start(), calls=%async_computation.11 | async-start | bytes 5242880 | tf_op jit(solution)/shard_map/reduce_scatter | solution.py:545
  454.2 26.5 %collective-permute-start.34 = (bf16[512,1024]{0,1:T(8,128)(2,1)}, bf16[512,1024]{0,1:T(8,128)(2,1)}, u32[]{:S(2)}, u32[]{:S(2)}) collective-permute-start(bf16[512,1024]{0,1:T(8,128)(2,1)} %bitcast.41), channel_id=1, source_target_pairs={{0,4},{4,0},{8,12},{12,8},{16,20},{20,16},{24,28},{28,24},{1,5},{5... | collective-permute-start | bytes 3145736 | tf_op jit(solution)/shard_map/ppermute | solution.py:375
  461.7 19.0 %collective-permute-start.37 = (bf16[512,512]{0,1:T(8,128)(2,1)}, bf16[512,512]{0,1:T(8,128)(2,1)}, u32[]{:S(2)}, u32[]{:S(2)}) collective-permute-start(bf16[512,512]{0,1:T(8,128)(2,1)} %bitcast.31), channel_id=1, source_target_pairs={{0,4},{4,0},{8,12},{12,8},{16,20},{20,16},{24,28},{28,24},{1,5},{5... | collective-permute-start | bytes 1572872 | tf_op jit(solution)/shard_map/ppermute | solution.py:375
  473.8 15.5 %collective-permute-start.32 = (bf16[512,1024]{0,1:T(8,128)(2,1)}, bf16[512,1024]{0,1:T(8,128)(2,1)}, u32[]{:S(2)}, u32[]{:S(2)}) collective-permute-start(bf16[512,1024]{0,1:T(8,128)(2,1)} %bitcast.164), channel_id=1, source_target_pairs={{0,4},{4,0},{8,12},{12,8},{16,20},{20,16},{24,28},{28,24},{1,5},{5... | collective-permute-start | bytes 3145736 | tf_op jit(solution)/shard_map/ppermute | solution.py:375
  474.3 12.2 %collective-permute-start.35 = (bf16[512,512]{0,1:T(8,128)(2,1)S(1)}, bf16[512,512]{0,1:T(8,128)(2,1)}, u32[]{:S(2)}, u32[]{:S(2)}) collective-permute-start(bf16[512,512]{0,1:T(8,128)(2,1)S(1)} %bitcast.146), channel_id=1, source_target_pairs={{0,4},{4,0},{8,12},{12,8},{16,20},{20,16},{24,28},{28,24},{1,5},{5... | collective-permute-start | bytes 1572872 | tf_op jit(solution)/shard_map/ppermute | solution.py:375
  494.2 224.7 %reduce-scatter.5.cloned.1.call-start = ((), (), s32[]{:S(2)}) async-start(), calls=%async_computation.12 | async-start | bytes 15728640 | tf_op jit(solution)/shard_map/reduce_scatter | solution.py:545
  494.3 32.9 %collective-permute-start.40 = (bf16[512,2048]{1,0:T(8,128)(2,1)}, bf16[512,2048]{1,0:T(8,128)(2,1)}, u32[]{:S(2)}, u32[]{:S(2)}) collective-permute-start(bf16[512,2048]{1,0:T(8,128)(2,1)} %copy-done.43), channel_id=1, source_target_pairs={{0,4},{4,0},{8,12},{12,8},{16,20},{20,16},{24,28},{28,24},{1,5},{5... | collective-permute-start | bytes 6291464 | tf_op jit(solution)/shard_map/ppermute | solution.py:375
  494.8 39.9 %collective-permute-start.39 = (bf16[512,2048]{1,0:T(8,128)(2,1)}, bf16[512,2048]{1,0:T(8,128)(2,1)}, u32[]{:S(2)}, u32[]{:S(2)}) collective-permute-start(bf16[512,2048]{1,0:T(8,128)(2,1)} %copy-done.41), channel_id=1, source_target_pairs={{0,4},{4,0},{8,12},{12,8},{16,20},{20,16},{24,28},{28,24},{1,5},{5... | collective-permute-start | bytes 6291464 | tf_op jit(solution)/shard_map/ppermute | solution.py:375
  517.4 9.8 %collective-permute-start.38 = (bf16[512,1024]{0,1:T(8,128)(2,1)}, bf16[512,1024]{0,1:T(8,128)(2,1)}, u32[]{:S(2)}, u32[]{:S(2)}) collective-permute-start(bf16[512,1024]{0,1:T(8,128)(2,1)} %bitcast.167), channel_id=1, source_target_pairs={{0,4},{4,0},{8,12},{12,8},{16,20},{20,16},{24,28},{28,24},{1,5},{5... | collective-permute-start | bytes 3145736 | tf_op jit(solution)/shard_map/ppermute | solution.py:375
  517.8 23.5 %collective-permute-start.42 = (bf16[512,2048]{1,0:T(8,128)(2,1)}, bf16[512,2048]{1,0:T(8,128)(2,1)}, u32[]{:S(2)}, u32[]{:S(2)}) collective-permute-start(bf16[512,2048]{1,0:T(8,128)(2,1)} %copy-done.39), channel_id=1, source_target_pairs={{0,4},{4,0},{8,12},{12,8},{16,20},{20,16},{24,28},{28,24},{1,5},{5... | collective-permute-start | bytes 6291464 | tf_op jit(solution)/shard_map/ppermute | solution.py:375
  520.9 20.4 %collective-permute-start.41 = (bf16[512,1024]{0,1:T(8,128)(2,1)}, bf16[512,1024]{0,1:T(8,128)(2,1)}, u32[]{:S(2)}, u32[]{:S(2)}) collective-permute-start(bf16[512,1024]{0,1:T(8,128)(2,1)} %bitcast.48), channel_id=1, source_target_pairs={{0,4},{4,0},{8,12},{12,8},{16,20},{20,16},{24,28},{28,24},{1,5},{5... | collective-permute-start | bytes 3145736 | tf_op jit(solution)/shard_map/ppermute | solution.py:375
  569.5 13.4 %collective-permute-start.20 = (bf16[128,2048]{1,0:T(8,128)(2,1)S(1)}, bf16[128,2048]{1,0:T(8,128)(2,1)S(1)}, u32[]{:S(2)}, u32[]{:S(2)}) collective-permute-start(bf16[128,2048]{1,0:T(8,128)(2,1)S(1)} %get-tuple-element.93), channel_id=1, source_target_pairs={{0,1},{4,5},{8,9},{12,13},{16,17},{20,21},{24,25},{28,29}} | collective-permute-start | bytes 1572872 | tf_op jit(solution)/shard_map/ppermute | solution.py:318
  571.6 11.3 %collective-permute-start.23 = (bf16[128,2048]{1,0:T(8,128)(2,1)S(1)}, bf16[128,2048]{1,0:T(8,128)(2,1)S(1)}, u32[]{:S(2)}, u32[]{:S(2)}) collective-permute-start(bf16[128,2048]{1,0:T(8,128)(2,1)S(1)} %get-tuple-element.94), channel_id=1, source_target_pairs={{3,2},{7,6},{11,10},{15,14},{19,18},{23,22},{27,26},{31,30}} | collective-permute-start | bytes 1572872 | tf_op jit(solution)/shard_map/ppermute | solution.py:321
  583.2 15.0 %collective-permute-start.21 = (bf16[128,2048]{1,0:T(8,128)(2,1)S(1)}, bf16[128,2048]{1,0:T(8,128)(2,1)S(1)}, u32[]{:S(2)}, u32[]{:S(2)}) collective-permute-start(bf16[128,2048]{1,0:T(8,128)(2,1)S(1)} %get-tuple-element.91), channel_id=1, source_target_pairs={{0,1},{1,2},{4,5},{5,6},{8,9},{9,10},{12,13},{13,14},{16,17},{17,1... | collective-permute-start | bytes 1572872 | tf_op jit(solution)/shard_map/ppermute | solution.py:318
  587.6 10.6 %collective-permute-start.24 = (bf16[128,2048]{1,0:T(8,128)(2,1)S(1)}, bf16[128,2048]{1,0:T(8,128)(2,1)S(1)}, u32[]{:S(2)}, u32[]{:S(2)}) collective-permute-start(bf16[128,2048]{1,0:T(8,128)(2,1)S(1)} %get-tuple-element.92), channel_id=1, source_target_pairs={{2,1},{3,2},{6,5},{7,6},{10,9},{11,10},{14,13},{15,14},{18,17},{19... | collective-permute-start | bytes 1572872 | tf_op jit(solution)/shard_map/ppermute | solution.py:321
  598.6 18.9 %collective-permute-start.25 = (bf16[128,2048]{1,0:T(8,128)(2,1)S(1)}, bf16[128,2048]{1,0:T(8,128)(2,1)S(1)}, u32[]{:S(2)}, u32[]{:S(2)}) collective-permute-start(bf16[128,2048]{1,0:T(8,128)(2,1)S(1)} %get-tuple-element.90), channel_id=1, source_target_pairs={{1,0},{2,1},{3,2},{5,4},{6,5},{7,6},{9,8},{10,9},{11,10},{13,12},{... | collective-permute-start | bytes 1572872 | tf_op jit(solution)/shard_map/ppermute | solution.py:321
  599.9 18.7 %collective-permute-start.22 = (bf16[128,2048]{1,0:T(8,128)(2,1)S(1)}, bf16[128,2048]{1,0:T(8,128)(2,1)S(1)}, u32[]{:S(2)}, u32[]{:S(2)}) collective-permute-start(bf16[128,2048]{1,0:T(8,128)(2,1)S(1)} %get-tuple-element.89), channel_id=1, source_target_pairs={{0,1},{1,2},{2,3},{4,5},{5,6},{6,7},{8,9},{9,10},{10,11},{12,13},{... | collective-permute-start | bytes 1572872 | tf_op jit(solution)/shard_map/ppermute | solution.py:318
  620.4 13.5 %collective-permute-start.27 = (bf16[128,2048]{1,0:T(8,128)(2,1)S(1)}, bf16[128,2048]{1,0:T(8,128)(2,1)S(1)}, u32[]{:S(2)}, u32[]{:S(2)}) collective-permute-start(bf16[128,2048]{1,0:T(8,128)(2,1)S(1)} %get-tuple-element.66), channel_id=1, source_target_pairs={{0,1},{1,2},{2,3},{4,5},{5,6},{6,7},{8,9},{9,10},{10,11},{12,13},{... | collective-permute-start | bytes 1572872 | tf_op jit(solution)/shard_map/ppermute | solution.py:305
  624.8 13.2 %collective-permute-start.26 = (bf16[128,2048]{1,0:T(8,128)(2,1)S(1)}, bf16[128,2048]{1,0:T(8,128)(2,1)S(1)}, u32[]{:S(2)}, u32[]{:S(2)}) collective-permute-start(bf16[128,2048]{1,0:T(8,128)(2,1)S(1)} %get-tuple-element.66), channel_id=1, source_target_pairs={{1,0},{2,1},{3,2},{5,4},{6,5},{7,6},{9,8},{10,9},{11,10},{13,12},{... | collective-permute-start | bytes 1572872 | tf_op jit(solution)/shard_map/ppermute | solution.py:306
  638.0 52.3 %collective-permute-start.30 = (bf16[128,2048]{1,0:T(8,128)(2,1)S(1)}, bf16[128,2048]{1,0:T(8,128)(2,1)S(1)}, u32[]{:S(2)}, u32[]{:S(2)}) collective-permute-start(bf16[128,2048]{1,0:T(8,128)(2,1)S(1)} %collective-permute-done.26), channel_id=1, source_target_pairs={{1,0},{2,1},{5,4},{6,5},{9,8},{10,9},{13,12},{14,13},{17,16},{18,1... | collective-permute-start | bytes 1572872 | tf_op jit(solution)/shard_map/ppermute | solution.py:306
  639.3 52.5 %collective-permute-start.29 = (bf16[128,2048]{1,0:T(8,128)(2,1)S(1)}, bf16[128,2048]{1,0:T(8,128)(2,1)S(1)}, u32[]{:S(2)}, u32[]{:S(2)}) collective-permute-start(bf16[128,2048]{1,0:T(8,128)(2,1)S(1)} %collective-permute-done.28), channel_id=1, source_target_pairs={{2,3},{6,7},{10,11},{14,15},{18,19},{22,23},{26,27},{30,31}} | collective-permute-start | bytes 1572872 | tf_op jit(solution)/shard_map/ppermute | solution.py:305
  690.3 14.8 %collective-permute-start.31 = (bf16[128,2048]{1,0:T(8,128)(2,1)S(1)}, bf16[128,2048]{1,0:T(8,128)(2,1)S(1)}, u32[]{:S(2)}, u32[]{:S(2)}) collective-permute-start(bf16[128,2048]{1,0:T(8,128)(2,1)S(1)} %collective-permute-done.30), channel_id=1, source_target_pairs={{1,0},{5,4},{9,8},{13,12},{17,16},{21,20},{25,24},{29,28}} | collective-permute-start | bytes 1572872 | tf_op jit(solution)/shard_map/ppermute | solution.py:306
  (51 other events, 455.3 us)
Sparse Core Ops, SparseCore 0:
  9.6 163.5 all-gather.3
  367.6 45.5 all-gather.7
  439.6 45.6 all-gather.5
  494.3 52.3 reduce-scatter.2
  559.5 120.8 reduce-scatter.4

commit v2 on v0

--- a/solution.py
+++ b/solution.py
@@ -1,8 +1,11 @@
+import functools
 import math
 
 import jax
 import jax.numpy as jnp
 from jax import lax
+from jax.experimental import pallas as pl
+from jax.experimental.pallas import tpu as pltpu
 from jax.sharding import PartitionSpec as P
 
 HEAD_WIDTH = 128
@@ -58,7 +61,7 @@
     return (weights, grad_scores)
 
 
-def local(
+def local_general(
     tokens,
     gain_attn,
     w_query,
@@ -299,6 +302,1093 @@
     )
 
 
+def dense(left, right):
+    return jnp.dot(left, right, preferred_element_type=jnp.float32)
+
+
+def dense_t(left, right):
+    return lax.dot_general(
+        left, right, (((1,), (1,)), ((), ())), preferred_element_type=jnp.float32
+    )
+
+
+def sigma_of(scores, length):
+    return 1.0 / (1.0 + jnp.exp(math.log(length) - scores * (1.0 / math.sqrt(HEAD_WIDTH))))
+
+
+def in_position_order(slot_places, own_ref, other_ref, own_first, span, scratch_refs):
+    head = HEAD_WIDTH
+    own_slots = own_ref.shape[0] // span
+    for slot in range(2 * own_slots):
+        source, first = (own_ref, own_first) if slot < own_slots else (other_ref, 0)
+        rows = slice((slot % own_slots) * span, (slot % own_slots + 1) * span)
+        target = pl.ds(pl.multiple_of(slot_places[slot] * span, span), span)
+        for index, scratch in enumerate(scratch_refs):
+            columns = slice(first + index * head, first + (index + 1) * head)
+            scratch[target, :] = source[rows, columns]
+    for scratch in scratch_refs:
+        scratch[2 * own_slots * span :, :] = jnp.zeros((span, head), scratch.dtype)
+
+
+def attend_kernel(
+    slot_places, key_low, own_ref, other_ref, start_ref, out_ref, key_ref, value_ref, *, span
+):
+    head = HEAD_WIDTH
+    own_slots = own_ref.shape[0] // span
+    length = 2 * own_ref.shape[0]
+    in_position_order(slot_places, own_ref, other_ref, head, span, (key_ref, value_ref))
+    row = lax.broadcasted_iota(jnp.int32, (span, 2 * span), 0)
+    column = lax.broadcasted_iota(jnp.int32, (span, 2 * span), 1)
+
+    def query_block(slot, carry):
+        rows = pl.ds(pl.multiple_of(slot * span, span), span)
+        place = slot_places[slot]
+        low = key_low[slot]
+        query = own_ref[rows, :head]
+        first = start_ref[rows, :]
+
+        def key_pair(step, total):
+            base = pl.multiple_of((low + 2 * step) * span, span)
+            keys = pl.ds(base, 2 * span)
+            scores = dense_t(query, key_ref[keys, :])
+            seen = (column >= first - base) & (column - row <= place * span - base)
+            probs = jnp.where(seen, sigma_of(scores, length), 0.0).astype(jnp.bfloat16)
+            return total + dense(probs, value_ref[keys, :])
+
+        total = lax.fori_loop(
+            0, (place - low) // 2 + 1, key_pair, jnp.zeros((span, head), jnp.float32)
+        )
+        out_ref[rows, :] = total.astype(jnp.bfloat16)
+        return carry
+
+    lax.fori_loop(0, own_slots, query_block, 0)
+
+
+def attend_back_kernel(
+    slot_places,
+    key_low,
+    own_ref,
+    other_ref,
+    start_ref,
+    grad_ref,
+    grad_query_ref,
+    grad_own_ref,
+    grad_other_ref,
+    key_ref,
+    value_ref,
+    sum_key_ref,
+    sum_value_ref,
+    *,
+    span,
+):
+    head = HEAD_WIDTH
+    own_slots = own_ref.shape[0] // span
+    length = 2 * own_ref.shape[0]
+    factor = 1.0 / math.sqrt(head)
+    in_position_order(slot_places, own_ref, other_ref, head, span, (key_ref, value_ref))
+    sum_key_ref[...] = jnp.zeros_like(sum_key_ref)
+    sum_value_ref[...] = jnp.zeros_like(sum_value_ref)
+    row = lax.broadcasted_iota(jnp.int32, (2 * span, span), 0)
+    column = lax.broadcasted_iota(jnp.int32, (2 * span, span), 1)
+
+    def query_block(slot, carry):
+        rows = pl.ds(pl.multiple_of(slot * span, span), span)
+        place = slot_places[slot]
+        low = key_low[slot]
+        query = own_ref[rows, :head]
+        grad = grad_ref[rows, :]
+        first = start_ref[pl.ds(slot, 1), :]
+
+        def key_pair(step, total):
+            base = pl.multiple_of((low + 2 * step) * span, span)
+            keys = pl.ds(base, 2 * span)
+            key = key_ref[keys, :]
+            seen = (row >= first - base) & (row - column <= place * span - base)
+            sigma = jnp.where(seen, sigma_of(dense_t(key, query), length), 0.0)
+            sum_value_ref[keys, :] += dense(sigma.astype(jnp.bfloat16), grad)
+            grad_probs = dense_t(value_ref[keys, :], grad)
+            grad_scores = (grad_probs * (sigma * (1.0 - sigma))).astype(jnp.bfloat16)
+            sum_key_ref[keys, :] += dense(grad_scores, query)
+            return total + lax.dot_general(
+                grad_scores, key, (((0,), (0,)), ((), ())), preferred_element_type=jnp.float32
+            )
+
+        total = lax.fori_loop(
+            0, (place - low) // 2 + 1, key_pair, jnp.zeros((span, head), jnp.float32)
+        )
+        grad_query_ref[rows, :] = total * factor
+        return carry
+
+    lax.fori_loop(0, own_slots, query_block, 0)
+    for slot in range(2 * own_slots):
+        target = grad_own_ref if slot < own_slots else grad_other_ref
+        rows = slice((slot % own_slots) * span, (slot % own_slots + 1) * span)
+        source = pl.ds(pl.multiple_of(slot_places[slot] * span, span), span)
+        target[rows, :head] = (sum_key_ref[source, :] * factor).astype(target.dtype)
+        target[rows, head:] = sum_value_ref[source, :].astype(target.dtype)
+
+
+SHORT = pl.CostEstimate(flops=1, bytes_accessed=1, transcendentals=0)
+SMALL = pl.BlockSpec(memory_space=pltpu.SMEM)
+WHOLE = pl.BlockSpec(memory_space=pltpu.VMEM)
+
+
+def attend_call(slot_places, key_low, own, other, start, span):
+    rows = own.shape[0]
+    return pl.pallas_call(
+        functools.partial(attend_kernel, span=span),
+        out_shape=jax.ShapeDtypeStruct((rows, HEAD_WIDTH), jnp.bfloat16),
+        in_specs=[SMALL, SMALL, WHOLE, WHOLE, WHOLE],
+        out_specs=WHOLE,
+        scratch_shapes=[pltpu.VMEM((2 * rows + span, HEAD_WIDTH), jnp.bfloat16)] * 2,
+        compiler_params=pltpu.CompilerParams(vmem_limit_bytes=8 << 20),
+        cost_estimate=SHORT,
+        name="attend",
+    )(slot_places, key_low, own, other, start)
+
+
+def attend_back_call(slot_places, key_low, own, other, start, grad, span):
+    rows = own.shape[0]
+    return pl.pallas_call(
+        functools.partial(attend_back_kernel, span=span),
+        out_shape=(
+            jax.ShapeDtypeStruct((rows, HEAD_WIDTH), jnp.float32),
+            jax.ShapeDtypeStruct((rows, 2 * HEAD_WIDTH), jnp.float32),
+            jax.ShapeDtypeStruct((rows, 2 * HEAD_WIDTH), jnp.bfloat16),
+        ),
+        in_specs=[SMALL, SMALL, WHOLE, WHOLE, WHOLE, WHOLE],
+        out_specs=(WHOLE, WHOLE, WHOLE),
+        scratch_shapes=[pltpu.VMEM((2 * rows + span, HEAD_WIDTH), jnp.bfloat16)] * 2
+        + [pltpu.VMEM((2 * rows + span, HEAD_WIDTH), jnp.float32)] * 2,
+        compiler_params=pltpu.CompilerParams(vmem_limit_bytes=14 << 20),
+        cost_estimate=SHORT,
+        name="attend_back",
+    )(slot_places, key_low, own, other, start, grad)
+
+
+def call(kernel, outs, ins, scratch=(), scalars=0, grid=None, in_specs=None, out_specs=None, work=0, name=None, room=12):
+    params = pltpu.CompilerParams(vmem_limit_bytes=room << 20)
+    if grid is None:
+        return pl.pallas_call(
+            kernel,
+            out_shape=tuple(outs),
+            in_specs=[SMALL] * scalars + [WHOLE] * (len(ins) - scalars),
+            out_specs=tuple([WHOLE] * len(outs)),
+            scratch_shapes=list(scratch),
+            compiler_params=params,
+            cost_estimate=SHORT,
+            name=name,
+        )(*ins)
+    return pl.pallas_call(
+        kernel,
+        out_shape=tuple(outs),
+        grid_spec=pltpu.PrefetchScalarGridSpec(
+            num_scalar_prefetch=scalars,
+            grid=grid,
+            in_specs=in_specs,
+            out_specs=tuple(out_specs),
+            scratch_shapes=list(scratch),
+        ),
+        compiler_params=params,
+        cost_estimate=SHORT,
+        name=name,
+    )(*ins)
+
+
+def made(shape, dtype):
+    return jax.ShapeDtypeStruct(shape, dtype)
+
+
+def norm_of(values):
+    rows = values.astype(jnp.float32)
+    scale = lax.rsqrt(jnp.mean(rows * rows, axis=-1, keepdims=True) + norm_eps)
+    return scale, rows * scale
+
+
+def norm_back(grad, gain, scale, unit):
+    back = grad * gain
+    return scale * (back - unit * jnp.mean(back * unit, axis=-1, keepdims=True))
+
+
+def project_kernel(
+    tokens_ref, gain_ref, live_ref, cosine_ref, sine_ref, query_ref, key_ref, value_ref, packed_ref, normed_ref
+):
+    head = HEAD_WIDTH
+    rows = tokens_ref.shape[0]
+
+    @pl.when(pl.program_id(0) == 0)
+    def _():
+        step = 128
+
+        def piece(index, carry):
+            at = pl.ds(pl.multiple_of(index * step, step), step)
+            normed_ref[at, :] = (norm_of(tokens_ref[at, :])[1] * gain_ref[...]).astype(jnp.bfloat16)
+            return carry
+
+        lax.fori_loop(0, rows // step, piece, 0)
+
+    normed = normed_ref[...]
+    for index, weight in enumerate((query_ref, key_ref, value_ref)):
+        both = dense(normed, weight[...])
+        for which in range(2):
+            values = both[:, which * head : (which + 1) * head]
+            if index < 2:
+                values = values * cosine_ref[...] + pltpu.roll(values, head // 2, 1) * sine_ref[...]
+            else:
+                values = jnp.where(live_ref[...] == 1, values, 0.0)
+            packed_ref[which, :, index * head : (index + 1) * head] = values.astype(jnp.bfloat16)
+
+
+def project_call(tokens, gain, live, cosine, sine, w_query, w_key, w_value):
+    rows, width = tokens.shape
+    heads = w_query.shape[1] // HEAD_WIDTH
+    whole = lambda shape: pl.BlockSpec(shape, lambda h: (0, 0))
+    weight = pl.BlockSpec((width, 2 * HEAD_WIDTH), lambda h: (0, h))
+    w_query, w_key, w_value = [
+        pltpu.with_memory_space_constraint(w, pltpu.HBM) for w in (w_query, w_key, w_value)
+    ]
+    return call(
+        project_kernel,
+        (made((heads, rows, 3 * HEAD_WIDTH), jnp.bfloat16), made((rows, width), jnp.bfloat16)),
+        (tokens, gain, live, cosine, sine, w_query, w_key, w_value),
+        grid=(heads // 2,),
+        in_specs=[
+            whole((rows, width)), whole((1, width)), whole((rows, 1)),
+            whole((rows, HEAD_WIDTH)), whole((rows, HEAD_WIDTH)), weight, weight, weight,
+        ],
+        out_specs=[
+            pl.BlockSpec((2, rows, 3 * HEAD_WIDTH), lambda h: (h, 0, 0)), whole((rows, width)),
+        ],
+        work=6 * rows * width * w_query.shape[1],
+        room=32,
+        name="project",
+    )
+
+
+def piece_at(own_tp, d, count):
+    return lax.rem(own_tp + d, count)
+
+
+def out_kernel(where_ref, tokens_ref, gain_ref, attended_ref, *refs):
+    *weights, middle_ref, normed_ref = refs
+    own_tp, core = where_ref[0], where_ref[1]
+    count, part, _ = attended_ref.shape
+    half = weights[0].shape[0]
+    total = tokens_ref[pl.ds(pl.multiple_of(own_tp * part, part), part), :].astype(jnp.float32)
+    for d in range(count):
+        for which in range(2):
+            side = core if which == 0 else 1 - core
+            columns = pl.ds(pl.multiple_of(side * half, half), half)
+            values = attended_ref[piece_at(own_tp, d, count), :, columns]
+            total = total + dense(values, weights[2 * d + which][...])
+    middle_ref[...] = total
+    normed_ref[...] = (norm_of(total)[1] * gain_ref[...]).astype(jnp.bfloat16)
+
+
+def ffn_kernel(where_ref, *refs, chunk, sources, first):
+    grad_act_ref, gate_ref, up_ref = refs[sources : sources + 3]
+    act_ref, gate_pre_ref, up_pre_ref, normed_ref, *grads, total_ref = refs[
+        sources + 3 + (0 if first else 4) :
+    ]
+    own_tp = where_ref[0]
+    part = grads[0].shape[0]
+    step = pl.program_id(0)
+
+    @pl.when(step == 0)
+    def _():
+        if first:
+            normed_ref[:part, :] = refs[0][...]
+            normed_ref[part:, :] = jnp.where(from_above(own_tp, 1), refs[1][...], refs[2][...])
+        elif chunk == 2:
+            normed_ref[...] = jnp.where(from_above(own_tp, 2), refs[0][...], refs[1][...])
+        else:
+            inner = jnp.where(own_tp == 1, refs[0][...], refs[1][...])
+            ends = jnp.where(own_tp == 0, refs[2][...], refs[3][...])
+            normed_ref[...] = jnp.where(is_inner(own_tp), inner, ends)
+
+    normed = normed_ref[...]
+    gate = dense(normed, gate_ref[...])
+    up = dense(normed, up_ref[...])
+    sig = jax.nn.sigmoid(gate)
+    grad_act = grad_act_ref[...]
+    act_ref[...] = (gate * sig * up).astype(jnp.bfloat16)
+    gate_pre = (grad_act * up * (sig * (1.0 + gate * (1.0 - sig)))).astype(jnp.bfloat16)
+    up_pre = (grad_act * (gate * sig)).astype(jnp.bfloat16)
+    gate_pre_ref[...] = gate_pre
+    up_pre_ref[...] = up_pre
+    term = dense_t(gate_pre, gate_ref[...]) + dense_t(up_pre, up_ref[...])
+
+    @pl.when(step == 0)
+    def _():
+        total_ref[...] = term
+
+    @pl.when(step > 0)
+    def _():
+        total_ref[...] += term
+
+    @pl.when(step == pl.num_programs(0) - 1)
+    def _():
+        for index, grad_ref in enumerate(grads):
+            rows = slice(index * part, (index + 1) * part)
+            grad_ref[...] = total_ref[rows, :].astype(jnp.bfloat16)
+
+
+def from_above(own_tp, chunk):
+    return own_tp % (2 * chunk) < chunk
+
+
+def is_inner(own_tp):
+    return (own_tp == 1) | (own_tp == 2)
+
+
+def ffn_call(where, chunk, sources, grad_act, w_gate, w_up, filled):
+    part, width = sources[0].shape
+    total, hidden = grad_act.shape
+    wide = 512
+    count = 2 if filled is None else 1
+    rows = count * part
+    whole = pl.BlockSpec((part, width), lambda f, w: (0, 0))
+    weight = pl.BlockSpec((width, wide), lambda f, w: (0, f))
+    block = pl.BlockSpec((rows, wide), lambda f, w: (chunk, f))
+    low = made((total, hidden), jnp.bfloat16)
+    w_gate, w_up = [pltpu.with_memory_space_constraint(w, pltpu.HBM) for w in (w_gate, w_up)]
+    ins = [where, *sources, grad_act, w_gate, w_up]
+    specs = [whole] * len(sources) + [block, weight, weight]
+    aliases = {}
+    if filled is not None:
+        aliases = {len(ins) + i: i for i in range(4)}
+        ins += list(filled)
+        specs += [pl.BlockSpec(memory_space=pl.ANY)] * 4
+    outs = pl.pallas_call(
+        functools.partial(ffn_kernel, chunk=chunk, sources=len(sources), first=not aliases),
+        out_shape=(low, low, low, made((total, width), jnp.bfloat16))
+        + (made((part, width), jnp.bfloat16),) * count,
+        grid_spec=pltpu.PrefetchScalarGridSpec(
+            num_scalar_prefetch=1,
+            grid=(hidden // wide,),
+            in_specs=specs,
+            out_specs=(
+                block, block, block, pl.BlockSpec((rows, width), lambda f, w: (chunk, 0)),
+            )
+            + (whole,) * count,
+            scratch_shapes=[pltpu.VMEM((rows, width), jnp.float32)],
+        ),
+        input_output_aliases=aliases,
+        compiler_params=pltpu.CompilerParams(vmem_limit_bytes=28 << 20),
+        cost_estimate=SHORT,
+        name="ffn",
+    )(*ins)
+    return outs[:4], outs[4:]
+
+
+def middle_kernel(where_ref, middle_ref, upstream_ref, gain_ref, *refs):
+    terms, refs = refs[: refs[-2].shape[0]], refs[refs[-2].shape[0] :]
+    *weights, low_ref, grad_ref, back_ref, gain_grad_ref = refs
+    own_tp, core = where_ref[0], where_ref[1]
+    count, part, _ = back_ref.shape
+    half = weights[0].shape[0]
+    scale, unit = norm_of(middle_ref[...])
+    grad = sum([t[...].astype(jnp.float32) for t in terms[1:]], terms[0][...].astype(jnp.float32))
+    gain_grad_ref[...] = jnp.sum(grad * unit, axis=0, keepdims=True)
+    at = pl.ds(pl.multiple_of(own_tp * part, part), part)
+    total = upstream_ref[at, :].astype(jnp.float32) + norm_back(grad, gain_ref[...], scale, unit)
+    grad_ref[...] = total
+    low = total.astype(jnp.bfloat16)
+    low_ref[...] = low
+    for d in range(count):
+        for which in range(2):
+            side = core if which == 0 else 1 - core
+            columns = pl.ds(pl.multiple_of(side * half, half), half)
+            back_ref[piece_at(own_tp, d, count), :, columns] = dense_t(
+                low, weights[2 * d + which][...]
+            ).astype(jnp.bfloat16)
+
+
+def back_kernel(where_ref, back_ref, live_ref, tokens_ref, query_ref, key_ref, value_ref, low_ref, gain_ref, *refs):
+    *outs, ordered_ref, unit_ref = refs
+    head = HEAD_WIDTH
+    heads = back_ref.shape[0]
+    count = len(outs)
+    part = outs[0].shape[0]
+    own = heads * head
+    step = pl.program_id(0)
+
+    @pl.when(step == 0)
+    def _():
+        for d in range(count):
+            at = pl.ds(pl.multiple_of(piece_at(where_ref[0], d, count) * part, part), part)
+            rows = slice(d * part, (d + 1) * part)
+            for index in range(3):
+                low = jnp.concatenate(
+                    [back_ref[h, at, index * head : (index + 1) * head] for h in range(heads)],
+                    axis=-1,
+                )
+                if index == 2:
+                    low = jnp.where(live_ref[at, :] == 1, low.astype(jnp.float32), 0.0)
+                    low = low.astype(jnp.bfloat16)
+                low_ref[at, index * own : (index + 1) * own] = low
+                ordered_ref[rows, index * own : (index + 1) * own] = low
+            unit = norm_of(tokens_ref[at, :])[1]
+            for block in range(unit_ref.shape[0]):
+                wide = unit_ref.shape[2]
+                unit_ref[block, rows, :] = unit[:, block * wide : (block + 1) * wide]
+
+    total = None
+    for index, weight in enumerate((query_ref, key_ref, value_ref)):
+        term = dense_t(ordered_ref[:, index * own : (index + 1) * own], weight[...])
+        total = term if total is None else total + term
+    gain_ref[...] = jnp.sum(total * unit_ref[step], axis=0, keepdims=True)
+    for d in range(count):
+        outs[d][...] = total[d * part : (d + 1) * part].astype(jnp.bfloat16)
+
+
+def back_call(where, back_heads, live, tokens, weights, count):
+    rows, width = tokens.shape
+    own = weights[0].shape[1]
+    part = rows // count
+    wide = 512
+    blocks = width // wide
+    weights = [pltpu.with_memory_space_constraint(w, pltpu.HBM) for w in weights]
+    whole = lambda x: pl.BlockSpec(x.shape, lambda f, w: (0,) * len(x.shape))
+    return pl.pallas_call(
+        back_kernel,
+        out_shape=(made((rows, 3 * own), jnp.bfloat16), made((1, width), jnp.float32))
+        + (made((part, width), jnp.bfloat16),) * count,
+        grid_spec=pltpu.PrefetchScalarGridSpec(
+            num_scalar_prefetch=1,
+            grid=(blocks,),
+            in_specs=[whole(back_heads), whole(live), whole(tokens)]
+            + [pl.BlockSpec((wide, own), lambda f, w: (f, 0))] * 3,
+            out_specs=(
+                pl.BlockSpec((rows, 3 * own), lambda f, w: (0, 0)),
+                pl.BlockSpec((1, wide), lambda f, w: (0, f)),
+            )
+            + (pl.BlockSpec((part, wide), lambda f, w: (0, f)),) * count,
+            scratch_shapes=[
+                pltpu.VMEM((rows, 3 * own), jnp.bfloat16),
+                pltpu.VMEM((blocks, rows, wide), jnp.float32),
+            ],
+        ),
+        compiler_params=pltpu.CompilerParams(vmem_limit_bytes=32 << 20),
+        cost_estimate=SHORT,
+        name="back",
+    )(where, back_heads, live, tokens, *weights)
+
+
+def tokens_kernel(where_ref, tokens_ref, gain_ref, middle_ref, gains_ref, own_ref, below_ref, above_ref, out_ref):
+    part = own_ref.shape[0]
+    at = pl.ds(pl.multiple_of(where_ref[0] * part, part), part)
+    scale, unit = norm_of(tokens_ref[at, :])
+    grad = own_ref[...].astype(jnp.float32) + (
+        below_ref[...].astype(jnp.float32) + above_ref[...].astype(jnp.float32)
+    )
+    total = middle_ref[...] + norm_back(grad, gain_ref[...], scale, unit)
+    out_ref[:part, :] = total.astype(jnp.bfloat16)
+    gains = gains_ref[...]
+    high = gains.astype(jnp.bfloat16)
+    low = (gains - high.astype(jnp.float32)).astype(jnp.bfloat16)
+    wide = gains.shape[1]
+    rows = out_ref.shape[0] - part
+    for index, values in enumerate((high, low)):
+        out_ref[part:, index * wide : (index + 1) * wide] = jnp.broadcast_to(values, (rows, wide))
+    out_ref[part:, 2 * wide :] = jnp.zeros((rows, out_ref.shape[1] - 2 * wide), jnp.bfloat16)
+
+
+def layer_kernel(middle_ref, branch_ref, out_ref):
+    out_ref[...] = (middle_ref[...] + branch_ref[...].astype(jnp.float32)).astype(jnp.bfloat16)
+
+
+def join_kernel(where_ref, own_ref, *refs, relative, part):
+    count = (len(refs) - (1 if own_ref.shape[0] == part else 3)) // 2 + 1
+    pieces, (out_ref, *rest) = refs[: 2 * count - 2], refs[2 * count - 2 :]
+    for d in range(count):
+        place = d if relative else piece_at(where_ref[0], d, count)
+        values = own_ref[...] if d == 0 else pieces[d - 1][...] + pieces[2 * count - 2 - d][...]
+        out_ref[pl.ds(pl.multiple_of(place * part, part), part), :] = values[:part].astype(out_ref.dtype)
+        if rest:
+            gains_ref, terms_ref = rest
+            wide = gains_ref.shape[1]
+            row = values[part:].astype(jnp.float32)
+            terms_ref[place] = row[:8, :wide] + row[:8, wide : 2 * wide]
+    if rest:
+        total = terms_ref[0]
+        for index in range(1, count):
+            total = total + terms_ref[index]
+        gains_ref[...] = total[:1]
+
+
+def join(where, gathered, dtype, relative, gains=0):
+    own, above, below = gathered
+    count = len(above) + 1
+    part, width = own.shape[0] - (16 if gains else 0), own.shape[1]
+    outs, scratch = [made((count * part, width), dtype)], []
+    if gains:
+        outs.append(made((1, gains), jnp.float32))
+        scratch.append(pltpu.VMEM((count, 8, gains), jnp.float32))
+    return call(
+        functools.partial(join_kernel, relative=relative, part=part),
+        outs,
+        (where, own, *above, *below),
+        scratch=scratch,
+        scalars=1,
+        name="join",
+    )
+
+
+def tie(*values):
+    return lax.optimization_barrier(values)
+
+
+def after(value, *others):
+    return lax.optimization_barrier((value, *others))[0]
+
+
+class Line:
+    def __init__(self, axis, count):
+        self.axis, self.count, self.at = axis, count, 0
+        self.upward, self.downward = None, None
+
+    def tie(self, *others):
+        self.upward, self.downward, *others = tie(self.upward, self.downward, *others)
+        return others[0] if len(others) == 1 else others
+
+    def send(self, up, down, up_pairs, down_pairs):
+        self.upward = lax.ppermute(up, self.axis, up_pairs)
+        self.downward = lax.ppermute(down, self.axis, down_pairs)
+
+
+class Gather(Line):
+    def __init__(self, shard, axis, count):
+        super().__init__(axis, count)
+        self.own, self.above, self.below = shard, [], []
+
+    def step(self):
+        if self.at:
+            self.keep()
+        up, down = (self.upward, self.downward) if self.at else (self.own, self.own)
+        self.at += 1
+        at, count = self.at, self.count
+        self.send(
+            up,
+            down,
+            [(i, i + 1) for i in range(at - 1, count - 1)],
+            [(i, i - 1) for i in range(1, count - at + 1)],
+        )
+
+    def keep(self):
+        self.below.append(self.upward)
+        self.above.append(self.downward)
+
+    def result(self):
+        while self.at < self.count - 1:
+            self.step()
+        self.keep()
+        return self.own, self.above, self.below
+
+
+class Sum(Line):
+    def __init__(self, parts, axis, count):
+        super().__init__(axis, count)
+        self.parts = parts
+
+    def step(self):
+        f32, bf16 = jnp.float32, jnp.bfloat16
+        first = self.at == 0
+        self.at += 1
+        at, count = self.at, self.count
+        up, down = self.parts[count - at], self.parts[at]
+        if not first:
+            up = (up.astype(f32) + self.upward.astype(f32)).astype(bf16)
+            down = (down.astype(f32) + self.downward.astype(f32)).astype(bf16)
+        self.send(
+            up,
+            down,
+            [(i, i + 1) for i in range(0, at)],
+            [(i, i - 1) for i in range(count - at, count)],
+        )
+
+    def result(self):
+        while self.at < self.count - 1:
+            self.step()
+        return self.parts[0], self.upward, self.downward
+
+
+def outer(left, right):
+    return lax.dot_general(
+        left, right, (((0,), (0,)), ((), ())), preferred_element_type=jnp.float32
+    )
+
+
+def chip_outer_kernel(where_ref, *refs, sides):
+    del where_ref
+    keep_x, sent_x, keep_y, sent_y = refs[-4:]
+    step = pl.program_id(0)
+    values = []
+    for side in range(sides):
+        left, left_other, right, right_other = refs[4 * side : 4 * side + 4]
+        product = outer(left[...], right[...]) + outer(left_other[...], right_other[...])
+        values.append(product.astype(jnp.bfloat16))
+    values = values[0] if sides == 1 else jnp.concatenate(values, axis=-1)
+    half = values.shape[1] // 2
+
+    for target, part, places in (
+        (keep_x, 0, (0, 1)),
+        (sent_x, 0, (2, 3)),
+        (keep_y, 1, (0, 3)),
+        (sent_y, 1, (1, 2)),
+    ):
+
+        @pl.when((step == places[0]) | (step == places[1]))
+        def _(target=target, part=part):
+            target[0] = values[:, part * half : (part + 1) * half]
+
+
+def chip_outer_call(where, pairs, seq_size, name, columns=1, column=0, into=None):
+    rows, width = pairs[0][0].shape
+    block = width // seq_size
+    half = sum(pair[2].shape[1] for pair in pairs) // 2
+
+    def left_index(k, w):
+        chip = jnp.where(k == 0, 0, jnp.where(k == 1, 2, jnp.where(k == 2, 3, 1)))
+        return 0, 2 * (w[2] ^ chip) + w[1]
+
+    specs, ins = [], []
+    for pair in pairs:
+        wide = pl.BlockSpec(pair[2].shape, lambda k, w: (0, 0))
+        specs += [pl.BlockSpec((rows, block), left_index)] * 2 + [wide, wide]
+        ins += list(pair)
+    aliases = {}
+    if into is not None:
+        aliases = {1 + len(ins) + i: i for i in range(4)}
+        specs += [pl.BlockSpec(memory_space=pltpu.HBM)] * 4
+        ins += list(into)
+
+    def target(place):
+        return pl.BlockSpec((1, block, half), lambda k, w: (place(k), 0, column))
+
+    return pl.pallas_call(
+        functools.partial(chip_outer_kernel, sides=len(pairs)),
+        out_shape=(pltpu.HBM((2, block, columns * half), jnp.bfloat16),) * 4,
+        grid_spec=pltpu.PrefetchScalarGridSpec(
+            num_scalar_prefetch=1,
+            grid=(4,),
+            in_specs=specs,
+            out_specs=(
+                target(lambda k: jnp.minimum(k, 1)),
+                target(lambda k: k // 3),
+                target(lambda k: k // 3),
+                target(lambda k: k // 2),
+            ),
+        ),
+        input_output_aliases=aliases,
+        compiler_params=pltpu.CompilerParams(vmem_limit_bytes=24 << 20),
+        cost_estimate=SHORT,
+        name=name,
+    )(where, *ins)
+
+
+class ChipSum:
+    def __init__(self, arrays, seq_size):
+        self.arrays, self.size = arrays, seq_size
+
+    def over(self, values, side):
+        return lax.ppermute(values, "seq", [(i, i ^ side) for i in range(self.size)])
+
+    def first(self, *earlier):
+        _, sent_x, _, sent_y = self.arrays
+        if earlier:
+            sent_x, sent_y = tie(sent_x, sent_y, *earlier)[:2]
+        self.got_x, self.got_y = self.over(sent_x, 2), self.over(sent_y, 4)
+
+    def tie(self, *others):
+        self.got_x, self.got_y, *others = tie(self.got_x, self.got_y, *others)
+        return others[0] if len(others) == 1 else others
+
+    def second(self, *earlier):
+        f32, bf16 = jnp.float32, jnp.bfloat16
+        if earlier:
+            self.got_x, self.got_y = tie(self.got_x, self.got_y, *earlier)[:2]
+        keep_x, _, keep_y, _ = self.arrays
+        through_x = (keep_x[1].astype(f32) + self.got_x[0].astype(f32)).astype(bf16)
+        through_y = (keep_y[1].astype(f32) + self.got_y[1].astype(f32)).astype(bf16)
+        self.last_x, self.last_y = self.over(through_x, 4), self.over(through_y, 2)
+
+    def tie_last(self, *values):
+        self.last_x, self.last_y, *values = tie(self.last_x, self.last_y, *values)
+        return values
+
+    def terms(self):
+        keep_x, _, keep_y, _ = self.arrays
+        return (keep_x, self.got_x, self.last_x), (keep_y, self.got_y, self.last_y)
+
+
+def widen_kernel(*refs, terms, turned):
+    f32 = jnp.float32
+    values_refs, outs = refs[: len(terms)], refs[len(terms) :]
+    column = 0
+    for index, out_ref in enumerate(outs):
+        wide = out_ref.shape[0] if turned[index] else out_ref.shape[1]
+        columns = slice(column, column + wide)
+        total = None
+        for ref, place in zip(values_refs, terms):
+            values = ref[:, columns] if place is None else ref[place, :, columns]
+            total = values.astype(f32) if total is None else total + values.astype(f32)
+        out_ref[...] = total.T if turned[index] else total
+        column += wide
+
+
+def widen(values, terms, widths, turned, name):
+    rows = values[-1].shape[0]
+    outs = [made((w, rows) if t else (rows, w), jnp.float32) for w, t in zip(widths, turned)]
+    kernel = functools.partial(widen_kernel, terms=terms, turned=turned)
+    return call(kernel, outs, tuple(values), name=name, room=24)
+
+
+def widen_pair_kernel(*refs, turned):
+    f32 = jnp.float32
+    outs = refs[6:]
+    for index, out_ref in enumerate(outs):
+        half = (out_ref.shape[0] if turned[index] else out_ref.shape[1]) // 2
+        columns = slice(index * half, (index + 1) * half)
+        for way, (got_place, keep, got, last) in enumerate(((1, *refs[:3]), (0, *refs[3:6]))):
+            total = keep[0, :, columns].astype(f32) + got[got_place, :, columns].astype(f32)
+            total = total + last[:, columns].astype(f32)
+            target = slice(way * half, (way + 1) * half)
+            if turned[index]:
+                out_ref[target, :] = total.T
+            else:
+                out_ref[:, target] = total
+
+
+def widen_pair(values, width, turned, name):
+    rows = values[2].shape[0]
+    outs = [made((width, rows) if t else (rows, width), jnp.float32) for t in turned]
+    kernel = functools.partial(widen_pair_kernel, turned=turned)
+    return call(kernel, outs, tuple(values), name=name, room=24)
+
+
+def matmul_kernel(where_ref, left_ref, right_ref, out_ref, *, turned, parts):
+    product = (dense_t if turned else dense)(left_ref[...], right_ref[...]).astype(out_ref.dtype)
+    if parts == 1:
+        out_ref[...] = product
+    part = product.shape[0] // parts
+    for k in range(parts if parts > 1 else 0):
+        place = where_ref[0] ^ k
+        rows = pl.ds(pl.multiple_of(place * part, part), part)
+        out_ref[rows, :] = product[k * part : (k + 1) * part]
+
+
+def matmul_call(where, left, right, dtype, turned, name, parts=1):
+    rows, depth = left.shape
+    columns = right.shape[0 if turned else 1]
+    wide = 512
+    right = pltpu.with_memory_space_constraint(right, pltpu.HBM)
+    if turned:
+        right_spec = pl.BlockSpec((wide, depth), lambda f, w: (f, 0))
+    else:
+        right_spec = pl.BlockSpec((depth, wide), lambda f, w: (0, f))
+    return pl.pallas_call(
+        functools.partial(matmul_kernel, turned=turned, parts=parts),
+        out_shape=made((rows, columns), dtype),
+        grid_spec=pltpu.PrefetchScalarGridSpec(
+            num_scalar_prefetch=1,
+            grid=(columns // wide,),
+            in_specs=[pl.BlockSpec((rows, depth), lambda f, w: (0, 0)), right_spec],
+            out_specs=pl.BlockSpec((rows, wide), lambda f, w: (0, f)),
+        ),
+        compiler_params=pltpu.CompilerParams(vmem_limit_bytes=20 << 20),
+        cost_estimate=SHORT,
+        name=name,
+    )(where, left, right)
+
+
+def turn_kernel(query_ref, both_ref, other_ref, cosine_ref, sine_ref, out_ref):
+    head = HEAD_WIDTH
+    step = 256
+
+    def piece(index, carry):
+        rows = pl.ds(pl.multiple_of(index * step, step), step)
+        both = both_ref[rows, :] + other_ref[rows, :].astype(jnp.float32)
+        cosine, sine = cosine_ref[rows, :], sine_ref[rows, :]
+        for place, values in ((0, query_ref[rows, :]), (1, both[:, :head])):
+            values = values * cosine - pltpu.roll(values, head // 2, 1) * sine
+            out_ref[rows, place * head : (place + 1) * head] = values.astype(jnp.bfloat16)
+        out_ref[rows, 2 * head :] = both[:, head:].astype(jnp.bfloat16)
+        return carry
+
+    lax.fori_loop(0, query_ref.shape[0] // step, piece, 0)
+
+
+def local_heads_apart(
+    tokens,
+    gain_attn,
+    w_query,
+    w_key,
+    w_value,
+    w_out,
+    gain_ffn,
+    w_gate,
+    w_up,
+    w_down,
+    cotangent,
+    doc_ids,
+    valid,
+    group_order,
+    *,
+    seq_size,
+    tp_size,
+):
+    _, row_count, width = tokens.shape
+    length = doc_ids.shape[1]
+    groups = group_order.shape[1]
+    span = length // groups
+    head = HEAD_WIDTH
+    heads = w_query.shape[1] // head
+    own_width = heads * head
+    hidden = w_gate.shape[1]
+    chips = seq_size // 2
+    part = row_count // tp_size
+    block = width // seq_size
+    bf16, f32, i32 = jnp.bfloat16, jnp.float32, jnp.int32
+    same_core = [[2 * p + c for p in range(chips)] for c in range(2)]
+    other_core = [(i, i ^ 1) for i in range(seq_size)]
+    own_seq, own_tp = lax.axis_index("seq"), lax.axis_index("tp")
+    core = own_seq % 2
+    where = jnp.stack([own_tp, core, own_seq // 2]).astype(i32)
+    tokens = tokens.reshape(row_count, width)
+    upstream = cotangent.reshape(row_count, width)
+    gain_attn, gain_ffn = gain_attn.reshape(1, width), gain_ffn.reshape(1, width)
+
+    def swap(values):
+        return lax.ppermute(values, "seq", other_core)
+
+    def to_heads(values):
+        return lax.all_to_all(values, "seq", 0, 0, axis_index_groups=same_core, tiled=True)
+
+    def part_of(values, place):
+        return lax.dynamic_slice_in_dim(values, place * part, part, 0)
+
+    def reordered(values):
+        return jnp.concatenate([part_of(values, own_tp ^ k) for k in range(tp_size)], axis=0)
+
+    def across(values, k):
+        return lax.ppermute(values, "tp", [(i, i ^ k) for i in range(tp_size)])
+
+    half = own_width // 2
+    weight_line = Gather(lax.dynamic_slice_in_dim(w_out, core * half, half, 0), "tp", tp_size)
+    weight_line.step()
+
+    order = group_order[0]
+    per_device = row_count // span
+
+    def blocks_of(which):
+        devices = 2 * jnp.arange(chips, dtype=i32) + which
+        storage = (devices[:, None] * per_device + jnp.arange(per_device)[None, :]).reshape(-1)
+        return jnp.take(order, storage)
+
+    def places_of(block_ids):
+        return (block_ids[:, None] * span + jnp.arange(span, dtype=i32)[None, :]).reshape(-1)
+
+    own_blocks, other_blocks = blocks_of(core), blocks_of(1 - core)
+    slot_places = jnp.concatenate([own_blocks, other_blocks])
+    docs = doc_ids[0]
+    first = jnp.sum(docs[None, :] < docs.reshape(groups, span)[:, :1], axis=1, dtype=i32)
+    position = jnp.arange(length, dtype=i32).reshape(groups, span)
+    change = jnp.where(docs != jnp.roll(docs, 1), jnp.arange(length, dtype=i32), 0)
+    change = change.reshape(groups, span)
+    start = jnp.max(
+        jnp.where(position[:, None, :] <= position[:, :, None], change[:, None, :], 0), axis=2
+    )
+    start = jnp.maximum(start, first[:, None])
+    start_q = jnp.take(start, own_blocks, axis=0)
+    key_low = jnp.take(first, own_blocks) // span
+    row_blocks = jnp.take(order, own_seq * per_device + jnp.arange(per_device, dtype=i32))
+    live = jnp.take(valid.reshape(groups, span), row_blocks, axis=0).reshape(row_count, 1)
+    cosine, sine = rope_tables(places_of(row_blocks), head)
+    cosine = jnp.concatenate([cosine, cosine], axis=-1)
+    sine = jnp.concatenate([-sine, sine], axis=-1)
+    cosine_q, sine_q = rope_tables(places_of(own_blocks), head)
+    cosine_q = jnp.concatenate([cosine_q, cosine_q], axis=-1)
+    sine_q = jnp.concatenate([-sine_q, sine_q], axis=-1)
+
+    packed, normed_attn = project_call(
+        tokens, gain_attn, live, cosine, sine, w_query, w_key, w_value
+    )
+    mine = to_heads(packed).reshape(chips * row_count, 3 * head)
+    upstream_rel = reordered(weight_line.tie(upstream))
+    weight_line.step()
+    grad_act = matmul_call(where, upstream_rel, w_down, f32, True, "grad_act")
+    upstream_pair = (upstream_rel, swap(upstream_rel))
+    normed_attn_pair = (normed_attn, swap(normed_attn))
+    mine, grad_act = weight_line.tie(mine, grad_act)
+    weight_line.step()
+    other = swap(mine[:, head:])
+
+    attended = attend_call(slot_places, key_low, mine, other, start_q.reshape(-1, 1), span)
+    attended = to_heads(attended.reshape(chips, row_count, head))
+    attended = attended.transpose(1, 0, 2).reshape(row_count, own_width)
+    attended_part = lax.all_to_all(
+        attended.reshape(tp_size, part, own_width), "tp", 0, 0, tiled=True
+    )
+    weight_line.tie(attended_part)
+    own_w, above_w, below_w = weight_line.result()
+    out_weights = []
+    for d in range(tp_size):
+        piece = own_w if d == 0 else above_w[d - 1] + below_w[tp_size - 1 - d]
+        out_weights += [piece, swap(piece)]
+    middle, normed_part = call(
+        out_kernel,
+        (made((part, width), f32), made((part, width), bf16)),
+        (where, tokens, gain_ffn, attended_part, *out_weights),
+        scalars=1,
+        work=2 * part * width * width,
+        name="out",
+    )
+
+    line = Gather(normed_part, "tp", tp_size)
+    line.step()
+    line.step()
+    above_1, below_1 = line.above[0], line.below[0]
+    filled, (own_grad, grad_1) = ffn_call(
+        where, 0, [normed_part, above_1, below_1], grad_act, w_gate, w_up, None
+    )
+    filled = line.tie(*filled)
+    line.step()
+    above_2, below_2 = line.above[1], line.below[1]
+    filled, (grad_2,) = ffn_call(where, 2, [above_2, below_2], grad_act, w_gate, w_up, filled)
+    *filled, grad_1, grad_2 = line.tie(*filled, grad_1, grad_2)
+    grad_1, grad_2 = across(grad_1, 1), across(grad_2, 2)
+    _, (_, _, above_3), (_, _, below_3) = line.result()
+    filled, (grad_3,) = ffn_call(
+        where, 3, [above_1, below_1, above_3, below_3], grad_act, w_gate, w_up, filled
+    )
+    grad_3 = across(grad_3, 3)
+    activated, gate_pre, up_pre, normed_ffn = filled
+
+    normed_pair = (normed_ffn, swap(normed_ffn))
+    outer_ffn = functools.partial(
+        chip_outer_call, where, seq_size=seq_size, name="ffn_outer"
+    )
+    gate_quad = (*normed_pair, gate_pre, swap(gate_pre))
+    up_quad = (*normed_pair, up_pre, swap(up_pre))
+    down_quad = (*upstream_pair, activated, swap(activated))
+    *gate_quad, grad_1, grad_2 = tie(*gate_quad, grad_1, grad_2)
+    gate_sum = ChipSum(outer_ffn([gate_quad]), seq_size)
+    gate_sum.first()
+    rest_grads = outer_ffn([up_quad], columns=2, column=0)
+    rest_grads = outer_ffn([down_quad], columns=2, column=1, into=rest_grads)
+    grad_3, *rest_grads = tie(grad_3, *rest_grads)
+    rest_sum = ChipSum(rest_grads, seq_size)
+    middle_low, grad_middle, grad_attended, gain_ffn_part = call(
+        middle_kernel,
+        (
+            made((part, width), bf16),
+            made((part, width), f32),
+            made((tp_size, part, own_width), bf16),
+            made((1, width), f32),
+        ),
+        (where, middle, upstream, gain_ffn, own_grad, grad_1, grad_2, grad_3, *out_weights),
+        scalars=1,
+        work=2 * part * width * width,
+        name="middle",
+    )
+    grad_attended = lax.all_to_all(grad_attended, "tp", 0, 0, tiled=True)
+    branch = matmul_call(where, after(activated, middle_low), w_down, bf16, False, "branch", tp_size)
+    grad_attended, branch = gate_sum.tie(grad_attended, branch)
+    branch = after(branch, grad_attended)
+    branch_part = lax.psum_scatter(branch, "tp", scatter_dimension=0, tiled=True)
+    middle_all = lax.all_gather(after(middle_low, grad_attended), "tp", axis=0, tiled=True)
+    grad_attended = grad_attended.reshape(row_count, heads, head).transpose(1, 0, 2)
+    grad_heads = to_heads(grad_attended).reshape(chips * row_count, head)
+    grad_query, both, both_other = attend_back_call(
+        slot_places, key_low, mine, other, start_q, grad_heads, span
+    )
+    other_term = swap(both_other)
+    packed_back = call(
+        turn_kernel,
+        (made((chips * row_count, 3 * head), bf16),),
+        (grad_query, both, other_term, cosine_q, sine_q),
+        name="turn",
+    )[0].reshape(chips, row_count, 3 * head)
+    back_heads = to_heads(packed_back)
+    rest_sum.first(packed_back)
+    attended_pair = (attended, swap(attended))
+    back_heads = after(back_heads, attended_pair[1])
+    layer_part = call(
+        layer_kernel,
+        (made((part, width), bf16),),
+        (middle, branch_part),
+        name="layer",
+    )[0]
+    layer_out = lax.all_gather(after(layer_part, middle_all), "tp", axis=0, tiled=True)
+    low, gain_attn_part, *parts = back_call(
+        where, back_heads, live, tokens, (w_query, w_key, w_value), tp_size
+    )
+    sums = Sum(parts, "tp", tp_size)
+    sums.step()
+    middle_all = after(middle_all, low)
+    middle_pair = (middle_all, swap(middle_all))
+    attn_grads = chip_outer_call(
+        where,
+        [(*middle_pair, *attended_pair), (*normed_attn_pair, low, swap(low))],
+        seq_size,
+        "attn_outer",
+    )
+    attn_grads, low = sums.tie(attn_grads, low)
+    attn_sum = ChipSum(attn_grads, seq_size)
+    attn_sum.first()
+    gate_sum.second(low)
+    sums.step()
+    gains = jnp.concatenate([gain_attn_part, gain_ffn_part], axis=0)
+    gains = after(gains.reshape(2, seq_size, block).transpose(1, 0, 2), low)
+    gains = jnp.sum(lax.all_to_all(gains, "seq", 0, 0, tiled=True), axis=0).reshape(1, 2 * block)
+    low = sums.tie(rest_sum.tie(low))
+    rest_sum.second(low)
+    sums.step()
+    tokens_part = call(
+        tokens_kernel,
+        (made((part + 16, width), bf16),),
+        (where, tokens, gain_attn, grad_middle, gains, *sums.result()),
+        scalars=1,
+        name="tokens",
+    )[0]
+    tokens_part, _ = gate_sum.tie_last(*rest_sum.tie_last(attn_sum.tie(after(tokens_part, layer_out)), low))
+    token_line = Gather(tokens_part, "tp", tp_size)
+    token_line.step()
+    attn_sum.second()
+    gate_x, gate_y = gate_sum.terms()
+    (grad_gate,) = widen_pair([*gate_x, *gate_y], hidden, (False,), "widen_gate")
+    rest_x, rest_y = rest_sum.terms()
+    grad_up, grad_down = widen_pair([*rest_x, *rest_y], hidden, (False, True), "widen_rest")
+    grad_gate = token_line.tie(grad_gate)
+    token_line.step()
+    terms_x, terms_y = attn_sum.terms()
+    grad_out, grad_query = widen(
+        terms_x, [0, 1, None], [own_width] * 2, (True, False), "widen_attn"
+    )
+    grad_key, grad_value = widen(
+        terms_y, [0, 0, None], [own_width] * 2, (False, False), "widen_attn"
+    )
+    grad_out, grad_key = token_line.tie(grad_out, grad_key)
+    token_line.step()
+    grad_tokens, gains = join(where, token_line.result(), f32, False, 2 * block)
+    gains = gains.reshape(2, block)
+
+    return (
+        layer_out.reshape(1, row_count, width),
+        grad_tokens.reshape(1, row_count, width),
+        gains[0],
+        grad_query,
+        grad_key,
+        grad_value,
+        grad_out,
+        gains[1],
+        grad_gate,
+        grad_up,
+        grad_down,
+    )
+
+
 def solution(mesh):
     placed = (
         P(None, "seq", None),
@@ -316,6 +1406,14 @@
         P(),
         P(),
     )
+    seq_size, tp_size = mesh.shape["seq"], mesh.shape["tp"]
+
+    def local(*args):
+        heads = args[2].shape[1] // HEAD_WIDTH
+        if seq_size == 8 and tp_size == 4 and heads == 4 and args[0].shape[0] == 1:
+            return local_heads_apart(*args, seq_size=seq_size, tp_size=tp_size)
+        return local_general(*args)
+
     return jax.shard_map(
         local,
         mesh=mesh,

time: 1540 us -> 534 us (0.35)
  waiting for transfers between devices: 1130 us -> 164 us
  matrix products: 241 us -> 0 us
  Pallas kernels: 0 us -> 157 us
  starting transfers between devices: 2.11 us -> 82.1 us
  other arithmetic: 56.7 us -> 33.1 us
    reduce_scatter x9 -> x1, waiting for transfers between devices: 646 us -> 0.02 us  [local_heads_apart(): lax.psum_scatter(branch, 'tp', scatter_dimension=0, tiled=True)]
    psum x4 -> x0, waiting for transfers between devices: 480 us -> none  [the longest x1 157 us: local(): lax.psum(jnp.dot(attended_flat, w_out, preferred_element_type=jnp.float32...]
    dot_general x27 -> x0, matrix products: 241 us -> none  [the longest x1 21.6 us: attend_back(): jnp.einsum('hqk,qhe->khe', weights, grad_heads, preferred_element_type=jn...]
    pallas_call x0 -> x23, Pallas kernels: none -> 157 us  [the longest x3 37.9 us: ffn_call(): pl.pallas_call(functools.partial(ffn_kernel, chunk=chunk, sources=len(sou...]
    ppermute x0 -> x54, waiting for transfers between devices: none -> 128 us  [the longest x12 52.6 us: send(): self.downward = lax.ppermute(down, self.axis, down_pairs)]
    ppermute x0 -> x54, starting transfers between devices: none -> 57.6 us  [the longest x12 22 us: send(): self.upward = lax.ppermute(up, self.axis, up_pairs)]
    gather x4 -> x6, local copies, waits for them, and re-layouts: 51.4 us -> 3.7 us  [the longest x2 1.28 us: blocks_of(): return jnp.take(order, storage)]
    all_to_all x0 -> x6, waiting for transfers between devices: none -> 34.8 us  [the longest x4 27.9 us: to_heads(): lax.all_to_all(values, 'seq', 0, 0, axis_index_groups=same_core, tiled=True)]
  transfers between devices with their start and end apart: 15 -> 63, of which waited for: 13 -> 26; matrix products, arithmetic and copies ran while one was open for 14% -> 9% of each run, Pallas kernels for 0% -> 27%
where the time goes in v2:
time: 534 us; the launch traced here: 525 us
  waiting for transfers between devices  164 us (31%)
  Pallas kernels  157 us (29%)
  starting transfers between devices  82.1 us (15%)
  local copies, waits for them, and re-layouts  57.2 us (11%)
  other arithmetic  33.1 us (6%)
  blocking collectives  16.4 us (3%)
  between operations  15 us (3%)
    ppermute x12, waiting for transfers between devices, send(): self.downward = lax.ppermute(down, self.axis, down_pairs)  52.6 us
    unnamed x132, local copies, waits for them, and re-layouts  41.7 us
    ppermute x12, waiting for transfers between devices, over(): lax.ppermute(values, 'seq', [(i, i ^ side) for i in range(self.size)])  40.5 us
    pallas_call x3, Pallas kernels, ffn_call(): pl.pallas_call(functools.partial(ffn_kernel, chunk=chunk, sources=len(sou...  37.9 us
    pallas_call x4, Pallas kernels, chip_outer_call(): pl.pallas_call(functools.partial(chip_outer_kernel, sides=len(pairs)), ou...  33.5 us
    pallas_call x10, Pallas kernels, call(): pl.pallas_call(kernel, out_shape=tuple(outs), in_specs=[SMALL] * scalars...  28 us
    all_to_all x4, waiting for transfers between devices, to_heads(): lax.all_to_all(values, 'seq', 0, 0, axis_index_groups=same_core, tiled=True)  27.9 us
    ppermute x12, starting transfers between devices, send(): self.upward = lax.ppermute(up, self.axis, up_pairs)  22 us
  transfers between devices with their start and end apart: 63, of which 26 were waited for; matrix products, arithmetic and copies ran while one was open for 9% of the time, Pallas kernels for 27%

profile of v2, /device:TPU:0, one launch (start us, length us, event | category | flops | bytes accessed | tf_op | source)
XLA Modules:
  0.0 524.9 jit_solution(12199751126780069065)
XLA Ops:
  8.9 6.1 %collective-permute-start = (bf16[256,2048]{1,0:T(8,128)(2,1)S(1)}, bf16[256,2048]{1,0:T(8,128)(2,1)}, u32[]{:S(2)}, u32[]{:S(2)}) collective-permute-start(bf16[256,2048]{1,0:T(8,128)(2,1)S(1)} %constant_dynamic-slice_fusion.4.refs_0_.refs_4_), channel_id=1, source_target_pairs={{0,1},{1,2},{2,3},{4,5},{5,6},{6,7},{8,9},{9,10},{10,11},{12,13},{... | collective-permute-start | bytes 3145736 | tf_op jit(solution)/shard_map/ppermute | solution.py:856
  20.3 6.5 %project.1 = (bf16[4,512,384]{2,1,0:T(8,128)(2,1)S(1)}, bf16[512,2048]{1,0:T(8,128)(2,1)S(1)}) custom-call(bf16[512,2048]{1,0:T(8,128)(2,1)S(1)} %bitcast.72, f32[1,2048]{1,0:T(1,128)S(1)} %bitcast.86, s32[512,1]{1,0:T(8,128)S(1)} %bitcast.80, f32[512,128]{1,0:T(8,128)S(1)} %get-tuple-element.310.cosine_ref, f32[512,128]{1,0:T(8,128)S(1)} %get-tuple-element.311.sine_ref, ...), custom_call_target="tpu_custom_call" | custom-call | flops 1 | bytes 1 | tf_op jit(solution)/shard_map/project/pallas_call | solution.py:482
  29.3 4.5 all-to-all-start
  37.3 4.3 collective-permute-done.1
  47.9 7.8 %grad_act.1.refs_3_.refs_2_.refs_4_ = f32[512,2048]{1,0:T(8,128)S(1)} custom-call(s32[3]{0:T(128)S(1)} %pad_add_fusion.1.where_ref, bf16[512,2048]{1,0:T(8,128)(2,1)S(1)} %pad_maximum_fusion.left_ref.refs_0_, bf16[2048,2048]{1,0:T(8,128)(2,1)} %right_ref.3), custom_call_target="tpu_custom_call" | custom-call | flops 1 | bytes 1 | tf_op jit(solution)/shard_map/grad_act/pallas_call | solution.py:1090
  59.1 11.4 %collective-permute-done.3 = bf16[256,2048]{1,0:T(8,128)(2,1)} collective-permute-done((bf16[256,2048]{1,0:T(8,128)(2,1)}, bf16[256,2048]{1,0:T(8,128)(2,1)}, u32[]{:S(2)}, u32[]{:S(2)}) %collective-permute-start.3) | collective-permute-done | bytes 1048608 | tf_op jit(solution)/shard_map/ppermute | solution.py:857
  77.5 10.7 %attend.1 = bf16[2048,128]{1,0:T(8,128)(2,1)S(1)} custom-call(s32[16]{0:T(128)S(1)} %pad_add_fusion.2.slot_places, s32[8]{0:T(128)S(1)} %get-tuple-element.292.key_low, bf16[2048,384]{1,0:T(8,128)(2,1)} %bitcast.13.own_ref, bf16[2048,256]{1,0:T(8,128)(2,1)} %collective-permute-done.4.other_ref, s32[2048,1]{1,0:T(8,128)S(1)} %bitcast.79), custom_call_target="tpu_custom_call" | custom-call | flops 1 | bytes 1 | tf_op jit(solution)/shard_map/attend/pallas_call | solution.py:438
  89.0 4.1 all-to-all-start.1
  96.1 5.1 all-to-all-done.1
  105.5 4.2 all-to-all-start.2
  113.1 15.5 %collective-permute-done.7 = bf16[256,2048]{1,0:T(8,128)(2,1)} collective-permute-done((bf16[256,2048]{1,0:T(8,128)(2,1)}, bf16[256,2048]{1,0:T(8,128)(2,1)}, u32[]{:S(2)}, u32[]{:S(2)}) %collective-permute-start.7) | collective-permute-done | bytes 1048608 | tf_op jit(solution)/shard_map/ppermute | solution.py:857
  136.9 3.6 out.1
  143.3 10.5 %collective-permute-done.12.refs_2_.refs_1_ = bf16[128,2048]{1,0:T(8,128)(2,1)S(1)} collective-permute-done((bf16[128,2048]{1,0:T(8,128)(2,1)S(1)}, bf16[128,2048]{1,0:T(8,128)(2,1)S(1)}, u32[]{:S(2)}, u32[]{:S(2)}) %collective-permute-start.12) | collective-permute-done | bytes 524320 | tf_op jit(solution)/shard_map/ppermute | solution.py:856
  154.5 3.5 collective-permute-done.11.refs_1_.refs_0_
  159.6 13.9 %ffn.3 = (bf16[512,2048]{1,0:T(8,128)(2,1)S(1)}, bf16[512,2048]{1,0:T(8,128)(2,1)S(1)}, bf16[512,2048]{1,0:T(8,128)(2,1)S(1)}, bf16[512,2048]{1,0:T(8,128)(2,1)S...) custom-call(s32[3]{0:T(128)S(1)} %pad_add_fusion.1.where_ref, ...), custom_call_target="tpu_custom_call" | custom-call | flops 1 | bytes 1 | tf_op jit(solution)/shard_map/ffn/pallas_call | solution.py:662
  175.5 12.0 %ffn.4 = (bf16[512,2048]{1,0:T(8,128)(2,1)S(1)}, bf16[512,2048]{1,0:T(8,128)(2,1)S(1)}, bf16[512,2048]{1,0:T(8,128)(2,1)S(1)}, bf16[512,2048]{1,0:T(8,128)(2,1)S(1)}, bf16[128,2048]{1,0:T(8,128)(2,1)S(1)}) custom-call(s32[3]{0:T(128)S(1)} %pad_add_fusion.1.where_ref, ...), custom_call_target="tpu_custom_call", output_to_operand_aliasing={{0}: (6, {}), {1}: (7, {}), {2}: (8, {}), {3}: (9, {})} | custom-call | flops 1 | bytes 1 | tf_op jit(solution)/shard_map/ffn/pallas_call | solution.py:662
  190.7 12.0 %ffn.5 = (bf16[512,2048]{1,0:T(8,128)(2,1)S(1)}, bf16[512,2048]{1,0:T(8,128)(2,1)S(1)}, bf16[512,2048]{1,0:T(8,128)(2,1)S(1)}, bf16[512,2048]{1,0:T(8,128)(2,1)S(1)}, bf16[128,2048]{1,0:T(8,128)(2,1)S(1)}) custom-call(s32[3]{0:T(128)S(1)} %pad_add_fusion.1.where_ref, ...), custom_call_target="tpu_custom_call", output_to_operand_aliasing={{0}: (8, {}), {1}: (9, {}), {2}: (10, {}), {3}: (11, {})} | custom-call | flops 1 | bytes 1 | tf_op jit(solution)/shard_map/ffn/pallas_call | solution.py:662
  203.4 8.4 %collective-permute-done.19.refs_1_ = bf16[128,2048]{1,0:T(8,128)(2,1)S(1)} collective-permute-done((bf16[128,2048]{1,0:T(8,128)(2,1)S(1)}, bf16[128,2048]{1,0:T(8,128)(2,1)S(1)}, u32[]{:S(2)}, u32[]{:S(2)}) %collective-permute-start.19) | collective-permute-done | bytes 524320 | tf_op jit(solution)/shard_map/ppermute | solution.py:1175
  211.7 3.3 collective-permute-done.20.refs_2_
  216.6 8.1 %ffn_outer.3 = (bf16[2,256,1024]{2,1,0:T(8,128)(2,1)}, bf16[2,256,1024]{2,1,0:T(8,128)(2,1)}, bf16[2,256,1024]{2,1,0:T(8,128)(2,1)}, bf16[2,256,1024]{2,1,0:T(8,128)(2,1)}) custom-call(s32[3]{0:T(128)S(1)} %pad_add_fusion.1.where_ref, bf16[512,2048]{1,0:T(8,128)(2,1)S(1)} %get-tuple-element.188.refs_0_, ...), custom_call_target="tpu_custom_call" | custom-call | flops 1 | bytes 1 | tf_op jit(solution)/shard_map/ffn_outer/pallas_call | solution.py:969
  227.9 8.1 %ffn_outer.4 = (bf16[2,256,2048]{2,1,0:T(8,128)(2,1)}, bf16[2,256,2048]{2,1,0:T(8,128)(2,1)}, bf16[2,256,2048]{2,1,0:T(8,128)(2,1)}, bf16[2,256,2048]{2,1,0:T(8,128)(2,1)}) custom-call(s32[3]{0:T(128)S(1)} %pad_add_fusion.1.where_ref, bf16[512,2048]{1,0:T(8,128)(2,1)S(1)} %get-tuple-element.188.refs_0_, ...), custom_call_target="tpu_custom_call" | custom-call | flops 1 | bytes 1 | tf_op jit(solution)/shard_map/ffn_outer/pallas_call | solution.py:969
  236.1 8.1 %ffn_outer.5 = (bf16[2,256,2048]{2,1,0:T(8,128)(2,1)}, bf16[2,256,2048]{2,1,0:T(8,128)(2,1)}, bf16[2,256,2048]{2,1,0:T(8,128)(2,1)}, bf16[2,256,2048]{2,1,0:T(8,128)(2,1)}) custom-call(s32[3]{0:T(128)S(1)} %pad_add_fusion.1.where_ref, bf16[512,2048]{1,0:T(8,128)(2,1)S(1)} %copy-done.7, ...), custom_call_target="tpu_custom_call", output_to_operand_aliasing={{0}: (5, {}), {1}: (6, {}), {2}: (7, {}), {3}: (8, {})} | custom-call | flops 1 | bytes 1 | tf_op jit(solution)/shard_map/ffn_outer/pallas_call | solution.py:969
  244.2 6.1 %middle.1 = (bf16[128,2048]{1,0:T(8,128)(2,1)}, f32[128,2048]{1,0:T(8,128)S(1)}, bf16[4,128,512]{2,1,0:T(8,128)(2,1)S(1)}, f32[1,2048]{1,0:T(1,128)S(1)}) custom-call(s32[3]{0:T(128)S(1)} %pad_add_fusion.1.where_ref, f32[128,2048]{1,0:T(8,128)S(1)} %get-tuple-element.159.middle_ref, bf16[512,2048]{1,0:T(8,128)(2,1)S(1)} %bitcast.77, f32[1,2048]{1,0:T(1,128)S(1)} %bitcast.85, ...), custom_call_target="tpu_custom_call" | custom-call | flops 1 | bytes 1 | tf_op jit(solution)/shard_map/middle/pallas_call | solution.py:472
  252.1 3.6 all-to-all-start.3
  255.6 7.7 %branch.1 = bf16[512,2048]{1,0:T(8,128)(2,1)S(1)} custom-call(s32[3]{0:T(128)S(1)} %pad_add_fusion.1.where_ref, bf16[512,2048]{1,0:T(8,128)(2,1)S(1)} %get-tuple-element.211.refs_2_.left_ref, bf16[2048,2048]{1,0:T(8,128)(2,1)} %right_ref.3), custom_call_target="tpu_custom_call" | custom-call | flops 1 | bytes 1 | tf_op jit(solution)/shard_map/branch/pallas_call | solution.py:1090
  264.7 5.5 %all-to-all-done.3 = bf16[4,128,512]{2,1,0:T(8,128)(2,1)S(1)} async-done(((bf16[4,128,512]{2,1,0:T(8,128)(2,1)}), bf16[4,128,512]{2,1,0:T(8,128)(2,1)S(1)}, u32[]{:S(2)}, u32[]{:S(2)}) %all-to-all-start.3) | async-done | bytes 524320 | tf_op jit(solution)/shard_map/all_to_all | solution.py:1295
  271.1 3.7 all-to-all-start.4
  274.9 7.4 %all-to-all-done.4 = bf16[4,512,128]{2,1,0:T(8,128)(2,1)S(1)} async-done(((bf16[4,512,128]{2,1,0:T(8,128)(2,1)}), bf16[4,512,128]{2,1,0:T(8,128)(2,1)S(1)}, u32[]{:S(2)}, u32[]{:S(2)}) %all-to-all-start.4) | async-done | bytes 524320 | tf_op jit(solution)/shard_map/all_to_all | solution.py:1166
  284.1 15.8 %attend_back.1 = (f32[2048,128]{1,0:T(8,128)S(1)}, f32[2048,256]{1,0:T(8,128)S(1)}, bf16[2048,256]{1,0:T(8,128)(2,1)S(1)}) custom-call(s32[16]{0:T(128)S(1)} %pad_add_fusion.2.slot_places, s32[8]{0:T(128)S(1)} %get-tuple-element.292.key_low, bf16[2048,384]{1,0:T(8,128)(2,1)} %bitcast.13.own_ref, bf16[2048,256]{1,0:T(8,128)(2,1)} %collective-permute-done.4.other_ref, ...), custom_call_target="tpu_custom_call" | custom-call | flops 1 | bytes 1 | tf_op jit(solution)/shard_map/attend_back/pallas_call | solution.py:452
  300.1 3.7 fusion.8
  306.8 4.3 all-to-all-start.5
  315.9 15.4 %all-to-all-done.5.back_ref = bf16[4,512,384]{2,1,0:T(8,128)(2,1)} async-done(((bf16[4,512,384]{2,1,0:T(8,128)(2,1)}), bf16[4,512,384]{2,1,0:T(8,128)(2,1)}, u32[]{:S(2)}, u32[]{:S(2)}) %all-to-all-start.5) | async-done | bytes 1572896 | tf_op jit(solution)/shard_map/all_to_all | solution.py:1166
  331.4 9.0 %back.1 = (bf16[512,1536]{1,0:T(8,128)(2,1)S(1)}, f32[1,2048]{1,0:T(1,128)S(1)}, bf16[128,2048]{1,0:T(8,128)(2,1)S(1)}, bf16[128,2048]{1,0:T(8,128)(2,1)}, bf16[...) custom-call(s32[3]{0:T(128)S(1)} %pad_add_fusion.1.where_ref, bf16[4,512,384]{2,1,0:T(8,128)(2,1)} %all-to-all-done.5.back_ref, ...), custom_call_target="tpu_custom_call" | custom-call | flops 1 | bytes 1 | tf_op jit(solution)/shard_map/back/pallas_call | solution.py:753
  358.0 9.1 %attn_outer.1 = (bf16[2,256,1024]{2,1,0:T(8,128)(2,1)}, bf16[2,256,1024]{2,1,0:T(8,128)(2,1)}, bf16[2,256,1024]{2,1,0:T(8,128)(2,1)}, bf16[2,256,1024]{2,1,0:T(8,128)(2,1)}) custom-call(s32[3]{0:T(128)S(1)} %pad_add_fusion.1.where_ref, bf16[512,2048]{1,0:T(8,128)(2,1)S(1)} %copy-done.29, bf16[512,2048]{1,0:T(8,128)(2,1)S(1)} %collective-permute-done.31.refs_1_, ...), custom_call_target="tpu_custom_call" | custom-call | flops 1 | bytes 1 | tf_op jit(solution)/shard_map/attn_outer/pallas_call | solution.py:969
  368.5 4.3 collective-permute-start.38
  376.4 16.0 %collective-permute-done.36.refs_1_ = bf16[2,256,2048]{2,1,0:T(8,128)(2,1)} collective-permute-done((bf16[2,256,2048]{2,1,0:T(8,128)(2,1)}, bf16[2,256,2048]{2,1,0:T(8,128)(2,1)}, u32[]{:S(2)}, u32[]{:S(2)}) %collective-permute-start.36) | collective-permute-done | bytes 2097184 | tf_op jit(solution)/shard_map/ppermute | solution.py:995
  395.6 2.9 fusion.2
  406.9 12.9 %collective-permute-done.42.refs_1_ = bf16[2,256,1024]{2,1,0:T(8,128)(2,1)S(1)} collective-permute-done((bf16[2,256,1024]{2,1,0:T(8,128)(2,1)}, bf16[2,256,1024]{2,1,0:T(8,128)(2,1)S(1)}, u32[]{:S(2)}, u32[]{:S(2)}) %collective-permute-start.42) | collective-permute-done | bytes 1048608 | tf_op jit(solution)/shard_map/ppermute | solution.py:995
  425.2 3.0 collective-permute-done.44.below_ref
  429.8 3.8 collective-permute-done.45.above_ref
  435.5 16.4 %all_to_all.35 = f32[8,2,256]{2,1,0:T(2,128)S(1)} all-to-all(f32[8,2,256]{2,1,0:T(2,128)S(1)} %bitcast.95), channel_id=1, replica_groups=mesh['seq'=8,'tp'=4] {'seq'}, dimensions={0} | all-to-all | bytes 32768 | tf_op jit(solution)/shard_map/all_to_all | solution.py:1344
  465.4 3.6 widen_gate.1
  469.1 4.3 collective-permute-done.46.refs_3_
  473.4 4.0 collective-permute-done.47.refs_0_
  483.4 10.5 %collective-permute-done.51.refs_2_ = bf16[256,1024]{1,0:T(8,128)(2,1)S(1)} collective-permute-done((bf16[256,1024]{1,0:T(8,128)(2,1)S(1)}, bf16[256,1024]{1,0:T(8,128)(2,1)S(1)}, u32[]{:S(2)}, u32[]{:S(2)}) %collective-permute-start.51) | collective-permute-done | bytes 524320 | tf_op jit(solution)/shard_map/ppermute | solution.py:995
  498.3 5.7 %widen_rest.1 = (f32[256,2048]{1,0:T(8,128)}, f32[2048,256]{1,0:T(8,128)}) custom-call(bf16[2,256,2048]{2,1,0:T(8,128)(2,1)S(1)} %copy-done.8, bf16[2,256,2048]{2,1,0:T(8,128)(2,1)} %collective-permute-done.36.refs_1_, bf16[256,2048]{1,0:T(8,128)(2,1)} %collective-permute-done.40.refs_2_, bf16[2,256,2048]{2,1,0:T(8,128)(2,1)S(1)} %copy-done.10, ...), custom_call_target="tpu_custom_call" | custom-call | flops 1 | bytes 1 | tf_op jit(solution)/shard_map/widen_rest/pallas_call | solution.py:472
  504.0 8.3 %collective-permute-done.52.refs_2_ = bf16[144,2048]{1,0:T(8,128)(2,1)S(1)} collective-permute-done((bf16[144,2048]{1,0:T(8,128)(2,1)S(1)}, bf16[144,2048]{1,0:T(8,128)(2,1)S(1)}, u32[]{:S(2)}, u32[]{:S(2)}) %collective-permute-start.52) | collective-permute-done | bytes 589856 | tf_op jit(solution)/shard_map/ppermute | solution.py:857
  512.3 2.9 join.1
  (311 shorter events, 148.1 us)
Async XLA Ops:
  8.9 28.4 %collective-permute-start = (bf16[256,2048]{1,0:T(8,128)(2,1)S(1)}, bf16[256,2048]{1,0:T(8,128)(2,1)}, u32[]{:S(2)}, u32[]{:S(2)}) collective-permute-start(bf16[256,2048]{1,0:T(8,128)(2,1)S(1)} %constant_dynamic-slice_fusion.4.refs_0_.refs_4_), channel_id=1, source_target_pairs={{0,1},{1,2},{2,3},{4,5},{5,6},{6,7},{8,9},{9,10},{10,11},{12,13},{... | collective-permute-start | bytes 3145736 | tf_op jit(solution)/shard_map/ppermute | solution.py:856
  15.0 26.6 %collective-permute-start.1 = (bf16[256,2048]{1,0:T(8,128)(2,1)S(1)}, bf16[256,2048]{1,0:T(8,128)(2,1)}, u32[]{:S(2)}, u32[]{:S(2)}) collective-permute-start(bf16[256,2048]{1,0:T(8,128)(2,1)S(1)} %constant_dynamic-slice_fusion.4.refs_0_.refs_4_), channel_id=1, source_target_pairs={{1,0},{2,1},{3,2},{5,4},{6,5},{7,6},{9,8},{10,9},{11,10},{13,12},{... | collective-permute-start | bytes 3145736 | tf_op jit(solution)/shard_map/ppermute | solution.py:857
  29.3 29.8 %all-to-all-start = ((bf16[4,512,384]{2,1,0:T(8,128)(2,1)}), bf16[4,512,384]{2,1,0:T(8,128)(2,1)}, u32[]{:S(2)}, u32[]{:S(2)}) async-start(bf16[4,512,384]{2,1,0:T(8,128)(2,1)} %copy-done.38), calls=%async_computation | async-start | bytes 3145728 | tf_op jit(solution)/shard_map/all_to_all | solution.py:1166
  41.6 17.5 %collective-permute-start.2 = (bf16[256,2048]{1,0:T(8,128)(2,1)}, bf16[256,2048]{1,0:T(8,128)(2,1)}, u32[]{:S(2)}, u32[]{:S(2)}) collective-permute-start(bf16[256,2048]{1,0:T(8,128)(2,1)} %collective-permute-done), channel_id=1, source_target_pairs={{1,2},{2,3},{5,6},{6,7},{9,10},{10,11},{13,14},{14,15},{17,18},{18... | collective-permute-start | bytes 3145736 | tf_op jit(solution)/shard_map/ppermute | solution.py:856
  43.2 27.3 %collective-permute-start.3 = (bf16[256,2048]{1,0:T(8,128)(2,1)}, bf16[256,2048]{1,0:T(8,128)(2,1)}, u32[]{:S(2)}, u32[]{:S(2)}) collective-permute-start(bf16[256,2048]{1,0:T(8,128)(2,1)} %collective-permute-done.1), channel_id=1, source_target_pairs={{1,0},{2,1},{5,4},{6,5},{9,8},{10,9},{13,12},{14,13},{17,16},{18,1... | collective-permute-start | bytes 3145736 | tf_op jit(solution)/shard_map/ppermute | solution.py:857
  93.2 20.0 %collective-permute-start.6 = (bf16[256,2048]{1,0:T(8,128)(2,1)}, bf16[256,2048]{1,0:T(8,128)(2,1)}, u32[]{:S(2)}, u32[]{:S(2)}) collective-permute-start(bf16[256,2048]{1,0:T(8,128)(2,1)} %collective-permute-done.2), channel_id=1, source_target_pairs={{2,3},{6,7},{10,11},{14,15},{18,19},{22,23},{26,27},{30,31}} | collective-permute-start | bytes 3145736 | tf_op jit(solution)/shard_map/ppermute | solution.py:856
  94.8 33.8 %collective-permute-start.7 = (bf16[256,2048]{1,0:T(8,128)(2,1)}, bf16[256,2048]{1,0:T(8,128)(2,1)}, u32[]{:S(2)}, u32[]{:S(2)}) collective-permute-start(bf16[256,2048]{1,0:T(8,128)(2,1)} %collective-permute-done.3), channel_id=1, source_target_pairs={{1,0},{5,4},{9,8},{13,12},{17,16},{21,20},{25,24},{29,28}} | collective-permute-start | bytes 3145736 | tf_op jit(solution)/shard_map/ppermute | solution.py:857
  105.5 24.6 %all-to-all-start.2 = ((bf16[4,128,512]{2,1,0:T(8,128)(2,1)}), bf16[4,128,512]{2,1,0:T(8,128)(2,1)}, u32[]{:S(2)}, u32[]{:S(2)}) async-start(bf16[4,128,512]{2,1,0:T(8,128)(2,1)} %reshape_reshape.3), calls=%async_computation.2 | async-start | bytes 1048576 | tf_op jit(solution)/shard_map/all_to_all | solution.py:1230
  109.6 24.9 %collective-permute-start.5 = (bf16[256,2048]{1,0:T(8,128)(2,1)S(1)}, bf16[256,2048]{1,0:T(8,128)(2,1)}, u32[]{:S(2)}, u32[]{:S(2)}) collective-permute-start(bf16[256,2048]{1,0:T(8,128)(2,1)S(1)} %constant_dynamic-slice_fusion.4.refs_0_.refs_4_), channel_id=1, source_target_pairs={{0,4},{4,0},{8,12},{12,8},{16,20},{20,16},{24,28},{28,24},{1,5},{5... | collective-permute-start | bytes 3145736 | tf_op jit(solution)/shard_map/ppermute | solution.py:1163
  112.6 21.9 %collective-permute-start.9 = (bf16[256,2048]{1,0:T(8,128)(2,1)}, bf16[256,2048]{1,0:T(8,128)(2,1)}, u32[]{:S(2)}, u32[]{:S(2)}) collective-permute-start(bf16[256,2048]{1,0:T(8,128)(2,1)} %add.284.refs_4_.refs_8_), channel_id=1, source_target_pairs={{0,4},{4,0},{8,12},{12,8},{16,20},{20,16},{24,28},{28,24},{1,5},{5... | collective-permute-start | bytes 3145736 | tf_op jit(solution)/shard_map/ppermute | solution.py:1163
  142.0 15.9 %collective-permute-start.11 = (bf16[128,2048]{1,0:T(8,128)(2,1)S(1)}, bf16[128,2048]{1,0:T(8,128)(2,1)S(1)}, u32[]{:S(2)}, u32[]{:S(2)}) collective-permute-start(bf16[128,2048]{1,0:T(8,128)(2,1)S(1)} %get-tuple-element.160.refs_0_), channel_id=1, source_target_pairs={{1,0},{2,1},{3,2},{5,4},{6,5},{7,6},{9,8},{10,9},{11,10},{13,12},{... | collective-permute-start | bytes 1572872 | tf_op jit(solution)/shard_map/ppermute | solution.py:857
  153.8 19.7 %collective-permute-start.13 = (bf16[128,2048]{1,0:T(8,128)(2,1)S(1)}, bf16[128,2048]{1,0:T(8,128)(2,1)S(1)}, u32[]{:S(2)}, u32[]{:S(2)}) collective-permute-start(bf16[128,2048]{1,0:T(8,128)(2,1)S(1)} %collective-permute-done.12.refs_2_.refs_1_), channel_id=1, source_target_pairs={{1,2},{2,3},{5,6},{6,7},{9,10},{10,11},{13,14},{14,15},{17,18},{18... | collective-permute-start | bytes 1572872 | tf_op jit(solution)/shard_map/ppermute | solution.py:856
  157.9 15.6 %collective-permute-start.14 = (bf16[128,2048]{1,0:T(8,128)(2,1)S(1)}, bf16[128,2048]{1,0:T(8,128)(2,1)S(1)}, u32[]{:S(2)}, u32[]{:S(2)}) collective-permute-start(bf16[128,2048]{1,0:T(8,128)(2,1)S(1)} %collective-permute-done.11.refs_1_.refs_0_), channel_id=1, source_target_pairs={{1,0},{2,1},{5,4},{6,5},{9,8},{10,9},{13,12},{14,13},{17,16},{18,1... | collective-permute-start | bytes 1572872 | tf_op jit(solution)/shard_map/ppermute | solution.py:857
  174.2 15.1 %collective-permute-start.16 = (bf16[128,2048]{1,0:T(8,128)(2,1)S(1)}, bf16[128,2048]{1,0:T(8,128)(2,1)S(1)}, u32[]{:S(2)}, u32[]{:S(2)}) collective-permute-start(bf16[128,2048]{1,0:T(8,128)(2,1)S(1)} %collective-permute-done.14.refs_0_), channel_id=1, source_target_pairs={{1,0},{5,4},{9,8},{13,12},{17,16},{21,20},{25,24},{29,28}} | collective-permute-start | bytes 1572872 | tf_op jit(solution)/shard_map/ppermute | solution.py:857
  189.3 22.4 %collective-permute-start.19 = (bf16[128,2048]{1,0:T(8,128)(2,1)S(1)}, bf16[128,2048]{1,0:T(8,128)(2,1)S(1)}, u32[]{:S(2)}, u32[]{:S(2)}) collective-permute-start(bf16[128,2048]{1,0:T(8,128)(2,1)S(1)} %get-tuple-element.186), channel_id=1, source_target_pairs={{0,1},{1,0},{2,3},{3,2},{4,5},{5,4},{6,7},{7,6},{8,9},{9,8},{10,11... | collective-permute-start | bytes 1572872 | tf_op jit(solution)/shard_map/ppermute | solution.py:1175
  190.3 24.8 %collective-permute-start.20 = (bf16[128,2048]{1,0:T(8,128)(2,1)S(1)}, bf16[128,2048]{1,0:T(8,128)(2,1)S(1)}, u32[]{:S(2)}, u32[]{:S(2)}) collective-permute-start(bf16[128,2048]{1,0:T(8,128)(2,1)S(1)} %get-tuple-element.187), channel_id=1, source_target_pairs={{0,2},{1,3},{2,0},{3,1},{4,6},{5,7},{6,4},{7,5},{8,10},{9,11},{10,... | collective-permute-start | bytes 1572872 | tf_op jit(solution)/shard_map/ppermute | solution.py:1175
  203.3 23.1 %collective-permute-start.26 = (bf16[512,2048]{1,0:T(8,128)(2,1)S(1)}, bf16[512,2048]{1,0:T(8,128)(2,1)S(1)}, u32[]{:S(2)}, u32[]{:S(2)}) collective-permute-start(bf16[512,2048]{1,0:T(8,128)(2,1)S(1)} %get-tuple-element.199.refs_2_), channel_id=1, source_target_pairs={{0,4},{4,0},{8,12},{12,8},{16,20},{20,16},{24,28},{28,24},{1,5},{5... | collective-permute-start | bytes 6291464 | tf_op jit(solution)/shard_map/ppermute | solution.py:1163
  211.7 24.3 %collective-permute-start.24 = (bf16[512,2048]{1,0:T(8,128)(2,1)S(1)}, bf16[512,2048]{1,0:T(8,128)(2,1)S(1)}, u32[]{:S(2)}, u32[]{:S(2)}) collective-permute-start(bf16[512,2048]{1,0:T(8,128)(2,1)S(1)} %copy-done.7), channel_id=1, source_target_pairs={{0,4},{4,0},{8,12},{12,8},{16,20},{20,16},{24,28},{28,24},{1,5},{5... | collective-permute-start | bytes 6291464 | tf_op jit(solution)/shard_map/ppermute | solution.py:1163
  215.1 21.0 %collective-permute-start.25 = (bf16[512,2048]{1,0:T(8,128)(2,1)S(1)}, bf16[512,2048]{1,0:T(8,128)(2,1)S(1)}, u32[]{:S(2)}, u32[]{:S(2)}) collective-permute-start(bf16[512,2048]{1,0:T(8,128)(2,1)S(1)} %get-tuple-element.211.refs_2_.left_ref), channel_id=1, source_target_pairs={{0,4},{4,0},{8,12},{12,8},{16,20},{20,16},{24,28},{28,24},{1,5},{5... | collective-permute-start | bytes 6291464 | tf_op jit(solution)/shard_map/ppermute | solution.py:1163
  215.1 29.1 %collective-permute-start.23 = (bf16[128,2048]{1,0:T(8,128)(2,1)S(1)}, bf16[128,2048]{1,0:T(8,128)(2,1)S(1)}, u32[]{:S(2)}, u32[]{:S(2)}) collective-permute-start(bf16[128,2048]{1,0:T(8,128)(2,1)S(1)} %get-tuple-element.197), channel_id=1, source_target_pairs={{0,3},{1,2},{2,1},{3,0},{4,7},{5,6},{6,5},{7,4},{8,11},{9,10},{10,... | collective-permute-start | bytes 1572872 | tf_op jit(solution)/shard_map/ppermute | solution.py:1175
  224.7 45.4 %collective-permute-start.21 = (bf16[2,256,1024]{2,1,0:T(8,128)(2,1)}, bf16[2,256,1024]{2,1,0:T(8,128)(2,1)}, u32[]{:S(2)}, u32[]{:S(2)}) collective-permute-start(bf16[2,256,1024]{2,1,0:T(8,128)(2,1)} %get-tuple-element.192), channel_id=1, source_target_pairs={{0,8},{4,12},{8,0},{12,4},{16,24},{20,28},{24,16},{28,20},{1,9},{5... | collective-permute-start | bytes 3145736 | tf_op jit(solution)/shard_map/ppermute | solution.py:995
  226.4 43.7 %collective-permute-start.22 = (bf16[2,256,1024]{2,1,0:T(8,128)(2,1)}, bf16[2,256,1024]{2,1,0:T(8,128)(2,1)}, u32[]{:S(2)}, u32[]{:S(2)}) collective-permute-start(bf16[2,256,1024]{2,1,0:T(8,128)(2,1)} %get-tuple-element.193), channel_id=1, source_target_pairs={{0,16},{4,20},{8,24},{12,28},{16,0},{20,4},{24,8},{28,12},{1,17},{... | collective-permute-start | bytes 3145736 | tf_op jit(solution)/shard_map/ppermute | solution.py:995
  252.1 18.0 %all-to-all-start.3 = ((bf16[4,128,512]{2,1,0:T(8,128)(2,1)}), bf16[4,128,512]{2,1,0:T(8,128)(2,1)S(1)}, u32[]{:S(2)}, u32[]{:S(2)}) async-start(bf16[4,128,512]{2,1,0:T(8,128)(2,1)} %copy-done.53), calls=%async_computation.3 | async-start | bytes 1048576 | tf_op jit(solution)/shard_map/all_to_all | solution.py:1295
  255.6 88.4 %all-gather.3.cloned.1.call-start = ((), (), s32[]{:S(2)}) async-start(), calls=%async_computation.9 | async-start | bytes 2621440 | tf_op jit(solution)/shard_map/all_gather | solution.py:1300
  306.8 24.6 %all-to-all-start.5 = ((bf16[4,512,384]{2,1,0:T(8,128)(2,1)}), bf16[4,512,384]{2,1,0:T(8,128)(2,1)}, u32[]{:S(2)}, u32[]{:S(2)}) async-start(bf16[4,512,384]{2,1,0:T(8,128)(2,1)} %bitcast.78), calls=%async_computation.6 | async-start | bytes 3145728 | tf_op jit(solution)/shard_map/all_to_all | solution.py:1166
  311.1 63.3 %reduce-scatter.2.cloned.1.call-start = ((), (), s32[]{:S(2)}) async-start(), calls=%async_computation.8 | async-start | bytes 2621440 | tf_op jit(solution)/shard_map/reduce_scatter | solution.py:1299
  311.9 146.5 %all-gather.5.cloned.1.call-start = ((), (), s32[]{:S(2)}) async-start(), calls=%async_computation.10 | async-start | bytes 2621440 | tf_op jit(solution)/shard_map/all_gather | solution.py:1323
  314.4 32.1 %collective-permute-start.32 = (bf16[512,2048]{1,0:T(8,128)(2,1)}, bf16[512,2048]{1,0:T(8,128)(2,1)}, u32[]{:S(2)}, u32[]{:S(2)}) collective-permute-start(bf16[512,2048]{1,0:T(8,128)(2,1)} %copy-done.27), channel_id=1, source_target_pairs={{0,4},{4,0},{8,12},{12,8},{16,20},{20,16},{24,28},{28,24},{1,5},{5... | collective-permute-start | bytes 6291464 | tf_op jit(solution)/shard_map/ppermute | solution.py:1163
  344.5 47.9 %collective-permute-start.36 = (bf16[2,256,2048]{2,1,0:T(8,128)(2,1)}, bf16[2,256,2048]{2,1,0:T(8,128)(2,1)}, u32[]{:S(2)}, u32[]{:S(2)}) collective-permute-start(bf16[2,256,2048]{2,1,0:T(8,128)(2,1)} %get-tuple-element.240), channel_id=1, source_target_pairs={{0,8},{4,12},{8,0},{12,4},{16,24},{20,28},{24,16},{28,20},{1,9},{5... | collective-permute-start | bytes 6291464 | tf_op jit(solution)/shard_map/ppermute | solution.py:995
  345.9 47.6 %collective-permute-start.37 = (bf16[2,256,2048]{2,1,0:T(8,128)(2,1)}, bf16[2,256,2048]{2,1,0:T(8,128)(2,1)}, u32[]{:S(2)}, u32[]{:S(2)}) collective-permute-start(bf16[2,256,2048]{2,1,0:T(8,128)(2,1)} %get-tuple-element.241), channel_id=1, source_target_pairs={{0,16},{4,20},{8,24},{12,28},{16,0},{20,4},{24,8},{28,12},{1,17},{... | collective-permute-start | bytes 6291464 | tf_op jit(solution)/shard_map/ppermute | solution.py:995
  346.5 20.7 %collective-permute-start.29 = (bf16[128,2048]{1,0:T(8,128)(2,1)}, bf16[128,2048]{1,0:T(8,128)(2,1)S(1)}, u32[]{:S(2)}, u32[]{:S(2)}) collective-permute-start(bf16[128,2048]{1,0:T(8,128)(2,1)} %copy-done.43), channel_id=1, source_target_pairs={{0,1},{4,5},{8,9},{12,13},{16,17},{20,21},{24,25},{28,29}} | collective-permute-start | bytes 1572872 | tf_op jit(solution)/shard_map/ppermute | solution.py:856
  350.6 16.5 %collective-permute-start.30 = (bf16[128,2048]{1,0:T(8,128)(2,1)}, bf16[128,2048]{1,0:T(8,128)(2,1)S(1)}, u32[]{:S(2)}, u32[]{:S(2)}) collective-permute-start(bf16[128,2048]{1,0:T(8,128)(2,1)} %get-tuple-element.225), channel_id=1, source_target_pairs={{3,2},{7,6},{11,10},{15,14},{19,18},{23,22},{27,26},{31,30}} | collective-permute-start | bytes 1572872 | tf_op jit(solution)/shard_map/ppermute | solution.py:857
  368.5 27.1 %collective-permute-start.38 = (bf16[128,2048]{1,0:T(8,128)(2,1)}, bf16[128,2048]{1,0:T(8,128)(2,1)}, u32[]{:S(2)}, u32[]{:S(2)}) collective-permute-start(bf16[128,2048]{1,0:T(8,128)(2,1)} %get-tuple-element.299), channel_id=1, source_target_pairs={{0,1},{1,2},{4,5},{5,6},{8,9},{9,10},{12,13},{13,14},{16,17},{17,1... | collective-permute-start | bytes 1572872 | tf_op jit(solution)/shard_map/ppermute | solution.py:856
  372.7 22.9 %collective-permute-start.39 = (bf16[128,2048]{1,0:T(8,128)(2,1)}, bf16[128,2048]{1,0:T(8,128)(2,1)}, u32[]{:S(2)}, u32[]{:S(2)}) collective-permute-start(bf16[128,2048]{1,0:T(8,128)(2,1)} %get-tuple-element.298), channel_id=1, source_target_pairs={{2,1},{3,2},{6,5},{7,6},{10,9},{11,10},{14,13},{15,14},{18,17},{19... | collective-permute-start | bytes 1572872 | tf_op jit(solution)/shard_map/ppermute | solution.py:857
  393.5 26.3 %collective-permute-start.42 = (bf16[2,256,1024]{2,1,0:T(8,128)(2,1)}, bf16[2,256,1024]{2,1,0:T(8,128)(2,1)S(1)}, u32[]{:S(2)}, u32[]{:S(2)}) collective-permute-start(bf16[2,256,1024]{2,1,0:T(8,128)(2,1)} %get-tuple-element.252), channel_id=1, source_target_pairs={{0,8},{4,12},{8,0},{12,4},{16,24},{20,28},{24,16},{28,20},{1,9},{5... | collective-permute-start | bytes 3145736 | tf_op jit(solution)/shard_map/ppermute | solution.py:995
  394.1 64.3 %collective-permute-start.43 = (bf16[2,256,1024]{2,1,0:T(8,128)(2,1)}, bf16[2,256,1024]{2,1,0:T(8,128)(2,1)}, u32[]{:S(2)}, u32[]{:S(2)}) collective-permute-start(bf16[2,256,1024]{2,1,0:T(8,128)(2,1)} %get-tuple-element.253), channel_id=1, source_target_pairs={{0,16},{4,20},{8,24},{12,28},{16,0},{20,4},{24,8},{28,12},{1,17},{... | collective-permute-start | bytes 3145736 | tf_op jit(solution)/shard_map/ppermute | solution.py:995
  398.5 59.9 %collective-permute-start.40 = (bf16[256,2048]{1,0:T(8,128)(2,1)}, bf16[256,2048]{1,0:T(8,128)(2,1)}, u32[]{:S(2)}, u32[]{:S(2)}) collective-permute-start(bf16[256,2048]{1,0:T(8,128)(2,1)} %fusion.2), channel_id=1, source_target_pairs={{0,16},{4,20},{8,24},{12,28},{16,0},{20,4},{24,8},{28,12},{1,17},{... | collective-permute-start | bytes 3145736 | tf_op jit(solution)/shard_map/ppermute | solution.py:995
  401.7 56.8 %collective-permute-start.41 = (bf16[256,2048]{1,0:T(8,128)(2,1)}, bf16[256,2048]{1,0:T(8,128)(2,1)}, u32[]{:S(2)}, u32[]{:S(2)}) collective-permute-start(bf16[256,2048]{1,0:T(8,128)(2,1)} %fusion.3), channel_id=1, source_target_pairs={{0,8},{4,12},{8,0},{12,4},{16,24},{20,28},{24,16},{28,20},{1,9},{5... | collective-permute-start | bytes 3145736 | tf_op jit(solution)/shard_map/ppermute | solution.py:995
  404.4 23.8 %collective-permute-start.44 = (bf16[128,2048]{1,0:T(8,128)(2,1)S(1)}, bf16[128,2048]{1,0:T(8,128)(2,1)S(1)}, u32[]{:S(2)}, u32[]{:S(2)}) collective-permute-start(bf16[128,2048]{1,0:T(8,128)(2,1)S(1)} %add_convert_fusion.5), channel_id=1, source_target_pairs={{0,1},{1,2},{2,3},{4,5},{5,6},{6,7},{8,9},{9,10},{10,11},{12,13},{... | collective-permute-start | bytes 1572872 | tf_op jit(solution)/shard_map/ppermute | solution.py:856
  429.0 29.4 %collective-permute-start.34 = (bf16[256,1024]{1,0:T(8,128)(2,1)}, bf16[256,1024]{1,0:T(8,128)(2,1)}, u32[]{:S(2)}, u32[]{:S(2)}) collective-permute-start(bf16[256,1024]{1,0:T(8,128)(2,1)} %fusion.4), channel_id=1, source_target_pairs={{0,16},{4,20},{8,24},{12,28},{16,0},{20,4},{24,8},{28,12},{1,17},{... | collective-permute-start | bytes 1572872 | tf_op jit(solution)/shard_map/ppermute | solution.py:995
  434.4 24.0 %collective-permute-start.35 = (bf16[256,1024]{1,0:T(8,128)(2,1)}, bf16[256,1024]{1,0:T(8,128)(2,1)}, u32[]{:S(2)}, u32[]{:S(2)}) collective-permute-start(bf16[256,1024]{1,0:T(8,128)(2,1)} %fusion.5), channel_id=1, source_target_pairs={{0,8},{4,12},{8,0},{12,4},{16,24},{20,28},{24,16},{28,20},{1,9},{5... | collective-permute-start | bytes 1572872 | tf_op jit(solution)/shard_map/ppermute | solution.py:995
  458.5 14.9 %collective-permute-start.46 = (bf16[144,2048]{1,0:T(8,128)(2,1)}, bf16[144,2048]{1,0:T(8,128)(2,1)S(1)}, u32[]{:S(2)}, u32[]{:S(2)}) collective-permute-start(bf16[144,2048]{1,0:T(8,128)(2,1)} %copy-done.17), channel_id=1, source_target_pairs={{0,1},{1,2},{2,3},{4,5},{5,6},{6,7},{8,9},{9,10},{10,11},{12,13},{... | collective-permute-start | bytes 1769480 | tf_op jit(solution)/shard_map/ppermute | solution.py:856
  459.9 17.5 %collective-permute-start.47 = (bf16[144,2048]{1,0:T(8,128)(2,1)}, bf16[144,2048]{1,0:T(8,128)(2,1)S(1)}, u32[]{:S(2)}, u32[]{:S(2)}) collective-permute-start(bf16[144,2048]{1,0:T(8,128)(2,1)} %copy-done.17), channel_id=1, source_target_pairs={{1,0},{2,1},{3,2},{5,4},{6,5},{7,6},{9,8},{10,9},{11,10},{13,12},{... | collective-permute-start | bytes 1769480 | tf_op jit(solution)/shard_map/ppermute | solution.py:857
  462.6 19.5 %collective-permute-start.50 = (bf16[256,1024]{1,0:T(8,128)(2,1)S(1)}, bf16[256,1024]{1,0:T(8,128)(2,1)S(1)}, u32[]{:S(2)}, u32[]{:S(2)}) collective-permute-start(bf16[256,1024]{1,0:T(8,128)(2,1)S(1)} %fusion.6), channel_id=1, source_target_pairs={{0,16},{4,20},{8,24},{12,28},{16,0},{20,4},{24,8},{28,12},{1,17},{... | collective-permute-start | bytes 1572872 | tf_op jit(solution)/shard_map/ppermute | solution.py:995
  477.4 18.7 %collective-permute-start.48 = (bf16[144,2048]{1,0:T(8,128)(2,1)S(1)}, bf16[144,2048]{1,0:T(8,128)(2,1)S(1)}, u32[]{:S(2)}, u32[]{:S(2)}) collective-permute-start(bf16[144,2048]{1,0:T(8,128)(2,1)S(1)} %collective-permute-done.46.refs_3_), channel_id=1, source_target_pairs={{1,2},{2,3},{5,6},{6,7},{9,10},{10,11},{13,14},{14,15},{17,18},{18... | collective-permute-start | bytes 1769480 | tf_op jit(solution)/shard_map/ppermute | solution.py:856
  478.1 18.0 %collective-permute-start.49 = (bf16[144,2048]{1,0:T(8,128)(2,1)S(1)}, bf16[144,2048]{1,0:T(8,128)(2,1)S(1)}, u32[]{:S(2)}, u32[]{:S(2)}) collective-permute-start(bf16[144,2048]{1,0:T(8,128)(2,1)S(1)} %collective-permute-done.47.refs_0_), channel_id=1, source_target_pairs={{1,0},{2,1},{5,4},{6,5},{9,8},{10,9},{13,12},{14,13},{17,16},{18,1... | collective-permute-start | bytes 1769480 | tf_op jit(solution)/shard_map/ppermute | solution.py:857
  496.1 16.1 %collective-permute-start.52 = (bf16[144,2048]{1,0:T(8,128)(2,1)S(1)}, bf16[144,2048]{1,0:T(8,128)(2,1)S(1)}, u32[]{:S(2)}, u32[]{:S(2)}) collective-permute-start(bf16[144,2048]{1,0:T(8,128)(2,1)S(1)} %collective-permute-done.49.refs_1_), channel_id=1, source_target_pairs={{1,0},{5,4},{9,8},{13,12},{17,16},{21,20},{25,24},{29,28}} | collective-permute-start | bytes 1769480 | tf_op jit(solution)/shard_map/ppermute | solution.py:857
  497.6 14.7 %collective-permute-start.53 = (bf16[144,2048]{1,0:T(8,128)(2,1)S(1)}, bf16[144,2048]{1,0:T(8,128)(2,1)S(1)}, u32[]{:S(2)}, u32[]{:S(2)}) collective-permute-start(bf16[144,2048]{1,0:T(8,128)(2,1)S(1)} %collective-permute-done.48.refs_4_), channel_id=1, source_target_pairs={{2,3},{6,7},{10,11},{14,15},{18,19},{22,23},{26,27},{30,31}} | collective-permute-start | bytes 1769480 | tf_op jit(solution)/shard_map/ppermute | solution.py:856
  (76 other events, 607.6 us)
Sparse Core Ops, SparseCore 0:
  270.3 43.1 all-gather.2
  316.3 46.4 reduce-scatter.1
  376.5 54.9 all-gather.4

commit v3 on v2

--- a/solution.py
+++ b/solution.py
@@ -573,16 +573,20 @@
     *weights, middle_ref, normed_ref = refs
     own_tp, core = where_ref[0], where_ref[1]
     count, part, _ = attended_ref.shape
-    half = weights[0].shape[0]
-    total = tokens_ref[pl.ds(pl.multiple_of(own_tp * part, part), part), :].astype(jnp.float32)
-    for d in range(count):
-        for which in range(2):
-            side = core if which == 0 else 1 - core
-            columns = pl.ds(pl.multiple_of(side * half, half), half)
-            values = attended_ref[piece_at(own_tp, d, count), :, columns]
-            total = total + dense(values, weights[2 * d + which][...])
-    middle_ref[...] = total
-    normed_ref[...] = (norm_of(total)[1] * gain_ref[...]).astype(jnp.bfloat16)
+    _, half, wide = weights[0].shape
+    starts = (0, wide, middle_ref.shape[1])
+    rows = tokens_ref[pl.ds(pl.multiple_of(own_tp * part, part), part), :].astype(jnp.float32)
+    for piece in range(2):
+        target = slice(starts[piece], starts[piece + 1])
+        total = rows[:, target]
+        for d in range(count):
+            for which in range(2):
+                side = core if which == 0 else 1 - core
+                columns = pl.ds(pl.multiple_of(side * half, half), half)
+                values = attended_ref[d, :, columns]
+                total = total + dense(values, weights[2 * piece + which][d])
+        middle_ref[:, target] = total
+    normed_ref[...] = (norm_of(middle_ref[...])[1] * gain_ref[...]).astype(jnp.bfloat16)
 
 
 def ffn_kernel(where_ref, *refs, chunk, sources, first):
@@ -686,7 +690,7 @@
     *weights, low_ref, grad_ref, back_ref, gain_grad_ref = refs
     own_tp, core = where_ref[0], where_ref[1]
     count, part, _ = back_ref.shape
-    half = weights[0].shape[0]
+    _, half, wide = weights[0].shape
     scale, unit = norm_of(middle_ref[...])
     grad = sum([t[...].astype(jnp.float32) for t in terms[1:]], terms[0][...].astype(jnp.float32))
     gain_grad_ref[...] = jnp.sum(grad * unit, axis=0, keepdims=True)
@@ -699,9 +703,9 @@
         for which in range(2):
             side = core if which == 0 else 1 - core
             columns = pl.ds(pl.multiple_of(side * half, half), half)
-            back_ref[piece_at(own_tp, d, count), :, columns] = dense_t(
-                low, weights[2 * d + which][...]
-            ).astype(jnp.bfloat16)
+            values = dense_t(low[:, :wide], weights[which][d])
+            values = values + dense_t(low[:, wide:], weights[2 + which][d])
+            back_ref[d, :, columns] = values.astype(jnp.bfloat16)
 
 
 def back_kernel(where_ref, back_ref, live_ref, tokens_ref, query_ref, key_ref, value_ref, low_ref, gain_ref, *refs):
@@ -775,61 +779,61 @@
     )(where, back_heads, live, tokens, *weights)
 
 
-def tokens_kernel(where_ref, tokens_ref, gain_ref, middle_ref, gains_ref, own_ref, below_ref, above_ref, out_ref):
+def tokens_kernel(
+    where_ref, tokens_ref, gain_ref, grad_ref, gains_ref, middle_ref, branch_ref, own_ref, below_ref, above_ref, out_ref
+):
     part = own_ref.shape[0]
     at = pl.ds(pl.multiple_of(where_ref[0] * part, part), part)
     scale, unit = norm_of(tokens_ref[at, :])
     grad = own_ref[...].astype(jnp.float32) + (
         below_ref[...].astype(jnp.float32) + above_ref[...].astype(jnp.float32)
     )
-    total = middle_ref[...] + norm_back(grad, gain_ref[...], scale, unit)
+    total = grad_ref[...] + norm_back(grad, gain_ref[...], scale, unit)
     out_ref[:part, :] = total.astype(jnp.bfloat16)
     gains = gains_ref[...]
     high = gains.astype(jnp.bfloat16)
     low = (gains - high.astype(jnp.float32)).astype(jnp.bfloat16)
     wide = gains.shape[1]
-    rows = out_ref.shape[0] - part
+    rows = out_ref.shape[0] - 2 * part
+    middle = slice(part, part + rows)
     for index, values in enumerate((high, low)):
-        out_ref[part:, index * wide : (index + 1) * wide] = jnp.broadcast_to(values, (rows, wide))
-    out_ref[part:, 2 * wide :] = jnp.zeros((rows, out_ref.shape[1] - 2 * wide), jnp.bfloat16)
-
-
-def layer_kernel(middle_ref, branch_ref, out_ref):
-    out_ref[...] = (middle_ref[...] + branch_ref[...].astype(jnp.float32)).astype(jnp.bfloat16)
-
-
-def join_kernel(where_ref, own_ref, *refs, relative, part):
-    count = (len(refs) - (1 if own_ref.shape[0] == part else 3)) // 2 + 1
-    pieces, (out_ref, *rest) = refs[: 2 * count - 2], refs[2 * count - 2 :]
+        out_ref[middle, index * wide : (index + 1) * wide] = jnp.broadcast_to(values, (rows, wide))
+    out_ref[middle, 2 * wide :] = jnp.zeros((rows, out_ref.shape[1] - 2 * wide), jnp.bfloat16)
+    layer = middle_ref[...] + branch_ref[...].astype(jnp.float32)
+    out_ref[part + rows :, :] = layer.astype(jnp.bfloat16)
+
+
+def join_kernel(where_ref, own_ref, *refs, part):
+    *pieces, out_ref, gains_ref, layer_ref, terms_ref = refs
+    count = len(pieces) // 2 + 1
+    wide = gains_ref.shape[1]
     for d in range(count):
-        place = d if relative else piece_at(where_ref[0], d, count)
+        place = piece_at(where_ref[0], d, count)
         values = own_ref[...] if d == 0 else pieces[d - 1][...] + pieces[2 * count - 2 - d][...]
-        out_ref[pl.ds(pl.multiple_of(place * part, part), part), :] = values[:part].astype(out_ref.dtype)
-        if rest:
-            gains_ref, terms_ref = rest
-            wide = gains_ref.shape[1]
-            row = values[part:].astype(jnp.float32)
-            terms_ref[place] = row[:8, :wide] + row[:8, wide : 2 * wide]
-    if rest:
-        total = terms_ref[0]
-        for index in range(1, count):
-            total = total + terms_ref[index]
-        gains_ref[...] = total[:1]
-
-
-def join(where, gathered, dtype, relative, gains=0):
+        at = pl.ds(pl.multiple_of(place * part, part), part)
+        out_ref[at, :] = values[:part].astype(jnp.float32)
+        row = values[part : part + 8].astype(jnp.float32)
+        terms_ref[place] = row[:, :wide] + row[:, wide : 2 * wide]
+        layer_ref[at, :] = values[values.shape[0] - part :]
+    total = terms_ref[0]
+    for index in range(1, count):
+        total = total + terms_ref[index]
+    gains_ref[...] = total[:1]
+
+
+def join(where, gathered, part, gains):
     own, above, below = gathered
     count = len(above) + 1
-    part, width = own.shape[0] - (16 if gains else 0), own.shape[1]
-    outs, scratch = [made((count * part, width), dtype)], []
-    if gains:
-        outs.append(made((1, gains), jnp.float32))
-        scratch.append(pltpu.VMEM((count, 8, gains), jnp.float32))
+    width = own.shape[1]
     return call(
-        functools.partial(join_kernel, relative=relative, part=part),
-        outs,
+        functools.partial(join_kernel, part=part),
+        (
+            made((count * part, width), jnp.float32),
+            made((1, gains), jnp.float32),
+            made((count * part, width), jnp.bfloat16),
+        ),
         (where, own, *above, *below),
-        scratch=scratch,
+        scratch=[pltpu.VMEM((count, 8, gains), jnp.float32)],
         scalars=1,
         name="join",
     )
@@ -886,20 +890,31 @@
         return self.own, self.above, self.below
 
 
+def add_kernel(up_ref, got_up_ref, down_ref, got_down_ref, sum_up_ref, sum_down_ref):
+    for part, got, total in (
+        (up_ref, got_up_ref, sum_up_ref),
+        (down_ref, got_down_ref, sum_down_ref),
+    ):
+        total[...] = (part[...].astype(jnp.float32) + got[...].astype(jnp.float32)).astype(
+            jnp.bfloat16
+        )
+
+
 class Sum(Line):
     def __init__(self, parts, axis, count):
         super().__init__(axis, count)
         self.parts = parts
 
     def step(self):
-        f32, bf16 = jnp.float32, jnp.bfloat16
         first = self.at == 0
         self.at += 1
         at, count = self.at, self.count
         up, down = self.parts[count - at], self.parts[at]
         if not first:
-            up = (up.astype(f32) + self.upward.astype(f32)).astype(bf16)
-            down = (down.astype(f32) + self.downward.astype(f32)).astype(bf16)
+            outs = (made(up.shape, jnp.bfloat16),) * 2
+            up, down = call(
+                add_kernel, outs, (up, self.upward, down, self.downward), name="add"
+            )
         self.send(
             up,
             down,
@@ -1175,8 +1190,15 @@
         return lax.ppermute(values, "tp", [(i, i ^ k) for i in range(tp_size)])
 
     half = own_width // 2
-    weight_line = Gather(lax.dynamic_slice_in_dim(w_out, core * half, half, 0), "tp", tp_size)
-    weight_line.step()
+    most = width * 5 // 8
+    w_half = lax.dynamic_slice_in_dim(w_out, core * half, half, 0)
+
+    def gathered(columns):
+        values = lax.all_gather(columns, "tp", axis=0, tiled=True)
+        return values.reshape(tp_size, half, columns.shape[1])
+
+    w_first = gathered(w_half[:, :most])
+    w_second = gathered(w_half[:, most:])
 
     order = group_order[0]
     per_device = row_count // span
@@ -1215,27 +1237,22 @@
         tokens, gain_attn, live, cosine, sine, w_query, w_key, w_value
     )
     mine = to_heads(packed).reshape(chips * row_count, 3 * head)
-    upstream_rel = reordered(weight_line.tie(upstream))
-    weight_line.step()
+    upstream_rel = reordered(upstream)
     grad_act = matmul_call(where, upstream_rel, w_down, f32, True, "grad_act")
     upstream_pair = (upstream_rel, swap(upstream_rel))
     normed_attn_pair = (normed_attn, swap(normed_attn))
-    mine, grad_act = weight_line.tie(mine, grad_act)
-    weight_line.step()
+    mine, grad_act = tie(mine, grad_act)
     other = swap(mine[:, head:])
 
     attended = attend_call(slot_places, key_low, mine, other, start_q.reshape(-1, 1), span)
+    attended, w_first = tie(attended, w_first)
     attended = to_heads(attended.reshape(chips, row_count, head))
     attended = attended.transpose(1, 0, 2).reshape(row_count, own_width)
     attended_part = lax.all_to_all(
         attended.reshape(tp_size, part, own_width), "tp", 0, 0, tiled=True
     )
-    weight_line.tie(attended_part)
-    own_w, above_w, below_w = weight_line.result()
-    out_weights = []
-    for d in range(tp_size):
-        piece = own_w if d == 0 else above_w[d - 1] + below_w[tp_size - 1 - d]
-        out_weights += [piece, swap(piece)]
+    w_second = after(w_second, attended_part)
+    out_weights = (w_first, swap(w_first), w_second, swap(w_second))
     middle, normed_part = call(
         out_kernel,
         (made((part, width), f32), made((part, width), bf16)),
@@ -1264,6 +1281,7 @@
     )
     grad_3 = across(grad_3, 3)
     activated, gate_pre, up_pre, normed_ffn = filled
+    gate_pre, grad_1, grad_2 = tie(gate_pre, grad_1, grad_2)
 
     normed_pair = (normed_ffn, swap(normed_ffn))
     outer_ffn = functools.partial(
@@ -1272,13 +1290,12 @@
     gate_quad = (*normed_pair, gate_pre, swap(gate_pre))
     up_quad = (*normed_pair, up_pre, swap(up_pre))
     down_quad = (*upstream_pair, activated, swap(activated))
-    *gate_quad, grad_1, grad_2 = tie(*gate_quad, grad_1, grad_2)
     gate_sum = ChipSum(outer_ffn([gate_quad]), seq_size)
     gate_sum.first()
-    rest_grads = outer_ffn([up_quad], columns=2, column=0)
-    rest_grads = outer_ffn([down_quad], columns=2, column=1, into=rest_grads)
-    grad_3, *rest_grads = tie(grad_3, *rest_grads)
-    rest_sum = ChipSum(rest_grads, seq_size)
+    up_sum = ChipSum(outer_ffn([up_quad]), seq_size)
+    down_sum = ChipSum(outer_ffn([down_quad]), seq_size)
+    grad_3, *arrays = tie(grad_3, *up_sum.arrays, *down_sum.arrays)
+    up_sum.arrays, down_sum.arrays = arrays[:4], arrays[4:]
     middle_low, grad_middle, grad_attended, gain_ffn_part = call(
         middle_kernel,
         (
@@ -1297,13 +1314,13 @@
     grad_attended, branch = gate_sum.tie(grad_attended, branch)
     branch = after(branch, grad_attended)
     branch_part = lax.psum_scatter(branch, "tp", scatter_dimension=0, tiled=True)
-    middle_all = lax.all_gather(after(middle_low, grad_attended), "tp", axis=0, tiled=True)
     grad_attended = grad_attended.reshape(row_count, heads, head).transpose(1, 0, 2)
     grad_heads = to_heads(grad_attended).reshape(chips * row_count, head)
     grad_query, both, both_other = attend_back_call(
         slot_places, key_low, mine, other, start_q, grad_heads, span
     )
     other_term = swap(both_other)
+    middle_all = lax.all_gather(after(middle_low, other_term), "tp", axis=0, tiled=True)
     packed_back = call(
         turn_kernel,
         (made((chips * row_count, 3 * head), bf16),),
@@ -1311,22 +1328,25 @@
         name="turn",
     )[0].reshape(chips, row_count, 3 * head)
     back_heads = to_heads(packed_back)
-    rest_sum.first(packed_back)
     attended_pair = (attended, swap(attended))
-    back_heads = after(back_heads, attended_pair[1])
-    layer_part = call(
-        layer_kernel,
-        (made((part, width), bf16),),
-        (middle, branch_part),
-        name="layer",
-    )[0]
-    layer_out = lax.all_gather(after(layer_part, middle_all), "tp", axis=0, tiled=True)
+    back_heads = after(back_heads, attended_pair[1], branch_part)
     low, gain_attn_part, *parts = back_call(
         where, back_heads, live, tokens, (w_query, w_key, w_value), tp_size
     )
     sums = Sum(parts, "tp", tp_size)
     sums.step()
-    middle_all = after(middle_all, low)
+    up_sum.first(low)
+    gains = jnp.concatenate([gain_attn_part, gain_ffn_part], axis=0)
+    gains = gains.reshape(2, seq_size, block).transpose(1, 0, 2)
+    gains = jnp.sum(lax.all_to_all(gains, "seq", 0, 0, tiled=True), axis=0).reshape(1, 2 * block)
+    up_sum.got_x, up_sum.got_y, low, gains = sums.tie(up_sum.got_x, up_sum.got_y, low, gains)
+    down_sum.first(low)
+    sums.step()
+    down_sum.got_x, down_sum.got_y, low, middle_all = sums.tie(
+        down_sum.got_x, down_sum.got_y, low, middle_all
+    )
+    up_sum.second(low)
+    sums.step()
     middle_pair = (middle_all, swap(middle_all))
     attn_grads = chip_outer_call(
         where,
@@ -1334,34 +1354,37 @@
         seq_size,
         "attn_outer",
     )
-    attn_grads, low = sums.tie(attn_grads, low)
+    up_sum.last_x, up_sum.last_y, *attn_grads = sums.tie(
+        up_sum.last_x, up_sum.last_y, *attn_grads
+    )
     attn_sum = ChipSum(attn_grads, seq_size)
-    attn_sum.first()
-    gate_sum.second(low)
-    sums.step()
-    gains = jnp.concatenate([gain_attn_part, gain_ffn_part], axis=0)
-    gains = after(gains.reshape(2, seq_size, block).transpose(1, 0, 2), low)
-    gains = jnp.sum(lax.all_to_all(gains, "seq", 0, 0, tiled=True), axis=0).reshape(1, 2 * block)
-    low = sums.tie(rest_sum.tie(low))
-    rest_sum.second(low)
-    sums.step()
     tokens_part = call(
         tokens_kernel,
-        (made((part + 16, width), bf16),),
-        (where, tokens, gain_attn, grad_middle, gains, *sums.result()),
+        (made((2 * part + 16, width), bf16),),
+        (where, tokens, gain_attn, grad_middle, gains, middle, branch_part, *sums.result()),
         scalars=1,
         name="tokens",
     )[0]
-    tokens_part, _ = gate_sum.tie_last(*rest_sum.tie_last(attn_sum.tie(after(tokens_part, layer_out)), low))
     token_line = Gather(tokens_part, "tp", tp_size)
     token_line.step()
-    attn_sum.second()
+    attn_sum.first(tokens_part)
+    attn_sum.got_x, attn_sum.got_y, low = token_line.tie(attn_sum.got_x, attn_sum.got_y, low)
+    token_line.step()
+    down_sum.second(low)
+    gate_sum.second(low)
+    (*last, low) = token_line.tie(
+        down_sum.last_x, down_sum.last_y, gate_sum.last_x, gate_sum.last_y, low
+    )
+    down_sum.last_x, down_sum.last_y, gate_sum.last_x, gate_sum.last_y = last
+    token_line.step()
+    attn_sum.second(low)
+    up_sum.last_x = after(up_sum.last_x, low)
+    up_x, up_y = up_sum.terms()
+    (grad_up,) = widen_pair([*up_x, *up_y], hidden, (False,), "widen_up")
+    down_x, down_y = down_sum.terms()
+    (grad_down,) = widen_pair([*down_x, *down_y], hidden, (True,), "widen_down")
     gate_x, gate_y = gate_sum.terms()
     (grad_gate,) = widen_pair([*gate_x, *gate_y], hidden, (False,), "widen_gate")
-    rest_x, rest_y = rest_sum.terms()
-    grad_up, grad_down = widen_pair([*rest_x, *rest_y], hidden, (False, True), "widen_rest")
-    grad_gate = token_line.tie(grad_gate)
-    token_line.step()
     terms_x, terms_y = attn_sum.terms()
     grad_out, grad_query = widen(
         terms_x, [0, 1, None], [own_width] * 2, (True, False), "widen_attn"
@@ -1369,9 +1392,8 @@
     grad_key, grad_value = widen(
         terms_y, [0, 0, None], [own_width] * 2, (False, False), "widen_attn"
     )
-    grad_out, grad_key = token_line.tie(grad_out, grad_key)
-    token_line.step()
-    grad_tokens, gains = join(where, token_line.result(), f32, False, 2 * block)
+    grad_out, grad_key, grad_gate, grad_up = token_line.tie(grad_out, grad_key, grad_gate, grad_up)
+    grad_tokens, gains, layer_out = join(where, token_line.result(), part, 2 * block)
     gains = gains.reshape(2, block)
 
     return (

time: 534 us -> 518 us (0.970)
  other arithmetic: 33.1 us -> 18.6 us
  local copies, waits for them, and re-layouts: 57.2 us -> 45.2 us
  waiting for transfers between devices: 164 us -> 174 us
  starting transfers between devices: 82.1 us -> 73.9 us
    all_gather x2 -> x3, waiting for transfers between devices: 0.01 us -> 34.3 us  [the longest x2 34.3 us: gathered(): values = lax.all_gather(columns, 'tp', axis=0, tiled=True)]
    ppermute x12 -> x9, waiting for transfers between devices: 52.6 us -> 19.2 us  [send(): self.downward = lax.ppermute(down, self.axis, down_pairs)]
    unnamed x132 -> x117, local copies, waits for them, and re-layouts: 41.7 us -> 26.1 us
    ppermute x12 -> x9, starting transfers between devices: 22 us -> 13.4 us  [send(): self.upward = lax.ppermute(up, self.axis, up_pairs)]
    ppermute x12 -> x16, waiting for transfers between devices: 40.5 us -> 47.5 us  [over(): lax.ppermute(values, 'seq', [(i, i ^ side) for i in range(self.size)])]
    add x3 -> x0, other arithmetic: 6.77 us -> none  [local_heads_apart(): piece = own_w if d == 0 else above_w[d - 1] + below_w[tp_size - 1 - d]]
    pallas_call x10 -> x12, Pallas kernels: 28 us -> 31.7 us  [call(): pl.pallas_call(kernel, out_shape=tuple(outs), in_specs=[SMALL] * scalars...]
    ppermute x12 -> x9, starting transfers between devices: 15.7 us -> 12.5 us  [send(): self.downward = lax.ppermute(down, self.axis, down_pairs)]
  transfers between devices with their start and end apart: 63 -> 60, of which waited for: 26 -> 27; matrix products, arithmetic and copies ran while one was open for 9% -> 7% of each run, Pallas kernels for 27% -> 30%
where the time goes in v3:
time: 518 us; the launch traced here: 508 us
  waiting for transfers between devices  174 us (34%)
  Pallas kernels  161 us (31%)
  starting transfers between devices  73.9 us (14%)
  local copies, waits for them, and re-layouts  45.2 us (9%)
  blocking collectives  20.8 us (4%)
  other arithmetic  18.6 us (4%)
  between operations  15.3 us (3%)
    ppermute x16, waiting for transfers between devices, over(): lax.ppermute(values, 'seq', [(i, i ^ side) for i in range(self.size)])  47.5 us
    pallas_call x3, Pallas kernels, ffn_call(): pl.pallas_call(functools.partial(ffn_kernel, chunk=chunk, sources=len(sou...  38.1 us
    all_gather x2, waiting for transfers between devices, gathered(): values = lax.all_gather(columns, 'tp', axis=0, tiled=True)  34.3 us
    pallas_call x4, Pallas kernels, chip_outer_call(): pl.pallas_call(functools.partial(chip_outer_kernel, sides=len(pairs)), ou...  33.5 us
    all_to_all x4, waiting for transfers between devices, to_heads(): lax.all_to_all(values, 'seq', 0, 0, axis_index_groups=same_core, tiled=True)  31.9 us
    pallas_call x12, Pallas kernels, call(): pl.pallas_call(kernel, out_shape=tuple(outs), in_specs=[SMALL] * scalars...  31.7 us
    unnamed x117, local copies, waits for them, and re-layouts  26.1 us
    all_to_all x1, blocking collectives, local_heads_apart(): lax.all_to_all(gains, 'seq', 0, 0, tiled=True)  20.8 us
  transfers between devices with their start and end apart: 60, of which 27 were waited for; matrix products, arithmetic and copies ran while one was open for 7% of the time, Pallas kernels for 30%

profile of v3, /device:TPU:0, one launch (start us, length us, event | category | flops | bytes accessed | tf_op | source)
XLA Modules:
  0.0 508.1 jit_solution(8472914863354247469)
XLA Ops:
  13.4 7.4 %project.1 = (bf16[4,512,384]{2,1,0:T(8,128)(2,1)S(1)}, bf16[512,2048]{1,0:T(8,128)(2,1)}) custom-call(bf16[512,2048]{1,0:T(8,128)(2,1)S(1)} %bitcast.89, f32[1,2048]{1,0:T(1,128)S(1)} %bitcast.107, s32[512,1]{1,0:T(8,128)S(1)} %bitcast.102, f32[512,128]{1,0:T(8,128)S(1)} %get-tuple-element.336.cosine_ref, f32[512,128]{1,0:T(8,128)S(1)} %get-tuple-element.337.sine_ref, ...), custom_call_target="tpu_custom_call" | custom-call | flops 1 | bytes 1 | tf_op jit(solution)/shard_map/project/pallas_call | solution.py:482
  21.9 5.3 %all-to-all-start = ((bf16[4,512,384]{2,1,0:T(8,128)(2,1)}), bf16[4,512,384]{2,1,0:T(8,128)(2,1)}, u32[]{:S(2)}, u32[]{:S(2)}) async-start(bf16[4,512,384]{2,1,0:T(8,128)(2,1)} %copy-done.37), calls=%async_computation | async-start | bytes 3145728 | tf_op jit(solution)/shard_map/all_to_all | solution.py:1181
  33.5 8.0 %grad_act.1.refs_3_.refs_2_.refs_4_ = f32[512,2048]{1,0:T(8,128)S(1)} custom-call(s32[3]{0:T(128)S(1)} %pad_add_fusion.1.where_ref, bf16[512,2048]{1,0:T(8,128)(2,1)S(1)} %pad_maximum_fusion.left_ref.refs_0_, bf16[2048,2048]{1,0:T(8,128)(2,1)} %right_ref.3), custom_call_target="tpu_custom_call" | custom-call | flops 1 | bytes 1 | tf_op jit(solution)/shard_map/grad_act/pallas_call | solution.py:1105
  54.0 10.0 %attend.1 = bf16[2048,128]{1,0:T(8,128)(2,1)S(1)} custom-call(s32[16]{0:T(128)S(1)} %pad_add_fusion.2.slot_places, s32[8]{0:T(128)S(1)} %get-tuple-element.320.key_low, bf16[2048,384]{1,0:T(8,128)(2,1)} %bitcast.12.own_ref, bf16[2048,256]{1,0:T(8,128)(2,1)S(1)} %collective-permute-done.other_ref, s32[2048,1]{1,0:T(8,128)S(1)} %bitcast.101), custom_call_target="tpu_custom_call" | custom-call | flops 1 | bytes 1 | tf_op jit(solution)/shard_map/attend/pallas_call | solution.py:438
  64.8 2.3 all-gather.4.cloned.1.call-done
  67.2 3.8 all-to-all-start.1
  70.9 8.1 %all-to-all-done.1 = bf16[4,512,128]{2,1,0:T(8,128)(2,1)S(1)} async-done(((bf16[4,512,128]{2,1,0:T(8,128)(2,1)}), bf16[4,512,128]{2,1,0:T(8,128)(2,1)S(1)}, u32[]{:S(2)}, u32[]{:S(2)}) %all-to-all-start.1) | async-done | bytes 524320 | tf_op jit(solution)/shard_map/all_to_all | solution.py:1181
  80.4 4.1 all-to-all-start.2
  84.5 31.9 %all-gather.6.cloned.1.call-done = bf16[1024,768]{1,0:T(8,128)(2,1)} async-done(((bf16[256,768]{1,0:T(8,128)(2,1)}), bf16[1024,768]{1,0:T(8,128)(2,1)}) %all-gather.6.cloned.1.call-update) | async-done | bytes 1572880 | tf_op jit(solution)/shard_map/all_gather | solution.py:1197
  117.2 3.6 collective-permute-done.2.refs_3_.refs_7_
  125.0 3.4 out.1
  131.0 10.4 %collective-permute-done.4.refs_2_.refs_1_ = bf16[128,2048]{1,0:T(8,128)(2,1)S(1)} collective-permute-done((bf16[128,2048]{1,0:T(8,128)(2,1)S(1)}, bf16[128,2048]{1,0:T(8,128)(2,1)S(1)}, u32[]{:S(2)}, u32[]{:S(2)}) %collective-permute-start.4) | collective-permute-done | bytes 524320 | tf_op jit(solution)/shard_map/ppermute | solution.py:860
  142.1 3.5 collective-permute-done.3.refs_1_.refs_0_
  147.0 14.0 %ffn.3 = (bf16[512,2048]{1,0:T(8,128)(2,1)S(1)}, bf16[512,2048]{1,0:T(8,128)(2,1)S(1)}, bf16[512,2048]{1,0:T(8,128)(2,1)S(1)}, bf16[512,2048]{1,0:T(8,128)(2,1)S...) custom-call(s32[3]{0:T(128)S(1)} %pad_add_fusion.1.where_ref, ...), custom_call_target="tpu_custom_call" | custom-call | flops 1 | bytes 1 | tf_op jit(solution)/shard_map/ffn/pallas_call | solution.py:666
  163.0 12.0 %ffn.4 = (bf16[512,2048]{1,0:T(8,128)(2,1)S(1)}, bf16[512,2048]{1,0:T(8,128)(2,1)S(1)}, bf16[512,2048]{1,0:T(8,128)(2,1)S(1)}, bf16[512,2048]{1,0:T(8,128)(2,1)S(1)}, bf16[128,2048]{1,0:T(8,128)(2,1)S(1)}) custom-call(s32[3]{0:T(128)S(1)} %pad_add_fusion.1.where_ref, ...), custom_call_target="tpu_custom_call", output_to_operand_aliasing={{0}: (6, {}), {1}: (7, {}), {2}: (8, {}), {3}: (9, {})} | custom-call | flops 1 | bytes 1 | tf_op jit(solution)/shard_map/ffn/pallas_call | solution.py:666
  178.3 12.1 %ffn.5 = (bf16[512,2048]{1,0:T(8,128)(2,1)S(1)}, bf16[512,2048]{1,0:T(8,128)(2,1)S(1)}, bf16[512,2048]{1,0:T(8,128)(2,1)S(1)}, bf16[512,2048]{1,0:T(8,128)(2,1)S(1)}, bf16[128,2048]{1,0:T(8,128)(2,1)S(1)}) custom-call(s32[3]{0:T(128)S(1)} %pad_add_fusion.1.where_ref, ...), custom_call_target="tpu_custom_call", output_to_operand_aliasing={{0}: (8, {}), {1}: (9, {}), {2}: (10, {}), {3}: (11, {})} | custom-call | flops 1 | bytes 1 | tf_op jit(solution)/shard_map/ffn/pallas_call | solution.py:666
  190.5 10.7 %collective-permute-done.10.refs_2_ = bf16[128,2048]{1,0:T(8,128)(2,1)S(1)} collective-permute-done((bf16[128,2048]{1,0:T(8,128)(2,1)S(1)}, bf16[128,2048]{1,0:T(8,128)(2,1)S(1)}, u32[]{:S(2)}, u32[]{:S(2)}) %collective-permute-start.10) | collective-permute-done | bytes 524320 | tf_op jit(solution)/shard_map/ppermute | solution.py:1190
  205.3 8.1 %ffn_outer.5 = (bf16[2,256,1024]{2,1,0:T(8,128)(2,1)}, bf16[2,256,1024]{2,1,0:T(8,128)(2,1)}, bf16[2,256,1024]{2,1,0:T(8,128)(2,1)}, bf16[2,256,1024]{2,1,0:T(8,128)(2,1)}) custom-call(s32[3]{0:T(128)S(1)} %pad_add_fusion.1.where_ref, bf16[512,2048]{1,0:T(8,128)(2,1)S(1)} %get-tuple-element.201.refs_0_, ...), custom_call_target="tpu_custom_call" | custom-call | flops 1 | bytes 1 | tf_op jit(solution)/shard_map/ffn_outer/pallas_call | solution.py:984
  216.4 8.1 %ffn_outer.3 = (bf16[2,256,1024]{2,1,0:T(8,128)(2,1)}, bf16[2,256,1024]{2,1,0:T(8,128)(2,1)}, bf16[2,256,1024]{2,1,0:T(8,128)(2,1)}, bf16[2,256,1024]{2,1,0:T(8,128)(2,1)}) custom-call(s32[3]{0:T(128)S(1)} %pad_add_fusion.1.where_ref, bf16[512,2048]{1,0:T(8,128)(2,1)S(1)} %get-tuple-element.201.refs_0_, ...), custom_call_target="tpu_custom_call" | custom-call | flops 1 | bytes 1 | tf_op jit(solution)/shard_map/ffn_outer/pallas_call | solution.py:984
  224.6 8.1 %ffn_outer.4 = (bf16[2,256,1024]{2,1,0:T(8,128)(2,1)}, bf16[2,256,1024]{2,1,0:T(8,128)(2,1)}, bf16[2,256,1024]{2,1,0:T(8,128)(2,1)}, bf16[2,256,1024]{2,1,0:T(8,128)(2,1)}) custom-call(s32[3]{0:T(128)S(1)} %pad_add_fusion.1.where_ref, bf16[512,2048]{1,0:T(8,128)(2,1)S(1)} %copy-done.8, bf16[512,2048]{1,0:T(8,128)(2,1)S(1)} %collective-permute-done.14.refs_1_, ...), custom_call_target="tpu_custom_call" | custom-call | flops 1 | bytes 1 | tf_op jit(solution)/shard_map/ffn_outer/pallas_call | solution.py:984
  232.7 5.3 %middle.1 = (bf16[128,2048]{1,0:T(8,128)(2,1)S(1)}, f32[128,2048]{1,0:T(8,128)S(1)}, bf16[4,128,512]{2,1,0:T(8,128)(2,1)S(1)}, f32[1,2048]{1,0:T(1,128)S(1)}) custom-call(s32[3]{0:T(128)S(1)} %pad_add_fusion.1.where_ref, f32[128,2048]{1,0:T(8,128)S(1)} %get-tuple-element.169.middle_ref, bf16[512,2048]{1,0:T(8,128)(2,1)S(1)} %bitcast.96, ...), custom_call_target="tpu_custom_call" | custom-call | flops 1 | bytes 1 | tf_op jit(solution)/shard_map/middle/pallas_call | solution.py:472
  240.7 4.1 all-to-all-start.3
  246.5 7.7 %branch.1 = bf16[512,2048]{1,0:T(8,128)(2,1)S(1)} custom-call(s32[3]{0:T(128)S(1)} %pad_add_fusion.1.where_ref, bf16[512,2048]{1,0:T(8,128)(2,1)S(1)} %copy-done.6, bf16[2048,2048]{1,0:T(8,128)(2,1)} %right_ref.3), custom_call_target="tpu_custom_call" | custom-call | flops 1 | bytes 1 | tf_op jit(solution)/shard_map/branch/pallas_call | solution.py:1105
  255.6 3.9 all-to-all-done.3
  263.3 4.4 all-to-all-start.4
  267.8 7.5 %all-to-all-done.4 = bf16[4,512,128]{2,1,0:T(8,128)(2,1)} async-done(((bf16[4,512,128]{2,1,0:T(8,128)(2,1)}), bf16[4,512,128]{2,1,0:T(8,128)(2,1)}, u32[]{:S(2)}, u32[]{:S(2)}) %all-to-all-start.4) | async-done | bytes 524320 | tf_op jit(solution)/shard_map/all_to_all | solution.py:1181
  276.5 15.0 %attend_back.1 = (f32[2048,128]{1,0:T(8,128)S(1)}, f32[2048,256]{1,0:T(8,128)S(1)}, bf16[2048,256]{1,0:T(8,128)(2,1)S(1)}) custom-call(s32[16]{0:T(128)S(1)} %pad_add_fusion.2.slot_places, s32[8]{0:T(128)S(1)} %get-tuple-element.320.key_low, bf16[2048,384]{1,0:T(8,128)(2,1)} %bitcast.12.own_ref, bf16[2048,256]{1,0:T(8,128)(2,1)S(1)} %copy-done.17, ...), custom_call_target="tpu_custom_call" | custom-call | flops 1 | bytes 1 | tf_op jit(solution)/shard_map/attend_back/pallas_call | solution.py:452
  291.7 3.7 fusion.8
  298.3 4.4 all-to-all-start.5
  307.2 15.7 %all-to-all-done.5.back_ref = bf16[4,512,384]{2,1,0:T(8,128)(2,1)} async-done(((bf16[4,512,384]{2,1,0:T(8,128)(2,1)}), bf16[4,512,384]{2,1,0:T(8,128)(2,1)}, u32[]{:S(2)}, u32[]{:S(2)}) %all-to-all-start.5) | async-done | bytes 1572896 | tf_op jit(solution)/shard_map/all_to_all | solution.py:1181
  322.9 9.1 %back.1 = (bf16[512,1536]{1,0:T(8,128)(2,1)S(1)}, f32[1,2048]{1,0:T(1,128)S(1)}, bf16[128,2048]{1,0:T(8,128)(2,1)S(1)}, bf16[128,2048]{1,0:T(8,128)(2,1)}, bf16[...) custom-call(s32[3]{0:T(128)S(1)} %pad_add_fusion.1.where_ref, bf16[4,512,384]{2,1,0:T(8,128)(2,1)} %all-to-all-done.5.back_ref, ...), custom_call_target="tpu_custom_call" | custom-call | flops 1 | bytes 1 | tf_op jit(solution)/shard_map/back/pallas_call | solution.py:757
  340.3 20.8 %all_to_all.35 = f32[8,2,256]{2,1,0:T(2,128)S(1)} all-to-all(f32[8,2,256]{2,1,0:T(2,128)S(1)} %bitcast.114), channel_id=1, replica_groups=mesh['seq'=8,'tp'=4] {'seq'}, dimensions={0} | all-to-all | bytes 32768 | tf_op jit(solution)/shard_map/all_to_all | solution.py:1341
  364.4 2.3 add.386
  370.3 9.2 %collective-permute-done.25.got_up_ref = bf16[128,2048]{1,0:T(8,128)(2,1)} collective-permute-done((bf16[128,2048]{1,0:T(8,128)(2,1)}, bf16[128,2048]{1,0:T(8,128)(2,1)}, u32[]{:S(2)}, u32[]{:S(2)}) %collective-permute-start.25) | collective-permute-done | bytes 524320 | tf_op jit(solution)/shard_map/ppermute | solution.py:860
  379.5 7.3 %collective-permute-done.27.refs_1_ = bf16[2,256,1024]{2,1,0:T(8,128)(2,1)} collective-permute-done((bf16[2,256,1024]{2,1,0:T(8,128)(2,1)}, bf16[2,256,1024]{2,1,0:T(8,128)(2,1)}, u32[]{:S(2)}, u32[]{:S(2)}) %collective-permute-start.27) | collective-permute-done | bytes 1048608 | tf_op jit(solution)/shard_map/ppermute | solution.py:1010
  397.8 9.1 %attn_outer.1 = (bf16[2,256,1024]{2,1,0:T(8,128)(2,1)}, bf16[2,256,1024]{2,1,0:T(8,128)(2,1)}, bf16[2,256,1024]{2,1,0:T(8,128)(2,1)}, bf16[2,256,1024]{2,1,0:T(8,128)(2,1)}) custom-call(s32[3]{0:T(128)S(1)} %pad_add_fusion.1.where_ref, bf16[512,2048]{1,0:T(8,128)(2,1)S(1)} %copy-done.27, bf16[512,2048]{1,0:T(8,128)(2,1)S(1)} %collective-permute-done.33.refs_1_, ...), custom_call_target="tpu_custom_call" | custom-call | flops 1 | bytes 1 | tf_op jit(solution)/shard_map/attn_outer/pallas_call | solution.py:984
  406.9 4.3 collective-permute-done.30.above_ref
  412.9 3.7 collective-permute-start.36
  419.9 21.1 %collective-permute-done.38.refs_1_ = bf16[2,256,1024]{2,1,0:T(8,128)(2,1)S(1)} collective-permute-done((bf16[2,256,1024]{2,1,0:T(8,128)(2,1)S(1)}, bf16[2,256,1024]{2,1,0:T(8,128)(2,1)S(1)}, u32[]{:S(2)}, u32[]{:S(2)}) %collective-permute-start.38) | collective-permute-done | bytes 1048608 | tf_op jit(solution)/shard_map/ppermute | solution.py:1010
  452.8 6.4 %collective-permute-done.45.refs_5_ = bf16[256,1024]{1,0:T(8,128)(2,1)S(1)} collective-permute-done((bf16[256,1024]{1,0:T(8,128)(2,1)S(1)}, bf16[256,1024]{1,0:T(8,128)(2,1)S(1)}, u32[]{:S(2)}, u32[]{:S(2)}) %collective-permute-start.45) | collective-permute-done | bytes 524320 | tf_op jit(solution)/shard_map/ppermute | solution.py:1010
  459.5 4.4 collective-permute-done.44.refs_2_
  464.0 2.3 collective-permute-done.43.refs_5_
  466.3 4.7 collective-permute-done.42.refs_2_
  476.6 3.5 widen_down.1
  480.1 3.3 widen_up.1
  483.4 3.3 widen_gate.1
  489.0 7.8 %collective-permute-done.47.refs_2_ = bf16[272,2048]{1,0:T(8,128)(2,1)S(1)} collective-permute-done((bf16[272,2048]{1,0:T(8,128)(2,1)S(1)}, bf16[272,2048]{1,0:T(8,128)(2,1)S(1)}, u32[]{:S(2)}, u32[]{:S(2)}) %collective-permute-start.47) | collective-permute-done | bytes 1114144 | tf_op jit(solution)/shard_map/ppermute | solution.py:861
  496.8 3.8 join.1
  (290 shorter events, 119.9 us)
Async XLA Ops:
  7.2 59.9 %all-gather.4.cloned.1.call-start = ((), (), s32[]{:S(2)}) async-start(), calls=%async_computation.8 | async-start | bytes 3276800 | tf_op jit(solution)/shard_map/all_gather | solution.py:1197
  21.9 25.3 %all-to-all-start = ((bf16[4,512,384]{2,1,0:T(8,128)(2,1)}), bf16[4,512,384]{2,1,0:T(8,128)(2,1)}, u32[]{:S(2)}, u32[]{:S(2)}) async-start(bf16[4,512,384]{2,1,0:T(8,128)(2,1)} %copy-done.37), calls=%async_computation | async-start | bytes 3145728 | tf_op jit(solution)/shard_map/all_to_all | solution.py:1181
  27.2 89.1 %all-gather.6.cloned.1.call-start = ((), (), s32[]{:S(2)}) async-start(), calls=%async_computation.9 | async-start | bytes 1966080 | tf_op jit(solution)/shard_map/all_gather | solution.py:1197
  70.9 46.3 %collective-permute-start.1 = (bf16[4,256,1280]{2,1,0:T(8,128)(2,1)}, bf16[4,256,1280]{2,1,0:T(8,128)(2,1)}, u32[]{:S(2)}, u32[]{:S(2)}) collective-permute-start(bf16[4,256,1280]{2,1,0:T(8,128)(2,1)} %bitcast.93), channel_id=1, source_target_pairs={{0,4},{4,0},{8,12},{12,8},{16,20},{20,16},{24,28},{28,24},{1,5},{5... | collective-permute-start | bytes 7864328 | tf_op jit(solution)/shard_map/ppermute | solution.py:1178
  80.4 36.0 %all-to-all-start.2 = ((bf16[4,128,512]{2,1,0:T(8,128)(2,1)}), bf16[4,128,512]{2,1,0:T(8,128)(2,1)S(1)}, u32[]{:S(2)}, u32[]{:S(2)}) async-start(bf16[4,128,512]{2,1,0:T(8,128)(2,1)} %reshape_reshape.3), calls=%async_computation.2 | async-start | bytes 1048576 | tf_op jit(solution)/shard_map/all_to_all | solution.py:1251
  128.4 13.0 %collective-permute-start.4 = (bf16[128,2048]{1,0:T(8,128)(2,1)S(1)}, bf16[128,2048]{1,0:T(8,128)(2,1)S(1)}, u32[]{:S(2)}, u32[]{:S(2)}) collective-permute-start(bf16[128,2048]{1,0:T(8,128)(2,1)S(1)} %get-tuple-element.170.refs_0_), channel_id=1, source_target_pairs={{0,1},{1,2},{2,3},{4,5},{5,6},{6,7},{8,9},{9,10},{10,11},{12,13},{... | collective-permute-start | bytes 1572872 | tf_op jit(solution)/shard_map/ppermute | solution.py:860
  129.7 15.9 %collective-permute-start.3 = (bf16[128,2048]{1,0:T(8,128)(2,1)S(1)}, bf16[128,2048]{1,0:T(8,128)(2,1)S(1)}, u32[]{:S(2)}, u32[]{:S(2)}) collective-permute-start(bf16[128,2048]{1,0:T(8,128)(2,1)S(1)} %get-tuple-element.170.refs_0_), channel_id=1, source_target_pairs={{1,0},{2,1},{3,2},{5,4},{6,5},{7,6},{9,8},{10,9},{11,10},{13,12},{... | collective-permute-start | bytes 1572872 | tf_op jit(solution)/shard_map/ppermute | solution.py:861
  141.4 19.6 %collective-permute-start.5 = (bf16[128,2048]{1,0:T(8,128)(2,1)S(1)}, bf16[128,2048]{1,0:T(8,128)(2,1)S(1)}, u32[]{:S(2)}, u32[]{:S(2)}) collective-permute-start(bf16[128,2048]{1,0:T(8,128)(2,1)S(1)} %collective-permute-done.4.refs_2_.refs_1_), channel_id=1, source_target_pairs={{1,2},{2,3},{5,6},{6,7},{9,10},{10,11},{13,14},{14,15},{17,18},{18... | collective-permute-start | bytes 1572872 | tf_op jit(solution)/shard_map/ppermute | solution.py:860
  145.5 15.5 %collective-permute-start.6 = (bf16[128,2048]{1,0:T(8,128)(2,1)S(1)}, bf16[128,2048]{1,0:T(8,128)(2,1)S(1)}, u32[]{:S(2)}, u32[]{:S(2)}) collective-permute-start(bf16[128,2048]{1,0:T(8,128)(2,1)S(1)} %collective-permute-done.3.refs_1_.refs_0_), channel_id=1, source_target_pairs={{1,0},{2,1},{5,4},{6,5},{9,8},{10,9},{13,12},{14,13},{17,16},{18,1... | collective-permute-start | bytes 1572872 | tf_op jit(solution)/shard_map/ppermute | solution.py:861
  161.0 14.1 %collective-permute-start.7 = (bf16[128,2048]{1,0:T(8,128)(2,1)S(1)}, bf16[128,2048]{1,0:T(8,128)(2,1)S(1)}, u32[]{:S(2)}, u32[]{:S(2)}) collective-permute-start(bf16[128,2048]{1,0:T(8,128)(2,1)S(1)} %collective-permute-done.5.refs_1_), channel_id=1, source_target_pairs={{2,3},{6,7},{10,11},{14,15},{18,19},{22,23},{26,27},{30,31}} | collective-permute-start | bytes 1572872 | tf_op jit(solution)/shard_map/ppermute | solution.py:860
  161.7 15.0 %collective-permute-start.8 = (bf16[128,2048]{1,0:T(8,128)(2,1)S(1)}, bf16[128,2048]{1,0:T(8,128)(2,1)S(1)}, u32[]{:S(2)}, u32[]{:S(2)}) collective-permute-start(bf16[128,2048]{1,0:T(8,128)(2,1)S(1)} %collective-permute-done.6.refs_0_), channel_id=1, source_target_pairs={{1,0},{5,4},{9,8},{13,12},{17,16},{21,20},{25,24},{29,28}} | collective-permute-start | bytes 1572872 | tf_op jit(solution)/shard_map/ppermute | solution.py:861
  176.8 24.3 %collective-permute-start.10 = (bf16[128,2048]{1,0:T(8,128)(2,1)S(1)}, bf16[128,2048]{1,0:T(8,128)(2,1)S(1)}, u32[]{:S(2)}, u32[]{:S(2)}) collective-permute-start(bf16[128,2048]{1,0:T(8,128)(2,1)S(1)} %get-tuple-element.197), channel_id=1, source_target_pairs={{0,2},{1,3},{2,0},{3,1},{4,6},{5,7},{6,4},{7,5},{8,10},{9,11},{10,... | collective-permute-start | bytes 1572872 | tf_op jit(solution)/shard_map/ppermute | solution.py:1190
  178.1 23.1 %collective-permute-start.9 = (bf16[128,2048]{1,0:T(8,128)(2,1)S(1)}, bf16[128,2048]{1,0:T(8,128)(2,1)S(1)}, u32[]{:S(2)}, u32[]{:S(2)}) collective-permute-start(bf16[128,2048]{1,0:T(8,128)(2,1)S(1)} %get-tuple-element.196), channel_id=1, source_target_pairs={{0,1},{1,0},{2,3},{3,2},{4,5},{5,4},{6,7},{7,6},{8,9},{9,8},{10,11... | collective-permute-start | bytes 1572872 | tf_op jit(solution)/shard_map/ppermute | solution.py:1190
  201.1 13.8 %collective-permute-start.13 = (bf16[512,2048]{1,0:T(8,128)(2,1)S(1)}, bf16[512,2048]{1,0:T(8,128)(2,1)S(1)}, u32[]{:S(2)}, u32[]{:S(2)}) collective-permute-start(bf16[512,2048]{1,0:T(8,128)(2,1)S(1)} %get-tuple-element.202.refs_2_), channel_id=1, source_target_pairs={{0,4},{4,0},{8,12},{12,8},{16,20},{20,16},{24,28},{28,24},{1,5},{5... | collective-permute-start | bytes 6291464 | tf_op jit(solution)/shard_map/ppermute | solution.py:1178
  201.6 22.9 %collective-permute-start.14 = (bf16[512,2048]{1,0:T(8,128)(2,1)S(1)}, bf16[512,2048]{1,0:T(8,128)(2,1)S(1)}, u32[]{:S(2)}, u32[]{:S(2)}) collective-permute-start(bf16[512,2048]{1,0:T(8,128)(2,1)S(1)} %copy-done.8), channel_id=1, source_target_pairs={{0,4},{4,0},{8,12},{12,8},{16,20},{20,16},{24,28},{28,24},{1,5},{5... | collective-permute-start | bytes 6291464 | tf_op jit(solution)/shard_map/ppermute | solution.py:1178
  201.6 22.9 %collective-permute-start.15 = (bf16[512,2048]{1,0:T(8,128)(2,1)S(1)}, bf16[512,2048]{1,0:T(8,128)(2,1)S(1)}, u32[]{:S(2)}, u32[]{:S(2)}) collective-permute-start(bf16[512,2048]{1,0:T(8,128)(2,1)S(1)} %get-tuple-element.219.refs_2_.left_ref), channel_id=1, source_target_pairs={{0,4},{4,0},{8,12},{12,8},{16,20},{20,16},{24,28},{28,24},{1,5},{5... | collective-permute-start | bytes 6291464 | tf_op jit(solution)/shard_map/ppermute | solution.py:1178
  202.1 30.6 %collective-permute-start.11 = (bf16[128,2048]{1,0:T(8,128)(2,1)S(1)}, bf16[128,2048]{1,0:T(8,128)(2,1)S(1)}, u32[]{:S(2)}, u32[]{:S(2)}) collective-permute-start(bf16[128,2048]{1,0:T(8,128)(2,1)S(1)} %get-tuple-element.200), channel_id=1, source_target_pairs={{0,3},{1,2},{2,1},{3,0},{4,7},{5,6},{6,5},{7,4},{8,11},{9,10},{10,... | collective-permute-start | bytes 1572872 | tf_op jit(solution)/shard_map/ppermute | solution.py:1190
  213.4 46.0 %collective-permute-start.17 = (bf16[2,256,1024]{2,1,0:T(8,128)(2,1)}, bf16[2,256,1024]{2,1,0:T(8,128)(2,1)}, u32[]{:S(2)}, u32[]{:S(2)}) collective-permute-start(bf16[2,256,1024]{2,1,0:T(8,128)(2,1)} %get-tuple-element.215), channel_id=1, source_target_pairs={{0,8},{4,12},{8,0},{12,4},{16,24},{20,28},{24,16},{28,20},{1,9},{5... | collective-permute-start | bytes 3145736 | tf_op jit(solution)/shard_map/ppermute | solution.py:1010
  214.9 44.5 %collective-permute-start.18 = (bf16[2,256,1024]{2,1,0:T(8,128)(2,1)}, bf16[2,256,1024]{2,1,0:T(8,128)(2,1)}, u32[]{:S(2)}, u32[]{:S(2)}) collective-permute-start(bf16[2,256,1024]{2,1,0:T(8,128)(2,1)} %get-tuple-element.216), channel_id=1, source_target_pairs={{0,16},{4,20},{8,24},{12,28},{16,0},{20,4},{24,8},{28,12},{1,17},{... | collective-permute-start | bytes 3145736 | tf_op jit(solution)/shard_map/ppermute | solution.py:1010
  240.7 18.7 %all-to-all-start.3 = ((bf16[4,128,512]{2,1,0:T(8,128)(2,1)}), bf16[4,128,512]{2,1,0:T(8,128)(2,1)}, u32[]{:S(2)}, u32[]{:S(2)}) async-start(bf16[4,128,512]{2,1,0:T(8,128)(2,1)} %copy-done.46), calls=%async_computation.3 | async-start | bytes 1048576 | tf_op jit(solution)/shard_map/all_to_all | solution.py:1312
  244.9 78.0 %reduce-scatter.2.cloned.1.call-start = ((), (), s32[]{:S(2)}) async-start(), calls=%async_computation.10 | async-start | bytes 2621440 | tf_op jit(solution)/shard_map/reduce_scatter | solution.py:1316
  298.3 24.6 %all-to-all-start.5 = ((bf16[4,512,384]{2,1,0:T(8,128)(2,1)}), bf16[4,512,384]{2,1,0:T(8,128)(2,1)}, u32[]{:S(2)}, u32[]{:S(2)}) async-start(bf16[4,512,384]{2,1,0:T(8,128)(2,1)} %bitcast.100), calls=%async_computation.5 | async-start | bytes 3145728 | tf_op jit(solution)/shard_map/all_to_all | solution.py:1181
  302.6 67.7 %all-gather.8.cloned.1.call-start = ((), (), s32[]{:S(2)}) async-start(), calls=%async_computation.11 | async-start | bytes 2621440 | tf_op jit(solution)/shard_map/all_gather | solution.py:1323
  334.7 26.4 %collective-permute-start.23 = (bf16[2,256,1024]{2,1,0:T(8,128)(2,1)}, bf16[2,256,1024]{2,1,0:T(8,128)(2,1)}, u32[]{:S(2)}, u32[]{:S(2)}) collective-permute-start(bf16[2,256,1024]{2,1,0:T(8,128)(2,1)} %get-tuple-element.232), channel_id=1, source_target_pairs={{0,8},{4,12},{8,0},{12,4},{16,24},{20,28},{24,16},{28,20},{1,9},{5... | collective-permute-start | bytes 3145736 | tf_op jit(solution)/shard_map/ppermute | solution.py:1010
  336.2 25.0 %collective-permute-start.24 = (bf16[2,256,1024]{2,1,0:T(8,128)(2,1)}, bf16[2,256,1024]{2,1,0:T(8,128)(2,1)}, u32[]{:S(2)}, u32[]{:S(2)}) collective-permute-start(bf16[2,256,1024]{2,1,0:T(8,128)(2,1)} %get-tuple-element.233), channel_id=1, source_target_pairs={{0,16},{4,20},{8,24},{12,28},{16,0},{20,4},{24,8},{28,12},{1,17},{... | collective-permute-start | bytes 3145736 | tf_op jit(solution)/shard_map/ppermute | solution.py:1010
  336.8 24.4 %collective-permute-start.21 = (bf16[128,2048]{1,0:T(8,128)(2,1)}, bf16[128,2048]{1,0:T(8,128)(2,1)}, u32[]{:S(2)}, u32[]{:S(2)}) collective-permute-start(bf16[128,2048]{1,0:T(8,128)(2,1)} %get-tuple-element.227.down_ref), channel_id=1, source_target_pairs={{0,1},{4,5},{8,9},{12,13},{16,17},{20,21},{24,25},{28,29}} | collective-permute-start | bytes 1572872 | tf_op jit(solution)/shard_map/ppermute | solution.py:860
  338.9 22.3 %collective-permute-start.22 = (bf16[128,2048]{1,0:T(8,128)(2,1)}, bf16[128,2048]{1,0:T(8,128)(2,1)}, u32[]{:S(2)}, u32[]{:S(2)}) collective-permute-start(bf16[128,2048]{1,0:T(8,128)(2,1)} %get-tuple-element.228.up_ref), channel_id=1, source_target_pairs={{3,2},{7,6},{11,10},{15,14},{19,18},{23,22},{27,26},{31,30}} | collective-permute-start | bytes 1572872 | tf_op jit(solution)/shard_map/ppermute | solution.py:861
  361.2 25.6 %collective-permute-start.27 = (bf16[2,256,1024]{2,1,0:T(8,128)(2,1)}, bf16[2,256,1024]{2,1,0:T(8,128)(2,1)}, u32[]{:S(2)}, u32[]{:S(2)}) collective-permute-start(bf16[2,256,1024]{2,1,0:T(8,128)(2,1)} %get-tuple-element.246), channel_id=1, source_target_pairs={{0,8},{4,12},{8,0},{12,4},{16,24},{20,28},{24,16},{28,20},{1,9},{5... | collective-permute-start | bytes 3145736 | tf_op jit(solution)/shard_map/ppermute | solution.py:1010
  361.9 25.2 %collective-permute-start.28 = (bf16[2,256,1024]{2,1,0:T(8,128)(2,1)}, bf16[2,256,1024]{2,1,0:T(8,128)(2,1)}, u32[]{:S(2)}, u32[]{:S(2)}) collective-permute-start(bf16[2,256,1024]{2,1,0:T(8,128)(2,1)} %get-tuple-element.247), channel_id=1, source_target_pairs={{0,16},{4,20},{8,24},{12,28},{16,0},{20,4},{24,8},{28,12},{1,17},{... | collective-permute-start | bytes 3145736 | tf_op jit(solution)/shard_map/ppermute | solution.py:1010
  366.7 12.8 %collective-permute-start.25 = (bf16[128,2048]{1,0:T(8,128)(2,1)}, bf16[128,2048]{1,0:T(8,128)(2,1)}, u32[]{:S(2)}, u32[]{:S(2)}) collective-permute-start(bf16[128,2048]{1,0:T(8,128)(2,1)} %get-tuple-element.241), channel_id=1, source_target_pairs={{0,1},{1,2},{4,5},{5,6},{8,9},{9,10},{12,13},{13,14},{16,17},{17,1... | collective-permute-start | bytes 1572872 | tf_op jit(solution)/shard_map/ppermute | solution.py:860
  370.3 24.4 %collective-permute-start.34 = (bf16[512,2048]{1,0:T(8,128)(2,1)}, bf16[512,2048]{1,0:T(8,128)(2,1)}, u32[]{:S(2)}, u32[]{:S(2)}) collective-permute-start(bf16[512,2048]{1,0:T(8,128)(2,1)} %get-tuple-element.261.refs_4_), channel_id=1, source_target_pairs={{0,4},{4,0},{8,12},{12,8},{16,20},{20,16},{24,28},{28,24},{1,5},{5... | collective-permute-start | bytes 6291464 | tf_op jit(solution)/shard_map/ppermute | solution.py:1178
  389.1 17.8 %collective-permute-start.32 = (bf16[256,1024]{1,0:T(8,128)(2,1)S(1)}, bf16[256,1024]{1,0:T(8,128)(2,1)S(1)}, u32[]{:S(2)}, u32[]{:S(2)}) collective-permute-start(bf16[256,1024]{1,0:T(8,128)(2,1)S(1)} %fusion.1), channel_id=1, source_target_pairs={{0,8},{4,12},{8,0},{12,4},{16,24},{20,28},{24,16},{28,20},{1,9},{5... | collective-permute-start | bytes 1572872 | tf_op jit(solution)/shard_map/ppermute | solution.py:1010
  392.0 14.9 %collective-permute-start.31 = (bf16[256,1024]{1,0:T(8,128)(2,1)S(1)}, bf16[256,1024]{1,0:T(8,128)(2,1)S(1)}, u32[]{:S(2)}, u32[]{:S(2)}) collective-permute-start(bf16[256,1024]{1,0:T(8,128)(2,1)S(1)} %fusion), channel_id=1, source_target_pairs={{0,16},{4,20},{8,24},{12,28},{16,0},{20,4},{24,8},{28,12},{1,17},{... | collective-permute-start | bytes 1572872 | tf_op jit(solution)/shard_map/ppermute | solution.py:1010
  394.7 12.3 %collective-permute-start.29 = (bf16[128,2048]{1,0:T(8,128)(2,1)S(1)}, bf16[128,2048]{1,0:T(8,128)(2,1)S(1)}, u32[]{:S(2)}, u32[]{:S(2)}) collective-permute-start(bf16[128,2048]{1,0:T(8,128)(2,1)S(1)} %get-tuple-element.251), channel_id=1, source_target_pairs={{0,1},{1,2},{2,3},{4,5},{5,6},{6,7},{8,9},{9,10},{10,11},{12,13},{... | collective-permute-start | bytes 1572872 | tf_op jit(solution)/shard_map/ppermute | solution.py:860
  396.0 15.2 %collective-permute-start.30 = (bf16[128,2048]{1,0:T(8,128)(2,1)S(1)}, bf16[128,2048]{1,0:T(8,128)(2,1)S(1)}, u32[]{:S(2)}, u32[]{:S(2)}) collective-permute-start(bf16[128,2048]{1,0:T(8,128)(2,1)S(1)} %get-tuple-element.252), channel_id=1, source_target_pairs={{1,0},{2,1},{3,2},{5,4},{6,5},{7,6},{9,8},{10,9},{11,10},{13,12},{... | collective-permute-start | bytes 1572872 | tf_op jit(solution)/shard_map/ppermute | solution.py:861
  412.9 29.1 %collective-permute-start.36 = (bf16[272,2048]{1,0:T(8,128)(2,1)S(1)}, bf16[272,2048]{1,0:T(8,128)(2,1)S(1)}, u32[]{:S(2)}, u32[]{:S(2)}) collective-permute-start(bf16[272,2048]{1,0:T(8,128)(2,1)S(1)} %tokens.1.own_ref), channel_id=1, source_target_pairs={{0,1},{1,2},{2,3},{4,5},{5,6},{6,7},{8,9},{9,10},{10,11},{12,13},{... | collective-permute-start | bytes 3342344 | tf_op jit(solution)/shard_map/ppermute | solution.py:860
  416.6 26.2 %collective-permute-start.37 = (bf16[272,2048]{1,0:T(8,128)(2,1)S(1)}, bf16[272,2048]{1,0:T(8,128)(2,1)S(1)}, u32[]{:S(2)}, u32[]{:S(2)}) collective-permute-start(bf16[272,2048]{1,0:T(8,128)(2,1)S(1)} %tokens.1.own_ref), channel_id=1, source_target_pairs={{1,0},{2,1},{3,2},{5,4},{6,5},{7,6},{9,8},{10,9},{11,10},{13,12},{... | collective-permute-start | bytes 3342344 | tf_op jit(solution)/shard_map/ppermute | solution.py:861
  418.0 23.0 %collective-permute-start.38 = (bf16[2,256,1024]{2,1,0:T(8,128)(2,1)S(1)}, bf16[2,256,1024]{2,1,0:T(8,128)(2,1)S(1)}, u32[]{:S(2)}, u32[]{:S(2)}) collective-permute-start(bf16[2,256,1024]{2,1,0:T(8,128)(2,1)S(1)} %copy-done.53), channel_id=1, source_target_pairs={{0,8},{4,12},{8,0},{12,4},{16,24},{20,28},{24,16},{28,20},{1,9},{5... | collective-permute-start | bytes 3145736 | tf_op jit(solution)/shard_map/ppermute | solution.py:1010
  419.3 22.7 %collective-permute-start.39 = (bf16[2,256,1024]{2,1,0:T(8,128)(2,1)S(1)}, bf16[2,256,1024]{2,1,0:T(8,128)(2,1)S(1)}, u32[]{:S(2)}, u32[]{:S(2)}) collective-permute-start(bf16[2,256,1024]{2,1,0:T(8,128)(2,1)S(1)} %copy-done.52), channel_id=1, source_target_pairs={{0,16},{4,20},{8,24},{12,28},{16,0},{20,4},{24,8},{28,12},{1,17},{... | collective-permute-start | bytes 3145736 | tf_op jit(solution)/shard_map/ppermute | solution.py:1010
  444.2 14.9 %collective-permute-start.45 = (bf16[256,1024]{1,0:T(8,128)(2,1)S(1)}, bf16[256,1024]{1,0:T(8,128)(2,1)S(1)}, u32[]{:S(2)}, u32[]{:S(2)}) collective-permute-start(bf16[256,1024]{1,0:T(8,128)(2,1)S(1)} %fusion.5), channel_id=1, source_target_pairs={{0,8},{4,12},{8,0},{12,4},{16,24},{20,28},{24,16},{28,20},{1,9},{5... | collective-permute-start | bytes 1572872 | tf_op jit(solution)/shard_map/ppermute | solution.py:1010
  445.6 25.3 %collective-permute-start.40 = (bf16[272,2048]{1,0:T(8,128)(2,1)S(1)}, bf16[272,2048]{1,0:T(8,128)(2,1)S(1)}, u32[]{:S(2)}, u32[]{:S(2)}) collective-permute-start(bf16[272,2048]{1,0:T(8,128)(2,1)S(1)} %collective-permute-done.36.refs_3_), channel_id=1, source_target_pairs={{1,2},{2,3},{5,6},{6,7},{9,10},{10,11},{13,14},{14,15},{17,18},{18... | collective-permute-start | bytes 3342344 | tf_op jit(solution)/shard_map/ppermute | solution.py:860
  446.4 25.6 %collective-permute-start.41 = (bf16[272,2048]{1,0:T(8,128)(2,1)S(1)}, bf16[272,2048]{1,0:T(8,128)(2,1)S(1)}, u32[]{:S(2)}, u32[]{:S(2)}) collective-permute-start(bf16[272,2048]{1,0:T(8,128)(2,1)S(1)} %collective-permute-done.37.refs_0_), channel_id=1, source_target_pairs={{1,0},{2,1},{5,4},{6,5},{9,8},{10,9},{13,12},{14,13},{17,16},{18,1... | collective-permute-start | bytes 3342344 | tf_op jit(solution)/shard_map/ppermute | solution.py:861
  449.0 14.9 %collective-permute-start.44 = (bf16[256,1024]{1,0:T(8,128)(2,1)S(1)}, bf16[256,1024]{1,0:T(8,128)(2,1)S(1)}, u32[]{:S(2)}, u32[]{:S(2)}) collective-permute-start(bf16[256,1024]{1,0:T(8,128)(2,1)S(1)} %fusion.4), channel_id=1, source_target_pairs={{0,16},{4,20},{8,24},{12,28},{16,0},{20,4},{24,8},{28,12},{1,17},{... | collective-permute-start | bytes 1572872 | tf_op jit(solution)/shard_map/ppermute | solution.py:1010
  450.8 15.4 %collective-permute-start.43 = (bf16[256,1024]{1,0:T(8,128)(2,1)S(1)}, bf16[256,1024]{1,0:T(8,128)(2,1)S(1)}, u32[]{:S(2)}, u32[]{:S(2)}) collective-permute-start(bf16[256,1024]{1,0:T(8,128)(2,1)S(1)} %fusion.3), channel_id=1, source_target_pairs={{0,8},{4,12},{8,0},{12,4},{16,24},{20,28},{24,16},{28,20},{1,9},{5... | collective-permute-start | bytes 1572872 | tf_op jit(solution)/shard_map/ppermute | solution.py:1010
  472.0 17.0 %collective-permute-start.46 = (bf16[272,2048]{1,0:T(8,128)(2,1)S(1)}, bf16[272,2048]{1,0:T(8,128)(2,1)S(1)}, u32[]{:S(2)}, u32[]{:S(2)}) collective-permute-start(bf16[272,2048]{1,0:T(8,128)(2,1)S(1)} %collective-permute-done.40.refs_4_), channel_id=1, source_target_pairs={{2,3},{6,7},{10,11},{14,15},{18,19},{22,23},{26,27},{30,31}} | collective-permute-start | bytes 3342344 | tf_op jit(solution)/shard_map/ppermute | solution.py:860
  472.7 24.1 %collective-permute-start.47 = (bf16[272,2048]{1,0:T(8,128)(2,1)S(1)}, bf16[272,2048]{1,0:T(8,128)(2,1)S(1)}, u32[]{:S(2)}, u32[]{:S(2)}) collective-permute-start(bf16[272,2048]{1,0:T(8,128)(2,1)S(1)} %collective-permute-done.41.refs_1_), channel_id=1, source_target_pairs={{1,0},{5,4},{9,8},{13,12},{17,16},{21,20},{25,24},{29,28}} | collective-permute-start | bytes 3342344 | tf_op jit(solution)/shard_map/ppermute | solution.py:861
  474.3 12.4 %collective-permute-start.49 = (bf16[256,1024]{1,0:T(8,128)(2,1)S(1)}, bf16[256,1024]{1,0:T(8,128)(2,1)S(1)}, u32[]{:S(2)}, u32[]{:S(2)}) collective-permute-start(bf16[256,1024]{1,0:T(8,128)(2,1)S(1)} %fusion.7), channel_id=1, source_target_pairs={{0,8},{4,12},{8,0},{12,4},{16,24},{20,28},{24,16},{28,20},{1,9},{5... | collective-permute-start | bytes 1572872 | tf_op jit(solution)/shard_map/ppermute | solution.py:1010
  475.6 12.1 %collective-permute-start.48 = (bf16[256,1024]{1,0:T(8,128)(2,1)S(1)}, bf16[256,1024]{1,0:T(8,128)(2,1)S(1)}, u32[]{:S(2)}, u32[]{:S(2)}) collective-permute-start(bf16[256,1024]{1,0:T(8,128)(2,1)S(1)} %fusion.6), channel_id=1, source_target_pairs={{0,16},{4,20},{8,24},{12,28},{16,0},{20,4},{24,8},{28,12},{1,17},{... | collective-permute-start | bytes 1572872 | tf_op jit(solution)/shard_map/ppermute | solution.py:1010
  (66 other events, 595.7 us)
Sparse Core Ops, SparseCore 0:
  9.6 57.4 all-gather.3
  69.3 47.0 all-gather.5
  259.6 41.0 reduce-scatter.1
  304.8 49.1 all-gather.7

commit v4 on v3

--- a/solution.py
+++ b/solution.py
@@ -1241,7 +1241,7 @@
     grad_act = matmul_call(where, upstream_rel, w_down, f32, True, "grad_act")
     upstream_pair = (upstream_rel, swap(upstream_rel))
     normed_attn_pair = (normed_attn, swap(normed_attn))
-    mine, grad_act = tie(mine, grad_act)
+    mine, grad_act, cosine_q, sine_q = tie(mine, grad_act, cosine_q, sine_q)
     other = swap(mine[:, head:])
 
     attended = attend_call(slot_places, key_low, mine, other, start_q.reshape(-1, 1), span)
@@ -1281,7 +1281,7 @@
     )
     grad_3 = across(grad_3, 3)
     activated, gate_pre, up_pre, normed_ffn = filled
-    gate_pre, grad_1, grad_2 = tie(gate_pre, grad_1, grad_2)
+    up_pre, grad_1, grad_2 = tie(up_pre, grad_1, grad_2)
 
     normed_pair = (normed_ffn, swap(normed_ffn))
     outer_ffn = functools.partial(
@@ -1293,9 +1293,9 @@
     gate_sum = ChipSum(outer_ffn([gate_quad]), seq_size)
     gate_sum.first()
     up_sum = ChipSum(outer_ffn([up_quad]), seq_size)
+    up_sum.first()
     down_sum = ChipSum(outer_ffn([down_quad]), seq_size)
-    grad_3, *arrays = tie(grad_3, *up_sum.arrays, *down_sum.arrays)
-    up_sum.arrays, down_sum.arrays = arrays[:4], arrays[4:]
+    grad_3, *down_sum.arrays = tie(grad_3, *down_sum.arrays)
     middle_low, grad_middle, grad_attended, gain_ffn_part = call(
         middle_kernel,
         (
@@ -1311,7 +1311,7 @@
     )
     grad_attended = lax.all_to_all(grad_attended, "tp", 0, 0, tiled=True)
     branch = matmul_call(where, after(activated, middle_low), w_down, bf16, False, "branch", tp_size)
-    grad_attended, branch = gate_sum.tie(grad_attended, branch)
+    grad_attended, branch = up_sum.tie(*gate_sum.tie(grad_attended, branch))
     branch = after(branch, grad_attended)
     branch_part = lax.psum_scatter(branch, "tp", scatter_dimension=0, tiled=True)
     grad_attended = grad_attended.reshape(row_count, heads, head).transpose(1, 0, 2)
@@ -1335,16 +1335,13 @@
     )
     sums = Sum(parts, "tp", tp_size)
     sums.step()
-    up_sum.first(low)
     gains = jnp.concatenate([gain_attn_part, gain_ffn_part], axis=0)
     gains = gains.reshape(2, seq_size, block).transpose(1, 0, 2)
     gains = jnp.sum(lax.all_to_all(gains, "seq", 0, 0, tiled=True), axis=0).reshape(1, 2 * block)
-    up_sum.got_x, up_sum.got_y, low, gains = sums.tie(up_sum.got_x, up_sum.got_y, low, gains)
     down_sum.first(low)
+    down_sum.got_x, down_sum.got_y, low = sums.tie(down_sum.got_x, down_sum.got_y, low)
     sums.step()
-    down_sum.got_x, down_sum.got_y, low, middle_all = sums.tie(
-        down_sum.got_x, down_sum.got_y, low, middle_all
-    )
+    gains, low, middle_all = sums.tie(gains, low, middle_all)
     up_sum.second(low)
     sums.step()
     middle_pair = (middle_all, swap(middle_all))

time: 518 us -> 517 us (level)
  blocking collectives: 20.8 us -> 7.46 us
  local copies, waits for them, and re-layouts: 45.2 us -> 53.8 us
  starting transfers between devices: 73.9 us -> 80.5 us
  waiting for transfers between devices: 174 us -> 168 us
    all_to_all x1, blocking collectives: 20.8 us -> 7.46 us  [local_heads_apart(): lax.all_to_all(gains, 'seq', 0, 0, tiled=True)]
    unnamed x117 -> x141, local copies, waits for them, and re-layouts: 26.1 us -> 34.7 us
    all_gather x2, waiting for transfers between devices: 34.3 us -> 26.9 us  [gathered(): values = lax.all_gather(columns, 'tp', axis=0, tiled=True)]
    ppermute x9, starting transfers between devices: 13.4 us -> 20 us  [send(): self.upward = lax.ppermute(up, self.axis, up_pairs)]
  transfers between devices with their start and end apart: 60 -> 60, of which waited for: 27 -> 28; matrix products, arithmetic and copies ran while one was open for 7% -> 7% of each run, Pallas kernels for 30% -> 30%
where the time goes in v4:
time: 517 us; the launch traced here: 507 us
  waiting for transfers between devices  168 us (32%)
  Pallas kernels  162 us (31%)
  starting transfers between devices  80.5 us (16%)
  local copies, waits for them, and re-layouts  53.8 us (10%)
  other arithmetic  20.3 us (4%)
  between operations  15.1 us (3%)
  blocking collectives  7.46 us (1%)
    ppermute x16, waiting for transfers between devices, over(): lax.ppermute(values, 'seq', [(i, i ^ side) for i in range(self.size)])  51.6 us
    pallas_call x3, Pallas kernels, ffn_call(): pl.pallas_call(functools.partial(ffn_kernel, chunk=chunk, sources=len(sou...  38 us
    unnamed x141, local copies, waits for them, and re-layouts  34.7 us
    pallas_call x4, Pallas kernels, chip_outer_call(): pl.pallas_call(functools.partial(chip_outer_kernel, sides=len(pairs)), ou...  33.7 us
    pallas_call x12, Pallas kernels, call(): pl.pallas_call(kernel, out_shape=tuple(outs), in_specs=[SMALL] * scalars...  30.2 us
    all_to_all x4, waiting for transfers between devices, to_heads(): lax.all_to_all(values, 'seq', 0, 0, axis_index_groups=same_core, tiled=True)  29.9 us
    all_gather x2, waiting for transfers between devices, gathered(): values = lax.all_gather(columns, 'tp', axis=0, tiled=True)  26.9 us
    ppermute x9, starting transfers between devices, send(): self.upward = lax.ppermute(up, self.axis, up_pairs)  20 us
  transfers between devices with their start and end apart: 60, of which 28 were waited for; matrix products, arithmetic and copies ran while one was open for 7% of the time, Pallas kernels for 30%

profile of v4, /device:TPU:0, one launch (start us, length us, event | category | flops | bytes accessed | tf_op | source)
XLA Modules:
  0.0 507.4 jit_solution(6396358642902395698)
XLA Ops:
  13.4 7.4 %project.1 = (bf16[4,512,384]{2,1,0:T(8,128)(2,1)S(1)}, bf16[512,2048]{1,0:T(8,128)(2,1)}) custom-call(bf16[512,2048]{1,0:T(8,128)(2,1)S(1)} %bitcast.89, f32[1,2048]{1,0:T(1,128)S(1)} %bitcast.107, s32[512,1]{1,0:T(8,128)S(1)} %bitcast.102, f32[512,128]{1,0:T(8,128)S(1)} %get-tuple-element.332.cosine_ref, f32[512,128]{1,0:T(8,128)S(1)} %get-tuple-element.333.sine_ref, ...), custom_call_target="tpu_custom_call" | custom-call | flops 1 | bytes 1 | tf_op jit(solution)/shard_map/project/pallas_call | solution.py:482
  22.0 5.3 %all-to-all-start = ((bf16[4,512,384]{2,1,0:T(8,128)(2,1)}), bf16[4,512,384]{2,1,0:T(8,128)(2,1)}, u32[]{:S(2)}, u32[]{:S(2)}) async-start(bf16[4,512,384]{2,1,0:T(8,128)(2,1)} %copy-done.39), calls=%async_computation | async-start | bytes 3145728 | tf_op jit(solution)/shard_map/all_to_all | solution.py:1181
  35.8 8.0 %grad_act.1.refs_3_.refs_2_.refs_4_ = f32[512,2048]{1,0:T(8,128)S(1)} custom-call(s32[3]{0:T(128)S(1)} %pad_add_fusion.1.where_ref, bf16[512,2048]{1,0:T(8,128)(2,1)S(1)} %pad_maximum_fusion.left_ref.refs_0_, bf16[2048,2048]{1,0:T(8,128)(2,1)} %right_ref.3), custom_call_target="tpu_custom_call" | custom-call | flops 1 | bytes 1 | tf_op jit(solution)/shard_map/grad_act/pallas_call | solution.py:1105
  45.9 3.7 fusion.8
  59.0 11.5 %attend.1 = bf16[2048,128]{1,0:T(8,128)(2,1)S(1)} custom-call(s32[16]{0:T(128)S(1)} %pad_add_fusion.2.slot_places, s32[8]{0:T(128)S(1)} %get-tuple-element.316.key_low, bf16[2048,384]{1,0:T(8,128)(2,1)} %bitcast.12.own_ref, bf16[2048,256]{1,0:T(8,128)(2,1)S(1)} %collective-permute-done.other_ref, s32[2048,1]{1,0:T(8,128)S(1)} %bitcast.101), custom_call_target="tpu_custom_call" | custom-call | flops 1 | bytes 1 | tf_op jit(solution)/shard_map/attend/pallas_call | solution.py:438
  71.3 4.9 all-to-all-start.1
  76.2 6.7 %all-to-all-done.1 = bf16[4,512,128]{2,1,0:T(8,128)(2,1)S(1)} async-done(((bf16[4,512,128]{2,1,0:T(8,128)(2,1)}), bf16[4,512,128]{2,1,0:T(8,128)(2,1)S(1)}, u32[]{:S(2)}, u32[]{:S(2)}) %all-to-all-start.1) | async-done | bytes 524320 | tf_op jit(solution)/shard_map/all_to_all | solution.py:1181
  84.3 5.2 %all-to-all-start.2 = ((bf16[4,128,512]{2,1,0:T(8,128)(2,1)}), bf16[4,128,512]{2,1,0:T(8,128)(2,1)S(1)}, u32[]{:S(2)}, u32[]{:S(2)}) async-start(bf16[4,128,512]{2,1,0:T(8,128)(2,1)} %reshape_reshape.3), calls=%async_computation.2 | async-start | bytes 1048576 | tf_op jit(solution)/shard_map/all_to_all | solution.py:1251
  89.5 26.9 %all-gather.6.cloned.1.call-done = bf16[1024,768]{1,0:T(8,128)(2,1)} async-done(((bf16[256,768]{1,0:T(8,128)(2,1)}), bf16[1024,768]{1,0:T(8,128)(2,1)}) %all-gather.6.cloned.1.call-update) | async-done | bytes 1572880 | tf_op jit(solution)/shard_map/all_gather | solution.py:1197
  117.2 3.6 collective-permute-done.2.refs_3_.refs_7_
  125.0 3.4 out.1
  131.0 10.4 %collective-permute-done.4.refs_2_.refs_1_ = bf16[128,2048]{1,0:T(8,128)(2,1)S(1)} collective-permute-done((bf16[128,2048]{1,0:T(8,128)(2,1)S(1)}, bf16[128,2048]{1,0:T(8,128)(2,1)S(1)}, u32[]{:S(2)}, u32[]{:S(2)}) %collective-permute-start.4) | collective-permute-done | bytes 524320 | tf_op jit(solution)/shard_map/ppermute | solution.py:860
  142.1 3.5 collective-permute-done.3.refs_1_.refs_0_
  146.9 14.0 %ffn.3 = (bf16[512,2048]{1,0:T(8,128)(2,1)S(1)}, bf16[512,2048]{1,0:T(8,128)(2,1)S(1)}, bf16[512,2048]{1,0:T(8,128)(2,1)S(1)}, bf16[512,2048]{1,0:T(8,128)(2,1)S...) custom-call(s32[3]{0:T(128)S(1)} %pad_add_fusion.1.where_ref, ...), custom_call_target="tpu_custom_call" | custom-call | flops 1 | bytes 1 | tf_op jit(solution)/shard_map/ffn/pallas_call | solution.py:666
  162.8 12.0 %ffn.4 = (bf16[512,2048]{1,0:T(8,128)(2,1)S(1)}, bf16[512,2048]{1,0:T(8,128)(2,1)S(1)}, bf16[512,2048]{1,0:T(8,128)(2,1)S(1)}, bf16[512,2048]{1,0:T(8,128)(2,1)S(1)}, bf16[128,2048]{1,0:T(8,128)(2,1)S(1)}) custom-call(s32[3]{0:T(128)S(1)} %pad_add_fusion.1.where_ref, ...), custom_call_target="tpu_custom_call", output_to_operand_aliasing={{0}: (6, {}), {1}: (7, {}), {2}: (8, {}), {3}: (9, {})} | custom-call | flops 1 | bytes 1 | tf_op jit(solution)/shard_map/ffn/pallas_call | solution.py:666
  178.1 12.0 %ffn.5 = (bf16[512,2048]{1,0:T(8,128)(2,1)S(1)}, bf16[512,2048]{1,0:T(8,128)(2,1)S(1)}, bf16[512,2048]{1,0:T(8,128)(2,1)S(1)}, bf16[512,2048]{1,0:T(8,128)(2,1)S(1)}, bf16[128,2048]{1,0:T(8,128)(2,1)S(1)}) custom-call(s32[3]{0:T(128)S(1)} %pad_add_fusion.1.where_ref, ...), custom_call_target="tpu_custom_call", output_to_operand_aliasing={{0}: (8, {}), {1}: (9, {}), {2}: (10, {}), {3}: (11, {})} | custom-call | flops 1 | bytes 1 | tf_op jit(solution)/shard_map/ffn/pallas_call | solution.py:666
  190.7 10.2 %collective-permute-done.10.refs_2_ = bf16[128,2048]{1,0:T(8,128)(2,1)S(1)} collective-permute-done((bf16[128,2048]{1,0:T(8,128)(2,1)S(1)}, bf16[128,2048]{1,0:T(8,128)(2,1)S(1)}, u32[]{:S(2)}, u32[]{:S(2)}) %collective-permute-start.10) | collective-permute-done | bytes 524320 | tf_op jit(solution)/shard_map/ppermute | solution.py:1190
  202.9 8.2 %ffn_outer.5 = (bf16[2,256,1024]{2,1,0:T(8,128)(2,1)}, bf16[2,256,1024]{2,1,0:T(8,128)(2,1)}, bf16[2,256,1024]{2,1,0:T(8,128)(2,1)}, bf16[2,256,1024]{2,1,0:T(8,128)(2,1)}) custom-call(s32[3]{0:T(128)S(1)} %pad_add_fusion.1.where_ref, bf16[512,2048]{1,0:T(8,128)(2,1)S(1)} %get-tuple-element.206.refs_0_, ...), custom_call_target="tpu_custom_call" | custom-call | flops 1 | bytes 1 | tf_op jit(solution)/shard_map/ffn_outer/pallas_call | solution.py:984
  214.1 8.2 %ffn_outer.4 = (bf16[2,256,1024]{2,1,0:T(8,128)(2,1)}, bf16[2,256,1024]{2,1,0:T(8,128)(2,1)}, bf16[2,256,1024]{2,1,0:T(8,128)(2,1)}, bf16[2,256,1024]{2,1,0:T(8,128)(2,1)}) custom-call(s32[3]{0:T(128)S(1)} %pad_add_fusion.1.where_ref, bf16[512,2048]{1,0:T(8,128)(2,1)S(1)} %get-tuple-element.206.refs_0_, ...), custom_call_target="tpu_custom_call" | custom-call | flops 1 | bytes 1 | tf_op jit(solution)/shard_map/ffn_outer/pallas_call | solution.py:984
  223.4 8.2 %ffn_outer.3 = (bf16[2,256,1024]{2,1,0:T(8,128)(2,1)}, bf16[2,256,1024]{2,1,0:T(8,128)(2,1)}, bf16[2,256,1024]{2,1,0:T(8,128)(2,1)}, bf16[2,256,1024]{2,1,0:T(8,128)(2,1)}) custom-call(s32[3]{0:T(128)S(1)} %pad_add_fusion.1.where_ref, bf16[512,2048]{1,0:T(8,128)(2,1)S(1)} %copy-done.8, bf16[512,2048]{1,0:T(8,128)(2,1)S(1)} %collective-permute-done.12.refs_1_, ...), custom_call_target="tpu_custom_call" | custom-call | flops 1 | bytes 1 | tf_op jit(solution)/shard_map/ffn_outer/pallas_call | solution.py:984
  231.6 5.3 %middle.1 = (bf16[128,2048]{1,0:T(8,128)(2,1)S(1)}, f32[128,2048]{1,0:T(8,128)S(1)}, bf16[4,128,512]{2,1,0:T(8,128)(2,1)S(1)}, f32[1,2048]{1,0:T(1,128)S(1)}) custom-call(s32[3]{0:T(128)S(1)} %pad_add_fusion.1.where_ref, f32[128,2048]{1,0:T(8,128)S(1)} %get-tuple-element.167.middle_ref, bf16[512,2048]{1,0:T(8,128)(2,1)S(1)} %bitcast.96, ...), custom_call_target="tpu_custom_call" | custom-call | flops 1 | bytes 1 | tf_op jit(solution)/shard_map/middle/pallas_call | solution.py:472
  239.6 4.1 all-to-all-start.3
  245.4 7.7 %branch.1 = bf16[512,2048]{1,0:T(8,128)(2,1)S(1)} custom-call(s32[3]{0:T(128)S(1)} %pad_add_fusion.1.where_ref, bf16[512,2048]{1,0:T(8,128)(2,1)S(1)} %copy-done.6, bf16[2048,2048]{1,0:T(8,128)(2,1)} %right_ref.3), custom_call_target="tpu_custom_call" | custom-call | flops 1 | bytes 1 | tf_op jit(solution)/shard_map/branch/pallas_call | solution.py:1105
  254.4 3.3 all-to-all-done.3
  264.2 4.2 all-to-all-start.4
  268.7 7.3 %all-to-all-done.4 = bf16[4,512,128]{2,1,0:T(8,128)(2,1)} async-done(((bf16[4,512,128]{2,1,0:T(8,128)(2,1)}), bf16[4,512,128]{2,1,0:T(8,128)(2,1)}, u32[]{:S(2)}, u32[]{:S(2)}) %all-to-all-start.4) | async-done | bytes 524320 | tf_op jit(solution)/shard_map/all_to_all | solution.py:1181
  277.2 17.3 %attend_back.1 = (f32[2048,128]{1,0:T(8,128)S(1)}, f32[2048,256]{1,0:T(8,128)S(1)}, bf16[2048,256]{1,0:T(8,128)(2,1)S(1)}) custom-call(s32[16]{0:T(128)S(1)} %pad_add_fusion.2.slot_places, s32[8]{0:T(128)S(1)} %get-tuple-element.316.key_low, bf16[2048,384]{1,0:T(8,128)(2,1)} %bitcast.12.own_ref, bf16[2048,256]{1,0:T(8,128)(2,1)S(1)} %copy-done.19, ...), custom_call_target="tpu_custom_call" | custom-call | flops 1 | bytes 1 | tf_op jit(solution)/shard_map/attend_back/pallas_call | solution.py:452
  309.3 4.4 all-to-all-start.5
  317.6 16.0 %all-to-all-done.5.back_ref = bf16[4,512,384]{2,1,0:T(8,128)(2,1)} async-done(((bf16[4,512,384]{2,1,0:T(8,128)(2,1)}), bf16[4,512,384]{2,1,0:T(8,128)(2,1)}, u32[]{:S(2)}, u32[]{:S(2)}) %all-to-all-start.5) | async-done | bytes 1572896 | tf_op jit(solution)/shard_map/all_to_all | solution.py:1181
  333.5 8.5 %back.1 = (bf16[512,1536]{1,0:T(8,128)(2,1)S(1)}, f32[1,2048]{1,0:T(1,128)S(1)}, bf16[128,2048]{1,0:T(8,128)(2,1)S(1)}, bf16[128,2048]{1,0:T(8,128)(2,1)S(1)}, b...) custom-call(s32[3]{0:T(128)S(1)} %pad_add_fusion.1.where_ref, bf16[4,512,384]{2,1,0:T(8,128)(2,1)} %all-to-all-done.5.back_ref, ...), custom_call_target="tpu_custom_call" | custom-call | flops 1 | bytes 1 | tf_op jit(solution)/shard_map/back/pallas_call | solution.py:757
  344.1 2.9 collective-permute-start.23
  349.3 8.7 %collective-permute-done.23.got_up_ref = bf16[128,2048]{1,0:T(8,128)(2,1)S(1)} collective-permute-done((bf16[128,2048]{1,0:T(8,128)(2,1)S(1)}, bf16[128,2048]{1,0:T(8,128)(2,1)S(1)}, u32[]{:S(2)}, u32[]{:S(2)}) %collective-permute-start.23) | collective-permute-done | bytes 524320 | tf_op jit(solution)/shard_map/ppermute | solution.py:860
  358.0 8.6 %collective-permute-done.25.refs_1_ = bf16[2,256,1024]{2,1,0:T(8,128)(2,1)} collective-permute-done((bf16[2,256,1024]{2,1,0:T(8,128)(2,1)S(1)}, bf16[2,256,1024]{2,1,0:T(8,128)(2,1)}, u32[]{:S(2)}, u32[]{:S(2)}) %collective-permute-start.25) | collective-permute-done | bytes 1048608 | tf_op jit(solution)/shard_map/ppermute | solution.py:1010
  368.9 3.6 collective-permute-start.27
  374.0 7.5 %all_to_all.35 = f32[8,2,256]{2,1,0:T(2,128)S(1)} all-to-all(f32[8,2,256]{2,1,0:T(2,128)S(1)} %bitcast.114), channel_id=1, replica_groups=mesh['seq'=8,'tp'=4] {'seq'}, dimensions={0} | all-to-all | bytes 32768 | tf_op jit(solution)/shard_map/all_to_all | solution.py:1340
  389.7 7.0 %collective-permute-start.29 = (bf16[128,2048]{1,0:T(8,128)(2,1)S(1)}, bf16[128,2048]{1,0:T(8,128)(2,1)S(1)}, u32[]{:S(2)}, u32[]{:S(2)}) collective-permute-start(bf16[128,2048]{1,0:T(8,128)(2,1)S(1)} %get-tuple-element.247), channel_id=1, source_target_pairs={{0,1},{1,2},{2,3},{4,5},{5,6},{6,7},{8,9},{9,10},{10,11},{12,13},{... | collective-permute-start | bytes 1572872 | tf_op jit(solution)/shard_map/ppermute | solution.py:860
  398.2 9.1 %attn_outer.1 = (bf16[2,256,1024]{2,1,0:T(8,128)(2,1)}, bf16[2,256,1024]{2,1,0:T(8,128)(2,1)}, bf16[2,256,1024]{2,1,0:T(8,128)(2,1)}, bf16[2,256,1024]{2,1,0:T(8,128)(2,1)}) custom-call(s32[3]{0:T(128)S(1)} %pad_add_fusion.1.where_ref, bf16[512,2048]{1,0:T(8,128)(2,1)S(1)} %copy-done.29, bf16[512,2048]{1,0:T(8,128)(2,1)S(1)} %collective-permute-done.33.refs_1_, ...), custom_call_target="tpu_custom_call" | custom-call | flops 1 | bytes 1 | tf_op jit(solution)/shard_map/attn_outer/pallas_call | solution.py:984
  407.5 4.3 collective-permute-done.30.above_ref
  419.2 21.3 %collective-permute-done.38.refs_1_ = bf16[2,256,1024]{2,1,0:T(8,128)(2,1)S(1)} collective-permute-done((bf16[2,256,1024]{2,1,0:T(8,128)(2,1)S(1)}, bf16[2,256,1024]{2,1,0:T(8,128)(2,1)S(1)}, u32[]{:S(2)}, u32[]{:S(2)}) %collective-permute-start.38) | collective-permute-done | bytes 1048608 | tf_op jit(solution)/shard_map/ppermute | solution.py:1010
  452.6 6.1 %collective-permute-done.45.refs_5_ = bf16[256,1024]{1,0:T(8,128)(2,1)S(1)} collective-permute-done((bf16[256,1024]{1,0:T(8,128)(2,1)S(1)}, bf16[256,1024]{1,0:T(8,128)(2,1)S(1)}, u32[]{:S(2)}, u32[]{:S(2)}) %collective-permute-start.45) | collective-permute-done | bytes 524320 | tf_op jit(solution)/shard_map/ppermute | solution.py:1010
  459.5 3.7 collective-permute-done.44.refs_2_
  463.2 3.1 collective-permute-done.43.refs_5_
  466.2 4.3 collective-permute-done.42.refs_2_
  476.1 3.5 widen_down.1
  479.6 3.3 widen_up.1
  483.0 3.3 widen_gate.1
  488.5 7.8 %collective-permute-done.47.refs_2_ = bf16[272,2048]{1,0:T(8,128)(2,1)S(1)} collective-permute-done((bf16[272,2048]{1,0:T(8,128)(2,1)S(1)}, bf16[272,2048]{1,0:T(8,128)(2,1)S(1)}, u32[]{:S(2)}, u32[]{:S(2)}) %collective-permute-start.47) | collective-permute-done | bytes 1114144 | tf_op jit(solution)/shard_map/ppermute | solution.py:861
  496.3 3.8 join.1
  (314 shorter events, 129.1 us)
Async XLA Ops:
  7.2 64.1 %all-gather.4.cloned.1.call-start = ((), (), s32[]{:S(2)}) async-start(), calls=%async_computation.8 | async-start | bytes 3276800 | tf_op jit(solution)/shard_map/all_gather | solution.py:1197
  22.0 30.3 %all-to-all-start = ((bf16[4,512,384]{2,1,0:T(8,128)(2,1)}), bf16[4,512,384]{2,1,0:T(8,128)(2,1)}, u32[]{:S(2)}, u32[]{:S(2)}) async-start(bf16[4,512,384]{2,1,0:T(8,128)(2,1)} %copy-done.39), calls=%async_computation | async-start | bytes 3145728 | tf_op jit(solution)/shard_map/all_to_all | solution.py:1181
  27.3 89.1 %all-gather.6.cloned.1.call-start = ((), (), s32[]{:S(2)}) async-start(), calls=%async_computation.9 | async-start | bytes 1966080 | tf_op jit(solution)/shard_map/all_gather | solution.py:1197
  76.2 41.0 %collective-permute-start.1 = (bf16[4,256,1280]{2,1,0:T(8,128)(2,1)}, bf16[4,256,1280]{2,1,0:T(8,128)(2,1)}, u32[]{:S(2)}, u32[]{:S(2)}) collective-permute-start(bf16[4,256,1280]{2,1,0:T(8,128)(2,1)} %bitcast.93), channel_id=1, source_target_pairs={{0,4},{4,0},{8,12},{12,8},{16,20},{20,16},{24,28},{28,24},{1,5},{5... | collective-permute-start | bytes 7864328 | tf_op jit(solution)/shard_map/ppermute | solution.py:1178
  84.3 32.1 %all-to-all-start.2 = ((bf16[4,128,512]{2,1,0:T(8,128)(2,1)}), bf16[4,128,512]{2,1,0:T(8,128)(2,1)S(1)}, u32[]{:S(2)}, u32[]{:S(2)}) async-start(bf16[4,128,512]{2,1,0:T(8,128)(2,1)} %reshape_reshape.3), calls=%async_computation.2 | async-start | bytes 1048576 | tf_op jit(solution)/shard_map/all_to_all | solution.py:1251
  128.4 13.0 %collective-permute-start.4 = (bf16[128,2048]{1,0:T(8,128)(2,1)S(1)}, bf16[128,2048]{1,0:T(8,128)(2,1)S(1)}, u32[]{:S(2)}, u32[]{:S(2)}) collective-permute-start(bf16[128,2048]{1,0:T(8,128)(2,1)S(1)} %get-tuple-element.168.refs_0_), channel_id=1, source_target_pairs={{0,1},{1,2},{2,3},{4,5},{5,6},{6,7},{8,9},{9,10},{10,11},{12,13},{... | collective-permute-start | bytes 1572872 | tf_op jit(solution)/shard_map/ppermute | solution.py:860
  129.7 15.9 %collective-permute-start.3 = (bf16[128,2048]{1,0:T(8,128)(2,1)S(1)}, bf16[128,2048]{1,0:T(8,128)(2,1)S(1)}, u32[]{:S(2)}, u32[]{:S(2)}) collective-permute-start(bf16[128,2048]{1,0:T(8,128)(2,1)S(1)} %get-tuple-element.168.refs_0_), channel_id=1, source_target_pairs={{1,0},{2,1},{3,2},{5,4},{6,5},{7,6},{9,8},{10,9},{11,10},{13,12},{... | collective-permute-start | bytes 1572872 | tf_op jit(solution)/shard_map/ppermute | solution.py:861
  141.4 19.4 %collective-permute-start.5 = (bf16[128,2048]{1,0:T(8,128)(2,1)S(1)}, bf16[128,2048]{1,0:T(8,128)(2,1)S(1)}, u32[]{:S(2)}, u32[]{:S(2)}) collective-permute-start(bf16[128,2048]{1,0:T(8,128)(2,1)S(1)} %collective-permute-done.4.refs_2_.refs_1_), channel_id=1, source_target_pairs={{1,2},{2,3},{5,6},{6,7},{9,10},{10,11},{13,14},{14,15},{17,18},{18... | collective-permute-start | bytes 1572872 | tf_op jit(solution)/shard_map/ppermute | solution.py:860
  145.6 15.3 %collective-permute-start.6 = (bf16[128,2048]{1,0:T(8,128)(2,1)S(1)}, bf16[128,2048]{1,0:T(8,128)(2,1)S(1)}, u32[]{:S(2)}, u32[]{:S(2)}) collective-permute-start(bf16[128,2048]{1,0:T(8,128)(2,1)S(1)} %collective-permute-done.3.refs_1_.refs_0_), channel_id=1, source_target_pairs={{1,0},{2,1},{5,4},{6,5},{9,8},{10,9},{13,12},{14,13},{17,16},{18,1... | collective-permute-start | bytes 1572872 | tf_op jit(solution)/shard_map/ppermute | solution.py:861
  160.8 14.0 %collective-permute-start.7 = (bf16[128,2048]{1,0:T(8,128)(2,1)S(1)}, bf16[128,2048]{1,0:T(8,128)(2,1)S(1)}, u32[]{:S(2)}, u32[]{:S(2)}) collective-permute-start(bf16[128,2048]{1,0:T(8,128)(2,1)S(1)} %collective-permute-done.5.refs_1_), channel_id=1, source_target_pairs={{2,3},{6,7},{10,11},{14,15},{18,19},{22,23},{26,27},{30,31}} | collective-permute-start | bytes 1572872 | tf_op jit(solution)/shard_map/ppermute | solution.py:860
  161.5 15.0 %collective-permute-start.8 = (bf16[128,2048]{1,0:T(8,128)(2,1)S(1)}, bf16[128,2048]{1,0:T(8,128)(2,1)S(1)}, u32[]{:S(2)}, u32[]{:S(2)}) collective-permute-start(bf16[128,2048]{1,0:T(8,128)(2,1)S(1)} %collective-permute-done.6.refs_0_), channel_id=1, source_target_pairs={{1,0},{5,4},{9,8},{13,12},{17,16},{21,20},{25,24},{29,28}} | collective-permute-start | bytes 1572872 | tf_op jit(solution)/shard_map/ppermute | solution.py:861
  176.6 24.3 %collective-permute-start.10 = (bf16[128,2048]{1,0:T(8,128)(2,1)S(1)}, bf16[128,2048]{1,0:T(8,128)(2,1)S(1)}, u32[]{:S(2)}, u32[]{:S(2)}) collective-permute-start(bf16[128,2048]{1,0:T(8,128)(2,1)S(1)} %get-tuple-element.195), channel_id=1, source_target_pairs={{0,2},{1,3},{2,0},{3,1},{4,6},{5,7},{6,4},{7,5},{8,10},{9,11},{10,... | collective-permute-start | bytes 1572872 | tf_op jit(solution)/shard_map/ppermute | solution.py:1190
  177.8 23.1 %collective-permute-start.9 = (bf16[128,2048]{1,0:T(8,128)(2,1)S(1)}, bf16[128,2048]{1,0:T(8,128)(2,1)S(1)}, u32[]{:S(2)}, u32[]{:S(2)}) collective-permute-start(bf16[128,2048]{1,0:T(8,128)(2,1)S(1)} %get-tuple-element.194), channel_id=1, source_target_pairs={{0,1},{1,0},{2,3},{3,2},{4,5},{5,4},{6,7},{7,6},{8,9},{9,8},{10,11... | collective-permute-start | bytes 1572872 | tf_op jit(solution)/shard_map/ppermute | solution.py:1190
  190.2 12.7 %collective-permute-start.18 = (bf16[512,2048]{1,0:T(8,128)(2,1)S(1)}, bf16[512,2048]{1,0:T(8,128)(2,1)S(1)}, u32[]{:S(2)}, u32[]{:S(2)}) collective-permute-start(bf16[512,2048]{1,0:T(8,128)(2,1)S(1)} %get-tuple-element.210.refs_2_), channel_id=1, source_target_pairs={{0,4},{4,0},{8,12},{12,8},{16,20},{20,16},{24,28},{28,24},{1,5},{5... | collective-permute-start | bytes 6291464 | tf_op jit(solution)/shard_map/ppermute | solution.py:1178
  200.9 21.3 %collective-permute-start.12 = (bf16[512,2048]{1,0:T(8,128)(2,1)S(1)}, bf16[512,2048]{1,0:T(8,128)(2,1)S(1)}, u32[]{:S(2)}, u32[]{:S(2)}) collective-permute-start(bf16[512,2048]{1,0:T(8,128)(2,1)S(1)} %copy-done.8), channel_id=1, source_target_pairs={{0,4},{4,0},{8,12},{12,8},{16,20},{20,16},{24,28},{28,24},{1,5},{5... | collective-permute-start | bytes 6291464 | tf_op jit(solution)/shard_map/ppermute | solution.py:1178
  201.4 21.4 %collective-permute-start.13 = (bf16[512,2048]{1,0:T(8,128)(2,1)S(1)}, bf16[512,2048]{1,0:T(8,128)(2,1)S(1)}, u32[]{:S(2)}, u32[]{:S(2)}) collective-permute-start(bf16[512,2048]{1,0:T(8,128)(2,1)S(1)} %get-tuple-element.215.refs_2_.left_ref), channel_id=1, source_target_pairs={{0,4},{4,0},{8,12},{12,8},{16,20},{20,16},{24,28},{28,24},{1,5},{5... | collective-permute-start | bytes 6291464 | tf_op jit(solution)/shard_map/ppermute | solution.py:1178
  201.5 30.1 %collective-permute-start.11 = (bf16[128,2048]{1,0:T(8,128)(2,1)S(1)}, bf16[128,2048]{1,0:T(8,128)(2,1)S(1)}, u32[]{:S(2)}, u32[]{:S(2)}) collective-permute-start(bf16[128,2048]{1,0:T(8,128)(2,1)S(1)} %get-tuple-element.198), channel_id=1, source_target_pairs={{0,3},{1,2},{2,1},{3,0},{4,7},{5,6},{6,5},{7,4},{8,11},{9,10},{10,... | collective-permute-start | bytes 1572872 | tf_op jit(solution)/shard_map/ppermute | solution.py:1190
  211.1 46.6 %collective-permute-start.19 = (bf16[2,256,1024]{2,1,0:T(8,128)(2,1)}, bf16[2,256,1024]{2,1,0:T(8,128)(2,1)}, u32[]{:S(2)}, u32[]{:S(2)}) collective-permute-start(bf16[2,256,1024]{2,1,0:T(8,128)(2,1)} %get-tuple-element.211), channel_id=1, source_target_pairs={{0,8},{4,12},{8,0},{12,4},{16,24},{20,28},{24,16},{28,20},{1,9},{5... | collective-permute-start | bytes 3145736 | tf_op jit(solution)/shard_map/ppermute | solution.py:1010
  212.6 45.1 %collective-permute-start.20 = (bf16[2,256,1024]{2,1,0:T(8,128)(2,1)}, bf16[2,256,1024]{2,1,0:T(8,128)(2,1)}, u32[]{:S(2)}, u32[]{:S(2)}) collective-permute-start(bf16[2,256,1024]{2,1,0:T(8,128)(2,1)} %get-tuple-element.212), channel_id=1, source_target_pairs={{0,16},{4,20},{8,24},{12,28},{16,0},{20,4},{24,8},{28,12},{1,17},{... | collective-permute-start | bytes 3145736 | tf_op jit(solution)/shard_map/ppermute | solution.py:1010
  222.2 36.9 %collective-permute-start.16 = (bf16[2,256,1024]{2,1,0:T(8,128)(2,1)}, bf16[2,256,1024]{2,1,0:T(8,128)(2,1)}, u32[]{:S(2)}, u32[]{:S(2)}) collective-permute-start(bf16[2,256,1024]{2,1,0:T(8,128)(2,1)} %get-tuple-element.208), channel_id=1, source_target_pairs={{0,8},{4,12},{8,0},{12,4},{16,24},{20,28},{24,16},{28,20},{1,9},{5... | collective-permute-start | bytes 3145736 | tf_op jit(solution)/shard_map/ppermute | solution.py:1010
  222.8 37.5 %collective-permute-start.17 = (bf16[2,256,1024]{2,1,0:T(8,128)(2,1)}, bf16[2,256,1024]{2,1,0:T(8,128)(2,1)}, u32[]{:S(2)}, u32[]{:S(2)}) collective-permute-start(bf16[2,256,1024]{2,1,0:T(8,128)(2,1)} %get-tuple-element.209), channel_id=1, source_target_pairs={{0,16},{4,20},{8,24},{12,28},{16,0},{20,4},{24,8},{28,12},{1,17},{... | collective-permute-start | bytes 3145736 | tf_op jit(solution)/shard_map/ppermute | solution.py:1010
  239.6 18.2 %all-to-all-start.3 = ((bf16[4,128,512]{2,1,0:T(8,128)(2,1)}), bf16[4,128,512]{2,1,0:T(8,128)(2,1)}, u32[]{:S(2)}, u32[]{:S(2)}) async-start(bf16[4,128,512]{2,1,0:T(8,128)(2,1)} %copy-done.52), calls=%async_computation.3 | async-start | bytes 1048576 | tf_op jit(solution)/shard_map/all_to_all | solution.py:1312
  243.7 89.8 %reduce-scatter.2.cloned.1.call-start = ((), (), s32[]{:S(2)}) async-start(), calls=%async_computation.10 | async-start | bytes 2621440 | tf_op jit(solution)/shard_map/reduce_scatter | solution.py:1316
  268.4 113.1 %all-gather.8.cloned.1.call-start = ((), (), s32[]{:S(2)}) async-start(), calls=%async_computation.11 | async-start | bytes 2621440 | tf_op jit(solution)/shard_map/all_gather | solution.py:1323
  309.3 24.3 %all-to-all-start.5 = ((bf16[4,512,384]{2,1,0:T(8,128)(2,1)}), bf16[4,512,384]{2,1,0:T(8,128)(2,1)}, u32[]{:S(2)}, u32[]{:S(2)}) async-start(bf16[4,512,384]{2,1,0:T(8,128)(2,1)} %bitcast.100), calls=%async_computation.5 | async-start | bytes 3145728 | tf_op jit(solution)/shard_map/all_to_all | solution.py:1181
  342.1 24.5 %collective-permute-start.25 = (bf16[2,256,1024]{2,1,0:T(8,128)(2,1)S(1)}, bf16[2,256,1024]{2,1,0:T(8,128)(2,1)}, u32[]{:S(2)}, u32[]{:S(2)}) collective-permute-start(bf16[2,256,1024]{2,1,0:T(8,128)(2,1)S(1)} %copy-done.63), channel_id=1, source_target_pairs={{0,8},{4,12},{8,0},{12,4},{16,24},{20,28},{24,16},{28,20},{1,9},{5... | collective-permute-start | bytes 3145736 | tf_op jit(solution)/shard_map/ppermute | solution.py:1010
  343.6 24.2 %collective-permute-start.26 = (bf16[2,256,1024]{2,1,0:T(8,128)(2,1)S(1)}, bf16[2,256,1024]{2,1,0:T(8,128)(2,1)}, u32[]{:S(2)}, u32[]{:S(2)}) collective-permute-start(bf16[2,256,1024]{2,1,0:T(8,128)(2,1)S(1)} %copy-done.62), channel_id=1, source_target_pairs={{0,16},{4,20},{8,24},{12,28},{16,0},{20,4},{24,8},{28,12},{1,17},{... | collective-permute-start | bytes 3145736 | tf_op jit(solution)/shard_map/ppermute | solution.py:1010
  344.1 13.9 %collective-permute-start.23 = (bf16[128,2048]{1,0:T(8,128)(2,1)S(1)}, bf16[128,2048]{1,0:T(8,128)(2,1)S(1)}, u32[]{:S(2)}, u32[]{:S(2)}) collective-permute-start(bf16[128,2048]{1,0:T(8,128)(2,1)S(1)} %get-tuple-element.228.down_ref), channel_id=1, source_target_pairs={{0,1},{4,5},{8,9},{12,13},{16,17},{20,21},{24,25},{28,29}} | collective-permute-start | bytes 1572872 | tf_op jit(solution)/shard_map/ppermute | solution.py:860
  368.9 12.7 %collective-permute-start.27 = (bf16[128,2048]{1,0:T(8,128)(2,1)}, bf16[128,2048]{1,0:T(8,128)(2,1)}, u32[]{:S(2)}, u32[]{:S(2)}) collective-permute-start(bf16[128,2048]{1,0:T(8,128)(2,1)} %get-tuple-element.237), channel_id=1, source_target_pairs={{0,1},{1,2},{4,5},{5,6},{8,9},{9,10},{12,13},{13,14},{16,17},{17,1... | collective-permute-start | bytes 1572872 | tf_op jit(solution)/shard_map/ppermute | solution.py:860
  374.0 15.7 %collective-permute-start.34 = (bf16[512,2048]{1,0:T(8,128)(2,1)}, bf16[512,2048]{1,0:T(8,128)(2,1)}, u32[]{:S(2)}, u32[]{:S(2)}) collective-permute-start(bf16[512,2048]{1,0:T(8,128)(2,1)} %get-tuple-element.257.refs_4_), channel_id=1, source_target_pairs={{0,4},{4,0},{8,12},{12,8},{16,20},{20,16},{24,28},{28,24},{1,5},{5... | collective-permute-start | bytes 6291464 | tf_op jit(solution)/shard_map/ppermute | solution.py:1178
  381.6 16.6 %collective-permute-start.33 = (bf16[512,2048]{1,0:T(8,128)(2,1)}, bf16[512,2048]{1,0:T(8,128)(2,1)S(1)}, u32[]{:S(2)}, u32[]{:S(2)}) collective-permute-start(bf16[512,2048]{1,0:T(8,128)(2,1)} %all-gather.8.cloned.1.call-done.refs_0_), channel_id=1, source_target_pairs={{0,4},{4,0},{8,12},{12,8},{16,20},{20,16},{24,28},{28,24},{1,5},{5... | collective-permute-start | bytes 6291464 | tf_op jit(solution)/shard_map/ppermute | solution.py:1178
  381.7 15.1 %collective-permute-start.35 = (bf16[512,1536]{1,0:T(8,128)(2,1)}, bf16[512,1536]{1,0:T(8,128)(2,1)S(1)}, u32[]{:S(2)}, u32[]{:S(2)}) collective-permute-start(bf16[512,1536]{1,0:T(8,128)(2,1)} %copy-done.37), channel_id=1, source_target_pairs={{0,4},{4,0},{8,12},{12,8},{16,20},{20,16},{24,28},{28,24},{1,5},{5... | collective-permute-start | bytes 4718600 | tf_op jit(solution)/shard_map/ppermute | solution.py:1178
  383.7 23.7 %collective-permute-start.32 = (bf16[256,1024]{1,0:T(8,128)(2,1)S(1)}, bf16[256,1024]{1,0:T(8,128)(2,1)S(1)}, u32[]{:S(2)}, u32[]{:S(2)}) collective-permute-start(bf16[256,1024]{1,0:T(8,128)(2,1)S(1)} %fusion.1), channel_id=1, source_target_pairs={{0,8},{4,12},{8,0},{12,4},{16,24},{20,28},{24,16},{28,20},{1,9},{5... | collective-permute-start | bytes 1572872 | tf_op jit(solution)/shard_map/ppermute | solution.py:1010
  386.0 21.4 %collective-permute-start.31 = (bf16[256,1024]{1,0:T(8,128)(2,1)S(1)}, bf16[256,1024]{1,0:T(8,128)(2,1)S(1)}, u32[]{:S(2)}, u32[]{:S(2)}) collective-permute-start(bf16[256,1024]{1,0:T(8,128)(2,1)S(1)} %fusion), channel_id=1, source_target_pairs={{0,16},{4,20},{8,24},{12,28},{16,0},{20,4},{24,8},{28,12},{1,17},{... | collective-permute-start | bytes 1572872 | tf_op jit(solution)/shard_map/ppermute | solution.py:1010
  389.7 17.7 %collective-permute-start.29 = (bf16[128,2048]{1,0:T(8,128)(2,1)S(1)}, bf16[128,2048]{1,0:T(8,128)(2,1)S(1)}, u32[]{:S(2)}, u32[]{:S(2)}) collective-permute-start(bf16[128,2048]{1,0:T(8,128)(2,1)S(1)} %get-tuple-element.247), channel_id=1, source_target_pairs={{0,1},{1,2},{2,3},{4,5},{5,6},{6,7},{8,9},{9,10},{10,11},{12,13},{... | collective-permute-start | bytes 1572872 | tf_op jit(solution)/shard_map/ppermute | solution.py:860
  396.8 15.0 %collective-permute-start.30 = (bf16[128,2048]{1,0:T(8,128)(2,1)S(1)}, bf16[128,2048]{1,0:T(8,128)(2,1)S(1)}, u32[]{:S(2)}, u32[]{:S(2)}) collective-permute-start(bf16[128,2048]{1,0:T(8,128)(2,1)S(1)} %get-tuple-element.248), channel_id=1, source_target_pairs={{1,0},{2,1},{3,2},{5,4},{6,5},{7,6},{9,8},{10,9},{11,10},{13,12},{... | collective-permute-start | bytes 1572872 | tf_op jit(solution)/shard_map/ppermute | solution.py:861
  413.5 27.8 %collective-permute-start.36 = (bf16[272,2048]{1,0:T(8,128)(2,1)S(1)}, bf16[272,2048]{1,0:T(8,128)(2,1)S(1)}, u32[]{:S(2)}, u32[]{:S(2)}) collective-permute-start(bf16[272,2048]{1,0:T(8,128)(2,1)S(1)} %tokens.1.own_ref), channel_id=1, source_target_pairs={{0,1},{1,2},{2,3},{4,5},{5,6},{6,7},{8,9},{9,10},{10,11},{12,13},{... | collective-permute-start | bytes 3342344 | tf_op jit(solution)/shard_map/ppermute | solution.py:860
  415.8 26.6 %collective-permute-start.37 = (bf16[272,2048]{1,0:T(8,128)(2,1)S(1)}, bf16[272,2048]{1,0:T(8,128)(2,1)S(1)}, u32[]{:S(2)}, u32[]{:S(2)}) collective-permute-start(bf16[272,2048]{1,0:T(8,128)(2,1)S(1)} %tokens.1.own_ref), channel_id=1, source_target_pairs={{1,0},{2,1},{3,2},{5,4},{6,5},{7,6},{9,8},{10,9},{11,10},{13,12},{... | collective-permute-start | bytes 3342344 | tf_op jit(solution)/shard_map/ppermute | solution.py:861
  417.1 23.4 %collective-permute-start.38 = (bf16[2,256,1024]{2,1,0:T(8,128)(2,1)S(1)}, bf16[2,256,1024]{2,1,0:T(8,128)(2,1)S(1)}, u32[]{:S(2)}, u32[]{:S(2)}) collective-permute-start(bf16[2,256,1024]{2,1,0:T(8,128)(2,1)S(1)} %copy-done.65), channel_id=1, source_target_pairs={{0,8},{4,12},{8,0},{12,4},{16,24},{20,28},{24,16},{28,20},{1,9},{5... | collective-permute-start | bytes 3145736 | tf_op jit(solution)/shard_map/ppermute | solution.py:1010
  418.1 23.1 %collective-permute-start.39 = (bf16[2,256,1024]{2,1,0:T(8,128)(2,1)S(1)}, bf16[2,256,1024]{2,1,0:T(8,128)(2,1)S(1)}, u32[]{:S(2)}, u32[]{:S(2)}) collective-permute-start(bf16[2,256,1024]{2,1,0:T(8,128)(2,1)S(1)} %copy-done.64), channel_id=1, source_target_pairs={{0,16},{4,20},{8,24},{12,28},{16,0},{20,4},{24,8},{28,12},{1,17},{... | collective-permute-start | bytes 3145736 | tf_op jit(solution)/shard_map/ppermute | solution.py:1010
  443.8 14.9 %collective-permute-start.45 = (bf16[256,1024]{1,0:T(8,128)(2,1)S(1)}, bf16[256,1024]{1,0:T(8,128)(2,1)S(1)}, u32[]{:S(2)}, u32[]{:S(2)}) collective-permute-start(bf16[256,1024]{1,0:T(8,128)(2,1)S(1)} %fusion.5), channel_id=1, source_target_pairs={{0,8},{4,12},{8,0},{12,4},{16,24},{20,28},{24,16},{28,20},{1,9},{5... | collective-permute-start | bytes 1572872 | tf_op jit(solution)/shard_map/ppermute | solution.py:1010
  444.9 25.6 %collective-permute-start.40 = (bf16[272,2048]{1,0:T(8,128)(2,1)S(1)}, bf16[272,2048]{1,0:T(8,128)(2,1)S(1)}, u32[]{:S(2)}, u32[]{:S(2)}) collective-permute-start(bf16[272,2048]{1,0:T(8,128)(2,1)S(1)} %collective-permute-done.36.refs_3_), channel_id=1, source_target_pairs={{1,2},{2,3},{5,6},{6,7},{9,10},{10,11},{13,14},{14,15},{17,18},{18... | collective-permute-start | bytes 3342344 | tf_op jit(solution)/shard_map/ppermute | solution.py:860
  445.6 25.8 %collective-permute-start.41 = (bf16[272,2048]{1,0:T(8,128)(2,1)S(1)}, bf16[272,2048]{1,0:T(8,128)(2,1)S(1)}, u32[]{:S(2)}, u32[]{:S(2)}) collective-permute-start(bf16[272,2048]{1,0:T(8,128)(2,1)S(1)} %collective-permute-done.37.refs_0_), channel_id=1, source_target_pairs={{1,0},{2,1},{5,4},{6,5},{9,8},{10,9},{13,12},{14,13},{17,16},{18,1... | collective-permute-start | bytes 3342344 | tf_op jit(solution)/shard_map/ppermute | solution.py:861
  448.2 14.9 %collective-permute-start.44 = (bf16[256,1024]{1,0:T(8,128)(2,1)S(1)}, bf16[256,1024]{1,0:T(8,128)(2,1)S(1)}, u32[]{:S(2)}, u32[]{:S(2)}) collective-permute-start(bf16[256,1024]{1,0:T(8,128)(2,1)S(1)} %fusion.4), channel_id=1, source_target_pairs={{0,16},{4,20},{8,24},{12,28},{16,0},{20,4},{24,8},{28,12},{1,17},{... | collective-permute-start | bytes 1572872 | tf_op jit(solution)/shard_map/ppermute | solution.py:1010
  450.5 15.8 %collective-permute-start.43 = (bf16[256,1024]{1,0:T(8,128)(2,1)S(1)}, bf16[256,1024]{1,0:T(8,128)(2,1)S(1)}, u32[]{:S(2)}, u32[]{:S(2)}) collective-permute-start(bf16[256,1024]{1,0:T(8,128)(2,1)S(1)} %fusion.3), channel_id=1, source_target_pairs={{0,8},{4,12},{8,0},{12,4},{16,24},{20,28},{24,16},{28,20},{1,9},{5... | collective-permute-start | bytes 1572872 | tf_op jit(solution)/shard_map/ppermute | solution.py:1010
  471.3 17.2 %collective-permute-start.46 = (bf16[272,2048]{1,0:T(8,128)(2,1)S(1)}, bf16[272,2048]{1,0:T(8,128)(2,1)S(1)}, u32[]{:S(2)}, u32[]{:S(2)}) collective-permute-start(bf16[272,2048]{1,0:T(8,128)(2,1)S(1)} %collective-permute-done.40.refs_4_), channel_id=1, source_target_pairs={{2,3},{6,7},{10,11},{14,15},{18,19},{22,23},{26,27},{30,31}} | collective-permute-start | bytes 3342344 | tf_op jit(solution)/shard_map/ppermute | solution.py:860
  472.1 24.2 %collective-permute-start.47 = (bf16[272,2048]{1,0:T(8,128)(2,1)S(1)}, bf16[272,2048]{1,0:T(8,128)(2,1)S(1)}, u32[]{:S(2)}, u32[]{:S(2)}) collective-permute-start(bf16[272,2048]{1,0:T(8,128)(2,1)S(1)} %collective-permute-done.41.refs_1_), channel_id=1, source_target_pairs={{1,0},{5,4},{9,8},{13,12},{17,16},{21,20},{25,24},{29,28}} | collective-permute-start | bytes 3342344 | tf_op jit(solution)/shard_map/ppermute | solution.py:861
  473.8 12.4 %collective-permute-start.49 = (bf16[256,1024]{1,0:T(8,128)(2,1)S(1)}, bf16[256,1024]{1,0:T(8,128)(2,1)S(1)}, u32[]{:S(2)}, u32[]{:S(2)}) collective-permute-start(bf16[256,1024]{1,0:T(8,128)(2,1)S(1)} %fusion.7), channel_id=1, source_target_pairs={{0,8},{4,12},{8,0},{12,4},{16,24},{20,28},{24,16},{28,20},{1,9},{5... | collective-permute-start | bytes 1572872 | tf_op jit(solution)/shard_map/ppermute | solution.py:1010
  (78 other events, 703.5 us)
Sparse Core Ops, SparseCore 0:
  9.6 57.4 all-gather.3
  69.3 47.0 all-gather.5
  260.5 42.9 reduce-scatter.1
  305.0 45.2 all-gather.7

commit v5 on v4

--- a/solution.py
+++ b/solution.py
@@ -316,11 +316,11 @@
     return 1.0 / (1.0 + jnp.exp(math.log(length) - scores * (1.0 / math.sqrt(HEAD_WIDTH))))
 
 
-def in_position_order(slot_places, own_ref, other_ref, own_first, span, scratch_refs):
+def in_position_order(slot_places, own_ref, other_ref, first, span, scratch_refs):
     head = HEAD_WIDTH
     own_slots = own_ref.shape[0] // span
     for slot in range(2 * own_slots):
-        source, first = (own_ref, own_first) if slot < own_slots else (other_ref, 0)
+        source = own_ref if slot < own_slots else other_ref
         rows = slice((slot % own_slots) * span, (slot % own_slots + 1) * span)
         target = pl.ds(pl.multiple_of(slot_places[slot] * span, span), span)
         for index, scratch in enumerate(scratch_refs):
@@ -1119,19 +1119,32 @@
 
 def turn_kernel(query_ref, both_ref, other_ref, cosine_ref, sine_ref, out_ref):
     head = HEAD_WIDTH
+    both = both_ref[...] + other_ref[...].astype(jnp.float32)
+    cosine, sine = cosine_ref[...], sine_ref[...]
+    for place, values in ((0, query_ref[...]), (1, both[:, :head])):
+        values = values * cosine - pltpu.roll(values, head // 2, 1) * sine
+        out_ref[:, place * head : (place + 1) * head] = values.astype(jnp.bfloat16)
+    out_ref[:, 2 * head :] = both[:, head:].astype(jnp.bfloat16)
+
+
+def turn_call(query, both, other, cosine, sine):
+    rows, head = query.shape
     step = 256
-
-    def piece(index, carry):
-        rows = pl.ds(pl.multiple_of(index * step, step), step)
-        both = both_ref[rows, :] + other_ref[rows, :].astype(jnp.float32)
-        cosine, sine = cosine_ref[rows, :], sine_ref[rows, :]
-        for place, values in ((0, query_ref[rows, :]), (1, both[:, :head])):
-            values = values * cosine - pltpu.roll(values, head // 2, 1) * sine
-            out_ref[rows, place * head : (place + 1) * head] = values.astype(jnp.bfloat16)
-        out_ref[rows, 2 * head :] = both[:, head:].astype(jnp.bfloat16)
-        return carry
-
-    lax.fori_loop(0, query_ref.shape[0] // step, piece, 0)
+    query, both, other, cosine, sine = [
+        pltpu.with_memory_space_constraint(x, pltpu.HBM)
+        for x in (query, both, other, cosine, sine)
+    ]
+    block = lambda x: pl.BlockSpec((step, x.shape[1]), lambda i: (i, 0))
+    return pl.pallas_call(
+        turn_kernel,
+        out_shape=made((rows, 3 * head), jnp.bfloat16),
+        grid=(rows // step,),
+        in_specs=[block(x) for x in (query, both, other, cosine, sine)],
+        out_specs=pl.BlockSpec((step, 3 * head), lambda i: (i, 0)),
+        compiler_params=pltpu.CompilerParams(vmem_limit_bytes=12 << 20),
+        cost_estimate=SHORT,
+        name="turn",
+    )(query, both, other, cosine, sine)
 
 
 def local_heads_apart(
@@ -1242,12 +1255,13 @@
     upstream_pair = (upstream_rel, swap(upstream_rel))
     normed_attn_pair = (normed_attn, swap(normed_attn))
     mine, grad_act, cosine_q, sine_q = tie(mine, grad_act, cosine_q, sine_q)
-    other = swap(mine[:, head:])
+    other = swap(mine)
 
     attended = attend_call(slot_places, key_low, mine, other, start_q.reshape(-1, 1), span)
     attended, w_first = tie(attended, w_first)
     attended = to_heads(attended.reshape(chips, row_count, head))
-    attended = attended.transpose(1, 0, 2).reshape(row_count, own_width)
+    attended = attended.reshape(heads, row_count, head)
+    attended = jnp.concatenate([attended[h] for h in range(heads)], axis=-1)
     attended_part = lax.all_to_all(
         attended.reshape(tp_size, part, own_width), "tp", 0, 0, tiled=True
     )
@@ -1314,19 +1328,18 @@
     grad_attended, branch = up_sum.tie(*gate_sum.tie(grad_attended, branch))
     branch = after(branch, grad_attended)
     branch_part = lax.psum_scatter(branch, "tp", scatter_dimension=0, tiled=True)
-    grad_attended = grad_attended.reshape(row_count, heads, head).transpose(1, 0, 2)
+    grad_attended = grad_attended.reshape(row_count, own_width)
+    grad_attended = jnp.stack(
+        [grad_attended[:, h * head : (h + 1) * head] for h in range(heads)]
+    )
     grad_heads = to_heads(grad_attended).reshape(chips * row_count, head)
     grad_query, both, both_other = attend_back_call(
         slot_places, key_low, mine, other, start_q, grad_heads, span
     )
     other_term = swap(both_other)
     middle_all = lax.all_gather(after(middle_low, other_term), "tp", axis=0, tiled=True)
-    packed_back = call(
-        turn_kernel,
-        (made((chips * row_count, 3 * head), bf16),),
-        (grad_query, both, other_term, cosine_q, sine_q),
-        name="turn",
-    )[0].reshape(chips, row_count, 3 * head)
+    packed_back = turn_call(grad_query, both, other_term, cosine_q, sine_q)
+    packed_back = packed_back.reshape(chips, row_count, 3 * head)
     back_heads = to_heads(packed_back)
     attended_pair = (attended, swap(attended))
     back_heads = after(back_heads, attended_pair[1], branch_part)

time: 517 us -> 513 us (level)
  local copies, waits for them, and re-layouts: 53.8 us -> 37.2 us
  starting transfers between devices: 80.5 us -> 88 us
  waiting for transfers between devices: 168 us -> 175 us
    unnamed x141 -> x121, local copies, waits for them, and re-layouts: 34.7 us -> 24.6 us
    ppermute x13, starting transfers between devices: 1.9 us -> 11.3 us  [swap(): return lax.ppermute(values, 'seq', other_core)]
    all_gather x2, waiting for transfers between devices: 26.9 us -> 36.2 us  [gathered(): values = lax.all_gather(columns, 'tp', axis=0, tiled=True)]
    ppermute x16, waiting for transfers between devices: 51.6 us -> 45.6 us  [over(): lax.ppermute(values, 'seq', [(i, i ^ side) for i in range(self.size)])]
    pallas_call x1, Pallas kernels: 17.3 us -> 11.8 us  [attend_back_call(): pl.pallas_call(functools.partial(attend_back_kernel, span=span), out_shap...]
    pallas_call x0 -> x1, Pallas kernels: none -> 5.53 us  [turn_call(): pl.pallas_call(turn_kernel, out_shape=made((rows, 3 * head), jnp.bfloat16...]
    ppermute x9, waiting for transfers between devices: 19.2 us -> 24.6 us  [send(): self.upward = lax.ppermute(up, self.axis, up_pairs)]
    pallas_call x12 -> x11, Pallas kernels: 30.2 us -> 29.1 us  [call(): pl.pallas_call(kernel, out_shape=tuple(outs), in_specs=[SMALL] * scalars...]
  transfers between devices with their start and end apart: 60 -> 60, of which waited for: 28 -> 30; matrix products, arithmetic and copies ran while one was open for 7% -> 7% of each run, Pallas kernels for 30% -> 30%
where the time goes in v5:
time: 513 us; the launch traced here: 503 us
  waiting for transfers between devices  175 us (34%)
  Pallas kernels  158 us (31%)
  starting transfers between devices  88 us (17%)
  local copies, waits for them, and re-layouts  37.2 us (7%)
  other arithmetic  23 us (4%)
  between operations  15.1 us (3%)
  blocking collectives  7.46 us (1%)
    ppermute x16, waiting for transfers between devices, over(): lax.ppermute(values, 'seq', [(i, i ^ side) for i in range(self.size)])  45.6 us
    pallas_call x3, Pallas kernels, ffn_call(): pl.pallas_call(functools.partial(ffn_kernel, chunk=chunk, sources=len(sou...  38 us
    all_gather x2, waiting for transfers between devices, gathered(): values = lax.all_gather(columns, 'tp', axis=0, tiled=True)  36.2 us
    pallas_call x4, Pallas kernels, chip_outer_call(): pl.pallas_call(functools.partial(chip_outer_kernel, sides=len(pairs)), ou...  33.7 us
    pallas_call x11, Pallas kernels, call(): pl.pallas_call(kernel, out_shape=tuple(outs), in_specs=[SMALL] * scalars...  29.1 us
    all_to_all x4, waiting for transfers between devices, to_heads(): lax.all_to_all(values, 'seq', 0, 0, axis_index_groups=same_core, tiled=True)  28 us
    unnamed x121, local copies, waits for them, and re-layouts  24.6 us
    ppermute x9, waiting for transfers between devices, send(): self.upward = lax.ppermute(up, self.axis, up_pairs)  24.6 us
  transfers between devices with their start and end apart: 60, of which 30 were waited for; matrix products, arithmetic and copies ran while one was open for 7% of the time, Pallas kernels for 30%

profile of v5, /device:TPU:0, one launch (start us, length us, event | category | flops | bytes accessed | tf_op | source)
XLA Modules:
  0.0 503.4 jit_solution(13221824593868309157)
XLA Ops:
  13.3 7.4 %project.1 = (bf16[4,512,384]{2,1,0:T(8,128)(2,1)S(1)}, bf16[512,2048]{1,0:T(8,128)(2,1)}) custom-call(bf16[512,2048]{1,0:T(8,128)(2,1)S(1)} %bitcast.101, f32[1,2048]{1,0:T(1,128)S(1)} %bitcast.119, s32[512,1]{1,0:T(8,128)S(1)} %bitcast.114, f32[512,128]{1,0:T(8,128)S(1)} %get-tuple-element.344.cosine_ref, f32[512,128]{1,0:T(8,128)S(1)} %get-tuple-element.345.sine_ref, ...), custom_call_target="tpu_custom_call" | custom-call | flops 1 | bytes 1 | tf_op jit(solution)/shard_map/project/pallas_call | solution.py:482
  21.9 5.3 %all-to-all-start = ((bf16[4,512,384]{2,1,0:T(8,128)(2,1)}), bf16[4,512,384]{2,1,0:T(8,128)(2,1)}, u32[]{:S(2)}, u32[]{:S(2)}) async-start(bf16[4,512,384]{2,1,0:T(8,128)(2,1)} %copy-done.33), calls=%async_computation | async-start | bytes 3145728 | tf_op jit(solution)/shard_map/all_to_all | solution.py:1194
  33.5 7.9 %grad_act.1.refs_3_.refs_2_.refs_4_ = f32[512,2048]{1,0:T(8,128)S(1)} custom-call(s32[3]{0:T(128)S(1)} %pad_add_fusion.1.where_ref, bf16[512,2048]{1,0:T(8,128)(2,1)S(1)} %pad_maximum_fusion.left_ref.refs_0_, bf16[2048,2048]{1,0:T(8,128)(2,1)} %right_ref.3), custom_call_target="tpu_custom_call" | custom-call | flops 1 | bytes 1 | tf_op jit(solution)/shard_map/grad_act/pallas_call | solution.py:1105
  45.8 3.7 fusion.8
  55.3 8.0 %attend.1 = bf16[2048,128]{1,0:T(8,128)(2,1)S(1)} custom-call(s32[16]{0:T(128)S(1)} %pad_add_fusion.2.slot_places, s32[8]{0:T(128)S(1)} %get-tuple-element.316.key_low, bf16[2048,384]{1,0:T(8,128)(2,1)} %bitcast.12.own_ref, bf16[2048,384]{1,0:T(8,128)(2,1)} %collective-permute-done.other_ref, s32[2048,1]{1,0:T(8,128)S(1)} %bitcast.113), custom_call_target="tpu_custom_call" | custom-call | flops 1 | bytes 1 | tf_op jit(solution)/shard_map/attend/pallas_call | solution.py:438
  64.1 3.7 all-gather.4.cloned.1.call-done
  67.7 4.0 all-to-all-start.1
  74.6 4.6 all-to-all-done.1
  80.9 3.5 all-to-all-start.2
  84.4 32.5 %all-gather.6.cloned.1.call-done = bf16[1024,768]{1,0:T(8,128)(2,1)} async-done(((bf16[256,768]{1,0:T(8,128)(2,1)}), bf16[1024,768]{1,0:T(8,128)(2,1)}) %all-gather.6.cloned.1.call-update) | async-done | bytes 1572880 | tf_op jit(solution)/shard_map/all_gather | solution.py:1210
  117.8 3.6 collective-permute-done.2.refs_3_.refs_7_
  125.6 3.3 out.1
  131.6 10.4 %collective-permute-done.4.refs_2_.refs_1_ = bf16[128,2048]{1,0:T(8,128)(2,1)S(1)} collective-permute-done((bf16[128,2048]{1,0:T(8,128)(2,1)S(1)}, bf16[128,2048]{1,0:T(8,128)(2,1)S(1)}, u32[]{:S(2)}, u32[]{:S(2)}) %collective-permute-start.4) | collective-permute-done | bytes 524320 | tf_op jit(solution)/shard_map/ppermute | solution.py:860
  142.7 3.5 collective-permute-done.3.refs_1_.refs_0_
  147.4 14.0 %ffn.3 = (bf16[512,2048]{1,0:T(8,128)(2,1)S(1)}, bf16[512,2048]{1,0:T(8,128)(2,1)S(1)}, bf16[512,2048]{1,0:T(8,128)(2,1)S(1)}, bf16[512,2048]{1,0:T(8,128)(2,1)S...) custom-call(s32[3]{0:T(128)S(1)} %pad_add_fusion.1.where_ref, ...), custom_call_target="tpu_custom_call" | custom-call | flops 1 | bytes 1 | tf_op jit(solution)/shard_map/ffn/pallas_call | solution.py:666
  163.4 12.0 %ffn.4 = (bf16[512,2048]{1,0:T(8,128)(2,1)S(1)}, bf16[512,2048]{1,0:T(8,128)(2,1)S(1)}, bf16[512,2048]{1,0:T(8,128)(2,1)S(1)}, bf16[512,2048]{1,0:T(8,128)(2,1)S(1)}, bf16[128,2048]{1,0:T(8,128)(2,1)S(1)}) custom-call(s32[3]{0:T(128)S(1)} %pad_add_fusion.1.where_ref, ...), custom_call_target="tpu_custom_call", output_to_operand_aliasing={{0}: (6, {}), {1}: (7, {}), {2}: (8, {}), {3}: (9, {})} | custom-call | flops 1 | bytes 1 | tf_op jit(solution)/shard_map/ffn/pallas_call | solution.py:666
  178.6 12.0 %ffn.5 = (bf16[512,2048]{1,0:T(8,128)(2,1)S(1)}, bf16[512,2048]{1,0:T(8,128)(2,1)S(1)}, bf16[512,2048]{1,0:T(8,128)(2,1)S(1)}, bf16[512,2048]{1,0:T(8,128)(2,1)S(1)}, bf16[128,2048]{1,0:T(8,128)(2,1)S(1)}) custom-call(s32[3]{0:T(128)S(1)} %pad_add_fusion.1.where_ref, ...), custom_call_target="tpu_custom_call", output_to_operand_aliasing={{0}: (8, {}), {1}: (9, {}), {2}: (10, {}), {3}: (11, {})} | custom-call | flops 1 | bytes 1 | tf_op jit(solution)/shard_map/ffn/pallas_call | solution.py:666
  191.3 10.2 %collective-permute-done.10.refs_2_ = bf16[128,2048]{1,0:T(8,128)(2,1)S(1)} collective-permute-done((bf16[128,2048]{1,0:T(8,128)(2,1)S(1)}, bf16[128,2048]{1,0:T(8,128)(2,1)S(1)}, u32[]{:S(2)}, u32[]{:S(2)}) %collective-permute-start.10) | collective-permute-done | bytes 524320 | tf_op jit(solution)/shard_map/ppermute | solution.py:1203
  203.5 8.1 %ffn_outer.5 = (bf16[2,256,1024]{2,1,0:T(8,128)(2,1)}, bf16[2,256,1024]{2,1,0:T(8,128)(2,1)}, bf16[2,256,1024]{2,1,0:T(8,128)(2,1)}, bf16[2,256,1024]{2,1,0:T(8,128)(2,1)}) custom-call(s32[3]{0:T(128)S(1)} %pad_add_fusion.1.where_ref, bf16[512,2048]{1,0:T(8,128)(2,1)S(1)} %get-tuple-element.206.refs_0_, ...), custom_call_target="tpu_custom_call" | custom-call | flops 1 | bytes 1 | tf_op jit(solution)/shard_map/ffn_outer/pallas_call | solution.py:984
  214.6 8.2 %ffn_outer.4 = (bf16[2,256,1024]{2,1,0:T(8,128)(2,1)}, bf16[2,256,1024]{2,1,0:T(8,128)(2,1)}, bf16[2,256,1024]{2,1,0:T(8,128)(2,1)}, bf16[2,256,1024]{2,1,0:T(8,128)(2,1)}) custom-call(s32[3]{0:T(128)S(1)} %pad_add_fusion.1.where_ref, bf16[512,2048]{1,0:T(8,128)(2,1)S(1)} %get-tuple-element.206.refs_0_, ...), custom_call_target="tpu_custom_call" | custom-call | flops 1 | bytes 1 | tf_op jit(solution)/shard_map/ffn_outer/pallas_call | solution.py:984
  224.0 8.2 %ffn_outer.3 = (bf16[2,256,1024]{2,1,0:T(8,128)(2,1)}, bf16[2,256,1024]{2,1,0:T(8,128)(2,1)}, bf16[2,256,1024]{2,1,0:T(8,128)(2,1)}, bf16[2,256,1024]{2,1,0:T(8,128)(2,1)}) custom-call(s32[3]{0:T(128)S(1)} %pad_add_fusion.1.where_ref, bf16[512,2048]{1,0:T(8,128)(2,1)S(1)} %copy-done.8, bf16[512,2048]{1,0:T(8,128)(2,1)S(1)} %collective-permute-done.12.refs_1_, ...), custom_call_target="tpu_custom_call" | custom-call | flops 1 | bytes 1 | tf_op jit(solution)/shard_map/ffn_outer/pallas_call | solution.py:984
  232.2 5.3 %middle.1 = (bf16[128,2048]{1,0:T(8,128)(2,1)S(1)}, f32[128,2048]{1,0:T(8,128)S(1)}, bf16[4,128,512]{2,1,0:T(8,128)(2,1)S(1)}, f32[1,2048]{1,0:T(1,128)S(1)}) custom-call(s32[3]{0:T(128)S(1)} %pad_add_fusion.1.where_ref, f32[128,2048]{1,0:T(8,128)S(1)} %get-tuple-element.167.middle_ref, bf16[512,2048]{1,0:T(8,128)(2,1)S(1)} %bitcast.108, ...), custom_call_target="tpu_custom_call" | custom-call | flops 1 | bytes 1 | tf_op jit(solution)/shard_map/middle/pallas_call | solution.py:472
  240.1 4.1 all-to-all-start.3
  245.9 7.7 %branch.1 = bf16[512,2048]{1,0:T(8,128)(2,1)S(1)} custom-call(s32[3]{0:T(128)S(1)} %pad_add_fusion.1.where_ref, bf16[512,2048]{1,0:T(8,128)(2,1)S(1)} %copy-done.6, bf16[2048,2048]{1,0:T(8,128)(2,1)} %right_ref.3), custom_call_target="tpu_custom_call" | custom-call | flops 1 | bytes 1 | tf_op jit(solution)/shard_map/branch/pallas_call | solution.py:1105
  262.9 4.1 all-to-all-start.4
  267.4 7.2 %all-to-all-done.4 = bf16[4,512,128]{2,1,0:T(8,128)(2,1)} async-done(((bf16[4,512,128]{2,1,0:T(8,128)(2,1)}), bf16[4,512,128]{2,1,0:T(8,128)(2,1)}, u32[]{:S(2)}, u32[]{:S(2)}) %all-to-all-start.4) | async-done | bytes 524320 | tf_op jit(solution)/shard_map/all_to_all | solution.py:1194
  274.6 11.8 %attend_back.1 = (f32[2048,128]{1,0:T(8,128)S(1)}, f32[2048,256]{1,0:T(8,128)S(1)}, bf16[2048,256]{1,0:T(8,128)(2,1)S(1)}) custom-call(s32[16]{0:T(128)S(1)} %pad_add_fusion.2.slot_places, s32[8]{0:T(128)S(1)} %get-tuple-element.316.key_low, bf16[2048,384]{1,0:T(8,128)(2,1)} %bitcast.12.own_ref, bf16[2048,384]{1,0:T(8,128)(2,1)} %collective-permute-done.other_ref, ...), custom_call_target="tpu_custom_call" | custom-call | flops 1 | bytes 1 | tf_op jit(solution)/shard_map/attend_back/pallas_call | solution.py:452
  288.6 6.4 %collective-permute-start.21 = (bf16[2048,256]{1,0:T(8,128)(2,1)S(1)}, bf16[2048,256]{1,0:T(8,128)(2,1)}, u32[]{:S(2)}, u32[]{:S(2)}) collective-permute-start(bf16[2048,256]{1,0:T(8,128)(2,1)S(1)} %get-tuple-element.221), channel_id=1, source_target_pairs={{0,4},{4,0},{8,12},{12,8},{16,20},{20,16},{24,28},{28,24},{1,5},{5... | collective-permute-start | bytes 3145736 | tf_op jit(solution)/shard_map/ppermute | solution.py:1191
  297.5 5.5 %turn.1 = bf16[2048,384]{1,0:T(8,128)(2,1)S(1)} custom-call(f32[2048,128]{1,0:T(8,128)} %copy-done.36, f32[2048,256]{1,0:T(8,128)} %copy-done.30, bf16[2048,256]{1,0:T(8,128)(2,1)} %collective-permute-done.21.other_ref, f32[2048,128]{1,0:T(8,128)} %get-tuple-element.222.cosine_ref, f32[2048,128]{1,0:T(8,128)} %get-tuple-element.223.sine_ref), custom_call_target="tpu_custom_call" | custom-call | flops 1 | bytes 1 | tf_op jit(solution)/shard_map/turn/pallas_call | solution.py:1138
  304.2 4.4 all-to-all-start.5
  312.5 16.1 %all-to-all-done.5.back_ref = bf16[4,512,384]{2,1,0:T(8,128)(2,1)} async-done(((bf16[4,512,384]{2,1,0:T(8,128)(2,1)}), bf16[4,512,384]{2,1,0:T(8,128)(2,1)}, u32[]{:S(2)}, u32[]{:S(2)}) %all-to-all-start.5) | async-done | bytes 1572896 | tf_op jit(solution)/shard_map/all_to_all | solution.py:1194
  328.7 8.5 %back.1 = (bf16[512,1536]{1,0:T(8,128)(2,1)S(1)}, f32[1,2048]{1,0:T(1,128)S(1)}, bf16[128,2048]{1,0:T(8,128)(2,1)S(1)}, bf16[128,2048]{1,0:T(8,128)(2,1)S(1)}, b...) custom-call(s32[3]{0:T(128)S(1)} %pad_add_fusion.1.where_ref, bf16[4,512,384]{2,1,0:T(8,128)(2,1)} %all-to-all-done.5.back_ref, ...), custom_call_target="tpu_custom_call" | custom-call | flops 1 | bytes 1 | tf_op jit(solution)/shard_map/back/pallas_call | solution.py:757
  344.5 14.0 %collective-permute-done.23.got_up_ref = bf16[128,2048]{1,0:T(8,128)(2,1)S(1)} collective-permute-done((bf16[128,2048]{1,0:T(8,128)(2,1)S(1)}, bf16[128,2048]{1,0:T(8,128)(2,1)S(1)}, u32[]{:S(2)}, u32[]{:S(2)}) %collective-permute-start.23) | collective-permute-done | bytes 524320 | tf_op jit(solution)/shard_map/ppermute | solution.py:860
  358.4 3.5 collective-permute-done.25.refs_1_
  364.2 3.8 collective-permute-start.27
  369.5 7.5 %all_to_all.35 = f32[8,2,256]{2,1,0:T(2,128)S(1)} all-to-all(f32[8,2,256]{2,1,0:T(2,128)S(1)} %bitcast.128), channel_id=1, replica_groups=mesh['seq'=8,'tp'=4] {'seq'}, dimensions={0} | all-to-all | bytes 32768 | tf_op jit(solution)/shard_map/all_to_all | solution.py:1353
  385.4 7.3 %collective-permute-start.29 = (bf16[128,2048]{1,0:T(8,128)(2,1)S(1)}, bf16[128,2048]{1,0:T(8,128)(2,1)S(1)}, u32[]{:S(2)}, u32[]{:S(2)}) collective-permute-start(bf16[128,2048]{1,0:T(8,128)(2,1)S(1)} %get-tuple-element.247), channel_id=1, source_target_pairs={{0,1},{1,2},{2,3},{4,5},{5,6},{6,7},{8,9},{9,10},{10,11},{12,13},{... | collective-permute-start | bytes 1572872 | tf_op jit(solution)/shard_map/ppermute | solution.py:860
  394.3 9.1 %attn_outer.1 = (bf16[2,256,1024]{2,1,0:T(8,128)(2,1)}, bf16[2,256,1024]{2,1,0:T(8,128)(2,1)}, bf16[2,256,1024]{2,1,0:T(8,128)(2,1)}, bf16[2,256,1024]{2,1,0:T(8,128)(2,1)}) custom-call(s32[3]{0:T(128)S(1)} %pad_add_fusion.1.where_ref, bf16[512,2048]{1,0:T(8,128)(2,1)S(1)} %copy-done.24, bf16[512,2048]{1,0:T(8,128)(2,1)S(1)} %collective-permute-done.33.refs_1_, ...), custom_call_target="tpu_custom_call" | custom-call | flops 1 | bytes 1 | tf_op jit(solution)/shard_map/attn_outer/pallas_call | solution.py:984
  403.5 4.3 collective-permute-done.30.above_ref
  415.2 21.3 %collective-permute-done.38.refs_1_ = bf16[2,256,1024]{2,1,0:T(8,128)(2,1)S(1)} collective-permute-done((bf16[2,256,1024]{2,1,0:T(8,128)(2,1)S(1)}, bf16[2,256,1024]{2,1,0:T(8,128)(2,1)S(1)}, u32[]{:S(2)}, u32[]{:S(2)}) %collective-permute-start.38) | collective-permute-done | bytes 1048608 | tf_op jit(solution)/shard_map/ppermute | solution.py:1010
  448.6 6.1 %collective-permute-done.45.refs_5_ = bf16[256,1024]{1,0:T(8,128)(2,1)S(1)} collective-permute-done((bf16[256,1024]{1,0:T(8,128)(2,1)S(1)}, bf16[256,1024]{1,0:T(8,128)(2,1)S(1)}, u32[]{:S(2)}, u32[]{:S(2)}) %collective-permute-start.45) | collective-permute-done | bytes 524320 | tf_op jit(solution)/shard_map/ppermute | solution.py:1010
  455.5 3.4 collective-permute-done.44.refs_2_
  458.9 3.4 collective-permute-done.43.refs_5_
  462.2 3.8 collective-permute-done.42.refs_2_
  472.1 3.5 widen_down.1
  475.7 3.3 widen_up.1
  484.5 7.8 %collective-permute-done.47.refs_2_ = bf16[272,2048]{1,0:T(8,128)(2,1)S(1)} collective-permute-done((bf16[272,2048]{1,0:T(8,128)(2,1)S(1)}, bf16[272,2048]{1,0:T(8,128)(2,1)S(1)}, u32[]{:S(2)}, u32[]{:S(2)}) %collective-permute-start.47) | collective-permute-done | bytes 1114144 | tf_op jit(solution)/shard_map/ppermute | solution.py:861
  492.3 3.8 join.1
  (293 shorter events, 127.1 us)
Async XLA Ops:
  7.2 60.5 %all-gather.4.cloned.1.call-start = ((), (), s32[]{:S(2)}) async-start(), calls=%async_computation.8 | async-start | bytes 3276800 | tf_op jit(solution)/shard_map/all_gather | solution.py:1210
  21.9 29.5 %all-to-all-start = ((bf16[4,512,384]{2,1,0:T(8,128)(2,1)}), bf16[4,512,384]{2,1,0:T(8,128)(2,1)}, u32[]{:S(2)}, u32[]{:S(2)}) async-start(bf16[4,512,384]{2,1,0:T(8,128)(2,1)} %copy-done.33), calls=%async_computation | async-start | bytes 3145728 | tf_op jit(solution)/shard_map/all_to_all | solution.py:1194
  27.2 89.7 %all-gather.6.cloned.1.call-start = ((), (), s32[]{:S(2)}) async-start(), calls=%async_computation.9 | async-start | bytes 1966080 | tf_op jit(solution)/shard_map/all_gather | solution.py:1210
  71.7 46.0 %collective-permute-start.1 = (bf16[4,256,1280]{2,1,0:T(8,128)(2,1)}, bf16[4,256,1280]{2,1,0:T(8,128)(2,1)}, u32[]{:S(2)}, u32[]{:S(2)}) collective-permute-start(bf16[4,256,1280]{2,1,0:T(8,128)(2,1)} %bitcast.105), channel_id=1, source_target_pairs={{0,4},{4,0},{8,12},{12,8},{16,20},{20,16},{24,28},{28,24},{1,5},{5... | collective-permute-start | bytes 7864328 | tf_op jit(solution)/shard_map/ppermute | solution.py:1191
  80.9 36.0 %all-to-all-start.2 = ((bf16[4,128,512]{2,1,0:T(8,128)(2,1)}), bf16[4,128,512]{2,1,0:T(8,128)(2,1)S(1)}, u32[]{:S(2)}, u32[]{:S(2)}) async-start(bf16[4,128,512]{2,1,0:T(8,128)(2,1)} %pad_maximum_fusion.3), calls=%async_computation.2 | async-start | bytes 1048576 | tf_op jit(solution)/shard_map/all_to_all | solution.py:1265
  128.9 13.0 %collective-permute-start.4 = (bf16[128,2048]{1,0:T(8,128)(2,1)S(1)}, bf16[128,2048]{1,0:T(8,128)(2,1)S(1)}, u32[]{:S(2)}, u32[]{:S(2)}) collective-permute-start(bf16[128,2048]{1,0:T(8,128)(2,1)S(1)} %get-tuple-element.168.refs_0_), channel_id=1, source_target_pairs={{0,1},{1,2},{2,3},{4,5},{5,6},{6,7},{8,9},{9,10},{10,11},{12,13},{... | collective-permute-start | bytes 1572872 | tf_op jit(solution)/shard_map/ppermute | solution.py:860
  130.3 15.9 %collective-permute-start.3 = (bf16[128,2048]{1,0:T(8,128)(2,1)S(1)}, bf16[128,2048]{1,0:T(8,128)(2,1)S(1)}, u32[]{:S(2)}, u32[]{:S(2)}) collective-permute-start(bf16[128,2048]{1,0:T(8,128)(2,1)S(1)} %get-tuple-element.168.refs_0_), channel_id=1, source_target_pairs={{1,0},{2,1},{3,2},{5,4},{6,5},{7,6},{9,8},{10,9},{11,10},{13,12},{... | collective-permute-start | bytes 1572872 | tf_op jit(solution)/shard_map/ppermute | solution.py:861
  142.0 19.4 %collective-permute-start.5 = (bf16[128,2048]{1,0:T(8,128)(2,1)S(1)}, bf16[128,2048]{1,0:T(8,128)(2,1)S(1)}, u32[]{:S(2)}, u32[]{:S(2)}) collective-permute-start(bf16[128,2048]{1,0:T(8,128)(2,1)S(1)} %collective-permute-done.4.refs_2_.refs_1_), channel_id=1, source_target_pairs={{1,2},{2,3},{5,6},{6,7},{9,10},{10,11},{13,14},{14,15},{17,18},{18... | collective-permute-start | bytes 1572872 | tf_op jit(solution)/shard_map/ppermute | solution.py:860
  146.1 15.3 %collective-permute-start.6 = (bf16[128,2048]{1,0:T(8,128)(2,1)S(1)}, bf16[128,2048]{1,0:T(8,128)(2,1)S(1)}, u32[]{:S(2)}, u32[]{:S(2)}) collective-permute-start(bf16[128,2048]{1,0:T(8,128)(2,1)S(1)} %collective-permute-done.3.refs_1_.refs_0_), channel_id=1, source_target_pairs={{1,0},{2,1},{5,4},{6,5},{9,8},{10,9},{13,12},{14,13},{17,16},{18,1... | collective-permute-start | bytes 1572872 | tf_op jit(solution)/shard_map/ppermute | solution.py:861
  161.4 14.0 %collective-permute-start.7 = (bf16[128,2048]{1,0:T(8,128)(2,1)S(1)}, bf16[128,2048]{1,0:T(8,128)(2,1)S(1)}, u32[]{:S(2)}, u32[]{:S(2)}) collective-permute-start(bf16[128,2048]{1,0:T(8,128)(2,1)S(1)} %collective-permute-done.5.refs_1_), channel_id=1, source_target_pairs={{2,3},{6,7},{10,11},{14,15},{18,19},{22,23},{26,27},{30,31}} | collective-permute-start | bytes 1572872 | tf_op jit(solution)/shard_map/ppermute | solution.py:860
  162.1 15.0 %collective-permute-start.8 = (bf16[128,2048]{1,0:T(8,128)(2,1)S(1)}, bf16[128,2048]{1,0:T(8,128)(2,1)S(1)}, u32[]{:S(2)}, u32[]{:S(2)}) collective-permute-start(bf16[128,2048]{1,0:T(8,128)(2,1)S(1)} %collective-permute-done.6.refs_0_), channel_id=1, source_target_pairs={{1,0},{5,4},{9,8},{13,12},{17,16},{21,20},{25,24},{29,28}} | collective-permute-start | bytes 1572872 | tf_op jit(solution)/shard_map/ppermute | solution.py:861
  177.1 24.4 %collective-permute-start.10 = (bf16[128,2048]{1,0:T(8,128)(2,1)S(1)}, bf16[128,2048]{1,0:T(8,128)(2,1)S(1)}, u32[]{:S(2)}, u32[]{:S(2)}) collective-permute-start(bf16[128,2048]{1,0:T(8,128)(2,1)S(1)} %get-tuple-element.195), channel_id=1, source_target_pairs={{0,2},{1,3},{2,0},{3,1},{4,6},{5,7},{6,4},{7,5},{8,10},{9,11},{10,... | collective-permute-start | bytes 1572872 | tf_op jit(solution)/shard_map/ppermute | solution.py:1203
  178.4 23.1 %collective-permute-start.9 = (bf16[128,2048]{1,0:T(8,128)(2,1)S(1)}, bf16[128,2048]{1,0:T(8,128)(2,1)S(1)}, u32[]{:S(2)}, u32[]{:S(2)}) collective-permute-start(bf16[128,2048]{1,0:T(8,128)(2,1)S(1)} %get-tuple-element.194), channel_id=1, source_target_pairs={{0,1},{1,0},{2,3},{3,2},{4,5},{5,4},{6,7},{7,6},{8,9},{9,8},{10,11... | collective-permute-start | bytes 1572872 | tf_op jit(solution)/shard_map/ppermute | solution.py:1203
  190.8 12.7 %collective-permute-start.18 = (bf16[512,2048]{1,0:T(8,128)(2,1)S(1)}, bf16[512,2048]{1,0:T(8,128)(2,1)S(1)}, u32[]{:S(2)}, u32[]{:S(2)}) collective-permute-start(bf16[512,2048]{1,0:T(8,128)(2,1)S(1)} %get-tuple-element.210.refs_2_), channel_id=1, source_target_pairs={{0,4},{4,0},{8,12},{12,8},{16,20},{20,16},{24,28},{28,24},{1,5},{5... | collective-permute-start | bytes 6291464 | tf_op jit(solution)/shard_map/ppermute | solution.py:1191
  201.5 21.4 %collective-permute-start.12 = (bf16[512,2048]{1,0:T(8,128)(2,1)S(1)}, bf16[512,2048]{1,0:T(8,128)(2,1)S(1)}, u32[]{:S(2)}, u32[]{:S(2)}) collective-permute-start(bf16[512,2048]{1,0:T(8,128)(2,1)S(1)} %copy-done.8), channel_id=1, source_target_pairs={{0,4},{4,0},{8,12},{12,8},{16,20},{20,16},{24,28},{28,24},{1,5},{5... | collective-permute-start | bytes 6291464 | tf_op jit(solution)/shard_map/ppermute | solution.py:1191
  202.0 21.4 %collective-permute-start.13 = (bf16[512,2048]{1,0:T(8,128)(2,1)S(1)}, bf16[512,2048]{1,0:T(8,128)(2,1)S(1)}, u32[]{:S(2)}, u32[]{:S(2)}) collective-permute-start(bf16[512,2048]{1,0:T(8,128)(2,1)S(1)} %get-tuple-element.215.refs_2_.left_ref), channel_id=1, source_target_pairs={{0,4},{4,0},{8,12},{12,8},{16,20},{20,16},{24,28},{28,24},{1,5},{5... | collective-permute-start | bytes 6291464 | tf_op jit(solution)/shard_map/ppermute | solution.py:1191
  202.1 30.1 %collective-permute-start.11 = (bf16[128,2048]{1,0:T(8,128)(2,1)S(1)}, bf16[128,2048]{1,0:T(8,128)(2,1)S(1)}, u32[]{:S(2)}, u32[]{:S(2)}) collective-permute-start(bf16[128,2048]{1,0:T(8,128)(2,1)S(1)} %get-tuple-element.198), channel_id=1, source_target_pairs={{0,3},{1,2},{2,1},{3,0},{4,7},{5,6},{6,5},{7,4},{8,11},{9,10},{10,... | collective-permute-start | bytes 1572872 | tf_op jit(solution)/shard_map/ppermute | solution.py:1203
  211.6 46.7 %collective-permute-start.19 = (bf16[2,256,1024]{2,1,0:T(8,128)(2,1)}, bf16[2,256,1024]{2,1,0:T(8,128)(2,1)}, u32[]{:S(2)}, u32[]{:S(2)}) collective-permute-start(bf16[2,256,1024]{2,1,0:T(8,128)(2,1)} %get-tuple-element.211), channel_id=1, source_target_pairs={{0,8},{4,12},{8,0},{12,4},{16,24},{20,28},{24,16},{28,20},{1,9},{5... | collective-permute-start | bytes 3145736 | tf_op jit(solution)/shard_map/ppermute | solution.py:1010
  213.1 45.2 %collective-permute-start.20 = (bf16[2,256,1024]{2,1,0:T(8,128)(2,1)}, bf16[2,256,1024]{2,1,0:T(8,128)(2,1)}, u32[]{:S(2)}, u32[]{:S(2)}) collective-permute-start(bf16[2,256,1024]{2,1,0:T(8,128)(2,1)} %get-tuple-element.212), channel_id=1, source_target_pairs={{0,16},{4,20},{8,24},{12,28},{16,0},{20,4},{24,8},{28,12},{1,17},{... | collective-permute-start | bytes 3145736 | tf_op jit(solution)/shard_map/ppermute | solution.py:1010
  222.9 36.8 %collective-permute-start.16 = (bf16[2,256,1024]{2,1,0:T(8,128)(2,1)}, bf16[2,256,1024]{2,1,0:T(8,128)(2,1)}, u32[]{:S(2)}, u32[]{:S(2)}) collective-permute-start(bf16[2,256,1024]{2,1,0:T(8,128)(2,1)} %get-tuple-element.208), channel_id=1, source_target_pairs={{0,8},{4,12},{8,0},{12,4},{16,24},{20,28},{24,16},{28,20},{1,9},{5... | collective-permute-start | bytes 3145736 | tf_op jit(solution)/shard_map/ppermute | solution.py:1010
  223.4 37.4 %collective-permute-start.17 = (bf16[2,256,1024]{2,1,0:T(8,128)(2,1)}, bf16[2,256,1024]{2,1,0:T(8,128)(2,1)}, u32[]{:S(2)}, u32[]{:S(2)}) collective-permute-start(bf16[2,256,1024]{2,1,0:T(8,128)(2,1)} %get-tuple-element.209), channel_id=1, source_target_pairs={{0,16},{4,20},{8,24},{12,28},{16,0},{20,4},{24,8},{28,12},{1,17},{... | collective-permute-start | bytes 3145736 | tf_op jit(solution)/shard_map/ppermute | solution.py:1010
  240.1 18.2 %all-to-all-start.3 = ((bf16[4,128,512]{2,1,0:T(8,128)(2,1)}), bf16[4,128,512]{2,1,0:T(8,128)(2,1)}, u32[]{:S(2)}, u32[]{:S(2)}) async-start(bf16[4,128,512]{2,1,0:T(8,128)(2,1)} %copy-done.43), calls=%async_computation.3 | async-start | bytes 1048576 | tf_op jit(solution)/shard_map/all_to_all | solution.py:1326
  244.3 84.4 %reduce-scatter.2.cloned.1.call-start = ((), (), s32[]{:S(2)}) async-start(), calls=%async_computation.10 | async-start | bytes 2621440 | tf_op jit(solution)/shard_map/reduce_scatter | solution.py:1330
  267.1 110.0 %all-gather.8.cloned.1.call-start = ((), (), s32[]{:S(2)}) async-start(), calls=%async_computation.11 | async-start | bytes 2621440 | tf_op jit(solution)/shard_map/all_gather | solution.py:1340
  304.2 24.4 %all-to-all-start.5 = ((bf16[4,512,384]{2,1,0:T(8,128)(2,1)}), bf16[4,512,384]{2,1,0:T(8,128)(2,1)}, u32[]{:S(2)}, u32[]{:S(2)}) async-start(bf16[4,512,384]{2,1,0:T(8,128)(2,1)} %bitcast.112), calls=%async_computation.5 | async-start | bytes 3145728 | tf_op jit(solution)/shard_map/all_to_all | solution.py:1194
  337.2 24.7 %collective-permute-start.25 = (bf16[2,256,1024]{2,1,0:T(8,128)(2,1)S(1)}, bf16[2,256,1024]{2,1,0:T(8,128)(2,1)}, u32[]{:S(2)}, u32[]{:S(2)}) collective-permute-start(bf16[2,256,1024]{2,1,0:T(8,128)(2,1)S(1)} %copy-done.53), channel_id=1, source_target_pairs={{0,8},{4,12},{8,0},{12,4},{16,24},{20,28},{24,16},{28,20},{1,9},{5... | collective-permute-start | bytes 3145736 | tf_op jit(solution)/shard_map/ppermute | solution.py:1010
  338.7 24.4 %collective-permute-start.26 = (bf16[2,256,1024]{2,1,0:T(8,128)(2,1)S(1)}, bf16[2,256,1024]{2,1,0:T(8,128)(2,1)}, u32[]{:S(2)}, u32[]{:S(2)}) collective-permute-start(bf16[2,256,1024]{2,1,0:T(8,128)(2,1)S(1)} %copy-done.52), channel_id=1, source_target_pairs={{0,16},{4,20},{8,24},{12,28},{16,0},{20,4},{24,8},{28,12},{1,17},{... | collective-permute-start | bytes 3145736 | tf_op jit(solution)/shard_map/ppermute | solution.py:1010
  339.2 19.2 %collective-permute-start.23 = (bf16[128,2048]{1,0:T(8,128)(2,1)S(1)}, bf16[128,2048]{1,0:T(8,128)(2,1)S(1)}, u32[]{:S(2)}, u32[]{:S(2)}) collective-permute-start(bf16[128,2048]{1,0:T(8,128)(2,1)S(1)} %get-tuple-element.228.down_ref), channel_id=1, source_target_pairs={{0,1},{4,5},{8,9},{12,13},{16,17},{20,21},{24,25},{28,29}} | collective-permute-start | bytes 1572872 | tf_op jit(solution)/shard_map/ppermute | solution.py:860
  343.0 15.4 %collective-permute-start.24 = (bf16[128,2048]{1,0:T(8,128)(2,1)S(1)}, bf16[128,2048]{1,0:T(8,128)(2,1)S(1)}, u32[]{:S(2)}, u32[]{:S(2)}) collective-permute-start(bf16[128,2048]{1,0:T(8,128)(2,1)S(1)} %get-tuple-element.229.up_ref), channel_id=1, source_target_pairs={{3,2},{7,6},{11,10},{15,14},{19,18},{23,22},{27,26},{31,30}} | collective-permute-start | bytes 1572872 | tf_op jit(solution)/shard_map/ppermute | solution.py:861
  364.2 12.9 %collective-permute-start.27 = (bf16[128,2048]{1,0:T(8,128)(2,1)}, bf16[128,2048]{1,0:T(8,128)(2,1)}, u32[]{:S(2)}, u32[]{:S(2)}) collective-permute-start(bf16[128,2048]{1,0:T(8,128)(2,1)} %get-tuple-element.237), channel_id=1, source_target_pairs={{0,1},{1,2},{4,5},{5,6},{8,9},{9,10},{12,13},{13,14},{16,17},{17,1... | collective-permute-start | bytes 1572872 | tf_op jit(solution)/shard_map/ppermute | solution.py:860
  369.5 16.0 %collective-permute-start.34 = (bf16[512,2048]{1,0:T(8,128)(2,1)}, bf16[512,2048]{1,0:T(8,128)(2,1)}, u32[]{:S(2)}, u32[]{:S(2)}) collective-permute-start(bf16[512,2048]{1,0:T(8,128)(2,1)} %get-tuple-element.257.refs_4_), channel_id=1, source_target_pairs={{0,4},{4,0},{8,12},{12,8},{16,20},{20,16},{24,28},{28,24},{1,5},{5... | collective-permute-start | bytes 6291464 | tf_op jit(solution)/shard_map/ppermute | solution.py:1191
  377.2 17.0 %collective-permute-start.33 = (bf16[512,2048]{1,0:T(8,128)(2,1)}, bf16[512,2048]{1,0:T(8,128)(2,1)S(1)}, u32[]{:S(2)}, u32[]{:S(2)}) collective-permute-start(bf16[512,2048]{1,0:T(8,128)(2,1)} %all-gather.8.cloned.1.call-done.refs_0_), channel_id=1, source_target_pairs={{0,4},{4,0},{8,12},{12,8},{16,20},{20,16},{24,28},{28,24},{1,5},{5... | collective-permute-start | bytes 6291464 | tf_op jit(solution)/shard_map/ppermute | solution.py:1191
  377.2 15.6 %collective-permute-start.35 = (bf16[512,1536]{1,0:T(8,128)(2,1)}, bf16[512,1536]{1,0:T(8,128)(2,1)S(1)}, u32[]{:S(2)}, u32[]{:S(2)}) collective-permute-start(bf16[512,1536]{1,0:T(8,128)(2,1)} %copy-done.31), channel_id=1, source_target_pairs={{0,4},{4,0},{8,12},{12,8},{16,20},{20,16},{24,28},{28,24},{1,5},{5... | collective-permute-start | bytes 4718600 | tf_op jit(solution)/shard_map/ppermute | solution.py:1191
  379.2 24.2 %collective-permute-start.32 = (bf16[256,1024]{1,0:T(8,128)(2,1)S(1)}, bf16[256,1024]{1,0:T(8,128)(2,1)S(1)}, u32[]{:S(2)}, u32[]{:S(2)}) collective-permute-start(bf16[256,1024]{1,0:T(8,128)(2,1)S(1)} %fusion.1), channel_id=1, source_target_pairs={{0,8},{4,12},{8,0},{12,4},{16,24},{20,28},{24,16},{28,20},{1,9},{5... | collective-permute-start | bytes 1572872 | tf_op jit(solution)/shard_map/ppermute | solution.py:1010
  381.5 21.9 %collective-permute-start.31 = (bf16[256,1024]{1,0:T(8,128)(2,1)S(1)}, bf16[256,1024]{1,0:T(8,128)(2,1)S(1)}, u32[]{:S(2)}, u32[]{:S(2)}) collective-permute-start(bf16[256,1024]{1,0:T(8,128)(2,1)S(1)} %fusion), channel_id=1, source_target_pairs={{0,16},{4,20},{8,24},{12,28},{16,0},{20,4},{24,8},{28,12},{1,17},{... | collective-permute-start | bytes 1572872 | tf_op jit(solution)/shard_map/ppermute | solution.py:1010
  385.4 18.0 %collective-permute-start.29 = (bf16[128,2048]{1,0:T(8,128)(2,1)S(1)}, bf16[128,2048]{1,0:T(8,128)(2,1)S(1)}, u32[]{:S(2)}, u32[]{:S(2)}) collective-permute-start(bf16[128,2048]{1,0:T(8,128)(2,1)S(1)} %get-tuple-element.247), channel_id=1, source_target_pairs={{0,1},{1,2},{2,3},{4,5},{5,6},{6,7},{8,9},{9,10},{10,11},{12,13},{... | collective-permute-start | bytes 1572872 | tf_op jit(solution)/shard_map/ppermute | solution.py:860
  392.8 15.0 %collective-permute-start.30 = (bf16[128,2048]{1,0:T(8,128)(2,1)S(1)}, bf16[128,2048]{1,0:T(8,128)(2,1)S(1)}, u32[]{:S(2)}, u32[]{:S(2)}) collective-permute-start(bf16[128,2048]{1,0:T(8,128)(2,1)S(1)} %get-tuple-element.248), channel_id=1, source_target_pairs={{1,0},{2,1},{3,2},{5,4},{6,5},{7,6},{9,8},{10,9},{11,10},{13,12},{... | collective-permute-start | bytes 1572872 | tf_op jit(solution)/shard_map/ppermute | solution.py:861
  409.5 27.5 %collective-permute-start.36 = (bf16[272,2048]{1,0:T(8,128)(2,1)S(1)}, bf16[272,2048]{1,0:T(8,128)(2,1)S(1)}, u32[]{:S(2)}, u32[]{:S(2)}) collective-permute-start(bf16[272,2048]{1,0:T(8,128)(2,1)S(1)} %tokens.1.own_ref), channel_id=1, source_target_pairs={{0,1},{1,2},{2,3},{4,5},{5,6},{6,7},{8,9},{9,10},{10,11},{12,13},{... | collective-permute-start | bytes 3342344 | tf_op jit(solution)/shard_map/ppermute | solution.py:860
  411.9 26.6 %collective-permute-start.37 = (bf16[272,2048]{1,0:T(8,128)(2,1)S(1)}, bf16[272,2048]{1,0:T(8,128)(2,1)S(1)}, u32[]{:S(2)}, u32[]{:S(2)}) collective-permute-start(bf16[272,2048]{1,0:T(8,128)(2,1)S(1)} %tokens.1.own_ref), channel_id=1, source_target_pairs={{1,0},{2,1},{3,2},{5,4},{6,5},{7,6},{9,8},{10,9},{11,10},{13,12},{... | collective-permute-start | bytes 3342344 | tf_op jit(solution)/shard_map/ppermute | solution.py:861
  413.2 23.4 %collective-permute-start.38 = (bf16[2,256,1024]{2,1,0:T(8,128)(2,1)S(1)}, bf16[2,256,1024]{2,1,0:T(8,128)(2,1)S(1)}, u32[]{:S(2)}, u32[]{:S(2)}) collective-permute-start(bf16[2,256,1024]{2,1,0:T(8,128)(2,1)S(1)} %copy-done.55), channel_id=1, source_target_pairs={{0,8},{4,12},{8,0},{12,4},{16,24},{20,28},{24,16},{28,20},{1,9},{5... | collective-permute-start | bytes 3145736 | tf_op jit(solution)/shard_map/ppermute | solution.py:1010
  414.0 23.0 %collective-permute-start.39 = (bf16[2,256,1024]{2,1,0:T(8,128)(2,1)S(1)}, bf16[2,256,1024]{2,1,0:T(8,128)(2,1)S(1)}, u32[]{:S(2)}, u32[]{:S(2)}) collective-permute-start(bf16[2,256,1024]{2,1,0:T(8,128)(2,1)S(1)} %copy-done.54), channel_id=1, source_target_pairs={{0,16},{4,20},{8,24},{12,28},{16,0},{20,4},{24,8},{28,12},{1,17},{... | collective-permute-start | bytes 3145736 | tf_op jit(solution)/shard_map/ppermute | solution.py:1010
  439.8 14.9 %collective-permute-start.45 = (bf16[256,1024]{1,0:T(8,128)(2,1)S(1)}, bf16[256,1024]{1,0:T(8,128)(2,1)S(1)}, u32[]{:S(2)}, u32[]{:S(2)}) collective-permute-start(bf16[256,1024]{1,0:T(8,128)(2,1)S(1)} %fusion.5), channel_id=1, source_target_pairs={{0,8},{4,12},{8,0},{12,4},{16,24},{20,28},{24,16},{28,20},{1,9},{5... | collective-permute-start | bytes 1572872 | tf_op jit(solution)/shard_map/ppermute | solution.py:1010
  440.6 25.5 %collective-permute-start.40 = (bf16[272,2048]{1,0:T(8,128)(2,1)S(1)}, bf16[272,2048]{1,0:T(8,128)(2,1)S(1)}, u32[]{:S(2)}, u32[]{:S(2)}) collective-permute-start(bf16[272,2048]{1,0:T(8,128)(2,1)S(1)} %collective-permute-done.36.refs_3_), channel_id=1, source_target_pairs={{1,2},{2,3},{5,6},{6,7},{9,10},{10,11},{13,14},{14,15},{17,18},{18... | collective-permute-start | bytes 3342344 | tf_op jit(solution)/shard_map/ppermute | solution.py:860
  441.3 26.1 %collective-permute-start.41 = (bf16[272,2048]{1,0:T(8,128)(2,1)S(1)}, bf16[272,2048]{1,0:T(8,128)(2,1)S(1)}, u32[]{:S(2)}, u32[]{:S(2)}) collective-permute-start(bf16[272,2048]{1,0:T(8,128)(2,1)S(1)} %collective-permute-done.37.refs_0_), channel_id=1, source_target_pairs={{1,0},{2,1},{5,4},{6,5},{9,8},{10,9},{13,12},{14,13},{17,16},{18,1... | collective-permute-start | bytes 3342344 | tf_op jit(solution)/shard_map/ppermute | solution.py:861
  444.0 14.9 %collective-permute-start.44 = (bf16[256,1024]{1,0:T(8,128)(2,1)S(1)}, bf16[256,1024]{1,0:T(8,128)(2,1)S(1)}, u32[]{:S(2)}, u32[]{:S(2)}) collective-permute-start(bf16[256,1024]{1,0:T(8,128)(2,1)S(1)} %fusion.4), channel_id=1, source_target_pairs={{0,16},{4,20},{8,24},{12,28},{16,0},{20,4},{24,8},{28,12},{1,17},{... | collective-permute-start | bytes 1572872 | tf_op jit(solution)/shard_map/ppermute | solution.py:1010
  446.5 15.8 %collective-permute-start.43 = (bf16[256,1024]{1,0:T(8,128)(2,1)S(1)}, bf16[256,1024]{1,0:T(8,128)(2,1)S(1)}, u32[]{:S(2)}, u32[]{:S(2)}) collective-permute-start(bf16[256,1024]{1,0:T(8,128)(2,1)S(1)} %fusion.3), channel_id=1, source_target_pairs={{0,8},{4,12},{8,0},{12,4},{16,24},{20,28},{24,16},{28,20},{1,9},{5... | collective-permute-start | bytes 1572872 | tf_op jit(solution)/shard_map/ppermute | solution.py:1010
  467.4 17.2 %collective-permute-start.46 = (bf16[272,2048]{1,0:T(8,128)(2,1)S(1)}, bf16[272,2048]{1,0:T(8,128)(2,1)S(1)}, u32[]{:S(2)}, u32[]{:S(2)}) collective-permute-start(bf16[272,2048]{1,0:T(8,128)(2,1)S(1)} %collective-permute-done.40.refs_4_), channel_id=1, source_target_pairs={{2,3},{6,7},{10,11},{14,15},{18,19},{22,23},{26,27},{30,31}} | collective-permute-start | bytes 3342344 | tf_op jit(solution)/shard_map/ppermute | solution.py:860
  468.1 24.2 %collective-permute-start.47 = (bf16[272,2048]{1,0:T(8,128)(2,1)S(1)}, bf16[272,2048]{1,0:T(8,128)(2,1)S(1)}, u32[]{:S(2)}, u32[]{:S(2)}) collective-permute-start(bf16[272,2048]{1,0:T(8,128)(2,1)S(1)} %collective-permute-done.41.refs_1_), channel_id=1, source_target_pairs={{1,0},{5,4},{9,8},{13,12},{17,16},{21,20},{25,24},{29,28}} | collective-permute-start | bytes 3342344 | tf_op jit(solution)/shard_map/ppermute | solution.py:861
  (68 other events, 685.5 us)
Sparse Core Ops, SparseCore 0:
  10.2 57.5 all-gather.3
  69.9 47.0 all-gather.5
  261.0 42.9 reduce-scatter.1
  305.5 47.0 all-gather.7

commit v6 on v5

--- a/solution.py
+++ b/solution.py
@@ -572,21 +572,48 @@
 def out_kernel(where_ref, tokens_ref, gain_ref, attended_ref, *refs):
     *weights, middle_ref, normed_ref = refs
     own_tp, core = where_ref[0], where_ref[1]
-    count, part, _ = attended_ref.shape
+    part, width = middle_ref.shape
     _, half, wide = weights[0].shape
-    starts = (0, wide, middle_ref.shape[1])
-    rows = tokens_ref[pl.ds(pl.multiple_of(own_tp * part, part), part), :].astype(jnp.float32)
+    starts = (0, wide, width)
+    step = pl.program_id(0)
+
+    @pl.when(step == 0)
+    def _():
+        rows = pl.ds(pl.multiple_of(own_tp * part, part), part)
+        middle_ref[...] = tokens_ref[rows, :].astype(jnp.float32)
+
     for piece in range(2):
         target = slice(starts[piece], starts[piece + 1])
-        total = rows[:, target]
-        for d in range(count):
-            for which in range(2):
-                side = core if which == 0 else 1 - core
-                columns = pl.ds(pl.multiple_of(side * half, half), half)
-                values = attended_ref[d, :, columns]
-                total = total + dense(values, weights[2 * piece + which][d])
+        total = middle_ref[:, target]
+        for which in range(2):
+            side = core if which == 0 else 1 - core
+            columns = pl.ds(pl.multiple_of(side * half, half), half)
+            total = total + dense(attended_ref[0, :, columns], weights[2 * piece + which][0])
         middle_ref[:, target] = total
-    normed_ref[...] = (norm_of(middle_ref[...])[1] * gain_ref[...]).astype(jnp.bfloat16)
+
+    @pl.when(step == pl.num_programs(0) - 1)
+    def _():
+        normed_ref[...] = (norm_of(middle_ref[...])[1] * gain_ref[...]).astype(jnp.bfloat16)
+
+
+def out_call(where, tokens, gain, attended, weights):
+    rows, width = tokens.shape
+    count, part, own = attended.shape
+    weights = [pltpu.with_memory_space_constraint(w, pltpu.HBM) for w in weights]
+    whole = lambda shape: pl.BlockSpec(shape, lambda d, w: (0, 0))
+    group = lambda x: pl.BlockSpec((1, *x.shape[1:]), lambda d, w: (d, 0, 0))
+    return call(
+        out_kernel,
+        (made((part, width), jnp.float32), made((part, width), jnp.bfloat16)),
+        (where, tokens, gain, attended, *weights),
+        scalars=1,
+        grid=(count,),
+        in_specs=[whole((rows, width)), whole((1, width)), group(attended)]
+        + [group(w) for w in weights],
+        out_specs=[whole((part, width))] * 2,
+        room=24,
+        name="out",
+    )
 
 
 def ffn_kernel(where_ref, *refs, chunk, sources, first):
@@ -1267,14 +1294,7 @@
     )
     w_second = after(w_second, attended_part)
     out_weights = (w_first, swap(w_first), w_second, swap(w_second))
-    middle, normed_part = call(
-        out_kernel,
-        (made((part, width), f32), made((part, width), bf16)),
-        (where, tokens, gain_ffn, attended_part, *out_weights),
-        scalars=1,
-        work=2 * part * width * width,
-        name="out",
-    )
+    middle, normed_part = out_call(where, tokens, gain_ffn, attended_part, out_weights)
 
     line = Gather(normed_part, "tp", tp_size)
     line.step()

time: 513 us -> 514 us (level)
  Pallas kernels: 158 us -> 164 us
    ppermute x13, starting transfers between devices: 11.3 us -> 5.34 us  [swap(): return lax.ppermute(values, 'seq', other_core)]
    pallas_call x1 -> x2, Pallas kernels: 7.44 us -> 13.3 us  [call(): pl.pallas_call(kernel, out_shape=tuple(outs), grid_spec=pltpu.PrefetchSca...]
    pallas_call x11 -> x10, Pallas kernels: 29.1 us -> 25.8 us  [call(): pl.pallas_call(kernel, out_shape=tuple(outs), in_specs=[SMALL] * scalars...]
  transfers between devices with their start and end apart: 60 -> 60, of which waited for: 30 -> 29; matrix products, arithmetic and copies ran while one was open for 7% -> 6% of each run, Pallas kernels for 30% -> 30%
where the time goes in v6:
time: 514 us; the launch traced here: 504 us
  waiting for transfers between devices  176 us (34%)
  Pallas kernels  164 us (32%)
  starting transfers between devices  83.2 us (16%)
  local copies, waits for them, and re-layouts  35.2 us (7%)
  other arithmetic  22.8 us (4%)
  between operations  15.1 us (3%)
  blocking collectives  7.45 us (1%)
    ppermute x16, waiting for transfers between devices, over(): lax.ppermute(values, 'seq', [(i, i ^ side) for i in range(self.size)])  44.1 us
    pallas_call x3, Pallas kernels, ffn_call(): pl.pallas_call(functools.partial(ffn_kernel, chunk=chunk, sources=len(sou...  38 us
    pallas_call x4, Pallas kernels, chip_outer_call(): pl.pallas_call(functools.partial(chip_outer_kernel, sides=len(pairs)), ou...  33.7 us
    all_gather x2, waiting for transfers between devices, gathered(): values = lax.all_gather(columns, 'tp', axis=0, tiled=True)  33.1 us
    all_to_all x4, waiting for transfers between devices, to_heads(): lax.all_to_all(values, 'seq', 0, 0, axis_index_groups=same_core, tiled=True)  31.1 us
    ppermute x9, waiting for transfers between devices, send(): self.upward = lax.ppermute(up, self.axis, up_pairs)  26.8 us
    pallas_call x10, Pallas kernels, call(): pl.pallas_call(kernel, out_shape=tuple(outs), in_specs=[SMALL] * scalars...  25.8 us
    unnamed x121, local copies, waits for them, and re-layouts  22.6 us
  transfers between devices with their start and end apart: 60, of which 29 were waited for; matrix products, arithmetic and copies ran while one was open for 6% of the time, Pallas kernels for 30%

profile of v6, /device:TPU:0, one launch (start us, length us, event | category | flops | bytes accessed | tf_op | source)
XLA Modules:
  0.0 503.7 jit_solution(8686302126317257673)
XLA Ops:
  13.3 7.4 %project.1 = (bf16[4,512,384]{2,1,0:T(8,128)(2,1)S(1)}, bf16[512,2048]{1,0:T(8,128)(2,1)}) custom-call(bf16[512,2048]{1,0:T(8,128)(2,1)S(1)} %bitcast.101, f32[1,2048]{1,0:T(1,128)S(1)} %bitcast.119, s32[512,1]{1,0:T(8,128)S(1)} %bitcast.114, f32[512,128]{1,0:T(8,128)S(1)} %get-tuple-element.344.cosine_ref, f32[512,128]{1,0:T(8,128)S(1)} %get-tuple-element.345.sine_ref, ...), custom_call_target="tpu_custom_call" | custom-call | flops 1 | bytes 1 | tf_op jit(solution)/shard_map/project/pallas_call | solution.py:482
  21.9 5.3 %all-to-all-start = ((bf16[4,512,384]{2,1,0:T(8,128)(2,1)}), bf16[4,512,384]{2,1,0:T(8,128)(2,1)}, u32[]{:S(2)}, u32[]{:S(2)}) async-start(bf16[4,512,384]{2,1,0:T(8,128)(2,1)} %copy-done.33), calls=%async_computation | async-start | bytes 3145728 | tf_op jit(solution)/shard_map/all_to_all | solution.py:1221
  33.5 7.9 %grad_act.1.refs_3_.refs_2_.refs_4_ = f32[512,2048]{1,0:T(8,128)S(1)} custom-call(s32[3]{0:T(128)S(1)} %pad_add_fusion.1.where_ref, bf16[512,2048]{1,0:T(8,128)(2,1)S(1)} %pad_maximum_fusion.left_ref.refs_0_, bf16[2048,2048]{1,0:T(8,128)(2,1)} %right_ref.3), custom_call_target="tpu_custom_call" | custom-call | flops 1 | bytes 1 | tf_op jit(solution)/shard_map/grad_act/pallas_call | solution.py:1132
  45.8 3.7 fusion.8
  55.3 9.5 %attend.1 = bf16[2048,128]{1,0:T(8,128)(2,1)S(1)} custom-call(s32[16]{0:T(128)S(1)} %pad_add_fusion.2.slot_places, s32[8]{0:T(128)S(1)} %get-tuple-element.316.key_low, bf16[2048,384]{1,0:T(8,128)(2,1)} %bitcast.12.own_ref, bf16[2048,384]{1,0:T(8,128)(2,1)} %collective-permute-done.other_ref, s32[2048,1]{1,0:T(8,128)S(1)} %bitcast.113), custom_call_target="tpu_custom_call" | custom-call | flops 1 | bytes 1 | tf_op jit(solution)/shard_map/attend/pallas_call | solution.py:438
  67.7 4.0 all-to-all-start.1
  73.1 7.7 %all-to-all-done.1 = bf16[4,512,128]{2,1,0:T(8,128)(2,1)S(1)} async-done(((bf16[4,512,128]{2,1,0:T(8,128)(2,1)}), bf16[4,512,128]{2,1,0:T(8,128)(2,1)S(1)}, u32[]{:S(2)}, u32[]{:S(2)}) %all-to-all-start.1) | async-done | bytes 524320 | tf_op jit(solution)/shard_map/all_to_all | solution.py:1221
  82.5 3.5 all-to-all-start.2
  86.0 30.9 %all-gather.6.cloned.1.call-done = bf16[1024,768]{1,0:T(8,128)(2,1)} async-done(((bf16[256,768]{1,0:T(8,128)(2,1)}), bf16[1024,768]{1,0:T(8,128)(2,1)}) %all-gather.6.cloned.1.call-update) | async-done | bytes 1572880 | tf_op jit(solution)/shard_map/all_gather | solution.py:1237
  117.8 3.6 collective-permute-done.2.refs_3_.refs_7_
  123.6 5.9 %out.1 = (f32[128,2048]{1,0:T(8,128)S(1)}, bf16[128,2048]{1,0:T(8,128)(2,1)S(1)}) custom-call(s32[3]{0:T(128)S(1)} %pad_add_fusion.1.where_ref, bf16[512,2048]{1,0:T(8,128)(2,1)S(1)} %bitcast.102, f32[1,2048]{1,0:T(1,128)S(1)} %bitcast.117, bf16[4,128,512]{2,1,0:T(8,128)(2,1)S(1)} %copy-done.28, bf16[4,256,1280]{2,1,0:T(8,128)(2,1)} %bitcast.106, ...), custom_call_target="tpu_custom_call" | custom-call | flops 1 | bytes 1 | tf_op jit(solution)/shard_map/out/pallas_call | solution.py:482
  132.1 10.4 %collective-permute-done.4.refs_2_.refs_1_ = bf16[128,2048]{1,0:T(8,128)(2,1)S(1)} collective-permute-done((bf16[128,2048]{1,0:T(8,128)(2,1)S(1)}, bf16[128,2048]{1,0:T(8,128)(2,1)S(1)}, u32[]{:S(2)}, u32[]{:S(2)}) %collective-permute-start.4) | collective-permute-done | bytes 524320 | tf_op jit(solution)/shard_map/ppermute | solution.py:887
  143.2 3.5 collective-permute-done.3.refs_1_.refs_0_
  147.9 14.0 %ffn.3 = (bf16[512,2048]{1,0:T(8,128)(2,1)S(1)}, bf16[512,2048]{1,0:T(8,128)(2,1)S(1)}, bf16[512,2048]{1,0:T(8,128)(2,1)S(1)}, bf16[512,2048]{1,0:T(8,128)(2,1)S...) custom-call(s32[3]{0:T(128)S(1)} %pad_add_fusion.1.where_ref, ...), custom_call_target="tpu_custom_call" | custom-call | flops 1 | bytes 1 | tf_op jit(solution)/shard_map/ffn/pallas_call | solution.py:693
  163.9 12.0 %ffn.4 = (bf16[512,2048]{1,0:T(8,128)(2,1)S(1)}, bf16[512,2048]{1,0:T(8,128)(2,1)S(1)}, bf16[512,2048]{1,0:T(8,128)(2,1)S(1)}, bf16[512,2048]{1,0:T(8,128)(2,1)S(1)}, bf16[128,2048]{1,0:T(8,128)(2,1)S(1)}) custom-call(s32[3]{0:T(128)S(1)} %pad_add_fusion.1.where_ref, ...), custom_call_target="tpu_custom_call", output_to_operand_aliasing={{0}: (6, {}), {1}: (7, {}), {2}: (8, {}), {3}: (9, {})} | custom-call | flops 1 | bytes 1 | tf_op jit(solution)/shard_map/ffn/pallas_call | solution.py:693
  179.2 12.0 %ffn.5 = (bf16[512,2048]{1,0:T(8,128)(2,1)S(1)}, bf16[512,2048]{1,0:T(8,128)(2,1)S(1)}, bf16[512,2048]{1,0:T(8,128)(2,1)S(1)}, bf16[512,2048]{1,0:T(8,128)(2,1)S(1)}, bf16[128,2048]{1,0:T(8,128)(2,1)S(1)}) custom-call(s32[3]{0:T(128)S(1)} %pad_add_fusion.1.where_ref, ...), custom_call_target="tpu_custom_call", output_to_operand_aliasing={{0}: (8, {}), {1}: (9, {}), {2}: (10, {}), {3}: (11, {})} | custom-call | flops 1 | bytes 1 | tf_op jit(solution)/shard_map/ffn/pallas_call | solution.py:693
  191.8 10.1 %collective-permute-done.10.refs_2_ = bf16[128,2048]{1,0:T(8,128)(2,1)S(1)} collective-permute-done((bf16[128,2048]{1,0:T(8,128)(2,1)S(1)}, bf16[128,2048]{1,0:T(8,128)(2,1)S(1)}, u32[]{:S(2)}, u32[]{:S(2)}) %collective-permute-start.10) | collective-permute-done | bytes 524320 | tf_op jit(solution)/shard_map/ppermute | solution.py:1230
  204.0 8.1 %ffn_outer.5 = (bf16[2,256,1024]{2,1,0:T(8,128)(2,1)}, bf16[2,256,1024]{2,1,0:T(8,128)(2,1)}, bf16[2,256,1024]{2,1,0:T(8,128)(2,1)}, bf16[2,256,1024]{2,1,0:T(8,128)(2,1)}) custom-call(s32[3]{0:T(128)S(1)} %pad_add_fusion.1.where_ref, bf16[512,2048]{1,0:T(8,128)(2,1)S(1)} %get-tuple-element.206.refs_0_, ...), custom_call_target="tpu_custom_call" | custom-call | flops 1 | bytes 1 | tf_op jit(solution)/shard_map/ffn_outer/pallas_call | solution.py:1011
  215.1 8.2 %ffn_outer.4 = (bf16[2,256,1024]{2,1,0:T(8,128)(2,1)}, bf16[2,256,1024]{2,1,0:T(8,128)(2,1)}, bf16[2,256,1024]{2,1,0:T(8,128)(2,1)}, bf16[2,256,1024]{2,1,0:T(8,128)(2,1)}) custom-call(s32[3]{0:T(128)S(1)} %pad_add_fusion.1.where_ref, bf16[512,2048]{1,0:T(8,128)(2,1)S(1)} %get-tuple-element.206.refs_0_, ...), custom_call_target="tpu_custom_call" | custom-call | flops 1 | bytes 1 | tf_op jit(solution)/shard_map/ffn_outer/pallas_call | solution.py:1011
  224.5 8.2 %ffn_outer.3 = (bf16[2,256,1024]{2,1,0:T(8,128)(2,1)}, bf16[2,256,1024]{2,1,0:T(8,128)(2,1)}, bf16[2,256,1024]{2,1,0:T(8,128)(2,1)}, bf16[2,256,1024]{2,1,0:T(8,128)(2,1)}) custom-call(s32[3]{0:T(128)S(1)} %pad_add_fusion.1.where_ref, bf16[512,2048]{1,0:T(8,128)(2,1)S(1)} %copy-done.8, bf16[512,2048]{1,0:T(8,128)(2,1)S(1)} %collective-permute-done.12.refs_1_, ...), custom_call_target="tpu_custom_call" | custom-call | flops 1 | bytes 1 | tf_op jit(solution)/shard_map/ffn_outer/pallas_call | solution.py:1011
  232.7 5.3 %middle.1 = (bf16[128,2048]{1,0:T(8,128)(2,1)S(1)}, f32[128,2048]{1,0:T(8,128)S(1)}, bf16[4,128,512]{2,1,0:T(8,128)(2,1)S(1)}, f32[1,2048]{1,0:T(1,128)S(1)}) custom-call(s32[3]{0:T(128)S(1)} %pad_add_fusion.1.where_ref, f32[128,2048]{1,0:T(8,128)S(1)} %get-tuple-element.167.middle_ref, bf16[512,2048]{1,0:T(8,128)(2,1)S(1)} %bitcast.108, ...), custom_call_target="tpu_custom_call" | custom-call | flops 1 | bytes 1 | tf_op jit(solution)/shard_map/middle/pallas_call | solution.py:472
  240.6 4.1 all-to-all-start.3
  246.4 7.7 %branch.1 = bf16[512,2048]{1,0:T(8,128)(2,1)S(1)} custom-call(s32[3]{0:T(128)S(1)} %pad_add_fusion.1.where_ref, bf16[512,2048]{1,0:T(8,128)(2,1)S(1)} %copy-done.6, bf16[2048,2048]{1,0:T(8,128)(2,1)} %right_ref.3), custom_call_target="tpu_custom_call" | custom-call | flops 1 | bytes 1 | tf_op jit(solution)/shard_map/branch/pallas_call | solution.py:1132
  255.5 3.3 all-to-all-done.3
  263.4 4.1 all-to-all-start.4
  267.8 7.2 %all-to-all-done.4 = bf16[4,512,128]{2,1,0:T(8,128)(2,1)} async-done(((bf16[4,512,128]{2,1,0:T(8,128)(2,1)}), bf16[4,512,128]{2,1,0:T(8,128)(2,1)}, u32[]{:S(2)}, u32[]{:S(2)}) %all-to-all-start.4) | async-done | bytes 524320 | tf_op jit(solution)/shard_map/all_to_all | solution.py:1221
  275.1 14.0 %attend_back.1 = (f32[2048,128]{1,0:T(8,128)S(1)}, f32[2048,256]{1,0:T(8,128)S(1)}, bf16[2048,256]{1,0:T(8,128)(2,1)S(1)}) custom-call(s32[16]{0:T(128)S(1)} %pad_add_fusion.2.slot_places, s32[8]{0:T(128)S(1)} %get-tuple-element.316.key_low, bf16[2048,384]{1,0:T(8,128)(2,1)} %bitcast.12.own_ref, bf16[2048,384]{1,0:T(8,128)(2,1)} %collective-permute-done.other_ref, ...), custom_call_target="tpu_custom_call" | custom-call | flops 1 | bytes 1 | tf_op jit(solution)/shard_map/attend_back/pallas_call | solution.py:452
  295.7 5.5 %turn.1 = bf16[2048,384]{1,0:T(8,128)(2,1)S(1)} custom-call(f32[2048,128]{1,0:T(8,128)} %copy-done.36, f32[2048,256]{1,0:T(8,128)} %copy-done.30, bf16[2048,256]{1,0:T(8,128)(2,1)} %collective-permute-done.21.other_ref, f32[2048,128]{1,0:T(8,128)} %get-tuple-element.222.cosine_ref, f32[2048,128]{1,0:T(8,128)} %get-tuple-element.223.sine_ref), custom_call_target="tpu_custom_call" | custom-call | flops 1 | bytes 1 | tf_op jit(solution)/shard_map/turn/pallas_call | solution.py:1165
  302.4 4.4 all-to-all-start.5
  310.7 16.2 %all-to-all-done.5.back_ref = bf16[4,512,384]{2,1,0:T(8,128)(2,1)} async-done(((bf16[4,512,384]{2,1,0:T(8,128)(2,1)}), bf16[4,512,384]{2,1,0:T(8,128)(2,1)}, u32[]{:S(2)}, u32[]{:S(2)}) %all-to-all-start.5) | async-done | bytes 1572896 | tf_op jit(solution)/shard_map/all_to_all | solution.py:1221
  326.9 8.5 %back.1 = (bf16[512,1536]{1,0:T(8,128)(2,1)S(1)}, f32[1,2048]{1,0:T(1,128)S(1)}, bf16[128,2048]{1,0:T(8,128)(2,1)S(1)}, bf16[128,2048]{1,0:T(8,128)(2,1)S(1)}, b...) custom-call(s32[3]{0:T(128)S(1)} %pad_add_fusion.1.where_ref, bf16[4,512,384]{2,1,0:T(8,128)(2,1)} %all-to-all-done.5.back_ref, ...), custom_call_target="tpu_custom_call" | custom-call | flops 1 | bytes 1 | tf_op jit(solution)/shard_map/back/pallas_call | solution.py:784
  337.5 3.0 collective-permute-start.23
  342.8 16.1 %collective-permute-done.23.got_up_ref = bf16[128,2048]{1,0:T(8,128)(2,1)S(1)} collective-permute-done((bf16[128,2048]{1,0:T(8,128)(2,1)S(1)}, bf16[128,2048]{1,0:T(8,128)(2,1)S(1)}, u32[]{:S(2)}, u32[]{:S(2)}) %collective-permute-start.23) | collective-permute-done | bytes 524320 | tf_op jit(solution)/shard_map/ppermute | solution.py:887
  362.5 3.9 collective-permute-start.27
  367.9 7.5 %all_to_all.35 = f32[8,2,256]{2,1,0:T(2,128)S(1)} all-to-all(f32[8,2,256]{2,1,0:T(2,128)S(1)} %bitcast.128), channel_id=1, replica_groups=mesh['seq'=8,'tp'=4] {'seq'}, dimensions={0} | all-to-all | bytes 32768 | tf_op jit(solution)/shard_map/all_to_all | solution.py:1373
  384.7 8.4 %collective-permute-start.29 = (bf16[128,2048]{1,0:T(8,128)(2,1)S(1)}, bf16[128,2048]{1,0:T(8,128)(2,1)S(1)}, u32[]{:S(2)}, u32[]{:S(2)}) collective-permute-start(bf16[128,2048]{1,0:T(8,128)(2,1)S(1)} %get-tuple-element.247), channel_id=1, source_target_pairs={{0,1},{1,2},{2,3},{4,5},{5,6},{6,7},{8,9},{9,10},{10,11},{12,13},{... | collective-permute-start | bytes 1572872 | tf_op jit(solution)/shard_map/ppermute | solution.py:887
  394.6 9.2 %attn_outer.1 = (bf16[2,256,1024]{2,1,0:T(8,128)(2,1)}, bf16[2,256,1024]{2,1,0:T(8,128)(2,1)}, bf16[2,256,1024]{2,1,0:T(8,128)(2,1)}, bf16[2,256,1024]{2,1,0:T(8,128)(2,1)}) custom-call(s32[3]{0:T(128)S(1)} %pad_add_fusion.1.where_ref, bf16[512,2048]{1,0:T(8,128)(2,1)S(1)} %copy-done.24, bf16[512,2048]{1,0:T(8,128)(2,1)S(1)} %collective-permute-done.33.refs_1_, ...), custom_call_target="tpu_custom_call" | custom-call | flops 1 | bytes 1 | tf_op jit(solution)/shard_map/attn_outer/pallas_call | solution.py:1011
  403.8 4.3 collective-permute-done.30.above_ref
  415.1 21.8 %collective-permute-done.38.refs_1_ = bf16[2,256,1024]{2,1,0:T(8,128)(2,1)S(1)} collective-permute-done((bf16[2,256,1024]{2,1,0:T(8,128)(2,1)S(1)}, bf16[2,256,1024]{2,1,0:T(8,128)(2,1)S(1)}, u32[]{:S(2)}, u32[]{:S(2)}) %collective-permute-start.38) | collective-permute-done | bytes 1048608 | tf_op jit(solution)/shard_map/ppermute | solution.py:1037
  448.7 6.3 %collective-permute-done.45.refs_5_ = bf16[256,1024]{1,0:T(8,128)(2,1)S(1)} collective-permute-done((bf16[256,1024]{1,0:T(8,128)(2,1)S(1)}, bf16[256,1024]{1,0:T(8,128)(2,1)S(1)}, u32[]{:S(2)}, u32[]{:S(2)}) %collective-permute-start.45) | collective-permute-done | bytes 524320 | tf_op jit(solution)/shard_map/ppermute | solution.py:1037
  455.6 3.5 collective-permute-done.44.refs_2_
  459.1 3.4 collective-permute-done.43.refs_5_
  462.6 3.7 collective-permute-done.42.refs_2_
  472.2 3.5 widen_down.1
  475.7 3.3 widen_up.1
  479.1 3.3 widen_gate.1
  484.6 8.0 %collective-permute-done.47.refs_2_ = bf16[272,2048]{1,0:T(8,128)(2,1)S(1)} collective-permute-done((bf16[272,2048]{1,0:T(8,128)(2,1)S(1)}, bf16[272,2048]{1,0:T(8,128)(2,1)S(1)}, u32[]{:S(2)}, u32[]{:S(2)}) %collective-permute-start.47) | collective-permute-done | bytes 1114144 | tf_op jit(solution)/shard_map/ppermute | solution.py:888
  492.6 3.8 join.1
  (293 shorter events, 119.2 us)
Async XLA Ops:
  7.2 60.5 %all-gather.4.cloned.1.call-start = ((), (), s32[]{:S(2)}) async-start(), calls=%async_computation.8 | async-start | bytes 3276800 | tf_op jit(solution)/shard_map/all_gather | solution.py:1237
  21.9 29.5 %all-to-all-start = ((bf16[4,512,384]{2,1,0:T(8,128)(2,1)}), bf16[4,512,384]{2,1,0:T(8,128)(2,1)}, u32[]{:S(2)}, u32[]{:S(2)}) async-start(bf16[4,512,384]{2,1,0:T(8,128)(2,1)} %copy-done.33), calls=%async_computation | async-start | bytes 3145728 | tf_op jit(solution)/shard_map/all_to_all | solution.py:1221
  27.2 89.7 %all-gather.6.cloned.1.call-start = ((), (), s32[]{:S(2)}) async-start(), calls=%async_computation.9 | async-start | bytes 1966080 | tf_op jit(solution)/shard_map/all_gather | solution.py:1237
  67.7 13.1 %all-to-all-start.1 = ((bf16[4,512,128]{2,1,0:T(8,128)(2,1)}), bf16[4,512,128]{2,1,0:T(8,128)(2,1)S(1)}, u32[]{:S(2)}, u32[]{:S(2)}) async-start(bf16[4,512,128]{2,1,0:T(8,128)(2,1)} %bitcast.116), calls=%async_computation.1 | async-start | bytes 1048576 | tf_op jit(solution)/shard_map/all_to_all | solution.py:1221
  71.7 46.0 %collective-permute-start.1 = (bf16[4,256,1280]{2,1,0:T(8,128)(2,1)}, bf16[4,256,1280]{2,1,0:T(8,128)(2,1)}, u32[]{:S(2)}, u32[]{:S(2)}) collective-permute-start(bf16[4,256,1280]{2,1,0:T(8,128)(2,1)} %bitcast.105), channel_id=1, source_target_pairs={{0,4},{4,0},{8,12},{12,8},{16,20},{20,16},{24,28},{28,24},{1,5},{5... | collective-permute-start | bytes 7864328 | tf_op jit(solution)/shard_map/ppermute | solution.py:1218
  82.5 34.4 %all-to-all-start.2 = ((bf16[4,128,512]{2,1,0:T(8,128)(2,1)}), bf16[4,128,512]{2,1,0:T(8,128)(2,1)S(1)}, u32[]{:S(2)}, u32[]{:S(2)}) async-start(bf16[4,128,512]{2,1,0:T(8,128)(2,1)} %pad_maximum_fusion.3), calls=%async_computation.2 | async-start | bytes 1048576 | tf_op jit(solution)/shard_map/all_to_all | solution.py:1292
  129.4 13.0 %collective-permute-start.4 = (bf16[128,2048]{1,0:T(8,128)(2,1)S(1)}, bf16[128,2048]{1,0:T(8,128)(2,1)S(1)}, u32[]{:S(2)}, u32[]{:S(2)}) collective-permute-start(bf16[128,2048]{1,0:T(8,128)(2,1)S(1)} %get-tuple-element.168.refs_0_), channel_id=1, source_target_pairs={{0,1},{1,2},{2,3},{4,5},{5,6},{6,7},{8,9},{9,10},{10,11},{12,13},{... | collective-permute-start | bytes 1572872 | tf_op jit(solution)/shard_map/ppermute | solution.py:887
  130.8 15.9 %collective-permute-start.3 = (bf16[128,2048]{1,0:T(8,128)(2,1)S(1)}, bf16[128,2048]{1,0:T(8,128)(2,1)S(1)}, u32[]{:S(2)}, u32[]{:S(2)}) collective-permute-start(bf16[128,2048]{1,0:T(8,128)(2,1)S(1)} %get-tuple-element.168.refs_0_), channel_id=1, source_target_pairs={{1,0},{2,1},{3,2},{5,4},{6,5},{7,6},{9,8},{10,9},{11,10},{13,12},{... | collective-permute-start | bytes 1572872 | tf_op jit(solution)/shard_map/ppermute | solution.py:888
  142.5 19.4 %collective-permute-start.5 = (bf16[128,2048]{1,0:T(8,128)(2,1)S(1)}, bf16[128,2048]{1,0:T(8,128)(2,1)S(1)}, u32[]{:S(2)}, u32[]{:S(2)}) collective-permute-start(bf16[128,2048]{1,0:T(8,128)(2,1)S(1)} %collective-permute-done.4.refs_2_.refs_1_), channel_id=1, source_target_pairs={{1,2},{2,3},{5,6},{6,7},{9,10},{10,11},{13,14},{14,15},{17,18},{18... | collective-permute-start | bytes 1572872 | tf_op jit(solution)/shard_map/ppermute | solution.py:887
  146.6 15.3 %collective-permute-start.6 = (bf16[128,2048]{1,0:T(8,128)(2,1)S(1)}, bf16[128,2048]{1,0:T(8,128)(2,1)S(1)}, u32[]{:S(2)}, u32[]{:S(2)}) collective-permute-start(bf16[128,2048]{1,0:T(8,128)(2,1)S(1)} %collective-permute-done.3.refs_1_.refs_0_), channel_id=1, source_target_pairs={{1,0},{2,1},{5,4},{6,5},{9,8},{10,9},{13,12},{14,13},{17,16},{18,1... | collective-permute-start | bytes 1572872 | tf_op jit(solution)/shard_map/ppermute | solution.py:888
  161.9 14.0 %collective-permute-start.7 = (bf16[128,2048]{1,0:T(8,128)(2,1)S(1)}, bf16[128,2048]{1,0:T(8,128)(2,1)S(1)}, u32[]{:S(2)}, u32[]{:S(2)}) collective-permute-start(bf16[128,2048]{1,0:T(8,128)(2,1)S(1)} %collective-permute-done.5.refs_1_), channel_id=1, source_target_pairs={{2,3},{6,7},{10,11},{14,15},{18,19},{22,23},{26,27},{30,31}} | collective-permute-start | bytes 1572872 | tf_op jit(solution)/shard_map/ppermute | solution.py:887
  162.6 15.0 %collective-permute-start.8 = (bf16[128,2048]{1,0:T(8,128)(2,1)S(1)}, bf16[128,2048]{1,0:T(8,128)(2,1)S(1)}, u32[]{:S(2)}, u32[]{:S(2)}) collective-permute-start(bf16[128,2048]{1,0:T(8,128)(2,1)S(1)} %collective-permute-done.6.refs_0_), channel_id=1, source_target_pairs={{1,0},{5,4},{9,8},{13,12},{17,16},{21,20},{25,24},{29,28}} | collective-permute-start | bytes 1572872 | tf_op jit(solution)/shard_map/ppermute | solution.py:888
  177.6 24.3 %collective-permute-start.10 = (bf16[128,2048]{1,0:T(8,128)(2,1)S(1)}, bf16[128,2048]{1,0:T(8,128)(2,1)S(1)}, u32[]{:S(2)}, u32[]{:S(2)}) collective-permute-start(bf16[128,2048]{1,0:T(8,128)(2,1)S(1)} %get-tuple-element.195), channel_id=1, source_target_pairs={{0,2},{1,3},{2,0},{3,1},{4,6},{5,7},{6,4},{7,5},{8,10},{9,11},{10,... | collective-permute-start | bytes 1572872 | tf_op jit(solution)/shard_map/ppermute | solution.py:1230
  178.9 23.0 %collective-permute-start.9 = (bf16[128,2048]{1,0:T(8,128)(2,1)S(1)}, bf16[128,2048]{1,0:T(8,128)(2,1)S(1)}, u32[]{:S(2)}, u32[]{:S(2)}) collective-permute-start(bf16[128,2048]{1,0:T(8,128)(2,1)S(1)} %get-tuple-element.194), channel_id=1, source_target_pairs={{0,1},{1,0},{2,3},{3,2},{4,5},{5,4},{6,7},{7,6},{8,9},{9,8},{10,11... | collective-permute-start | bytes 1572872 | tf_op jit(solution)/shard_map/ppermute | solution.py:1230
  202.0 21.4 %collective-permute-start.12 = (bf16[512,2048]{1,0:T(8,128)(2,1)S(1)}, bf16[512,2048]{1,0:T(8,128)(2,1)S(1)}, u32[]{:S(2)}, u32[]{:S(2)}) collective-permute-start(bf16[512,2048]{1,0:T(8,128)(2,1)S(1)} %copy-done.8), channel_id=1, source_target_pairs={{0,4},{4,0},{8,12},{12,8},{16,20},{20,16},{24,28},{28,24},{1,5},{5... | collective-permute-start | bytes 6291464 | tf_op jit(solution)/shard_map/ppermute | solution.py:1218
  202.5 21.5 %collective-permute-start.13 = (bf16[512,2048]{1,0:T(8,128)(2,1)S(1)}, bf16[512,2048]{1,0:T(8,128)(2,1)S(1)}, u32[]{:S(2)}, u32[]{:S(2)}) collective-permute-start(bf16[512,2048]{1,0:T(8,128)(2,1)S(1)} %get-tuple-element.215.refs_2_.left_ref), channel_id=1, source_target_pairs={{0,4},{4,0},{8,12},{12,8},{16,20},{20,16},{24,28},{28,24},{1,5},{5... | collective-permute-start | bytes 6291464 | tf_op jit(solution)/shard_map/ppermute | solution.py:1218
  202.5 30.2 %collective-permute-start.11 = (bf16[128,2048]{1,0:T(8,128)(2,1)S(1)}, bf16[128,2048]{1,0:T(8,128)(2,1)S(1)}, u32[]{:S(2)}, u32[]{:S(2)}) collective-permute-start(bf16[128,2048]{1,0:T(8,128)(2,1)S(1)} %get-tuple-element.198), channel_id=1, source_target_pairs={{0,3},{1,2},{2,1},{3,0},{4,7},{5,6},{6,5},{7,4},{8,11},{9,10},{10,... | collective-permute-start | bytes 1572872 | tf_op jit(solution)/shard_map/ppermute | solution.py:1230
  212.1 46.7 %collective-permute-start.19 = (bf16[2,256,1024]{2,1,0:T(8,128)(2,1)}, bf16[2,256,1024]{2,1,0:T(8,128)(2,1)}, u32[]{:S(2)}, u32[]{:S(2)}) collective-permute-start(bf16[2,256,1024]{2,1,0:T(8,128)(2,1)} %get-tuple-element.211), channel_id=1, source_target_pairs={{0,8},{4,12},{8,0},{12,4},{16,24},{20,28},{24,16},{28,20},{1,9},{5... | collective-permute-start | bytes 3145736 | tf_op jit(solution)/shard_map/ppermute | solution.py:1037
  213.6 45.2 %collective-permute-start.20 = (bf16[2,256,1024]{2,1,0:T(8,128)(2,1)}, bf16[2,256,1024]{2,1,0:T(8,128)(2,1)}, u32[]{:S(2)}, u32[]{:S(2)}) collective-permute-start(bf16[2,256,1024]{2,1,0:T(8,128)(2,1)} %get-tuple-element.212), channel_id=1, source_target_pairs={{0,16},{4,20},{8,24},{12,28},{16,0},{20,4},{24,8},{28,12},{1,17},{... | collective-permute-start | bytes 3145736 | tf_op jit(solution)/shard_map/ppermute | solution.py:1037
  223.4 36.8 %collective-permute-start.16 = (bf16[2,256,1024]{2,1,0:T(8,128)(2,1)}, bf16[2,256,1024]{2,1,0:T(8,128)(2,1)}, u32[]{:S(2)}, u32[]{:S(2)}) collective-permute-start(bf16[2,256,1024]{2,1,0:T(8,128)(2,1)} %get-tuple-element.208), channel_id=1, source_target_pairs={{0,8},{4,12},{8,0},{12,4},{16,24},{20,28},{24,16},{28,20},{1,9},{5... | collective-permute-start | bytes 3145736 | tf_op jit(solution)/shard_map/ppermute | solution.py:1037
  223.9 37.4 %collective-permute-start.17 = (bf16[2,256,1024]{2,1,0:T(8,128)(2,1)}, bf16[2,256,1024]{2,1,0:T(8,128)(2,1)}, u32[]{:S(2)}, u32[]{:S(2)}) collective-permute-start(bf16[2,256,1024]{2,1,0:T(8,128)(2,1)} %get-tuple-element.209), channel_id=1, source_target_pairs={{0,16},{4,20},{8,24},{12,28},{16,0},{20,4},{24,8},{28,12},{1,17},{... | collective-permute-start | bytes 3145736 | tf_op jit(solution)/shard_map/ppermute | solution.py:1037
  240.6 18.2 %all-to-all-start.3 = ((bf16[4,128,512]{2,1,0:T(8,128)(2,1)}), bf16[4,128,512]{2,1,0:T(8,128)(2,1)}, u32[]{:S(2)}, u32[]{:S(2)}) async-start(bf16[4,128,512]{2,1,0:T(8,128)(2,1)} %copy-done.43), calls=%async_computation.3 | async-start | bytes 1048576 | tf_op jit(solution)/shard_map/all_to_all | solution.py:1346
  244.8 82.1 %reduce-scatter.2.cloned.1.call-start = ((), (), s32[]{:S(2)}) async-start(), calls=%async_computation.10 | async-start | bytes 2621440 | tf_op jit(solution)/shard_map/reduce_scatter | solution.py:1350
  267.6 107.9 %all-gather.8.cloned.1.call-start = ((), (), s32[]{:S(2)}) async-start(), calls=%async_computation.11 | async-start | bytes 2621440 | tf_op jit(solution)/shard_map/all_gather | solution.py:1360
  302.4 24.5 %all-to-all-start.5 = ((bf16[4,512,384]{2,1,0:T(8,128)(2,1)}), bf16[4,512,384]{2,1,0:T(8,128)(2,1)}, u32[]{:S(2)}, u32[]{:S(2)}) async-start(bf16[4,512,384]{2,1,0:T(8,128)(2,1)} %bitcast.112), calls=%async_computation.5 | async-start | bytes 3145728 | tf_op jit(solution)/shard_map/all_to_all | solution.py:1221
  335.4 24.8 %collective-permute-start.25 = (bf16[2,256,1024]{2,1,0:T(8,128)(2,1)S(1)}, bf16[2,256,1024]{2,1,0:T(8,128)(2,1)}, u32[]{:S(2)}, u32[]{:S(2)}) collective-permute-start(bf16[2,256,1024]{2,1,0:T(8,128)(2,1)S(1)} %copy-done.53), channel_id=1, source_target_pairs={{0,8},{4,12},{8,0},{12,4},{16,24},{20,28},{24,16},{28,20},{1,9},{5... | collective-permute-start | bytes 3145736 | tf_op jit(solution)/shard_map/ppermute | solution.py:1037
  336.9 24.4 %collective-permute-start.26 = (bf16[2,256,1024]{2,1,0:T(8,128)(2,1)S(1)}, bf16[2,256,1024]{2,1,0:T(8,128)(2,1)}, u32[]{:S(2)}, u32[]{:S(2)}) collective-permute-start(bf16[2,256,1024]{2,1,0:T(8,128)(2,1)S(1)} %copy-done.52), channel_id=1, source_target_pairs={{0,16},{4,20},{8,24},{12,28},{16,0},{20,4},{24,8},{28,12},{1,17},{... | collective-permute-start | bytes 3145736 | tf_op jit(solution)/shard_map/ppermute | solution.py:1037
  337.5 21.4 %collective-permute-start.23 = (bf16[128,2048]{1,0:T(8,128)(2,1)S(1)}, bf16[128,2048]{1,0:T(8,128)(2,1)S(1)}, u32[]{:S(2)}, u32[]{:S(2)}) collective-permute-start(bf16[128,2048]{1,0:T(8,128)(2,1)S(1)} %get-tuple-element.228.down_ref), channel_id=1, source_target_pairs={{0,1},{4,5},{8,9},{12,13},{16,17},{20,21},{24,25},{28,29}} | collective-permute-start | bytes 1572872 | tf_op jit(solution)/shard_map/ppermute | solution.py:887
  341.3 17.6 %collective-permute-start.24 = (bf16[128,2048]{1,0:T(8,128)(2,1)S(1)}, bf16[128,2048]{1,0:T(8,128)(2,1)S(1)}, u32[]{:S(2)}, u32[]{:S(2)}) collective-permute-start(bf16[128,2048]{1,0:T(8,128)(2,1)S(1)} %get-tuple-element.229.up_ref), channel_id=1, source_target_pairs={{3,2},{7,6},{11,10},{15,14},{19,18},{23,22},{27,26},{31,30}} | collective-permute-start | bytes 1572872 | tf_op jit(solution)/shard_map/ppermute | solution.py:888
  362.5 13.2 %collective-permute-start.27 = (bf16[128,2048]{1,0:T(8,128)(2,1)}, bf16[128,2048]{1,0:T(8,128)(2,1)}, u32[]{:S(2)}, u32[]{:S(2)}) collective-permute-start(bf16[128,2048]{1,0:T(8,128)(2,1)} %get-tuple-element.237), channel_id=1, source_target_pairs={{0,1},{1,2},{4,5},{5,6},{8,9},{9,10},{12,13},{13,14},{16,17},{17,1... | collective-permute-start | bytes 1572872 | tf_op jit(solution)/shard_map/ppermute | solution.py:887
  367.9 16.8 %collective-permute-start.34 = (bf16[512,2048]{1,0:T(8,128)(2,1)}, bf16[512,2048]{1,0:T(8,128)(2,1)}, u32[]{:S(2)}, u32[]{:S(2)}) collective-permute-start(bf16[512,2048]{1,0:T(8,128)(2,1)} %get-tuple-element.257.refs_4_), channel_id=1, source_target_pairs={{0,4},{4,0},{8,12},{12,8},{16,20},{20,16},{24,28},{28,24},{1,5},{5... | collective-permute-start | bytes 6291464 | tf_op jit(solution)/shard_map/ppermute | solution.py:1218
  375.7 18.9 %collective-permute-start.33 = (bf16[512,2048]{1,0:T(8,128)(2,1)}, bf16[512,2048]{1,0:T(8,128)(2,1)S(1)}, u32[]{:S(2)}, u32[]{:S(2)}) collective-permute-start(bf16[512,2048]{1,0:T(8,128)(2,1)} %all-gather.8.cloned.1.call-done.refs_0_), channel_id=1, source_target_pairs={{0,4},{4,0},{8,12},{12,8},{16,20},{20,16},{24,28},{28,24},{1,5},{5... | collective-permute-start | bytes 6291464 | tf_op jit(solution)/shard_map/ppermute | solution.py:1218
  375.7 17.4 %collective-permute-start.35 = (bf16[512,1536]{1,0:T(8,128)(2,1)}, bf16[512,1536]{1,0:T(8,128)(2,1)S(1)}, u32[]{:S(2)}, u32[]{:S(2)}) collective-permute-start(bf16[512,1536]{1,0:T(8,128)(2,1)} %copy-done.31), channel_id=1, source_target_pairs={{0,4},{4,0},{8,12},{12,8},{16,20},{20,16},{24,28},{28,24},{1,5},{5... | collective-permute-start | bytes 4718600 | tf_op jit(solution)/shard_map/ppermute | solution.py:1218
  377.7 26.0 %collective-permute-start.32 = (bf16[256,1024]{1,0:T(8,128)(2,1)S(1)}, bf16[256,1024]{1,0:T(8,128)(2,1)S(1)}, u32[]{:S(2)}, u32[]{:S(2)}) collective-permute-start(bf16[256,1024]{1,0:T(8,128)(2,1)S(1)} %fusion.1), channel_id=1, source_target_pairs={{0,8},{4,12},{8,0},{12,4},{16,24},{20,28},{24,16},{28,20},{1,9},{5... | collective-permute-start | bytes 1572872 | tf_op jit(solution)/shard_map/ppermute | solution.py:1037
  380.5 23.2 %collective-permute-start.31 = (bf16[256,1024]{1,0:T(8,128)(2,1)S(1)}, bf16[256,1024]{1,0:T(8,128)(2,1)S(1)}, u32[]{:S(2)}, u32[]{:S(2)}) collective-permute-start(bf16[256,1024]{1,0:T(8,128)(2,1)S(1)} %fusion), channel_id=1, source_target_pairs={{0,16},{4,20},{8,24},{12,28},{16,0},{20,4},{24,8},{28,12},{1,17},{... | collective-permute-start | bytes 1572872 | tf_op jit(solution)/shard_map/ppermute | solution.py:1037
  384.7 19.1 %collective-permute-start.29 = (bf16[128,2048]{1,0:T(8,128)(2,1)S(1)}, bf16[128,2048]{1,0:T(8,128)(2,1)S(1)}, u32[]{:S(2)}, u32[]{:S(2)}) collective-permute-start(bf16[128,2048]{1,0:T(8,128)(2,1)S(1)} %get-tuple-element.247), channel_id=1, source_target_pairs={{0,1},{1,2},{2,3},{4,5},{5,6},{6,7},{8,9},{9,10},{10,11},{12,13},{... | collective-permute-start | bytes 1572872 | tf_op jit(solution)/shard_map/ppermute | solution.py:887
  393.1 15.0 %collective-permute-start.30 = (bf16[128,2048]{1,0:T(8,128)(2,1)S(1)}, bf16[128,2048]{1,0:T(8,128)(2,1)S(1)}, u32[]{:S(2)}, u32[]{:S(2)}) collective-permute-start(bf16[128,2048]{1,0:T(8,128)(2,1)S(1)} %get-tuple-element.248), channel_id=1, source_target_pairs={{1,0},{2,1},{3,2},{5,4},{6,5},{7,6},{9,8},{10,9},{11,10},{13,12},{... | collective-permute-start | bytes 1572872 | tf_op jit(solution)/shard_map/ppermute | solution.py:888
  409.8 27.4 %collective-permute-start.36 = (bf16[272,2048]{1,0:T(8,128)(2,1)S(1)}, bf16[272,2048]{1,0:T(8,128)(2,1)S(1)}, u32[]{:S(2)}, u32[]{:S(2)}) collective-permute-start(bf16[272,2048]{1,0:T(8,128)(2,1)S(1)} %tokens.1.own_ref), channel_id=1, source_target_pairs={{0,1},{1,2},{2,3},{4,5},{5,6},{6,7},{8,9},{9,10},{10,11},{12,13},{... | collective-permute-start | bytes 3342344 | tf_op jit(solution)/shard_map/ppermute | solution.py:887
  412.2 26.6 %collective-permute-start.37 = (bf16[272,2048]{1,0:T(8,128)(2,1)S(1)}, bf16[272,2048]{1,0:T(8,128)(2,1)S(1)}, u32[]{:S(2)}, u32[]{:S(2)}) collective-permute-start(bf16[272,2048]{1,0:T(8,128)(2,1)S(1)} %tokens.1.own_ref), channel_id=1, source_target_pairs={{1,0},{2,1},{3,2},{5,4},{6,5},{7,6},{9,8},{10,9},{11,10},{13,12},{... | collective-permute-start | bytes 3342344 | tf_op jit(solution)/shard_map/ppermute | solution.py:888
  413.5 23.4 %collective-permute-start.38 = (bf16[2,256,1024]{2,1,0:T(8,128)(2,1)S(1)}, bf16[2,256,1024]{2,1,0:T(8,128)(2,1)S(1)}, u32[]{:S(2)}, u32[]{:S(2)}) collective-permute-start(bf16[2,256,1024]{2,1,0:T(8,128)(2,1)S(1)} %copy-done.55), channel_id=1, source_target_pairs={{0,8},{4,12},{8,0},{12,4},{16,24},{20,28},{24,16},{28,20},{1,9},{5... | collective-permute-start | bytes 3145736 | tf_op jit(solution)/shard_map/ppermute | solution.py:1037
  414.3 22.9 %collective-permute-start.39 = (bf16[2,256,1024]{2,1,0:T(8,128)(2,1)S(1)}, bf16[2,256,1024]{2,1,0:T(8,128)(2,1)S(1)}, u32[]{:S(2)}, u32[]{:S(2)}) collective-permute-start(bf16[2,256,1024]{2,1,0:T(8,128)(2,1)S(1)} %copy-done.54), channel_id=1, source_target_pairs={{0,16},{4,20},{8,24},{12,28},{16,0},{20,4},{24,8},{28,12},{1,17},{... | collective-permute-start | bytes 3145736 | tf_op jit(solution)/shard_map/ppermute | solution.py:1037
  440.1 14.9 %collective-permute-start.45 = (bf16[256,1024]{1,0:T(8,128)(2,1)S(1)}, bf16[256,1024]{1,0:T(8,128)(2,1)S(1)}, u32[]{:S(2)}, u32[]{:S(2)}) collective-permute-start(bf16[256,1024]{1,0:T(8,128)(2,1)S(1)} %fusion.5), channel_id=1, source_target_pairs={{0,8},{4,12},{8,0},{12,4},{16,24},{20,28},{24,16},{28,20},{1,9},{5... | collective-permute-start | bytes 1572872 | tf_op jit(solution)/shard_map/ppermute | solution.py:1037
  440.8 25.5 %collective-permute-start.40 = (bf16[272,2048]{1,0:T(8,128)(2,1)S(1)}, bf16[272,2048]{1,0:T(8,128)(2,1)S(1)}, u32[]{:S(2)}, u32[]{:S(2)}) collective-permute-start(bf16[272,2048]{1,0:T(8,128)(2,1)S(1)} %collective-permute-done.36.refs_3_), channel_id=1, source_target_pairs={{1,2},{2,3},{5,6},{6,7},{9,10},{10,11},{13,14},{14,15},{17,18},{18... | collective-permute-start | bytes 3342344 | tf_op jit(solution)/shard_map/ppermute | solution.py:887
  441.5 26.2 %collective-permute-start.41 = (bf16[272,2048]{1,0:T(8,128)(2,1)S(1)}, bf16[272,2048]{1,0:T(8,128)(2,1)S(1)}, u32[]{:S(2)}, u32[]{:S(2)}) collective-permute-start(bf16[272,2048]{1,0:T(8,128)(2,1)S(1)} %collective-permute-done.37.refs_0_), channel_id=1, source_target_pairs={{1,0},{2,1},{5,4},{6,5},{9,8},{10,9},{13,12},{14,13},{17,16},{18,1... | collective-permute-start | bytes 3342344 | tf_op jit(solution)/shard_map/ppermute | solution.py:888
  444.2 14.9 %collective-permute-start.44 = (bf16[256,1024]{1,0:T(8,128)(2,1)S(1)}, bf16[256,1024]{1,0:T(8,128)(2,1)S(1)}, u32[]{:S(2)}, u32[]{:S(2)}) collective-permute-start(bf16[256,1024]{1,0:T(8,128)(2,1)S(1)} %fusion.4), channel_id=1, source_target_pairs={{0,16},{4,20},{8,24},{12,28},{16,0},{20,4},{24,8},{28,12},{1,17},{... | collective-permute-start | bytes 1572872 | tf_op jit(solution)/shard_map/ppermute | solution.py:1037
  446.4 16.1 %collective-permute-start.43 = (bf16[256,1024]{1,0:T(8,128)(2,1)S(1)}, bf16[256,1024]{1,0:T(8,128)(2,1)S(1)}, u32[]{:S(2)}, u32[]{:S(2)}) collective-permute-start(bf16[256,1024]{1,0:T(8,128)(2,1)S(1)} %fusion.3), channel_id=1, source_target_pairs={{0,8},{4,12},{8,0},{12,4},{16,24},{20,28},{24,16},{28,20},{1,9},{5... | collective-permute-start | bytes 1572872 | tf_op jit(solution)/shard_map/ppermute | solution.py:1037
  467.7 16.9 %collective-permute-start.46 = (bf16[272,2048]{1,0:T(8,128)(2,1)S(1)}, bf16[272,2048]{1,0:T(8,128)(2,1)S(1)}, u32[]{:S(2)}, u32[]{:S(2)}) collective-permute-start(bf16[272,2048]{1,0:T(8,128)(2,1)S(1)} %collective-permute-done.40.refs_4_), channel_id=1, source_target_pairs={{2,3},{6,7},{10,11},{14,15},{18,19},{22,23},{26,27},{30,31}} | collective-permute-start | bytes 3342344 | tf_op jit(solution)/shard_map/ppermute | solution.py:887
  468.4 24.2 %collective-permute-start.47 = (bf16[272,2048]{1,0:T(8,128)(2,1)S(1)}, bf16[272,2048]{1,0:T(8,128)(2,1)S(1)}, u32[]{:S(2)}, u32[]{:S(2)}) collective-permute-start(bf16[272,2048]{1,0:T(8,128)(2,1)S(1)} %collective-permute-done.41.refs_1_), channel_id=1, source_target_pairs={{1,0},{5,4},{9,8},{13,12},{17,16},{21,20},{25,24},{29,28}} | collective-permute-start | bytes 3342344 | tf_op jit(solution)/shard_map/ppermute | solution.py:888
  (68 other events, 699.1 us)
Sparse Core Ops, SparseCore 0:
  10.2 57.5 all-gather.3
  69.9 47.0 all-gather.5
  261.5 42.9 reduce-scatter.1
  306.0 49.2 all-gather.7

commit v7 on v6

--- a/solution.py
+++ b/solution.py
@@ -1328,8 +1328,7 @@
     gate_sum.first()
     up_sum = ChipSum(outer_ffn([up_quad]), seq_size)
     up_sum.first()
-    down_sum = ChipSum(outer_ffn([down_quad]), seq_size)
-    grad_3, *down_sum.arrays = tie(grad_3, *down_sum.arrays)
+    grad_3 = after(grad_3, up_sum.arrays[0])
     middle_low, grad_middle, grad_attended, gain_ffn_part = call(
         middle_kernel,
         (
@@ -1345,7 +1344,11 @@
     )
     grad_attended = lax.all_to_all(grad_attended, "tp", 0, 0, tiled=True)
     branch = matmul_call(where, after(activated, middle_low), w_down, bf16, False, "branch", tp_size)
-    grad_attended, branch = up_sum.tie(*gate_sum.tie(grad_attended, branch))
+    down_quad = (after(down_quad[0], middle_low), *down_quad[1:])
+    down_sum = ChipSum(outer_ffn([down_quad]), seq_size)
+    grad_attended, branch, *down_sum.arrays = up_sum.tie(
+        *gate_sum.tie(grad_attended, branch, *down_sum.arrays)
+    )
     branch = after(branch, grad_attended)
     branch_part = lax.psum_scatter(branch, "tp", scatter_dimension=0, tiled=True)
     grad_attended = grad_attended.reshape(row_count, own_width)

time: 514 us -> 519 us (level)
  waiting for transfers between devices: 176 us -> 163 us
  Pallas kernels: 164 us -> 176 us
  starting transfers between devices: 83.2 us -> 88.6 us
    unnamed x121 -> x123, local copies, waits for them, and re-layouts: 22.6 us -> 24.3 us
  transfers between devices with their start and end apart: 60 -> 60, of which waited for: 29 -> 25; matrix products, arithmetic and copies ran while one was open for 6% -> 6% of each run, Pallas kernels for 30% -> 32%
where the time goes in v7:
time: 519 us; the launch traced here: 509 us
  Pallas kernels  176 us (34%)
  waiting for transfers between devices  163 us (31%)
  starting transfers between devices  88.6 us (17%)
  local copies, waits for them, and re-layouts  36.8 us (7%)
  other arithmetic  23.1 us (4%)
  between operations  15.1 us (3%)
  blocking collectives  7.45 us (1%)
    ppermute x16, waiting for transfers between devices, over(): lax.ppermute(values, 'seq', [(i, i ^ side) for i in range(self.size)])  43.8 us
    pallas_call x3, Pallas kernels, ffn_call(): pl.pallas_call(functools.partial(ffn_kernel, chunk=chunk, sources=len(sou...  39.8 us
    pallas_call x4, Pallas kernels, chip_outer_call(): pl.pallas_call(functools.partial(chip_outer_kernel, sides=len(pairs)), ou...  35.7 us
    all_gather x2, waiting for transfers between devices, gathered(): values = lax.all_gather(columns, 'tp', axis=0, tiled=True)  30.1 us
    all_to_all x4, waiting for transfers between devices, to_heads(): lax.all_to_all(values, 'seq', 0, 0, axis_index_groups=same_core, tiled=True)  30 us
    pallas_call x10, Pallas kernels, call(): pl.pallas_call(kernel, out_shape=tuple(outs), in_specs=[SMALL] * scalars...  25.8 us
    unnamed x123, local copies, waits for them, and re-layouts  24.3 us
    ppermute x9, starting transfers between devices, send(): self.upward = lax.ppermute(up, self.axis, up_pairs)  23.7 us
  transfers between devices with their start and end apart: 60, of which 25 were waited for; matrix products, arithmetic and copies ran while one was open for 6% of the time, Pallas kernels for 32%

profile of v7, /device:TPU:0, one launch (start us, length us, event | category | flops | bytes accessed | tf_op | source)
XLA Modules:
  0.0 509.4 jit_solution(16718819264841092437)
XLA Ops:
  13.3 7.4 %project.1 = (bf16[4,512,384]{2,1,0:T(8,128)(2,1)S(1)}, bf16[512,2048]{1,0:T(8,128)(2,1)}) custom-call(bf16[512,2048]{1,0:T(8,128)(2,1)S(1)} %bitcast.101, f32[1,2048]{1,0:T(1,128)S(1)} %bitcast.119, s32[512,1]{1,0:T(8,128)S(1)} %bitcast.114, f32[512,128]{1,0:T(8,128)S(1)} %get-tuple-element.354.cosine_ref, f32[512,128]{1,0:T(8,128)S(1)} %get-tuple-element.355.sine_ref, ...), custom_call_target="tpu_custom_call" | custom-call | flops 1 | bytes 1 | tf_op jit(solution)/shard_map/project/pallas_call | solution.py:482
  21.9 5.3 %all-to-all-start = ((bf16[4,512,384]{2,1,0:T(8,128)(2,1)}), bf16[4,512,384]{2,1,0:T(8,128)(2,1)}, u32[]{:S(2)}, u32[]{:S(2)}) async-start(bf16[4,512,384]{2,1,0:T(8,128)(2,1)} %copy-done.34), calls=%async_computation | async-start | bytes 3145728 | tf_op jit(solution)/shard_map/all_to_all | solution.py:1221
  33.5 7.9 %grad_act.1.refs_3_.refs_2_.refs_4_ = f32[512,2048]{1,0:T(8,128)S(1)} custom-call(s32[3]{0:T(128)S(1)} %pad_add_fusion.1.where_ref, bf16[512,2048]{1,0:T(8,128)(2,1)S(1)} %pad_maximum_fusion.left_ref.refs_0_, bf16[2048,2048]{1,0:T(8,128)(2,1)} %right_ref.3), custom_call_target="tpu_custom_call" | custom-call | flops 1 | bytes 1 | tf_op jit(solution)/shard_map/grad_act/pallas_call | solution.py:1132
  45.8 3.7 fusion.8
  55.3 12.4 %attend.1 = bf16[2048,128]{1,0:T(8,128)(2,1)S(1)} custom-call(s32[16]{0:T(128)S(1)} %pad_add_fusion.2.slot_places, s32[8]{0:T(128)S(1)} %get-tuple-element.326.key_low, bf16[2048,384]{1,0:T(8,128)(2,1)} %bitcast.12.own_ref, bf16[2048,384]{1,0:T(8,128)(2,1)} %collective-permute-done.other_ref, s32[2048,1]{1,0:T(8,128)S(1)} %bitcast.113), custom_call_target="tpu_custom_call" | custom-call | flops 1 | bytes 1 | tf_op jit(solution)/shard_map/attend/pallas_call | solution.py:438
  68.6 4.7 all-to-all-start.1
  73.4 6.5 %all-to-all-done.1 = bf16[4,512,128]{2,1,0:T(8,128)(2,1)S(1)} async-done(((bf16[4,512,128]{2,1,0:T(8,128)(2,1)}), bf16[4,512,128]{2,1,0:T(8,128)(2,1)S(1)}, u32[]{:S(2)}, u32[]{:S(2)}) %all-to-all-start.1) | async-done | bytes 524320 | tf_op jit(solution)/shard_map/all_to_all | solution.py:1221
  81.6 5.2 %all-to-all-start.2 = ((bf16[4,128,512]{2,1,0:T(8,128)(2,1)}), bf16[4,128,512]{2,1,0:T(8,128)(2,1)S(1)}, u32[]{:S(2)}, u32[]{:S(2)}) async-start(bf16[4,128,512]{2,1,0:T(8,128)(2,1)} %pad_maximum_fusion.3), calls=%async_computation.2 | async-start | bytes 1048576 | tf_op jit(solution)/shard_map/all_to_all | solution.py:1292
  86.9 30.1 %all-gather.6.cloned.1.call-done = bf16[1024,768]{1,0:T(8,128)(2,1)} async-done(((bf16[256,768]{1,0:T(8,128)(2,1)}), bf16[1024,768]{1,0:T(8,128)(2,1)}) %all-gather.6.cloned.1.call-update) | async-done | bytes 1572880 | tf_op jit(solution)/shard_map/all_gather | solution.py:1237
  117.8 3.6 collective-permute-done.2.refs_3_.refs_7_
  123.6 5.9 %out.1 = (f32[128,2048]{1,0:T(8,128)S(1)}, bf16[128,2048]{1,0:T(8,128)(2,1)S(1)}) custom-call(s32[3]{0:T(128)S(1)} %pad_add_fusion.1.where_ref, bf16[512,2048]{1,0:T(8,128)(2,1)S(1)} %bitcast.102, f32[1,2048]{1,0:T(1,128)S(1)} %bitcast.117, bf16[4,128,512]{2,1,0:T(8,128)(2,1)S(1)} %copy-done.27, bf16[4,256,1280]{2,1,0:T(8,128)(2,1)} %bitcast.106, ...), custom_call_target="tpu_custom_call" | custom-call | flops 1 | bytes 1 | tf_op jit(solution)/shard_map/out/pallas_call | solution.py:482
  132.1 10.4 %collective-permute-done.4.refs_2_.refs_1_ = bf16[128,2048]{1,0:T(8,128)(2,1)S(1)} collective-permute-done((bf16[128,2048]{1,0:T(8,128)(2,1)S(1)}, bf16[128,2048]{1,0:T(8,128)(2,1)S(1)}, u32[]{:S(2)}, u32[]{:S(2)}) %collective-permute-start.4) | collective-permute-done | bytes 524320 | tf_op jit(solution)/shard_map/ppermute | solution.py:887
  143.2 3.5 collective-permute-done.3.refs_1_.refs_0_
  147.9 14.5 %ffn.3 = (bf16[512,2048]{1,0:T(8,128)(2,1)}, bf16[512,2048]{1,0:T(8,128)(2,1)S(1)}, bf16[512,2048]{1,0:T(8,128)(2,1)S(1)}, bf16[512,2048]{1,0:T(8,128)(2,1)S(1)}...) custom-call(s32[3]{0:T(128)S(1)} %pad_add_fusion.1.where_ref, ...), custom_call_target="tpu_custom_call" | custom-call | flops 1 | bytes 1 | tf_op jit(solution)/shard_map/ffn/pallas_call | solution.py:693
  164.5 12.6 %ffn.4 = (bf16[512,2048]{1,0:T(8,128)(2,1)}, bf16[512,2048]{1,0:T(8,128)(2,1)S(1)}, bf16[512,2048]{1,0:T(8,128)(2,1)S(1)}, bf16[512,2048]{1,0:T(8,128)(2,1)S(1)}, bf16[128,2048]{1,0:T(8,128)(2,1)S(1)}) custom-call(s32[3]{0:T(128)S(1)} %pad_add_fusion.1.where_ref, ...), custom_call_target="tpu_custom_call", output_to_operand_aliasing={{0}: (6, {}), {1}: (7, {}), {2}: (8, {}), {3}: (9, {})} | custom-call | flops 1 | bytes 1 | tf_op jit(solution)/shard_map/ffn/pallas_call | solution.py:693
  180.0 12.6 %ffn.5 = (bf16[512,2048]{1,0:T(8,128)(2,1)}, bf16[512,2048]{1,0:T(8,128)(2,1)S(1)}, bf16[512,2048]{1,0:T(8,128)(2,1)S(1)}, bf16[512,2048]{1,0:T(8,128)(2,1)S(1)}, bf16[128,2048]{1,0:T(8,128)(2,1)S(1)}) custom-call(s32[3]{0:T(128)S(1)} %pad_add_fusion.1.where_ref, ...), custom_call_target="tpu_custom_call", output_to_operand_aliasing={{0}: (8, {}), {1}: (9, {}), {2}: (10, {}), {3}: (11, {})} | custom-call | flops 1 | bytes 1 | tf_op jit(solution)/shard_map/ffn/pallas_call | solution.py:693
  193.2 9.4 %collective-permute-done.10.refs_2_ = bf16[128,2048]{1,0:T(8,128)(2,1)S(1)} collective-permute-done((bf16[128,2048]{1,0:T(8,128)(2,1)S(1)}, bf16[128,2048]{1,0:T(8,128)(2,1)S(1)}, u32[]{:S(2)}, u32[]{:S(2)}) %collective-permute-start.10) | collective-permute-done | bytes 524320 | tf_op jit(solution)/shard_map/ppermute | solution.py:1230
  205.2 8.1 %ffn_outer.4 = (bf16[2,256,1024]{2,1,0:T(8,128)(2,1)}, bf16[2,256,1024]{2,1,0:T(8,128)(2,1)}, bf16[2,256,1024]{2,1,0:T(8,128)(2,1)}, bf16[2,256,1024]{2,1,0:T(8,128)(2,1)}) custom-call(s32[3]{0:T(128)S(1)} %pad_add_fusion.1.where_ref, bf16[512,2048]{1,0:T(8,128)(2,1)S(1)} %get-tuple-element.204.refs_0_, ...), custom_call_target="tpu_custom_call" | custom-call | flops 1 | bytes 1 | tf_op jit(solution)/shard_map/ffn_outer/pallas_call | solution.py:1011
  216.3 8.2 %ffn_outer.3 = (bf16[2,256,1024]{2,1,0:T(8,128)(2,1)}, bf16[2,256,1024]{2,1,0:T(8,128)(2,1)}, bf16[2,256,1024]{2,1,0:T(8,128)(2,1)}, bf16[2,256,1024]{2,1,0:T(8,128)(2,1)}) custom-call(s32[3]{0:T(128)S(1)} %pad_add_fusion.1.where_ref, bf16[512,2048]{1,0:T(8,128)(2,1)S(1)} %get-tuple-element.204.refs_0_, ...), custom_call_target="tpu_custom_call" | custom-call | flops 1 | bytes 1 | tf_op jit(solution)/shard_map/ffn_outer/pallas_call | solution.py:1011
  225.8 5.3 %middle.1 = (bf16[128,2048]{1,0:T(8,128)(2,1)S(1)}, f32[128,2048]{1,0:T(8,128)S(1)}, bf16[4,128,512]{2,1,0:T(8,128)(2,1)S(1)}, f32[1,2048]{1,0:T(1,128)S(1)}) custom-call(s32[3]{0:T(128)S(1)} %pad_add_fusion.1.where_ref, f32[128,2048]{1,0:T(8,128)S(1)} %get-tuple-element.172.middle_ref, bf16[512,2048]{1,0:T(8,128)(2,1)S(1)} %bitcast.108, ...), custom_call_target="tpu_custom_call" | custom-call | flops 1 | bytes 1 | tf_op jit(solution)/shard_map/middle/pallas_call | solution.py:472
  233.7 8.0 %all-to-all-start.3 = ((bf16[4,128,512]{2,1,0:T(8,128)(2,1)}), bf16[4,128,512]{2,1,0:T(8,128)(2,1)}, u32[]{:S(2)}, u32[]{:S(2)}) async-start(bf16[4,128,512]{2,1,0:T(8,128)(2,1)} %copy-done.44), calls=%async_computation.3 | async-start | bytes 1048576 | tf_op jit(solution)/shard_map/all_to_all | solution.py:1345
  241.7 8.4 %branch.1 = bf16[512,2048]{1,0:T(8,128)(2,1)S(1)} custom-call(s32[3]{0:T(128)S(1)} %pad_add_fusion.1.where_ref, bf16[512,2048]{1,0:T(8,128)(2,1)} %get-tuple-element.217.left_ref.refs_2_, bf16[2048,2048]{1,0:T(8,128)(2,1)} %right_ref.3), custom_call_target="tpu_custom_call" | custom-call | flops 1 | bytes 1 | tf_op jit(solution)/shard_map/branch/pallas_call | solution.py:1132
  254.6 10.2 %ffn_outer.5 = (bf16[2,256,1024]{2,1,0:T(8,128)(2,1)}, bf16[2,256,1024]{2,1,0:T(8,128)(2,1)}, bf16[2,256,1024]{2,1,0:T(8,128)(2,1)}, bf16[2,256,1024]{2,1,0:T(8,128)(2,1)}) custom-call(s32[3]{0:T(128)S(1)} %pad_add_fusion.1.where_ref, bf16[512,2048]{1,0:T(8,128)(2,1)S(1)} %copy-done.7, bf16[512,2048]{1,0:T(8,128)(2,1)S(1)} %copy-done.30, ...), custom_call_target="tpu_custom_call" | custom-call | flops 1 | bytes 1 | tf_op jit(solution)/shard_map/ffn_outer/pallas_call | solution.py:1011
  266.9 4.1 all-to-all-start.4
  271.3 7.5 %all-to-all-done.4 = bf16[4,512,128]{2,1,0:T(8,128)(2,1)} async-done(((bf16[4,512,128]{2,1,0:T(8,128)(2,1)}), bf16[4,512,128]{2,1,0:T(8,128)(2,1)}, u32[]{:S(2)}, u32[]{:S(2)}) %all-to-all-start.4) | async-done | bytes 524320 | tf_op jit(solution)/shard_map/all_to_all | solution.py:1221
  278.8 18.5 %attend_back.1 = (f32[2048,128]{1,0:T(8,128)S(1)}, f32[2048,256]{1,0:T(8,128)S(1)}, bf16[2048,256]{1,0:T(8,128)(2,1)S(1)}) custom-call(s32[16]{0:T(128)S(1)} %pad_add_fusion.2.slot_places, s32[8]{0:T(128)S(1)} %get-tuple-element.326.key_low, bf16[2048,384]{1,0:T(8,128)(2,1)} %bitcast.12.own_ref, bf16[2048,384]{1,0:T(8,128)(2,1)} %collective-permute-done.other_ref, ...), custom_call_target="tpu_custom_call" | custom-call | flops 1 | bytes 1 | tf_op jit(solution)/shard_map/attend_back/pallas_call | solution.py:452
  299.7 2.8 collective-permute-done.21.other_ref
  302.5 5.5 %turn.1 = bf16[2048,384]{1,0:T(8,128)(2,1)S(1)} custom-call(f32[2048,128]{1,0:T(8,128)} %copy-done.37, f32[2048,256]{1,0:T(8,128)} %copy-done.31, bf16[2048,256]{1,0:T(8,128)(2,1)} %collective-permute-done.21.other_ref, f32[2048,128]{1,0:T(8,128)} %get-tuple-element.233.cosine_ref, f32[2048,128]{1,0:T(8,128)} %get-tuple-element.234.sine_ref), custom_call_target="tpu_custom_call" | custom-call | flops 1 | bytes 1 | tf_op jit(solution)/shard_map/turn/pallas_call | solution.py:1165
  309.1 4.4 all-to-all-start.5
  317.4 16.0 %all-to-all-done.5.back_ref = bf16[4,512,384]{2,1,0:T(8,128)(2,1)} async-done(((bf16[4,512,384]{2,1,0:T(8,128)(2,1)}), bf16[4,512,384]{2,1,0:T(8,128)(2,1)}, u32[]{:S(2)}, u32[]{:S(2)}) %all-to-all-start.5) | async-done | bytes 1572896 | tf_op jit(solution)/shard_map/all_to_all | solution.py:1221
  333.4 8.5 %back.1 = (bf16[512,1536]{1,0:T(8,128)(2,1)S(1)}, f32[1,2048]{1,0:T(1,128)S(1)}, bf16[128,2048]{1,0:T(8,128)(2,1)S(1)}, bf16[128,2048]{1,0:T(8,128)(2,1)S(1)}, b...) custom-call(s32[3]{0:T(128)S(1)} %pad_add_fusion.1.where_ref, bf16[4,512,384]{2,1,0:T(8,128)(2,1)} %all-to-all-done.5.back_ref, ...), custom_call_target="tpu_custom_call" | custom-call | flops 1 | bytes 1 | tf_op jit(solution)/shard_map/back/pallas_call | solution.py:784
  344.0 4.6 collective-permute-start.23
  350.9 12.9 %collective-permute-done.23.got_up_ref = bf16[128,2048]{1,0:T(8,128)(2,1)S(1)} collective-permute-done((bf16[128,2048]{1,0:T(8,128)(2,1)S(1)}, bf16[128,2048]{1,0:T(8,128)(2,1)S(1)}, u32[]{:S(2)}, u32[]{:S(2)}) %collective-permute-start.23) | collective-permute-done | bytes 524320 | tf_op jit(solution)/shard_map/ppermute | solution.py:887
  368.9 5.2 %collective-permute-start.27 = (bf16[128,2048]{1,0:T(8,128)(2,1)}, bf16[128,2048]{1,0:T(8,128)(2,1)}, u32[]{:S(2)}, u32[]{:S(2)}) collective-permute-start(bf16[128,2048]{1,0:T(8,128)(2,1)} %get-tuple-element.248), channel_id=1, source_target_pairs={{0,1},{1,2},{4,5},{5,6},{8,9},{9,10},{12,13},{13,14},{16,17},{17,1... | collective-permute-start | bytes 1572872 | tf_op jit(solution)/shard_map/ppermute | solution.py:887
  375.6 7.5 %all_to_all.35 = f32[8,2,256]{2,1,0:T(2,128)S(1)} all-to-all(f32[8,2,256]{2,1,0:T(2,128)S(1)} %bitcast.128), channel_id=1, replica_groups=mesh['seq'=8,'tp'=4] {'seq'}, dimensions={0} | all-to-all | bytes 32768 | tf_op jit(solution)/shard_map/all_to_all | solution.py:1376
  391.3 7.3 %collective-permute-start.29 = (bf16[128,2048]{1,0:T(8,128)(2,1)S(1)}, bf16[128,2048]{1,0:T(8,128)(2,1)S(1)}, u32[]{:S(2)}, u32[]{:S(2)}) collective-permute-start(bf16[128,2048]{1,0:T(8,128)(2,1)S(1)} %get-tuple-element.258), channel_id=1, source_target_pairs={{0,1},{1,2},{2,3},{4,5},{5,6},{6,7},{8,9},{9,10},{10,11},{12,13},{... | collective-permute-start | bytes 1572872 | tf_op jit(solution)/shard_map/ppermute | solution.py:887
  400.1 9.1 %attn_outer.1 = (bf16[2,256,1024]{2,1,0:T(8,128)(2,1)}, bf16[2,256,1024]{2,1,0:T(8,128)(2,1)}, bf16[2,256,1024]{2,1,0:T(8,128)(2,1)}, bf16[2,256,1024]{2,1,0:T(8,128)(2,1)}) custom-call(s32[3]{0:T(128)S(1)} %pad_add_fusion.1.where_ref, bf16[512,2048]{1,0:T(8,128)(2,1)S(1)} %copy-done.23, bf16[512,2048]{1,0:T(8,128)(2,1)S(1)} %collective-permute-done.33.refs_1_, ...), custom_call_target="tpu_custom_call" | custom-call | flops 1 | bytes 1 | tf_op jit(solution)/shard_map/attn_outer/pallas_call | solution.py:1011
  409.3 4.3 collective-permute-done.30.above_ref
  421.1 21.3 %collective-permute-done.38.refs_1_ = bf16[2,256,1024]{2,1,0:T(8,128)(2,1)S(1)} collective-permute-done((bf16[2,256,1024]{2,1,0:T(8,128)(2,1)S(1)}, bf16[2,256,1024]{2,1,0:T(8,128)(2,1)S(1)}, u32[]{:S(2)}, u32[]{:S(2)}) %collective-permute-start.38) | collective-permute-done | bytes 1048608 | tf_op jit(solution)/shard_map/ppermute | solution.py:1037
  454.4 6.2 %collective-permute-done.45.refs_5_ = bf16[256,1024]{1,0:T(8,128)(2,1)S(1)} collective-permute-done((bf16[256,1024]{1,0:T(8,128)(2,1)S(1)}, bf16[256,1024]{1,0:T(8,128)(2,1)S(1)}, u32[]{:S(2)}, u32[]{:S(2)}) %collective-permute-start.45) | collective-permute-done | bytes 524320 | tf_op jit(solution)/shard_map/ppermute | solution.py:1037
  461.3 4.0 collective-permute-done.44.refs_2_
  465.3 2.8 collective-permute-done.43.refs_5_
  468.1 4.6 collective-permute-done.42.refs_2_
  478.0 3.5 widen_down.1
  481.5 3.3 widen_up.1
  484.9 3.3 widen_gate.1
  490.4 7.8 %collective-permute-done.47.refs_2_ = bf16[272,2048]{1,0:T(8,128)(2,1)S(1)} collective-permute-done((bf16[272,2048]{1,0:T(8,128)(2,1)S(1)}, bf16[272,2048]{1,0:T(8,128)(2,1)S(1)}, u32[]{:S(2)}, u32[]{:S(2)}) %collective-permute-start.47) | collective-permute-done | bytes 1114144 | tf_op jit(solution)/shard_map/ppermute | solution.py:888
  498.3 3.8 join.1
  (295 shorter events, 111.2 us)
Async XLA Ops:
  7.2 61.3 %all-gather.4.cloned.1.call-start = ((), (), s32[]{:S(2)}) async-start(), calls=%async_computation.8 | async-start | bytes 3276800 | tf_op jit(solution)/shard_map/all_gather | solution.py:1237
  21.9 29.5 %all-to-all-start = ((bf16[4,512,384]{2,1,0:T(8,128)(2,1)}), bf16[4,512,384]{2,1,0:T(8,128)(2,1)}, u32[]{:S(2)}, u32[]{:S(2)}) async-start(bf16[4,512,384]{2,1,0:T(8,128)(2,1)} %copy-done.34), calls=%async_computation | async-start | bytes 3145728 | tf_op jit(solution)/shard_map/all_to_all | solution.py:1221
  27.2 89.8 %all-gather.6.cloned.1.call-start = ((), (), s32[]{:S(2)}) async-start(), calls=%async_computation.9 | async-start | bytes 1966080 | tf_op jit(solution)/shard_map/all_gather | solution.py:1237
  73.3 44.5 %collective-permute-start.1 = (bf16[4,256,1280]{2,1,0:T(8,128)(2,1)}, bf16[4,256,1280]{2,1,0:T(8,128)(2,1)}, u32[]{:S(2)}, u32[]{:S(2)}) collective-permute-start(bf16[4,256,1280]{2,1,0:T(8,128)(2,1)} %bitcast.105), channel_id=1, source_target_pairs={{0,4},{4,0},{8,12},{12,8},{16,20},{20,16},{24,28},{28,24},{1,5},{5... | collective-permute-start | bytes 7864328 | tf_op jit(solution)/shard_map/ppermute | solution.py:1218
  81.6 35.4 %all-to-all-start.2 = ((bf16[4,128,512]{2,1,0:T(8,128)(2,1)}), bf16[4,128,512]{2,1,0:T(8,128)(2,1)S(1)}, u32[]{:S(2)}, u32[]{:S(2)}) async-start(bf16[4,128,512]{2,1,0:T(8,128)(2,1)} %pad_maximum_fusion.3), calls=%async_computation.2 | async-start | bytes 1048576 | tf_op jit(solution)/shard_map/all_to_all | solution.py:1292
  129.5 13.0 %collective-permute-start.4 = (bf16[128,2048]{1,0:T(8,128)(2,1)S(1)}, bf16[128,2048]{1,0:T(8,128)(2,1)S(1)}, u32[]{:S(2)}, u32[]{:S(2)}) collective-permute-start(bf16[128,2048]{1,0:T(8,128)(2,1)S(1)} %get-tuple-element.173.refs_0_), channel_id=1, source_target_pairs={{0,1},{1,2},{2,3},{4,5},{5,6},{6,7},{8,9},{9,10},{10,11},{12,13},{... | collective-permute-start | bytes 1572872 | tf_op jit(solution)/shard_map/ppermute | solution.py:887
  130.8 15.9 %collective-permute-start.3 = (bf16[128,2048]{1,0:T(8,128)(2,1)S(1)}, bf16[128,2048]{1,0:T(8,128)(2,1)S(1)}, u32[]{:S(2)}, u32[]{:S(2)}) collective-permute-start(bf16[128,2048]{1,0:T(8,128)(2,1)S(1)} %get-tuple-element.173.refs_0_), channel_id=1, source_target_pairs={{1,0},{2,1},{3,2},{5,4},{6,5},{7,6},{9,8},{10,9},{11,10},{13,12},{... | collective-permute-start | bytes 1572872 | tf_op jit(solution)/shard_map/ppermute | solution.py:888
  142.5 20.0 %collective-permute-start.5 = (bf16[128,2048]{1,0:T(8,128)(2,1)S(1)}, bf16[128,2048]{1,0:T(8,128)(2,1)S(1)}, u32[]{:S(2)}, u32[]{:S(2)}) collective-permute-start(bf16[128,2048]{1,0:T(8,128)(2,1)S(1)} %collective-permute-done.4.refs_2_.refs_1_), channel_id=1, source_target_pairs={{1,2},{2,3},{5,6},{6,7},{9,10},{10,11},{13,14},{14,15},{17,18},{18... | collective-permute-start | bytes 1572872 | tf_op jit(solution)/shard_map/ppermute | solution.py:887
  146.7 15.8 %collective-permute-start.6 = (bf16[128,2048]{1,0:T(8,128)(2,1)S(1)}, bf16[128,2048]{1,0:T(8,128)(2,1)S(1)}, u32[]{:S(2)}, u32[]{:S(2)}) collective-permute-start(bf16[128,2048]{1,0:T(8,128)(2,1)S(1)} %collective-permute-done.3.refs_1_.refs_0_), channel_id=1, source_target_pairs={{1,0},{2,1},{5,4},{6,5},{9,8},{10,9},{13,12},{14,13},{17,16},{18,1... | collective-permute-start | bytes 1572872 | tf_op jit(solution)/shard_map/ppermute | solution.py:888
  162.5 14.6 %collective-permute-start.7 = (bf16[128,2048]{1,0:T(8,128)(2,1)S(1)}, bf16[128,2048]{1,0:T(8,128)(2,1)S(1)}, u32[]{:S(2)}, u32[]{:S(2)}) collective-permute-start(bf16[128,2048]{1,0:T(8,128)(2,1)S(1)} %collective-permute-done.5.refs_1_), channel_id=1, source_target_pairs={{2,3},{6,7},{10,11},{14,15},{18,19},{22,23},{26,27},{30,31}} | collective-permute-start | bytes 1572872 | tf_op jit(solution)/shard_map/ppermute | solution.py:887
  163.2 15.0 %collective-permute-start.8 = (bf16[128,2048]{1,0:T(8,128)(2,1)S(1)}, bf16[128,2048]{1,0:T(8,128)(2,1)S(1)}, u32[]{:S(2)}, u32[]{:S(2)}) collective-permute-start(bf16[128,2048]{1,0:T(8,128)(2,1)S(1)} %collective-permute-done.6.refs_0_), channel_id=1, source_target_pairs={{1,0},{5,4},{9,8},{13,12},{17,16},{21,20},{25,24},{29,28}} | collective-permute-start | bytes 1572872 | tf_op jit(solution)/shard_map/ppermute | solution.py:888
  178.2 24.3 %collective-permute-start.10 = (bf16[128,2048]{1,0:T(8,128)(2,1)S(1)}, bf16[128,2048]{1,0:T(8,128)(2,1)S(1)}, u32[]{:S(2)}, u32[]{:S(2)}) collective-permute-start(bf16[128,2048]{1,0:T(8,128)(2,1)S(1)} %get-tuple-element.200), channel_id=1, source_target_pairs={{0,2},{1,3},{2,0},{3,1},{4,6},{5,7},{6,4},{7,5},{8,10},{9,11},{10,... | collective-permute-start | bytes 1572872 | tf_op jit(solution)/shard_map/ppermute | solution.py:1230
  180.0 22.6 %collective-permute-start.9 = (bf16[128,2048]{1,0:T(8,128)(2,1)S(1)}, bf16[128,2048]{1,0:T(8,128)(2,1)S(1)}, u32[]{:S(2)}, u32[]{:S(2)}) collective-permute-start(bf16[128,2048]{1,0:T(8,128)(2,1)S(1)} %get-tuple-element.199), channel_id=1, source_target_pairs={{0,1},{1,0},{2,3},{3,2},{4,5},{5,4},{6,7},{7,6},{8,9},{9,8},{10,11... | collective-permute-start | bytes 1572872 | tf_op jit(solution)/shard_map/ppermute | solution.py:1230
  192.6 12.6 %collective-permute-start.16 = (bf16[512,2048]{1,0:T(8,128)(2,1)S(1)}, bf16[512,2048]{1,0:T(8,128)(2,1)S(1)}, u32[]{:S(2)}, u32[]{:S(2)}) collective-permute-start(bf16[512,2048]{1,0:T(8,128)(2,1)S(1)} %get-tuple-element.211.refs_2_), channel_id=1, source_target_pairs={{0,4},{4,0},{8,12},{12,8},{16,20},{20,16},{24,28},{28,24},{1,5},{5... | collective-permute-start | bytes 6291464 | tf_op jit(solution)/shard_map/ppermute | solution.py:1218
  202.6 22.0 %collective-permute-start.19 = (bf16[512,2048]{1,0:T(8,128)(2,1)S(1)}, bf16[512,2048]{1,0:T(8,128)(2,1)S(1)}, u32[]{:S(2)}, u32[]{:S(2)}) collective-permute-start(bf16[512,2048]{1,0:T(8,128)(2,1)S(1)} %copy-done.6), channel_id=1, source_target_pairs={{0,4},{4,0},{8,12},{12,8},{16,20},{20,16},{24,28},{28,24},{1,5},{5... | collective-permute-start | bytes 6291464 | tf_op jit(solution)/shard_map/ppermute | solution.py:1218
  203.1 48.3 %collective-permute-start.20 = (bf16[512,2048]{1,0:T(8,128)(2,1)}, bf16[512,2048]{1,0:T(8,128)(2,1)}, u32[]{:S(2)}, u32[]{:S(2)}) collective-permute-start(bf16[512,2048]{1,0:T(8,128)(2,1)} %get-tuple-element.217.left_ref.refs_2_), channel_id=1, source_target_pairs={{0,4},{4,0},{8,12},{12,8},{16,20},{20,16},{24,28},{28,24},{1,5},{5... | collective-permute-start | bytes 6291464 | tf_op jit(solution)/shard_map/ppermute | solution.py:1218
  203.2 22.0 %collective-permute-start.11 = (bf16[128,2048]{1,0:T(8,128)(2,1)S(1)}, bf16[128,2048]{1,0:T(8,128)(2,1)S(1)}, u32[]{:S(2)}, u32[]{:S(2)}) collective-permute-start(bf16[128,2048]{1,0:T(8,128)(2,1)S(1)} %get-tuple-element.203), channel_id=1, source_target_pairs={{0,3},{1,2},{2,1},{3,0},{4,7},{5,6},{6,5},{7,4},{8,11},{9,10},{10,... | collective-permute-start | bytes 1572872 | tf_op jit(solution)/shard_map/ppermute | solution.py:1230
  213.3 51.5 %collective-permute-start.17 = (bf16[2,256,1024]{2,1,0:T(8,128)(2,1)}, bf16[2,256,1024]{2,1,0:T(8,128)(2,1)}, u32[]{:S(2)}, u32[]{:S(2)}) collective-permute-start(bf16[2,256,1024]{2,1,0:T(8,128)(2,1)} %get-tuple-element.212), channel_id=1, source_target_pairs={{0,8},{4,12},{8,0},{12,4},{16,24},{20,28},{24,16},{28,20},{1,9},{5... | collective-permute-start | bytes 3145736 | tf_op jit(solution)/shard_map/ppermute | solution.py:1037
  214.8 50.0 %collective-permute-start.18 = (bf16[2,256,1024]{2,1,0:T(8,128)(2,1)}, bf16[2,256,1024]{2,1,0:T(8,128)(2,1)}, u32[]{:S(2)}, u32[]{:S(2)}) collective-permute-start(bf16[2,256,1024]{2,1,0:T(8,128)(2,1)} %get-tuple-element.213), channel_id=1, source_target_pairs={{0,16},{4,20},{8,24},{12,28},{16,0},{20,4},{24,8},{28,12},{1,17},{... | collective-permute-start | bytes 3145736 | tf_op jit(solution)/shard_map/ppermute | solution.py:1037
  224.6 40.3 %collective-permute-start.14 = (bf16[2,256,1024]{2,1,0:T(8,128)(2,1)}, bf16[2,256,1024]{2,1,0:T(8,128)(2,1)}, u32[]{:S(2)}, u32[]{:S(2)}) collective-permute-start(bf16[2,256,1024]{2,1,0:T(8,128)(2,1)} %get-tuple-element.209), channel_id=1, source_target_pairs={{0,8},{4,12},{8,0},{12,4},{16,24},{20,28},{24,16},{28,20},{1,9},{5... | collective-permute-start | bytes 3145736 | tf_op jit(solution)/shard_map/ppermute | solution.py:1037
  225.2 39.7 %collective-permute-start.15 = (bf16[2,256,1024]{2,1,0:T(8,128)(2,1)}, bf16[2,256,1024]{2,1,0:T(8,128)(2,1)}, u32[]{:S(2)}, u32[]{:S(2)}) collective-permute-start(bf16[2,256,1024]{2,1,0:T(8,128)(2,1)} %get-tuple-element.210), channel_id=1, source_target_pairs={{0,16},{4,20},{8,24},{12,28},{16,0},{20,4},{24,8},{28,12},{1,17},{... | collective-permute-start | bytes 3145736 | tf_op jit(solution)/shard_map/ppermute | solution.py:1037
  233.7 31.1 %all-to-all-start.3 = ((bf16[4,128,512]{2,1,0:T(8,128)(2,1)}), bf16[4,128,512]{2,1,0:T(8,128)(2,1)}, u32[]{:S(2)}, u32[]{:S(2)}) async-start(bf16[4,128,512]{2,1,0:T(8,128)(2,1)} %copy-done.44), calls=%async_computation.3 | async-start | bytes 1048576 | tf_op jit(solution)/shard_map/all_to_all | solution.py:1345
  241.7 91.7 %reduce-scatter.2.cloned.1.call-start = ((), (), s32[]{:S(2)}) async-start(), calls=%async_computation.10 | async-start | bytes 2621440 | tf_op jit(solution)/shard_map/reduce_scatter | solution.py:1353
  271.0 112.1 %all-gather.8.cloned.1.call-start = ((), (), s32[]{:S(2)}) async-start(), calls=%async_computation.11 | async-start | bytes 2621440 | tf_op jit(solution)/shard_map/all_gather | solution.py:1363
  309.1 24.3 %all-to-all-start.5 = ((bf16[4,512,384]{2,1,0:T(8,128)(2,1)}), bf16[4,512,384]{2,1,0:T(8,128)(2,1)}, u32[]{:S(2)}, u32[]{:S(2)}) async-start(bf16[4,512,384]{2,1,0:T(8,128)(2,1)} %bitcast.112), calls=%async_computation.5 | async-start | bytes 3145728 | tf_op jit(solution)/shard_map/all_to_all | solution.py:1221
  342.0 24.6 %collective-permute-start.25 = (bf16[2,256,1024]{2,1,0:T(8,128)(2,1)S(1)}, bf16[2,256,1024]{2,1,0:T(8,128)(2,1)}, u32[]{:S(2)}, u32[]{:S(2)}) collective-permute-start(bf16[2,256,1024]{2,1,0:T(8,128)(2,1)S(1)} %copy-done.54), channel_id=1, source_target_pairs={{0,8},{4,12},{8,0},{12,4},{16,24},{20,28},{24,16},{28,20},{1,9},{5... | collective-permute-start | bytes 3145736 | tf_op jit(solution)/shard_map/ppermute | solution.py:1037
  343.5 24.2 %collective-permute-start.26 = (bf16[2,256,1024]{2,1,0:T(8,128)(2,1)S(1)}, bf16[2,256,1024]{2,1,0:T(8,128)(2,1)}, u32[]{:S(2)}, u32[]{:S(2)}) collective-permute-start(bf16[2,256,1024]{2,1,0:T(8,128)(2,1)S(1)} %copy-done.53), channel_id=1, source_target_pairs={{0,16},{4,20},{8,24},{12,28},{16,0},{20,4},{24,8},{28,12},{1,17},{... | collective-permute-start | bytes 3145736 | tf_op jit(solution)/shard_map/ppermute | solution.py:1037
  344.0 19.8 %collective-permute-start.23 = (bf16[128,2048]{1,0:T(8,128)(2,1)S(1)}, bf16[128,2048]{1,0:T(8,128)(2,1)S(1)}, u32[]{:S(2)}, u32[]{:S(2)}) collective-permute-start(bf16[128,2048]{1,0:T(8,128)(2,1)S(1)} %get-tuple-element.239.down_ref), channel_id=1, source_target_pairs={{0,1},{4,5},{8,9},{12,13},{16,17},{20,21},{24,25},{28,29}} | collective-permute-start | bytes 1572872 | tf_op jit(solution)/shard_map/ppermute | solution.py:887
  349.4 14.4 %collective-permute-start.24 = (bf16[128,2048]{1,0:T(8,128)(2,1)S(1)}, bf16[128,2048]{1,0:T(8,128)(2,1)S(1)}, u32[]{:S(2)}, u32[]{:S(2)}) collective-permute-start(bf16[128,2048]{1,0:T(8,128)(2,1)S(1)} %get-tuple-element.240.up_ref), channel_id=1, source_target_pairs={{3,2},{7,6},{11,10},{15,14},{19,18},{23,22},{27,26},{31,30}} | collective-permute-start | bytes 1572872 | tf_op jit(solution)/shard_map/ppermute | solution.py:888
  368.9 14.3 %collective-permute-start.27 = (bf16[128,2048]{1,0:T(8,128)(2,1)}, bf16[128,2048]{1,0:T(8,128)(2,1)}, u32[]{:S(2)}, u32[]{:S(2)}) collective-permute-start(bf16[128,2048]{1,0:T(8,128)(2,1)} %get-tuple-element.248), channel_id=1, source_target_pairs={{0,1},{1,2},{4,5},{5,6},{8,9},{9,10},{12,13},{13,14},{16,17},{17,1... | collective-permute-start | bytes 1572872 | tf_op jit(solution)/shard_map/ppermute | solution.py:887
  375.6 15.7 %collective-permute-start.34 = (bf16[512,2048]{1,0:T(8,128)(2,1)}, bf16[512,2048]{1,0:T(8,128)(2,1)}, u32[]{:S(2)}, u32[]{:S(2)}) collective-permute-start(bf16[512,2048]{1,0:T(8,128)(2,1)} %get-tuple-element.267.refs_4_), channel_id=1, source_target_pairs={{0,4},{4,0},{8,12},{12,8},{16,20},{20,16},{24,28},{28,24},{1,5},{5... | collective-permute-start | bytes 6291464 | tf_op jit(solution)/shard_map/ppermute | solution.py:1218
  383.1 16.9 %collective-permute-start.33 = (bf16[512,2048]{1,0:T(8,128)(2,1)}, bf16[512,2048]{1,0:T(8,128)(2,1)S(1)}, u32[]{:S(2)}, u32[]{:S(2)}) collective-permute-start(bf16[512,2048]{1,0:T(8,128)(2,1)} %all-gather.8.cloned.1.call-done.refs_0_), channel_id=1, source_target_pairs={{0,4},{4,0},{8,12},{12,8},{16,20},{20,16},{24,28},{28,24},{1,5},{5... | collective-permute-start | bytes 6291464 | tf_op jit(solution)/shard_map/ppermute | solution.py:1218
  383.2 15.4 %collective-permute-start.35 = (bf16[512,1536]{1,0:T(8,128)(2,1)}, bf16[512,1536]{1,0:T(8,128)(2,1)S(1)}, u32[]{:S(2)}, u32[]{:S(2)}) collective-permute-start(bf16[512,1536]{1,0:T(8,128)(2,1)} %copy-done.32), channel_id=1, source_target_pairs={{0,4},{4,0},{8,12},{12,8},{16,20},{20,16},{24,28},{28,24},{1,5},{5... | collective-permute-start | bytes 4718600 | tf_op jit(solution)/shard_map/ppermute | solution.py:1218
  385.3 24.0 %collective-permute-start.32 = (bf16[256,1024]{1,0:T(8,128)(2,1)S(1)}, bf16[256,1024]{1,0:T(8,128)(2,1)S(1)}, u32[]{:S(2)}, u32[]{:S(2)}) collective-permute-start(bf16[256,1024]{1,0:T(8,128)(2,1)S(1)} %fusion.1), channel_id=1, source_target_pairs={{0,8},{4,12},{8,0},{12,4},{16,24},{20,28},{24,16},{28,20},{1,9},{5... | collective-permute-start | bytes 1572872 | tf_op jit(solution)/shard_map/ppermute | solution.py:1037
  387.6 21.7 %collective-permute-start.31 = (bf16[256,1024]{1,0:T(8,128)(2,1)S(1)}, bf16[256,1024]{1,0:T(8,128)(2,1)S(1)}, u32[]{:S(2)}, u32[]{:S(2)}) collective-permute-start(bf16[256,1024]{1,0:T(8,128)(2,1)S(1)} %fusion), channel_id=1, source_target_pairs={{0,16},{4,20},{8,24},{12,28},{16,0},{20,4},{24,8},{28,12},{1,17},{... | collective-permute-start | bytes 1572872 | tf_op jit(solution)/shard_map/ppermute | solution.py:1037
  391.3 18.1 %collective-permute-start.29 = (bf16[128,2048]{1,0:T(8,128)(2,1)S(1)}, bf16[128,2048]{1,0:T(8,128)(2,1)S(1)}, u32[]{:S(2)}, u32[]{:S(2)}) collective-permute-start(bf16[128,2048]{1,0:T(8,128)(2,1)S(1)} %get-tuple-element.258), channel_id=1, source_target_pairs={{0,1},{1,2},{2,3},{4,5},{5,6},{6,7},{8,9},{9,10},{10,11},{12,13},{... | collective-permute-start | bytes 1572872 | tf_op jit(solution)/shard_map/ppermute | solution.py:887
  398.6 15.0 %collective-permute-start.30 = (bf16[128,2048]{1,0:T(8,128)(2,1)S(1)}, bf16[128,2048]{1,0:T(8,128)(2,1)S(1)}, u32[]{:S(2)}, u32[]{:S(2)}) collective-permute-start(bf16[128,2048]{1,0:T(8,128)(2,1)S(1)} %get-tuple-element.259), channel_id=1, source_target_pairs={{1,0},{2,1},{3,2},{5,4},{6,5},{7,6},{9,8},{10,9},{11,10},{13,12},{... | collective-permute-start | bytes 1572872 | tf_op jit(solution)/shard_map/ppermute | solution.py:888
  415.3 28.0 %collective-permute-start.36 = (bf16[272,2048]{1,0:T(8,128)(2,1)S(1)}, bf16[272,2048]{1,0:T(8,128)(2,1)S(1)}, u32[]{:S(2)}, u32[]{:S(2)}) collective-permute-start(bf16[272,2048]{1,0:T(8,128)(2,1)S(1)} %tokens.1.own_ref), channel_id=1, source_target_pairs={{0,1},{1,2},{2,3},{4,5},{5,6},{6,7},{8,9},{9,10},{10,11},{12,13},{... | collective-permute-start | bytes 3342344 | tf_op jit(solution)/shard_map/ppermute | solution.py:887
  417.7 26.6 %collective-permute-start.37 = (bf16[272,2048]{1,0:T(8,128)(2,1)S(1)}, bf16[272,2048]{1,0:T(8,128)(2,1)S(1)}, u32[]{:S(2)}, u32[]{:S(2)}) collective-permute-start(bf16[272,2048]{1,0:T(8,128)(2,1)S(1)} %tokens.1.own_ref), channel_id=1, source_target_pairs={{1,0},{2,1},{3,2},{5,4},{6,5},{7,6},{9,8},{10,9},{11,10},{13,12},{... | collective-permute-start | bytes 3342344 | tf_op jit(solution)/shard_map/ppermute | solution.py:888
  419.0 23.4 %collective-permute-start.38 = (bf16[2,256,1024]{2,1,0:T(8,128)(2,1)S(1)}, bf16[2,256,1024]{2,1,0:T(8,128)(2,1)S(1)}, u32[]{:S(2)}, u32[]{:S(2)}) collective-permute-start(bf16[2,256,1024]{2,1,0:T(8,128)(2,1)S(1)} %copy-done.56), channel_id=1, source_target_pairs={{0,8},{4,12},{8,0},{12,4},{16,24},{20,28},{24,16},{28,20},{1,9},{5... | collective-permute-start | bytes 3145736 | tf_op jit(solution)/shard_map/ppermute | solution.py:1037
  420.1 23.2 %collective-permute-start.39 = (bf16[2,256,1024]{2,1,0:T(8,128)(2,1)S(1)}, bf16[2,256,1024]{2,1,0:T(8,128)(2,1)S(1)}, u32[]{:S(2)}, u32[]{:S(2)}) collective-permute-start(bf16[2,256,1024]{2,1,0:T(8,128)(2,1)S(1)} %copy-done.55), channel_id=1, source_target_pairs={{0,16},{4,20},{8,24},{12,28},{16,0},{20,4},{24,8},{28,12},{1,17},{... | collective-permute-start | bytes 3145736 | tf_op jit(solution)/shard_map/ppermute | solution.py:1037
  445.7 14.9 %collective-permute-start.45 = (bf16[256,1024]{1,0:T(8,128)(2,1)S(1)}, bf16[256,1024]{1,0:T(8,128)(2,1)S(1)}, u32[]{:S(2)}, u32[]{:S(2)}) collective-permute-start(bf16[256,1024]{1,0:T(8,128)(2,1)S(1)} %fusion.5), channel_id=1, source_target_pairs={{0,8},{4,12},{8,0},{12,4},{16,24},{20,28},{24,16},{28,20},{1,9},{5... | collective-permute-start | bytes 1572872 | tf_op jit(solution)/shard_map/ppermute | solution.py:1037
  447.0 25.8 %collective-permute-start.40 = (bf16[272,2048]{1,0:T(8,128)(2,1)S(1)}, bf16[272,2048]{1,0:T(8,128)(2,1)S(1)}, u32[]{:S(2)}, u32[]{:S(2)}) collective-permute-start(bf16[272,2048]{1,0:T(8,128)(2,1)S(1)} %collective-permute-done.36.refs_3_), channel_id=1, source_target_pairs={{1,2},{2,3},{5,6},{6,7},{9,10},{10,11},{13,14},{14,15},{17,18},{18... | collective-permute-start | bytes 3342344 | tf_op jit(solution)/shard_map/ppermute | solution.py:887
  447.7 25.6 %collective-permute-start.41 = (bf16[272,2048]{1,0:T(8,128)(2,1)S(1)}, bf16[272,2048]{1,0:T(8,128)(2,1)S(1)}, u32[]{:S(2)}, u32[]{:S(2)}) collective-permute-start(bf16[272,2048]{1,0:T(8,128)(2,1)S(1)} %collective-permute-done.37.refs_0_), channel_id=1, source_target_pairs={{1,0},{2,1},{5,4},{6,5},{9,8},{10,9},{13,12},{14,13},{17,16},{18,1... | collective-permute-start | bytes 3342344 | tf_op jit(solution)/shard_map/ppermute | solution.py:888
  450.3 14.9 %collective-permute-start.44 = (bf16[256,1024]{1,0:T(8,128)(2,1)S(1)}, bf16[256,1024]{1,0:T(8,128)(2,1)S(1)}, u32[]{:S(2)}, u32[]{:S(2)}) collective-permute-start(bf16[256,1024]{1,0:T(8,128)(2,1)S(1)} %fusion.4), channel_id=1, source_target_pairs={{0,16},{4,20},{8,24},{12,28},{16,0},{20,4},{24,8},{28,12},{1,17},{... | collective-permute-start | bytes 1572872 | tf_op jit(solution)/shard_map/ppermute | solution.py:1037
  452.3 15.8 %collective-permute-start.43 = (bf16[256,1024]{1,0:T(8,128)(2,1)S(1)}, bf16[256,1024]{1,0:T(8,128)(2,1)S(1)}, u32[]{:S(2)}, u32[]{:S(2)}) collective-permute-start(bf16[256,1024]{1,0:T(8,128)(2,1)S(1)} %fusion.3), channel_id=1, source_target_pairs={{0,8},{4,12},{8,0},{12,4},{16,24},{20,28},{24,16},{28,20},{1,9},{5... | collective-permute-start | bytes 1572872 | tf_op jit(solution)/shard_map/ppermute | solution.py:1037
  473.3 17.1 %collective-permute-start.46 = (bf16[272,2048]{1,0:T(8,128)(2,1)S(1)}, bf16[272,2048]{1,0:T(8,128)(2,1)S(1)}, u32[]{:S(2)}, u32[]{:S(2)}) collective-permute-start(bf16[272,2048]{1,0:T(8,128)(2,1)S(1)} %collective-permute-done.40.refs_4_), channel_id=1, source_target_pairs={{2,3},{6,7},{10,11},{14,15},{18,19},{22,23},{26,27},{30,31}} | collective-permute-start | bytes 3342344 | tf_op jit(solution)/shard_map/ppermute | solution.py:887
  474.0 24.3 %collective-permute-start.47 = (bf16[272,2048]{1,0:T(8,128)(2,1)S(1)}, bf16[272,2048]{1,0:T(8,128)(2,1)S(1)}, u32[]{:S(2)}, u32[]{:S(2)}) collective-permute-start(bf16[272,2048]{1,0:T(8,128)(2,1)S(1)} %collective-permute-done.41.refs_1_), channel_id=1, source_target_pairs={{1,0},{5,4},{9,8},{13,12},{17,16},{21,20},{25,24},{29,28}} | collective-permute-start | bytes 3342344 | tf_op jit(solution)/shard_map/ppermute | solution.py:888
  (69 other events, 669.4 us)
Sparse Core Ops, SparseCore 0:
  10.2 57.4 all-gather.3
  69.9 47.0 all-gather.5
  265.0 44.3 reduce-scatter.1
  310.9 46.2 all-gather.7
